TPU v7x, 32 devices: a whole 2x2x4 slice. The times are simulated.
32 devices in a mesh: dp: 8 (over z, y), bfly: 4 (over x, core).
Axes of the slice: x: 2, y: 2, z: 4, core: 2. Of those that a mesh axis runs over, the one named last changes fastest.
Arguments:
- tokens: bfloat16 [2048, 12288], P('dp', 'bfly'), may hold values from -6 to 6
- grad_out: bfloat16 [2048, 12288], P('dp', 'bfly'), may hold values from -6 to 6
- weight_a: bfloat16 [48, 256, 512], P('bfly', 'dp'), may hold values from -0.375 to 0.375
- weight_b: bfloat16 [96, 256, 256], P('bfly', 'dp'), may hold values from -0.375 to 0.375
- weight_c: bfloat16 [96, 256, 256], P('bfly', 'dp'), may hold values from -0.375 to 0.375
- weight_e: bfloat16 [48, 512, 256], P('bfly', 'dp'), may hold values from -0.25 to 0.25
Outputs:
- output: bfloat16 [2048, 12288], P('dp', 'bfly')
- grad_in: bfloat16 [2048, 12288], P('dp', 'bfly')
- grad_a: float32 [48, 256, 512], P('bfly', 'dp')
- grad_b: float32 [96, 256, 256], P('bfly', 'dp')
- grad_c: float32 [96, 256, 256], P('bfly', 'dp')
- grad_e: float32 [48, 512, 256], P('bfly', 'dp')
All inputs are finite; a program needn't handle non-finite values.
Results may differ from a plain program's by a relative error of at most 0.03.
Values may be sent and summed in bfloat16 or wider, within the bound.
No kernel may reach another device: no remote copies, remote signals or barrier semaphores. Data moves between devices by JAX's collectives and lax.ppermute only.
A program may use at most 128 MiB of HBM per device.

v0:
```python
import jax
import jax.numpy as jnp
from jax import lax
from jax.sharding import PartitionSpec as P

BLK = 256


gelu_scale = 0.7978845608028654


def gelu_pair(hidden):
    inner_arg = gelu_scale * (hidden + 0.044715 * hidden * hidden * hidden)
    tangent = jnp.tanh(inner_arg)
    gelu_value = 0.5 * hidden * (1.0 + tangent)
    gelu_slope = 0.5 * (1.0 + tangent) + 0.5 * hidden * (1.0 - tangent * tangent) * gelu_scale * (
        1.0 + 3.0 * 0.044715 * hidden * hidden
    )
    return (gelu_value, gelu_slope)


def regroup(parcels, group_count, after_fns):
    parcel_count = len(parcels)
    local_blocks, block_width, token_count = parcels[0].shape
    sub_width = block_width // group_count
    stacked = jnp.stack(parcels, axis=0).reshape(
        parcel_count, local_blocks, group_count, sub_width, token_count
    )
    arrived = lax.all_to_all(stacked, "bfly", split_axis=2, concat_axis=2, tiled=True)
    flat_results = []
    piece = arrived[0].reshape(local_blocks, block_width, arrived.shape[4])
    flat_results.extend(after_fns[0](piece))
    return tuple(flat_results)


def per_device(tokens, grad_out, weight_a, weight_b, weight_c, weight_e):
    group_count = lax.axis_size("bfly")
    full_a, full_b, full_c, full_e = (
        lax.all_gather(weight_a, "dp", axis=1, tiled=True),
        lax.all_gather(weight_b, "dp", axis=1, tiled=True),
        lax.all_gather(weight_c, "dp", axis=1, tiled=True),
        lax.all_gather(weight_e, "dp", axis=1, tiled=True),
    )
    token_count = tokens.shape[0]
    inner_blocks = full_a.shape[0]
    spread_width = full_a.shape[2]
    local_blocks = full_b.shape[0]
    inputs = tokens.reshape(token_count, inner_blocks, BLK).transpose(1, 2, 0)
    upstream = grad_out.reshape(token_count, inner_blocks, BLK).transpose(1, 2, 0)
    spread = jnp.einsum("kit,kio->kot", inputs, full_a, preferred_element_type=jnp.float32)
    spread = spread.astype(jnp.bfloat16).reshape(local_blocks, BLK, token_count)
    back_out = jnp.einsum("kjt,koj->kot", upstream, full_e, preferred_element_type=jnp.float32)
    back_out = back_out.astype(jnp.bfloat16).reshape(local_blocks, BLK, token_count)

    def up_second(permuted):
        return (
            permuted,
            jnp.einsum("qit,qij->qjt", permuted, full_b, preferred_element_type=jnp.float32),
        )

    def back_second(back_mid):
        return (
            back_mid,
            jnp.einsum("qjt,qij->qit", back_mid, full_c, preferred_element_type=jnp.float32),
        )

    def down_second(returned):
        wide_view = returned.reshape(inner_blocks, spread_width, returned.shape[2])
        return (
            returned,
            jnp.einsum("kot,koj->kjt", wide_view, full_e, preferred_element_type=jnp.float32),
        )

    def back_last(back_spread):
        wide_view = back_spread.reshape(inner_blocks, spread_width, back_spread.shape[2])
        return (
            back_spread,
            jnp.einsum("kot,kio->kit", wide_view, full_a, preferred_element_type=jnp.float32),
        )

    permuted, hidden = regroup((spread,), group_count, (up_second,))
    gelu_value, gelu_slope = gelu_pair(hidden)
    active = gelu_value.astype(jnp.bfloat16)
    narrowed = jnp.einsum(
        "qit,qij->qjt", active, full_c, preferred_element_type=jnp.float32
    ).astype(jnp.bfloat16)
    returned, output = regroup((narrowed,), group_count, (down_second,))
    back_mid, back_act = regroup((back_out,), group_count, (back_second,))
    back_hidden = (back_act * gelu_slope).astype(jnp.bfloat16)
    back_first = jnp.einsum(
        "qjt,qij->qit", back_hidden, full_b, preferred_element_type=jnp.float32
    ).astype(jnp.bfloat16)
    back_spread, back_input = regroup((back_first,), group_count, (back_last,))
    spread_back = back_spread.reshape(inner_blocks, spread_width, token_count)
    returned_wide = returned.reshape(inner_blocks, spread_width, token_count)
    part_a = jnp.einsum("kit,kot->kio", inputs, spread_back, preferred_element_type=jnp.float32)
    part_b = jnp.einsum("qit,qjt->qij", permuted, back_hidden, preferred_element_type=jnp.float32)
    part_c = jnp.einsum("qit,qjt->qij", active, back_mid, preferred_element_type=jnp.float32)
    part_e = jnp.einsum("kot,kjt->koj", returned_wide, upstream, preferred_element_type=jnp.float32)
    grad_a, grad_b, grad_c, grad_e = (
        lax.psum_scatter(part_a.astype(jnp.bfloat16), "dp", scatter_dimension=1, tiled=True).astype(
            jnp.float32
        ),
        lax.psum_scatter(part_b.astype(jnp.bfloat16), "dp", scatter_dimension=1, tiled=True).astype(
            jnp.float32
        ),
        lax.psum_scatter(part_c.astype(jnp.bfloat16), "dp", scatter_dimension=1, tiled=True).astype(
            jnp.float32
        ),
        lax.psum_scatter(part_e.astype(jnp.bfloat16), "dp", scatter_dimension=1, tiled=True).astype(
            jnp.float32
        ),
    )
    output = output.astype(jnp.bfloat16).transpose(2, 0, 1).reshape(token_count, inner_blocks * BLK)
    grad_in = (
        back_input.astype(jnp.bfloat16).transpose(2, 0, 1).reshape(token_count, inner_blocks * BLK)
    )
    return (output, grad_in, grad_a, grad_b, grad_c, grad_e)


def solution(mesh):
    in_specs = (
        P("dp", "bfly"),
        P("dp", "bfly"),
        P("bfly", "dp", None),
        P("bfly", "dp", None),
        P("bfly", "dp", None),
        P("bfly", "dp", None),
    )
    out_specs = (
        P("dp", "bfly"),
        P("dp", "bfly"),
        P("bfly", "dp", None),
        P("bfly", "dp", None),
        P("bfly", "dp", None),
        P("bfly", "dp", None),
    )
    return jax.shard_map(
        per_device, mesh=mesh, in_specs=in_specs, out_specs=out_specs, check_vma=False
    )
```

profile of v0, /device:TPU:0, one launch (start us, length us, event | category | flops | bytes accessed | tf_op | source)
XLA Modules:
  0.0 599.6 jit_solution(6045464597825398712)
XLA Ops:
  11.7 61.7 %all-gather.5.cloned.1.call-done = bf16[12,256,512]{2,1,0:T(8,128)(2,1)} async-done(((bf16[12,32,512]{2,1,0:T(8,128)(2,1)}), bf16[12,256,512]{2,1,0:T(8,128)(2,1)}) %all-gather.5.cloned.1.call-update) | async-done | bytes 3145744 | tf_op jit(solution)/shard_map/all_gather | solution.py:39
  73.4 3.0 convolution_convert_fusion.2
  78.3 4.8 all-to-all-start
  83.9 50.9 %all-gather.11.cloned.1.call-done = bf16[12,512,256]{2,1,0:T(8,128)(2,1)} async-done(((bf16[12,64,256]{2,1,0:T(8,128)(2,1)}), bf16[12,512,256]{2,1,0:T(8,128)(2,1)}) %all-gather.11.cloned.1.call-update) | async-done | bytes 3145744 | tf_op jit(solution)/shard_map/all_gather | solution.py:42
  134.8 2.9 convolution_convert_fusion.1
  137.7 2.1 copy.44
  139.8 4.7 all-to-all-start.2
  144.5 2.1 copy.38
  146.6 34.8 %all-to-all-done.2 = bf16[1,24,4,64,256]{4,3,1,0,2:T(8,128)(2,1)} async-done(((bf16[1,24,4,64,256]{4,3,1,0,2:T(8,128)(2,1)}), bf16[1,24,4,64,256]{4,3,1,0,2:T(8,128)(2,1)}, u32[]{:S(2)}, u32[]{:S(2)}) %all-to-all-start.2) | async-done | bytes 3145760 | tf_op jit(solution)/shard_map/all_to_all | solution.py:29
  181.5 4.0 copy.45
  185.5 10.7 %all-gather.7.cloned.1.call-done = bf16[24,256,256]{2,1,0:T(8,128)(2,1)} async-done(((bf16[24,32,256]{2,1,0:T(8,128)(2,1)}), bf16[24,256,256]{2,1,0:T(8,128)(2,1)}) %all-gather.7.cloned.1.call-update) | async-done | bytes 3145744 | tf_op jit(solution)/shard_map/all_gather | solution.py:40
  196.1 5.6 fusion.7
  201.7 55.6 %all-gather.9.cloned.1.call-done = bf16[24,256,256]{2,1,0:T(8,128)(2,1)} async-done(((bf16[24,32,256]{2,1,0:T(8,128)(2,1)}), bf16[24,256,256]{2,1,0:T(8,128)(2,1)}) %all-gather.9.cloned.1.call-update) | async-done | bytes 3145744 | tf_op jit(solution)/shard_map/all_gather | solution.py:41
  257.4 8.4 %fusion.6 = bf16[24,256,256]{1,2,0:T(8,128)(2,1)S(1)} fusion(f32[24,256,256]{2,1,0:T(8,128)} %fusion.7, bf16[24,256,256]{2,1,0:T(8,128)(2,1)} %bitcast.79, bf16[24,256,256]{2,1,0:T(8,128)(2,1)} %all-gather.9.cloned.1.call-done), kind=kOutput, calls=%fused_computation.8 | convolution fusion | flops 835190784 | bytes 15728640 | tf_op jit(solution)/shard_map/qjt,qij->qit/dot_general | solution.py:64
  267.4 2.7 convolution_convert_fusion.4
  272.0 7.0 %convolution_convert_fusion.3 = bf16[24,256,256]{2,1,0:T(8,128)(2,1)} fusion(bf16[24,256,256]{2,1,0:T(8,128)(2,1)S(1)} %bitcast.80, f32[24,256,256]{2,1,0:T(8,128)} %fusion.7), kind=kOutput, calls=%fused_computation.15 | convolution fusion | flops 821035008 | bytes 12582912 | tf_op jit(solution)/shard_map/qit,qjt->qij/dot_general | solution.py:98
  280.8 2.9 convolution_convert_fusion.5
  284.2 39.5 %all_to_all.20 = bf16[1,24,4,64,256]{4,3,1,0,2:T(8,128)(2,1)S(1)} all-to-all(bf16[1,24,4,64,256]{4,3,1,0,2:T(8,128)(2,1)S(1)} %copy.48), channel_id=1, replica_groups=mesh['dp'=8,'bfly'=4] {'bfly'}, dimensions={2} | all-to-all | bytes 6291456 | tf_op jit(solution)/shard_map/all_to_all | solution.py:29
  325.0 2.7 convert_bitcast_fusion
  327.7 7.8 %copy.50 = bf16[12,256,512]{2,0,1:T(8,128)(2,1)} copy(bf16[12,256,512]{1,2,0:T(8,128)(2,1)} %convert_bitcast_fusion) | data formatting | bytes 6291456 | tf_op jit(solution)/shard_map/convert_element_type | solution.py:101
  335.6 6.6 %convolution_convert_fusion.6 = bf16[24,256,256]{1,2,0:T(8,128)(2,1)S(1)} fusion(bf16[24,256,256]{2,1,0:T(8,128)(2,1)} %all-gather.9.cloned.1.call-done, f32[24,256,256]{2,1,0:T(8,128)} %fusion.7), kind=kOutput, calls=%fused_computation.18 | convolution fusion | flops 821035008 | bytes 12582912 | tf_op jit(solution)/shard_map/qit,qij->qjt/dot_general | solution.py:84
  342.4 39.4 %all_to_all.21 = bf16[1,24,4,64,256]{4,3,1,0,2:T(8,128)(2,1)S(1)} all-to-all(bf16[1,24,4,64,256]{4,3,1,0,2:T(8,128)(2,1)S(1)} %copy.41), channel_id=1, replica_groups=mesh['dp'=8,'bfly'=4] {'bfly'}, dimensions={2} | all-to-all | bytes 6291456 | tf_op jit(solution)/shard_map/all_to_all | solution.py:29
  383.9 2.6 convolution_convert_fusion
  386.6 5.1 convolution_convert_fusion.8
  391.7 2.6 copy.53
  394.3 4.0 convolution_convert_fusion.7
  398.3 2.6 copy.54
  400.9 2.0 convert_element_type.81
  402.8 18.3 %reduce-scatter.9.cloned.1.call-done = bf16[24,32,256]{2,1,0:T(8,128)(2,1)} async-done(((bf16[24,256,256]{2,1,0:T(8,128)(2,1)}), bf16[24,32,256]{2,1,0:T(8,128)(2,1)}) %reduce-scatter.9.cloned.1.call-update) | async-done | bytes 393232 | tf_op jit(solution)/shard_map/reduce_scatter | solution.py:107
  423.1 88.9 %reduce-scatter.5.cloned.1.call-done = bf16[12,32,512]{2,0,1:T(8,128)(2,1)} async-done(((bf16[12,256,512]{2,0,1:T(8,128)(2,1)}), bf16[12,32,512]{2,0,1:T(8,128)(2,1)}) %reduce-scatter.5.cloned.1.call-update) | async-done | bytes 393232 | tf_op jit(solution)/shard_map/reduce_scatter | solution.py:101
  512.0 2.2 copy.55
  514.2 76.7 %reduce-scatter.11.cloned.1.call-done = bf16[12,64,256]{2,1,0:T(8,128)(2,1)} async-done(((bf16[12,512,256]{2,1,0:T(8,128)(2,1)}), bf16[12,64,256]{2,1,0:T(8,128)(2,1)}) %reduce-scatter.11.cloned.1.call-update) | async-done | bytes 393232 | tf_op jit(solution)/shard_map/reduce_scatter | solution.py:110
  (45 shorter events, 20.5 us)
Async XLA Ops:
  7.2 66.3 %all-gather.5.cloned.1.call-start = ((), (), s32[]{:S(2)}) async-start(), calls=%async_computation.8 | async-start | bytes 3538944 | tf_op jit(solution)/shard_map/all_gather | solution.py:39
  7.9 126.9 %all-gather.11.cloned.1.call-start = ((), (), s32[]{:S(2)}) async-start(), calls=%async_computation.11 | async-start | bytes 3538944 | tf_op jit(solution)/shard_map/all_gather | solution.py:42
  8.6 187.5 %all-gather.7.cloned.1.call-start = ((), (), s32[]{:S(2)}) async-start(), calls=%async_computation.9 | async-start | bytes 3538944 | tf_op jit(solution)/shard_map/all_gather | solution.py:40
  9.4 248.0 %all-gather.9.cloned.1.call-start = ((), (), s32[]{:S(2)}) async-start(), calls=%async_computation.10 | async-start | bytes 3538944 | tf_op jit(solution)/shard_map/all_gather | solution.py:41
  11.7 64.8 %copy-start.3 = (bf16[256,3072]{0,1:T(8,128)(2,1)}, bf16[256,3072]{0,1:T(8,128)(2,1)S(1)}, u32[]{:S(2)}) copy-start(bf16[256,3072]{0,1:T(8,128)(2,1)S(1)} %copy.36) | copy-start | bytes 4718596
  78.3 4.8 copy-start.8
  78.3 61.4 %all-to-all-start = ((bf16[1,24,4,64,256]{4,3,1,0,2:T(8,128)(2,1)}), bf16[1,24,4,64,256]{4,3,1,0,2:T(8,128)(2,1)}, u32[]{:S(2)}, u32[]{:S(2)}) async-start(bf16[1,24,4,64,256]{4,3,1,0,2:T(8,128)(2,1)} %copy.37), calls=%async_computation | async-start | bytes 6291456 | tf_op jit(solution)/shard_map/all_to_all | solution.py:29
  83.9 53.8 %copy-start.1 = (bf16[256,3072]{0,1:T(8,128)(2,1)}, bf16[256,3072]{0,1:T(8,128)(2,1)S(1)}, u32[]{:S(2)}) copy-start(bf16[256,3072]{0,1:T(8,128)(2,1)S(1)} %copy.43) | copy-start | bytes 4718596
  139.8 41.7 %all-to-all-start.2 = ((bf16[1,24,4,64,256]{4,3,1,0,2:T(8,128)(2,1)}), bf16[1,24,4,64,256]{4,3,1,0,2:T(8,128)(2,1)}, u32[]{:S(2)}, u32[]{:S(2)}) async-start(bf16[1,24,4,64,256]{4,3,1,0,2:T(8,128)(2,1)} %copy.44), calls=%async_computation.2 | async-start | bytes 6291456 | tf_op jit(solution)/shard_map/all_to_all | solution.py:29
  144.5 256.4 %reduce-scatter.7.cloned.1.call-start = ((), (), s32[]{:S(2)}) async-start(), calls=%async_computation.13 | async-start | bytes 3538944 | tf_op jit(solution)/shard_map/reduce_scatter | solution.py:104
  265.7 1.7 copy-start.6
  270.1 1.9 copy-start.7
  270.1 151.0 %reduce-scatter.9.cloned.1.call-start = ((), (), s32[]{:S(2)}) async-start(), calls=%async_computation.14 | async-start | bytes 3538944 | tf_op jit(solution)/shard_map/reduce_scatter | solution.py:107
  279.0 1.9 copy-start.5
  279.0 233.0 %reduce-scatter.5.cloned.1.call-start = ((), (), s32[]{:S(2)}) async-start(), calls=%async_computation.12 | async-start | bytes 4718592 | tf_op jit(solution)/shard_map/reduce_scatter | solution.py:101
  323.6 1.4 copy-start.4
  335.5 255.3 %reduce-scatter.11.cloned.1.call-start = ((), (), s32[]{:S(2)}) async-start(), calls=%async_computation.15 | async-start | bytes 3538944 | tf_op jit(solution)/shard_map/reduce_scatter | solution.py:110
  381.9 2.1 copy-start.2
  382.3 1.6 copy-start
Sparse Core Ops, SparseCore 0:
  10.2 63.2 all-gather.4
  75.6 59.1 all-gather.10
  137.0 59.1 all-gather.6
  198.2 59.1 all-gather.8
  270.2 73.3 reduce-scatter.6
  347.1 73.9 reduce-scatter.8
  424.8 87.2 reduce-scatter.4
  516.1 74.7 reduce-scatter.10
where the time goes:
time: 601 us; the launch traced here: 600 us
  waiting for transfers between devices  400 us (67%)
  blocking collectives  78.9 us (13%)
  matrix products  53.5 us (9%)
  local copies, waits for them, and re-layouts  36.8 us (6%)
  between operations  14.3 us (2%)
  starting transfers between devices  10 us (2%)
    reduce_scatter x1, waiting for transfers between devices, per_device(): lax.psum_scatter(part_a.astype(jnp.bfloat16), 'dp', scatter_dimension=1,...  88.9 us
    all_to_all x2, blocking collectives, regroup(): lax.all_to_all(stacked, 'bfly', split_axis=2, concat_axis=2, tiled=True)  78.9 us
    reduce_scatter x1, waiting for transfers between devices, per_device(): lax.psum_scatter(part_e.astype(jnp.bfloat16), 'dp', scatter_dimension=1,...  76.7 us
    all_gather x1, waiting for transfers between devices, per_device(): lax.all_gather(weight_a, 'dp', axis=1, tiled=True)  61.7 us
    all_gather x1, waiting for transfers between devices, per_device(): lax.all_gather(weight_c, 'dp', axis=1, tiled=True)  55.6 us
    all_gather x1, waiting for transfers between devices, per_device(): lax.all_gather(weight_e, 'dp', axis=1, tiled=True)  50.9 us
    all_to_all x2, waiting for transfers between devices, regroup(): lax.all_to_all(stacked, 'bfly', split_axis=2, concat_axis=2, tiled=True)  34.8 us
    reduce_scatter x1, waiting for transfers between devices, per_device(): lax.psum_scatter(part_c.astype(jnp.bfloat16), 'dp', scatter_dimension=1,...  18.3 us
  transfers between devices with their start and end apart: 10, of which 8 were waited for; matrix products, arithmetic and copies ran while one was open for 13% of the time, Pallas kernels for 0%

commit v1 on v0

v1 whole, which is shorter than its diff:
```python
import jax
import jax.numpy as jnp
from jax import lax
from jax.sharding import PartitionSpec as P

BLK = 256

gelu_scale = 0.7978845608028654


def gelu_pair(hidden):
    inner_arg = gelu_scale * (hidden + 0.044715 * hidden * hidden * hidden)
    tangent = jnp.tanh(inner_arg)
    gelu_value = 0.5 * hidden * (1.0 + tangent)
    gelu_slope = 0.5 * (1.0 + tangent) + 0.5 * hidden * (1.0 - tangent * tangent) * gelu_scale * (
        1.0 + 3.0 * 0.044715 * hidden * hidden
    )
    return (gelu_value, gelu_slope)


def mm(spec, a, b):
    return jnp.einsum(spec, a, b, preferred_element_type=jnp.float32)


def regroup(piece, group_count):
    local_blocks, block_width, token_count = piece.shape
    stacked = piece.reshape(local_blocks, group_count, block_width // group_count, token_count)
    arrived = lax.all_to_all(stacked, "bfly", split_axis=1, concat_axis=1, tiled=True)
    return arrived.reshape(local_blocks, block_width, token_count)


def any_mesh(tokens, grad_out, weight_a, weight_b, weight_c, weight_e):
    group_count = lax.axis_size("bfly")
    full_a, full_b, full_c, full_e = (
        lax.all_gather(w, "dp", axis=1, tiled=True)
        for w in (weight_a, weight_b, weight_c, weight_e)
    )
    token_count = tokens.shape[0]
    inner_blocks = full_a.shape[0]
    spread_width = full_a.shape[2]
    local_blocks = full_b.shape[0]
    inputs = tokens.reshape(token_count, inner_blocks, BLK).transpose(1, 2, 0)
    upstream = grad_out.reshape(token_count, inner_blocks, BLK).transpose(1, 2, 0)
    hidden_view = (local_blocks, BLK, token_count)
    wide_view = (inner_blocks, spread_width, token_count)
    spread = mm("kit,kio->kot", inputs, full_a).astype(jnp.bfloat16).reshape(hidden_view)
    back_out = mm("kjt,koj->kot", upstream, full_e).astype(jnp.bfloat16).reshape(hidden_view)
    permuted = regroup(spread, group_count)
    back_mid = regroup(back_out, group_count)
    gelu_value, gelu_slope = gelu_pair(mm("qit,qij->qjt", permuted, full_b))
    active = gelu_value.astype(jnp.bfloat16)
    narrowed = mm("qit,qij->qjt", active, full_c).astype(jnp.bfloat16)
    back_hidden = (mm("qjt,qij->qit", back_mid, full_c) * gelu_slope).astype(jnp.bfloat16)
    back_first = mm("qjt,qij->qit", back_hidden, full_b).astype(jnp.bfloat16)
    returned = regroup(narrowed, group_count).reshape(wide_view)
    back_spread = regroup(back_first, group_count).reshape(wide_view)
    output = mm("kot,koj->kjt", returned, full_e)
    back_input = mm("kot,kio->kit", back_spread, full_a)
    parts = (
        mm("kit,kot->kio", inputs, back_spread),
        mm("qit,qjt->qij", permuted, back_hidden),
        mm("qit,qjt->qij", active, back_mid),
        mm("kot,kjt->koj", returned, upstream),
    )
    grads = tuple(
        lax.psum_scatter(part.astype(jnp.bfloat16), "dp", scatter_dimension=1, tiled=True).astype(
            jnp.float32
        )
        for part in parts
    )

    def rows(x):
        return x.astype(jnp.bfloat16).transpose(2, 0, 1).reshape(token_count, inner_blocks * BLK)

    return (rows(output), rows(back_input)) + grads


def xor_permute(x, mask):
    n = lax.axis_size("bfly")
    return lax.ppermute(x, "bfly", [(i, i ^ mask) for i in range(n)])


def deal_weight(w):
    pairs = lax.axis_size("dp") // 2
    sets = w.reshape(pairs, 3, 2, w.shape[1], w.shape[2])
    own = jnp.stack([sets[:, 0], sets[:, 2]], axis=1)
    mid = jnp.stack([sets[:, 1], sets[:, 1]], axis=1)
    return jnp.stack([own, mid], axis=2).reshape((pairs * 2, 2) + sets.shape[2:])


def gather_bfly(w):
    index = lax.axis_index("bfly")
    high = index // 2 == 1
    other = xor_permute(w, 2)
    pair = jnp.stack([jnp.where(high, other, w), jnp.where(high, w, other)], axis=0)
    odd = index % 2 == 1
    swap = xor_permute(pair, 1)
    both = jnp.stack([jnp.where(odd, swap, pair), jnp.where(odd, pair, swap)], axis=1)
    return both.reshape((4,) + w.shape)


def scatter_bfly(g):
    index = lax.axis_index("bfly")
    high, odd = index // 2, index % 2
    quads = g.astype(jnp.bfloat16).reshape((2, 2) + g.shape[1:])
    keep = lax.dynamic_index_in_dim(quads, odd, 1, keepdims=False)
    send = lax.dynamic_index_in_dim(quads, 1 - odd, 1, keepdims=False)
    got = xor_permute(send, 1)
    half = (keep.astype(jnp.float32) + got.astype(jnp.float32)).astype(jnp.bfloat16)
    keep = lax.dynamic_index_in_dim(half, high, 0, keepdims=False)
    send = lax.dynamic_index_in_dim(half, 1 - high, 0, keepdims=False)
    got = xor_permute(send, 2)
    return (keep.astype(jnp.float32) + got.astype(jnp.float32)).astype(jnp.bfloat16)


def exchange(x, axes):
    return lax.all_to_all(x, axes, split_axis=0, concat_axis=0, tiled=True)


def deal_tokens(x):
    ndp, nb = lax.axis_size("dp"), lax.axis_size("bfly")
    pairs, count = ndp // 2, x.shape[0]
    view = x.reshape(count, pairs, 3, BLK)
    own = view[:, :, 0::2].reshape(nb, count // nb, ndp, BLK).transpose(2, 0, 1, 3)
    mid = view[:, :, 1].reshape(2, nb, count // nb // 2, pairs, BLK).transpose(3, 0, 1, 2, 4)
    mid = mid.reshape(ndp, nb, count // nb // 2, BLK)
    return jnp.concatenate([own, mid], axis=2).reshape(ndp * nb, -1, BLK)


def tokens_in(x):
    ndp, nb = lax.axis_size("dp"), lax.axis_size("bfly")
    own_count = x.shape[0] // nb
    got = exchange(deal_tokens(x), ("dp", "bfly")).reshape(ndp, nb, -1, BLK)
    own, mid = got[:, :, :own_count], got[:, :, own_count:]
    return tuple(part.transpose(1, 0, 2, 3).reshape(nb, -1, BLK) for part in (own, mid))


def tokens_out(own, mid):
    ndp, nb = lax.axis_size("dp"), lax.axis_size("bfly")
    pairs = ndp // 2
    parts = [
        part.reshape(nb, ndp, -1, BLK).transpose(1, 0, 2, 3).reshape(ndp * nb, -1, BLK)
        for part in (own, mid)
    ]
    own_count = parts[0].shape[1]
    got = exchange(jnp.concatenate(parts, axis=1), ("dp", "bfly"))
    count = own_count * nb
    own, mid = got[:, :own_count], got[:, own_count:]
    own = own.reshape(pairs, 2, count, BLK)
    mid = mid.reshape(pairs, 1, count, BLK)
    sets = jnp.concatenate([own[:, :1], mid, own[:, 1:]], axis=1)
    return sets.transpose(2, 0, 1, 3).reshape(count, pairs * 3 * BLK)


def swap_sub(x):
    n, parts, width, count = x.shape
    return x.reshape(n, parts, n, width // n, count).transpose(2, 1, 0, 3, 4).reshape(x.shape)


def one_set(x, g, a, b, c, e):
    spread = mm("dti,drio->drot", x, a).astype(jnp.bfloat16)
    permuted = swap_sub(spread)
    gelu_value, gelu_slope = gelu_pair(mm("srit,srij->srjt", permuted, b))
    active = gelu_value.astype(jnp.bfloat16)
    returned = swap_sub(mm("srit,srij->srjt", active, c).astype(jnp.bfloat16))
    output = mm("drot,droj->dtj", returned, e).astype(jnp.bfloat16)
    back_mid = swap_sub(mm("dtj,droj->drot", g, e).astype(jnp.bfloat16))
    back_hidden = (mm("srjt,srij->srit", back_mid, c) * gelu_slope).astype(jnp.bfloat16)
    back_spread = swap_sub(mm("srjt,srij->srit", back_hidden, b).astype(jnp.bfloat16))
    grad_in = mm("drot,drio->dti", back_spread, a).astype(jnp.bfloat16)
    grad_a = mm("dti,drot->drio", x, back_spread).astype(jnp.bfloat16)
    grad_b = mm("srit,srjt->srij", permuted, back_hidden).astype(jnp.bfloat16)
    grad_c = mm("srit,srjt->srij", active, back_mid).astype(jnp.bfloat16)
    grad_e = mm("drot,dtj->droj", returned, g).astype(jnp.bfloat16)
    return output, grad_in, (grad_a, grad_b, grad_c, grad_e)


def token_plan(tokens, grad_out, weight_a, weight_b, weight_c, weight_e):
    ndp, nb = lax.axis_size("dp"), lax.axis_size("bfly")
    blocks, rows, _ = weight_a.shape
    parts = 2 * blocks
    dealt_a = weight_a.reshape(blocks, rows, 2, BLK).transpose(0, 2, 1, 3).reshape(parts, rows, BLK)
    dealt_e = weight_e.reshape(parts, rows, BLK)

    def weights_in(first, second):
        both = jnp.stack([deal_weight(first), deal_weight(second)], axis=1)
        full = gather_bfly(exchange(both, "dp"))
        return full

    ab = weights_in(dealt_a, weight_b)
    x_own, x_mid = tokens_in(tokens)
    ce = weights_in(weight_c, dealt_e)
    g_own, g_mid = tokens_in(grad_out)

    def by_rows(full, which, slot):
        return full[:, :, which, slot].transpose(0, 2, 1, 3, 4).reshape(nb, 2, BLK, BLK)

    def by_wide_rows(full, which, slot):
        return full[:, :, which, slot].reshape(nb, 2, BLK, BLK)

    results = []
    for slot, (x, g) in enumerate(((x_own, g_own), (x_mid, g_mid))):
        results.append(
            one_set(
                x,
                g,
                by_rows(ab, 0, slot),
                by_rows(ab, 1, slot),
                by_rows(ce, 0, slot),
                by_wide_rows(ce, 1, slot),
            )
        )
    output = tokens_out(results[0][0], results[1][0])
    grad_in = tokens_out(results[0][1], results[1][1])

    def grads_out(which, wide):
        own, mid = results[0][2][which], results[1][2][which]
        mine = scatter_bfly(jnp.stack([own, mid], axis=1))
        if wide:
            dealt = mine.reshape(2, ndp, 2, rows, BLK).transpose(1, 0, 2, 3, 4)
        else:
            dealt = mine.reshape(2, 2, ndp, rows, BLK).transpose(2, 0, 1, 3, 4)
        got = exchange(dealt, "dp").astype(jnp.float32)
        got = got.reshape(ndp // 2, 2, 2, 2, rows, BLK)
        mid = got[:, 0, 1] + got[:, 1, 1]
        return jnp.stack([got[:, 0, 0], mid, got[:, 1, 0]], axis=1).reshape(parts, rows, BLK)

    grad_e = grads_out(3, True).reshape(weight_e.shape)
    grad_c = grads_out(2, False)
    grad_b = grads_out(1, False)
    grad_a = grads_out(0, False)
    grad_a = grad_a.reshape(blocks, 2, rows, BLK).transpose(0, 2, 1, 3).reshape(weight_a.shape)
    return (output, grad_in, grad_a, grad_b, grad_c, grad_e)


def per_device(tokens, grad_out, weight_a, weight_b, weight_c, weight_e):
    ndp, nb = lax.axis_size("dp"), lax.axis_size("bfly")
    fits = nb == 4 and ndp % 2 == 0 and 2 * weight_a.shape[0] == 3 * ndp
    fits = fits and tokens.shape[0] % (32 * nb) == 0 and weight_a.shape[1] * ndp == BLK
    fits = fits and weight_a.shape[2] == 2 * BLK and weight_e.shape[1] == 2 * weight_a.shape[1]
    plan = token_plan if fits else any_mesh
    return plan(tokens, grad_out, weight_a, weight_b, weight_c, weight_e)


def solution(mesh):
    in_specs = (P("dp", "bfly"),) * 2 + (P("bfly", "dp", None),) * 4
    return jax.shard_map(
        per_device, mesh=mesh, in_specs=in_specs, out_specs=in_specs, check_vma=False
    )
```

time: 601 us -> 375 us (0.62)
  waiting for transfers between devices: 400 us -> 211 us
  blocking collectives: 78.9 us -> 0 us
  starting transfers between devices: 10 us -> 54.8 us
  matrix products: 53.5 us -> 23 us
  other arithmetic: 5.85 us -> 31.7 us
  between operations: 14.3 us -> 2.27 us
  local copies, waits for them, and re-layouts: 36.8 us -> 47.8 us
    reduce_scatter x4 -> x0, waiting for transfers between devices: 184 us -> none  [the longest x1 88.9 us: per_device(): lax.psum_scatter(part_a.astype(jnp.bfloat16), 'dp', scatter_dimension=1,...]
    all_gather x4 -> x0, waiting for transfers between devices: 179 us -> none  [the longest x1 61.7 us: per_device(): lax.all_gather(weight_a, 'dp', axis=1, tiled=True)]
    all_to_all x2 -> x10, waiting for transfers between devices: 34.8 us -> 143 us  [exchange(): return lax.all_to_all(x, axes, split_axis=0, concat_axis=0, tiled=True)]
    all_to_all x2 -> x0, blocking collectives: 78.9 us -> none  [regroup(): lax.all_to_all(stacked, 'bfly', split_axis=2, concat_axis=2, tiled=True)]
    ppermute x0 -> x12, waiting for transfers between devices: none -> 67.4 us  [xor_permute(): return lax.ppermute(x, 'bfly', [(i, i ^ mask) for i in range(n)])]
    all_to_all x2 -> x10, starting transfers between devices: 9.5 us -> 47.3 us  [exchange(): return lax.all_to_all(x, axes, split_axis=0, concat_axis=0, tiled=True)]
    dot_general x12 -> x24, matrix products: 53.5 us -> 23 us  [mm(): return jnp.einsum(spec, a, b, preferred_element_type=jnp.float32)]
    another operation x0 -> x22, other arithmetic: none -> 15.4 us  [the longest x4 6.46 us: gather_bfly(): jnp.stack([jnp.where(high, other, w), jnp.where(high, w, other)], axis=0)]
  transfers between devices with their start and end apart: 10 -> 22, of which waited for: 8 -> 11; matrix products, arithmetic and copies ran while one was open for 13% -> 18% of each run, Pallas kernels for 0% -> 0%
where the time goes in v1:
time: 375 us; the launch traced here: 370 us
  waiting for transfers between devices  211 us (56%)
  starting transfers between devices  54.8 us (15%)
  local copies, waits for them, and re-layouts  47.8 us (13%)
  other arithmetic  31.7 us (8%)
  matrix products  23 us (6%)
    all_to_all x10, waiting for transfers between devices, exchange(): return lax.all_to_all(x, axes, split_axis=0, concat_axis=0, tiled=True)  143 us
    ppermute x12, waiting for transfers between devices, xor_permute(): return lax.ppermute(x, 'bfly', [(i, i ^ mask) for i in range(n)])  67.4 us
    all_to_all x10, starting transfers between devices, exchange(): return lax.all_to_all(x, axes, split_axis=0, concat_axis=0, tiled=True)  47.3 us
    dot_general x24, matrix products, mm(): return jnp.einsum(spec, a, b, preferred_element_type=jnp.float32)  23 us
    unnamed x76, local copies, waits for them, and re-layouts  19.8 us
    ppermute x12, starting transfers between devices, xor_permute(): return lax.ppermute(x, 'bfly', [(i, i ^ mask) for i in range(n)])  7.51 us
  transfers between devices with their start and end apart: 22, of which 11 were waited for; matrix products, arithmetic and copies ran while one was open for 18% of the time, Pallas kernels for 0%

profile of v1, /device:TPU:0, one launch (start us, length us, event | category | flops | bytes accessed | tf_op | source)
XLA Modules:
  0.0 370.1 jit_solution(3259361624463584661)
XLA Ops:
  3.1 7.4 %all-to-all-start.1 = ((bf16[8,2,2,2,32,256]{5,4,3,2,1,0:T(8,128)(2,1)}), bf16[8,2,2,2,32,256]{5,4,3,2,1,0:T(8,128)(2,1)S(1)}, u32[]{:S(2)}, u32[]{:S(2)}) async-start(bf16[8,2,2,2,32,256]{5,4,3,2,1,0:T(8,128)(2,1)} %maximum_maximum_fusion.1), calls=%async_computation.1 | async-start | bytes 2097152 | tf_op jit(solution)/shard_map/all_to_all | solution.py:117
  11.8 24.5 %all-to-all-done.1 = bf16[8,2,2,2,32,256]{5,4,3,2,1,0:T(8,128)(2,1)S(1)} async-done(((bf16[8,2,2,2,32,256]{5,4,3,2,1,0:T(8,128)(2,1)}), bf16[8,2,2,2,32,256]{5,4,3,2,1,0:T(8,128)(2,1)S(1)}, u32[]{:S(2)}, u32[]{:S(2)}) %all-to-all-start.1) | async-done | bytes 1048608 | tf_op jit(solution)/shard_map/all_to_all | solution.py:117
  37.3 4.2 %all-to-all-start = ((bf16[8,2,2,2,32,256]{5,4,3,2,1,0:T(8,128)(2,1)}), bf16[8,2,2,2,32,256]{5,4,3,2,1,0:T(8,128)(2,1)}, u32[]{:S(2)}, u32[]{:S(2)}) async-start(bf16[8,2,2,2,32,256]{5,4,3,2,1,0:T(8,128)(2,1)} %maximum_maximum_fusion), calls=%async_computation | async-start | bytes 2097152 | tf_op jit(solution)/shard_map/all_to_all | solution.py:117
  44.4 22.8 %all-to-all-done = bf16[8,2,2,2,32,256]{5,4,3,2,1,0:T(8,128)(2,1)} async-done(((bf16[8,2,2,2,32,256]{5,4,3,2,1,0:T(8,128)(2,1)}), bf16[8,2,2,2,32,256]{5,4,3,2,1,0:T(8,128)(2,1)}, u32[]{:S(2)}, u32[]{:S(2)}) %all-to-all-start) | async-done | bytes 1048608 | tf_op jit(solution)/shard_map/all_to_all | solution.py:117
  67.1 3.4 all-to-all-start.2
  70.5 1.7 copy.373
  76.7 1.8 collective-permute-start
  78.5 2.3 pad_maximum_fusion.6
  80.8 27.7 %all-to-all-done.2 = bf16[32,96,256]{2,1,0:T(8,128)(2,1)S(1)} async-done(((bf16[32,96,256]{2,1,0:T(8,128)(2,1)}), bf16[32,96,256]{2,1,0:T(8,128)(2,1)S(1)}, u32[]{:S(2)}, u32[]{:S(2)}) %all-to-all-start.2) | async-done | bytes 1572896 | tf_op jit(solution)/shard_map/all_to_all | solution.py:117
  108.4 4.0 %all-to-all-start.4 = ((bf16[32,96,256]{2,1,0:T(8,128)(2,1)}), bf16[32,96,256]{2,1,0:T(8,128)(2,1)}, u32[]{:S(2)}, u32[]{:S(2)}) async-start(bf16[32,96,256]{2,1,0:T(8,128)(2,1)} %pad_maximum_fusion.6), calls=%async_computation.4 | async-start | bytes 3145728 | tf_op jit(solution)/shard_map/all_to_all | solution.py:117
  112.4 1.8 collective-permute-start.2
  117.4 37.0 %collective-permute-done.2 = bf16[8,2,2,2,32,256]{5,4,3,2,1,0:T(8,128)(2,1)} collective-permute-done((bf16[8,2,2,2,32,256]{5,4,3,2,1,0:T(8,128)(2,1)S(1)}, bf16[8,2,2,2,32,256]{5,4,3,2,1,0:T(8,128)(2,1)}, u32[]{:S(2)}, u32[]{:S(2)}) %collective-permute-start.2) | collective-permute-done | bytes 1048608 | tf_op jit(solution)/shard_map/ppermute | solution.py:80
  163.2 1.9 select_bitcast_fusion.3
  168.5 2.0 select_bitcast_fusion.1
  183.5 3.0 fusion.6
  186.5 1.7 convolution_convert_fusion.2
  201.5 8.4 %collective-permute-done.9 = bf16[2,2,256,256]{3,2,1,0:T(8,128)(2,1)S(1)} collective-permute-done((bf16[2,2,256,256]{3,2,1,0:T(8,128)(2,1)S(1)}, bf16[2,2,256,256]{3,2,1,0:T(8,128)(2,1)S(1)}, u32[]{:S(2)}, u32[]{:S(2)}) %collective-permute-start.9) | collective-permute-done | bytes 524320 | tf_op jit(solution)/shard_map/ppermute | solution.py:80
  210.9 5.8 %all-to-all-start.8 = ((bf16[8,2,2,32,256]{4,3,2,1,0:T(8,128)(2,1)}), bf16[8,2,2,32,256]{4,3,2,1,0:T(8,128)(2,1)}, u32[]{:S(2)}, u32[]{:S(2)}) async-start(bf16[8,2,2,32,256]{4,3,2,1,0:T(8,128)(2,1)} %copy.407), calls=%async_computation.8 | async-start | bytes 1048576 | tf_op jit(solution)/shard_map/all_to_all | solution.py:117
  216.7 2.2 convolution_convert_fusion.7
  223.5 6.2 %all-to-all-done.8 = bf16[8,2,2,32,256]{4,3,2,1,0:T(8,128)(2,1)} async-done(((bf16[8,2,2,32,256]{4,3,2,1,0:T(8,128)(2,1)}), bf16[8,2,2,32,256]{4,3,2,1,0:T(8,128)(2,1)}, u32[]{:S(2)}, u32[]{:S(2)}) %all-to-all-start.8) | async-done | bytes 524320 | tf_op jit(solution)/shard_map/all_to_all | solution.py:117
  229.7 4.1 %all-to-all-start.9 = ((bf16[8,2,2,32,256]{4,3,2,1,0:T(8,128)(2,1)}), bf16[8,2,2,32,256]{4,3,2,1,0:T(8,128)(2,1)}, u32[]{:S(2)}, u32[]{:S(2)}) async-start(bf16[8,2,2,32,256]{4,3,2,1,0:T(8,128)(2,1)} %copy.414), calls=%async_computation.9 | async-start | bytes 1048576 | tf_op jit(solution)/shard_map/all_to_all | solution.py:117
  236.1 11.6 %collective-permute-done.5 = bf16[2,2,256,256]{3,2,1,0:T(8,128)(2,1)S(1)} collective-permute-done((bf16[2,2,256,256]{3,2,1,0:T(8,128)(2,1)S(1)}, bf16[2,2,256,256]{3,2,1,0:T(8,128)(2,1)S(1)}, u32[]{:S(2)}, u32[]{:S(2)}) %collective-permute-start.5) | collective-permute-done | bytes 524320 | tf_op jit(solution)/shard_map/ppermute | solution.py:80
  248.7 5.7 %all-to-all-start.6 = ((bf16[8,2,2,32,256]{4,3,2,1,0:T(8,128)(2,1)}), bf16[8,2,2,32,256]{4,3,2,1,0:T(8,128)(2,1)}, u32[]{:S(2)}, u32[]{:S(2)}) async-start(bf16[8,2,2,32,256]{4,3,2,1,0:T(8,128)(2,1)} %copy.392), calls=%async_computation.6 | async-start | bytes 1048576 | tf_op jit(solution)/shard_map/all_to_all | solution.py:117
  256.6 10.3 %collective-permute-done.7 = bf16[2,2,256,256]{3,2,1,0:T(8,128)(2,1)S(1)} collective-permute-done((bf16[2,2,256,256]{3,2,1,0:T(8,128)(2,1)S(1)}, bf16[2,2,256,256]{3,2,1,0:T(8,128)(2,1)S(1)}, u32[]{:S(2)}, u32[]{:S(2)}) %collective-permute-start.7) | collective-permute-done | bytes 524320 | tf_op jit(solution)/shard_map/ppermute | solution.py:80
  267.9 5.7 %all-to-all-start.7 = ((bf16[8,2,2,32,256]{4,3,2,1,0:T(8,128)(2,1)}), bf16[8,2,2,32,256]{4,3,2,1,0:T(8,128)(2,1)}, u32[]{:S(2)}, u32[]{:S(2)}) async-start(bf16[8,2,2,32,256]{4,3,2,1,0:T(8,128)(2,1)} %copy.400), calls=%async_computation.7 | async-start | bytes 1048576 | tf_op jit(solution)/shard_map/all_to_all | solution.py:117
  277.7 6.6 %all-to-all-done.7 = bf16[8,2,2,32,256]{4,3,2,1,0:T(8,128)(2,1)} async-done(((bf16[8,2,2,32,256]{4,3,2,1,0:T(8,128)(2,1)}), bf16[8,2,2,32,256]{4,3,2,1,0:T(8,128)(2,1)}, u32[]{:S(2)}, u32[]{:S(2)}) %all-to-all-start.7) | async-done | bytes 524320 | tf_op jit(solution)/shard_map/all_to_all | solution.py:117
  284.3 3.4 all-to-all-start.5
  291.9 33.6 %all-to-all-done.5 = bf16[32,96,256]{2,1,0:T(8,128)(2,1)} async-done(((bf16[32,96,256]{2,1,0:T(8,128)(2,1)}), bf16[32,96,256]{2,1,0:T(8,128)(2,1)}, u32[]{:S(2)}, u32[]{:S(2)}) %all-to-all-start.5) | async-done | bytes 1572896 | tf_op jit(solution)/shard_map/all_to_all | solution.py:117
  325.6 3.6 all-to-all-start.3
  342.5 2.6 copy.420
  345.1 21.8 %all-to-all-done.3 = bf16[32,96,256]{2,1,0:T(8,128)(2,1)S(1)} async-done(((bf16[32,96,256]{2,1,0:T(8,128)(2,1)}), bf16[32,96,256]{2,1,0:T(8,128)(2,1)S(1)}, u32[]{:S(2)}, u32[]{:S(2)}) %all-to-all-start.3) | async-done | bytes 1572896 | tf_op jit(solution)/shard_map/all_to_all | solution.py:117
  367.9 1.7 copy.419
  (221 shorter events, 87.4 us)
Async XLA Ops:
  2.0 8.5 %copy-start.32 = (bf16[24,32,256]{2,1,0:T(8,128)(2,1)S(1)}, bf16[24,32,256]{2,1,0:T(8,128)(2,1)}, u32[]{:S(2)}) copy-start(bf16[24,32,256]{2,1,0:T(8,128)(2,1)} %param.10) | copy-start | bytes 1179652
  3.1 7.5 %copy-start.33 = (bf16[12,64,256]{2,1,0:T(8,128)(2,1)S(1)}, bf16[12,64,256]{2,1,0:T(8,128)(2,1)}, u32[]{:S(2)}) copy-start(bf16[12,64,256]{2,1,0:T(8,128)(2,1)} %param.11) | copy-start | bytes 1179652
  3.1 33.2 %all-to-all-start.1 = ((bf16[8,2,2,2,32,256]{5,4,3,2,1,0:T(8,128)(2,1)}), bf16[8,2,2,2,32,256]{5,4,3,2,1,0:T(8,128)(2,1)S(1)}, u32[]{:S(2)}, u32[]{:S(2)}) async-start(bf16[8,2,2,2,32,256]{5,4,3,2,1,0:T(8,128)(2,1)} %maximum_maximum_fusion.1), calls=%async_computation.1 | async-start | bytes 2097152 | tf_op jit(solution)/shard_map/all_to_all | solution.py:117
  10.7 30.8 %copy-start.30 = (bf16[256,3072]{1,0:T(8,128)(2,1)S(1)}, bf16[256,3072]{1,0:T(8,128)(2,1)}, u32[]{:S(2)}) copy-start(bf16[256,3072]{1,0:T(8,128)(2,1)} %param.6) | copy-start | bytes 4718596
  37.3 29.8 %all-to-all-start = ((bf16[8,2,2,2,32,256]{5,4,3,2,1,0:T(8,128)(2,1)}), bf16[8,2,2,2,32,256]{5,4,3,2,1,0:T(8,128)(2,1)}, u32[]{:S(2)}, u32[]{:S(2)}) async-start(bf16[8,2,2,2,32,256]{5,4,3,2,1,0:T(8,128)(2,1)} %maximum_maximum_fusion), calls=%async_computation | async-start | bytes 2097152 | tf_op jit(solution)/shard_map/all_to_all | solution.py:117
  67.1 41.3 %all-to-all-start.2 = ((bf16[32,96,256]{2,1,0:T(8,128)(2,1)}), bf16[32,96,256]{2,1,0:T(8,128)(2,1)S(1)}, u32[]{:S(2)}, u32[]{:S(2)}) async-start(bf16[32,96,256]{2,1,0:T(8,128)(2,1)} %pad_maximum_fusion.4), calls=%async_computation.2 | async-start | bytes 3145728 | tf_op jit(solution)/shard_map/all_to_all | solution.py:117
  76.7 37.5 %collective-permute-start = (bf16[8,2,2,2,32,256]{5,4,3,2,1,0:T(8,128)(2,1)}, bf16[8,2,2,2,32,256]{5,4,3,2,1,0:T(8,128)(2,1)}, u32[]{:S(2)}, u32[]{:S(2)}) collective-permute-start(bf16[8,2,2,2,32,256]{5,4,3,2,1,0:T(8,128)(2,1)} %all-to-all-done), channel_id=1, source_target_pairs={{0,2},{1,3},{2,0},{3,1},{4,6},{5,7},{6,4},{7,5},{8,10},{9,11},{10,... | collective-permute-start | bytes 3145736 | tf_op jit(solution)/shard_map/ppermute | solution.py:80
  80.8 31.6 %copy-start.26 = (bf16[8,2,2,2,32,256]{5,4,3,2,1,0:T(8,128)(2,1)S(1)}, bf16[8,2,2,2,32,256]{5,4,3,2,1,0:T(8,128)(2,1)}, u32[]{:S(2)}) copy-start(bf16[8,2,2,2,32,256]{5,4,3,2,1,0:T(8,128)(2,1)} %copy-done.25) | copy-start | bytes 3145732
  108.4 52.2 %all-to-all-start.4 = ((bf16[32,96,256]{2,1,0:T(8,128)(2,1)}), bf16[32,96,256]{2,1,0:T(8,128)(2,1)}, u32[]{:S(2)}, u32[]{:S(2)}) async-start(bf16[32,96,256]{2,1,0:T(8,128)(2,1)} %pad_maximum_fusion.6), calls=%async_computation.4 | async-start | bytes 3145728 | tf_op jit(solution)/shard_map/all_to_all | solution.py:117
  112.4 42.0 %collective-permute-start.2 = (bf16[8,2,2,2,32,256]{5,4,3,2,1,0:T(8,128)(2,1)S(1)}, bf16[8,2,2,2,32,256]{5,4,3,2,1,0:T(8,128)(2,1)}, u32[]{:S(2)}, u32[]{:S(2)}) collective-permute-start(bf16[8,2,2,2,32,256]{5,4,3,2,1,0:T(8,128)(2,1)S(1)} %copy-done.26), channel_id=1, source_target_pairs={{0,2},{1,3},{2,0},{3,1},{4,6},{5,7},{6,4},{7,5},{8,10},{9,11},{10,... | collective-permute-start | bytes 3145736 | tf_op jit(solution)/shard_map/ppermute | solution.py:80
  117.4 45.8 %collective-permute-start.1 = (bf16[2,8,2,2,2,32,256]{6,5,4,3,2,1,0:T(8,128)(2,1)}, bf16[2,8,2,2,2,32,256]{6,5,4,3,2,1,0:T(8,128)(2,1)}, u32[]{:S(2)}, u32[]{:S(2)}) collective-permute-start(bf16[2,8,2,2,2,32,256]{6,5,4,3,2,1,0:T(8,128)(2,1)} %pad_maximum_fusion.2), channel_id=1, source_target_pairs={{0,1},{1,0},{2,3},{3,2},{4,5},{5,4},{6,7},{7,6},{8,9},{9,8},{10,11... | collective-permute-start | bytes 6291464 | tf_op jit(solution)/shard_map/ppermute | solution.py:80
  157.7 10.1 %collective-permute-start.3 = (bf16[2,8,2,2,2,32,256]{6,5,4,3,2,1,0:T(8,128)(2,1)}, bf16[2,8,2,2,2,32,256]{6,5,4,3,2,1,0:T(8,128)(2,1)}, u32[]{:S(2)}, u32[]{:S(2)}) collective-permute-start(bf16[2,8,2,2,2,32,256]{6,5,4,3,2,1,0:T(8,128)(2,1)} %pad_maximum_fusion.3), channel_id=1, source_target_pairs={{0,1},{1,0},{2,3},{3,2},{4,5},{5,4},{6,7},{7,6},{8,9},{9,8},{10,11... | collective-permute-start | bytes 6291464 | tf_op jit(solution)/shard_map/ppermute | solution.py:80
  172.0 6.9 %copy-start.16 = (bf16[4,8,1,1,2,32,256]{6,5,1,4,0,3,2:T(8,128)(2,1)}, bf16[4,8,1,1,2,32,256]{6,5,1,4,0,3,2:T(8,128)(2,1)S(1)}, u32[]{:S(2)}) copy-start(bf16[4,8,1,1,2,32,256]{6,5,1,4,0,3,2:T(8,128)(2,1)S(1)} %get-tuple-element.40) | copy-start | bytes 3145732
  176.5 12.2 %copy-start.23 = (bf16[4,2,256,256]{3,2,1,0:T(8,128)(2,1)}, bf16[4,2,256,256]{3,2,1,0:T(8,128)(2,1)S(1)}, u32[]{:S(2)}) copy-start(bf16[4,2,256,256]{3,2,1,0:T(8,128)(2,1)S(1)} %fusion.13) | copy-start | bytes 3145732
  191.0 3.7 %collective-permute-start.8 = (bf16[2,2,2,256,256]{4,3,2,1,0:T(8,128)(2,1)S(1)}, bf16[2,2,2,256,256]{4,3,2,1,0:T(8,128)(2,1)S(1)}, u32[]{:S(2)}, u32[]{:S(2)}) collective-permute-start(bf16[2,2,2,256,256]{4,3,2,1,0:T(8,128)(2,1)S(1)} %bitcast.492), channel_id=1, source_target_pairs={{0,1},{1,0},{2,3},{3,2},{4,5},{5,4},{6,7},{7,6},{8,9},{9,8},{10,11... | collective-permute-start | bytes 3145736 | tf_op jit(solution)/shard_map/ppermute | solution.py:80
  191.4 6.4 %collective-permute-start.10 = (bf16[2,2,2,256,256]{4,3,2,1,0:T(8,128)(2,1)S(1)}, bf16[2,2,2,256,256]{4,3,2,1,0:T(8,128)(2,1)S(1)}, u32[]{:S(2)}, u32[]{:S(2)}) collective-permute-start(bf16[2,2,2,256,256]{4,3,2,1,0:T(8,128)(2,1)S(1)} %bitcast.489), channel_id=1, source_target_pairs={{0,1},{1,0},{2,3},{3,2},{4,5},{5,4},{6,7},{7,6},{8,9},{9,8},{10,11... | collective-permute-start | bytes 3145736 | tf_op jit(solution)/shard_map/ppermute | solution.py:80
  195.1 14.8 %collective-permute-start.9 = (bf16[2,2,256,256]{3,2,1,0:T(8,128)(2,1)S(1)}, bf16[2,2,256,256]{3,2,1,0:T(8,128)(2,1)S(1)}, u32[]{:S(2)}, u32[]{:S(2)}) collective-permute-start(bf16[2,2,256,256]{3,2,1,0:T(8,128)(2,1)S(1)} %dynamic-slice_bitcast_fusion.1), channel_id=1, source_target_pairs={{0,2},{1,3},{2,0},{3,1},{4,6},{5,7},{6,4},{7,5},{8,10},{9,11},{10,... | collective-permute-start | bytes 1572872 | tf_op jit(solution)/shard_map/ppermute | solution.py:80
  197.8 36.1 %collective-permute-start.4 = (bf16[2,2,2,256,256]{4,3,2,1,0:T(8,128)(2,1)}, bf16[2,2,2,256,256]{4,3,2,1,0:T(8,128)(2,1)}, u32[]{:S(2)}, u32[]{:S(2)}) collective-permute-start(bf16[2,2,2,256,256]{4,3,2,1,0:T(8,128)(2,1)} %bitcast.406), channel_id=1, source_target_pairs={{0,1},{1,0},{2,3},{3,2},{4,5},{5,4},{6,7},{7,6},{8,9},{9,8},{10,11... | collective-permute-start | bytes 3145736 | tf_op jit(solution)/shard_map/ppermute | solution.py:80
  199.9 21.1 %collective-permute-start.11 = (bf16[2,2,256,256]{3,2,1,0:T(8,128)(2,1)}, bf16[2,2,256,256]{3,2,1,0:T(8,128)(2,1)}, u32[]{:S(2)}, u32[]{:S(2)}) collective-permute-start(bf16[2,2,256,256]{3,2,1,0:T(8,128)(2,1)} %dynamic-slice_bitcast_fusion), channel_id=1, source_target_pairs={{0,2},{1,3},{2,0},{3,1},{4,6},{5,7},{6,4},{7,5},{8,10},{9,11},{10,... | collective-permute-start | bytes 1572872 | tf_op jit(solution)/shard_map/ppermute | solution.py:80
  210.9 18.8 %all-to-all-start.8 = ((bf16[8,2,2,32,256]{4,3,2,1,0:T(8,128)(2,1)}), bf16[8,2,2,32,256]{4,3,2,1,0:T(8,128)(2,1)}, u32[]{:S(2)}, u32[]{:S(2)}) async-start(bf16[8,2,2,32,256]{4,3,2,1,0:T(8,128)(2,1)} %copy.407), calls=%async_computation.8 | async-start | bytes 1048576 | tf_op jit(solution)/shard_map/all_to_all | solution.py:117
  221.0 12.9 %copy-start.24 = (bf16[2,1,2,2,256,256]{5,4,3,1,0,2:T(8,128)(2,1)S(1)}, bf16[2,1,2,2,256,256]{5,4,3,1,0,2:T(8,128)(2,1)}, u32[]{:S(2)}) copy-start(bf16[2,1,2,2,256,256]{5,4,3,1,0,2:T(8,128)(2,1)} %get-tuple-element.54) | copy-start | bytes 3145732
  221.0 33.4 %collective-permute-start.6 = (bf16[2,2,2,256,256]{4,3,2,1,0:T(8,128)(2,1)}, bf16[2,2,2,256,256]{4,3,2,1,0:T(8,128)(2,1)}, u32[]{:S(2)}, u32[]{:S(2)}) collective-permute-start(bf16[2,2,2,256,256]{4,3,2,1,0:T(8,128)(2,1)} %bitcast.405), channel_id=1, source_target_pairs={{0,1},{1,0},{2,3},{3,2},{4,5},{5,4},{6,7},{7,6},{8,9},{9,8},{10,11... | collective-permute-start | bytes 3145736 | tf_op jit(solution)/shard_map/ppermute | solution.py:80
  229.7 18.9 %all-to-all-start.9 = ((bf16[8,2,2,32,256]{4,3,2,1,0:T(8,128)(2,1)}), bf16[8,2,2,32,256]{4,3,2,1,0:T(8,128)(2,1)}, u32[]{:S(2)}, u32[]{:S(2)}) async-start(bf16[8,2,2,32,256]{4,3,2,1,0:T(8,128)(2,1)} %copy.414), calls=%async_computation.9 | async-start | bytes 1048576 | tf_op jit(solution)/shard_map/all_to_all | solution.py:117
  235.4 12.2 %collective-permute-start.5 = (bf16[2,2,256,256]{3,2,1,0:T(8,128)(2,1)S(1)}, bf16[2,2,256,256]{3,2,1,0:T(8,128)(2,1)S(1)}, u32[]{:S(2)}, u32[]{:S(2)}) collective-permute-start(bf16[2,2,256,256]{3,2,1,0:T(8,128)(2,1)S(1)} %dynamic-slice_bitcast_fusion.3), channel_id=1, source_target_pairs={{0,2},{1,3},{2,0},{3,1},{4,6},{5,7},{6,4},{7,5},{8,10},{9,11},{10,... | collective-permute-start | bytes 1572872 | tf_op jit(solution)/shard_map/ppermute | solution.py:80
  248.7 19.2 %all-to-all-start.6 = ((bf16[8,2,2,32,256]{4,3,2,1,0:T(8,128)(2,1)}), bf16[8,2,2,32,256]{4,3,2,1,0:T(8,128)(2,1)}, u32[]{:S(2)}, u32[]{:S(2)}) async-start(bf16[8,2,2,32,256]{4,3,2,1,0:T(8,128)(2,1)} %copy.392), calls=%async_computation.6 | async-start | bytes 1048576 | tf_op jit(solution)/shard_map/all_to_all | solution.py:117
  255.9 17.7 %copy-start.9 = (bf16[4,2,4,64,256]{4,3,2,1,0:T(8,128)(2,1)S(1)}, bf16[4,2,4,64,256]{4,3,2,1,0:T(8,128)(2,1)}, u32[]{:S(2)}) copy-start(bf16[4,2,4,64,256]{4,3,2,1,0:T(8,128)(2,1)} %copy-done.8) | copy-start | bytes 3145732
  255.9 17.7 %copy-start.15 = (bf16[4,8,1,1,2,32,256]{6,5,1,4,0,3,2:T(8,128)(2,1)S(1)}, bf16[4,8,1,1,2,32,256]{6,5,1,4,0,3,2:T(8,128)(2,1)}, u32[]{:S(2)}) copy-start(bf16[4,8,1,1,2,32,256]{6,5,1,4,0,3,2:T(8,128)(2,1)} %copy-done.14) | copy-start | bytes 3145732
  255.9 10.9 %collective-permute-start.7 = (bf16[2,2,256,256]{3,2,1,0:T(8,128)(2,1)S(1)}, bf16[2,2,256,256]{3,2,1,0:T(8,128)(2,1)S(1)}, u32[]{:S(2)}, u32[]{:S(2)}) collective-permute-start(bf16[2,2,256,256]{3,2,1,0:T(8,128)(2,1)S(1)} %dynamic-slice_bitcast_fusion.2), channel_id=1, source_target_pairs={{0,2},{1,3},{2,0},{3,1},{4,6},{5,7},{6,4},{7,5},{8,10},{9,11},{10,... | collective-permute-start | bytes 1572872 | tf_op jit(solution)/shard_map/ppermute | solution.py:80
  267.9 16.4 %all-to-all-start.7 = ((bf16[8,2,2,32,256]{4,3,2,1,0:T(8,128)(2,1)}), bf16[8,2,2,32,256]{4,3,2,1,0:T(8,128)(2,1)}, u32[]{:S(2)}, u32[]{:S(2)}) async-start(bf16[8,2,2,32,256]{4,3,2,1,0:T(8,128)(2,1)} %copy.400), calls=%async_computation.7 | async-start | bytes 1048576 | tf_op jit(solution)/shard_map/all_to_all | solution.py:117
  277.7 10.0 %copy-start.7 = (bf16[4,8,1,1,2,32,256]{6,5,4,1,0,3,2:T(8,128)(2,1)S(1)}, bf16[4,8,1,1,2,32,256]{6,5,4,1,0,3,2:T(8,128)(2,1)}, u32[]{:S(2)}) copy-start(bf16[4,8,1,1,2,32,256]{6,5,4,1,0,3,2:T(8,128)(2,1)} %copy-done.6) | copy-start | bytes 3145732
  284.3 41.3 %all-to-all-start.5 = ((bf16[32,96,256]{2,1,0:T(8,128)(2,1)}), bf16[32,96,256]{2,1,0:T(8,128)(2,1)}, u32[]{:S(2)}, u32[]{:S(2)}) async-start(bf16[32,96,256]{2,1,0:T(8,128)(2,1)} %pad_maximum_fusion.7), calls=%async_computation.5 | async-start | bytes 3145728 | tf_op jit(solution)/shard_map/all_to_all | solution.py:117
  325.6 41.3 %all-to-all-start.3 = ((bf16[32,96,256]{2,1,0:T(8,128)(2,1)}), bf16[32,96,256]{2,1,0:T(8,128)(2,1)S(1)}, u32[]{:S(2)}, u32[]{:S(2)}) async-start(bf16[32,96,256]{2,1,0:T(8,128)(2,1)} %pad_maximum_fusion.5), calls=%async_computation.3 | async-start | bytes 3145728 | tf_op jit(solution)/shard_map/all_to_all | solution.py:117
  (24 other events, 42.7 us)

commit v2 on v1

v2 whole, which is shorter than its diff:
```python
import jax
import jax.numpy as jnp
from jax import lax
from jax.experimental import pallas as pl
from jax.experimental.pallas import tpu as pltpu
from jax.sharding import PartitionSpec as P

BLK = 256

gelu_scale = 0.7978845608028654


def gelu_pair(hidden):
    inner_arg = gelu_scale * (hidden + 0.044715 * hidden * hidden * hidden)
    tangent = jnp.tanh(inner_arg)
    gelu_value = 0.5 * hidden * (1.0 + tangent)
    gelu_slope = 0.5 * (1.0 + tangent) + 0.5 * hidden * (1.0 - tangent * tangent) * gelu_scale * (
        1.0 + 3.0 * 0.044715 * hidden * hidden
    )
    return (gelu_value, gelu_slope)


def mm(spec, a, b):
    return jnp.einsum(spec, a, b, preferred_element_type=jnp.float32)


def regroup(piece, group_count):
    local_blocks, block_width, token_count = piece.shape
    stacked = piece.reshape(local_blocks, group_count, block_width // group_count, token_count)
    arrived = lax.all_to_all(stacked, "bfly", split_axis=1, concat_axis=1, tiled=True)
    return arrived.reshape(local_blocks, block_width, token_count)


def any_mesh(tokens, grad_out, weight_a, weight_b, weight_c, weight_e):
    group_count = lax.axis_size("bfly")
    full_a, full_b, full_c, full_e = (
        lax.all_gather(w, "dp", axis=1, tiled=True)
        for w in (weight_a, weight_b, weight_c, weight_e)
    )
    token_count = tokens.shape[0]
    inner_blocks = full_a.shape[0]
    spread_width = full_a.shape[2]
    local_blocks = full_b.shape[0]
    inputs = tokens.reshape(token_count, inner_blocks, BLK).transpose(1, 2, 0)
    upstream = grad_out.reshape(token_count, inner_blocks, BLK).transpose(1, 2, 0)
    hidden_view = (local_blocks, BLK, token_count)
    wide_view = (inner_blocks, spread_width, token_count)
    spread = mm("kit,kio->kot", inputs, full_a).astype(jnp.bfloat16).reshape(hidden_view)
    back_out = mm("kjt,koj->kot", upstream, full_e).astype(jnp.bfloat16).reshape(hidden_view)
    permuted = regroup(spread, group_count)
    back_mid = regroup(back_out, group_count)
    gelu_value, gelu_slope = gelu_pair(mm("qit,qij->qjt", permuted, full_b))
    active = gelu_value.astype(jnp.bfloat16)
    narrowed = mm("qit,qij->qjt", active, full_c).astype(jnp.bfloat16)
    back_hidden = (mm("qjt,qij->qit", back_mid, full_c) * gelu_slope).astype(jnp.bfloat16)
    back_first = mm("qjt,qij->qit", back_hidden, full_b).astype(jnp.bfloat16)
    returned = regroup(narrowed, group_count).reshape(wide_view)
    back_spread = regroup(back_first, group_count).reshape(wide_view)
    output = mm("kot,koj->kjt", returned, full_e)
    back_input = mm("kot,kio->kit", back_spread, full_a)
    parts = (
        mm("kit,kot->kio", inputs, back_spread),
        mm("qit,qjt->qij", permuted, back_hidden),
        mm("qit,qjt->qij", active, back_mid),
        mm("kot,kjt->koj", returned, upstream),
    )
    grads = tuple(
        lax.psum_scatter(part.astype(jnp.bfloat16), "dp", scatter_dimension=1, tiled=True).astype(
            jnp.float32
        )
        for part in parts
    )

    def rows(x):
        return x.astype(jnp.bfloat16).transpose(2, 0, 1).reshape(token_count, inner_blocks * BLK)

    return (rows(output), rows(back_input)) + grads


def xor_permute(x, mask):
    n = lax.axis_size("bfly")
    return lax.ppermute(x, "bfly", [(i, i ^ mask) for i in range(n)])


def exchange(x, axes):
    return lax.all_to_all(x, axes, split_axis=0, concat_axis=0, tiled=True)


def deal_weight(w):
    pairs = lax.axis_size("dp") // 2
    sets = w.reshape(pairs, 3, 2, w.shape[1], w.shape[2])
    own = jnp.stack([sets[:, 0], sets[:, 2]], axis=1)
    mid = jnp.stack([sets[:, 1], sets[:, 1]], axis=1)
    return jnp.stack([own, mid], axis=2).reshape((pairs * 2, 2) + sets.shape[2:])


def gather_bfly(w):
    across = xor_permute(w, 2)
    return [w, xor_permute(w, 1), across, xor_permute(across, 1)]


def add(x, y):
    return (x.astype(jnp.float32) + y.astype(jnp.float32)).astype(jnp.bfloat16)


def scatter_bfly(keep, send):
    half = add(keep, xor_permute(send, 1))
    return add(half[0], xor_permute(half[1], 2))


def deal_tokens(x):
    ndp, nb = lax.axis_size("dp"), lax.axis_size("bfly")
    pairs, count = ndp // 2, x.shape[0]
    view = x.reshape(count, pairs, 3, BLK)
    own = view[:, :, 0::2].reshape(nb, count // nb, ndp, BLK).transpose(2, 0, 1, 3)
    mid = view[:, :, 1].reshape(2, nb, count // nb // 2, pairs, BLK).transpose(3, 0, 1, 2, 4)
    mid = mid.reshape(ndp, nb, count // nb // 2, BLK)
    return jnp.concatenate([own, mid], axis=2).reshape(ndp * nb, -1, BLK)


def undeal_tokens(got, count):
    ndp, nb = lax.axis_size("dp"), lax.axis_size("bfly")
    pairs, own_count = ndp // 2, count // nb
    own = got[:, :own_count].reshape(pairs, 2, count, BLK)
    mid = got[:, own_count:].reshape(pairs, 1, count, BLK)
    sets = jnp.concatenate([own[:, :1], mid, own[:, 1:]], axis=1)
    return sets.transpose(2, 0, 1, 3).reshape(count, pairs * 3 * BLK)


def dot(x, y, contract_x, contract_y):
    dims = (((contract_x,), (contract_y,)), ((), ()))
    return lax.dot_general(x, y, dims, preferred_element_type=jnp.float32)


def square(x):
    return x.reshape(BLK, BLK)


def half_src(part, r):
    return pl.ds(r * (part // 2), part // 2)


def forward_kernel(f_ref, x_ref, *refs):
    ab, ce, (out_ref,), saved = refs[:4], refs[4:8], refs[8:9], (refs[9:13], refs[13:17])
    ndp, nb, all_rows, _ = x_ref.shape
    own_rows = 2 * all_rows // 3
    f = f_ref[0]
    for slot, (lo, hi) in enumerate(((0, own_rows), (own_rows, all_rows))):
        perm, active, slope, ret = saved[slot]
        count = ndp * (hi - lo)
        tiles = (nb, BLK // nb, count)
        for m in range(nb):
            d = f ^ m
            x = x_ref[:, d, lo:hi, :].reshape(count, BLK)
            for r in range(2):
                spread = dot(square(ab[m][:, 0, slot, r]), x, 0, 1).astype(jnp.bfloat16)
                perm[r, :, d] = spread.reshape(tiles)
        for m in range(nb):
            s = f ^ m
            for r in range(2):
                p = perm[r, s].reshape(BLK, count)
                value, grade = gelu_pair(dot(square(ab[m][:, 1, slot, r]), p, 0, 0))
                value = value.astype(jnp.bfloat16)
                active[r, s] = value
                slope[r, s] = grade.astype(jnp.bfloat16)
                narrowed = dot(square(ce[m][:, 0, slot, r]), value, 0, 0).astype(jnp.bfloat16)
                ret[r, :, s] = narrowed.reshape(tiles)
        for m in range(nb):
            d = f ^ m
            total = 0.0
            for r in range(2):
                e = square(ce[m][half_src(ndp, r), 1, slot])
                total = total + dot(ret[r, d].reshape(BLK, count), e, 0, 0)
            out_ref[:, d, lo:hi, :] = total.astype(jnp.bfloat16).reshape(ndp, hi - lo, BLK)


def backward_kernel(f_ref, x_ref, g_ref, *refs):
    ab, ce, saved = refs[:4], refs[4:8], (refs[8:12], refs[12:16])
    gin_ref, keep_ref, send_ref = refs[16:19]
    scratch = (refs[19:21], refs[21:23])
    ndp, nb, all_rows, _ = x_ref.shape
    own_rows = 2 * all_rows // 3
    rows = BLK // ndp
    f = f_ref[0]

    def grads(m):
        return (send_ref if m % 2 else keep_ref), m // 2

    for slot, (lo, hi) in enumerate(((0, own_rows), (own_rows, all_rows))):
        perm, active, slope, ret = saved[slot]
        mid, spread = scratch[slot]
        count = ndp * (hi - lo)
        tiles = (nb, BLK // nb, count)
        for m in range(nb):
            d = f ^ m
            g = g_ref[:, d, lo:hi, :].reshape(count, BLK)
            ref, at = grads(m)
            for r in range(2):
                e = square(ce[m][half_src(ndp, r), 1, slot])
                mid[r, :, d] = dot(e, g, 1, 1).astype(jnp.bfloat16).reshape(tiles)
                part = dot(ret[r, d].reshape(BLK, count), g, 1, 0).astype(jnp.bfloat16)
                ref[at, half_src(ndp, r), 3, slot] = part.reshape(ndp // 2, 2, rows, BLK)
        for m in range(nb):
            s = f ^ m
            ref, at = grads(m)
            for r in range(2):
                p = perm[r, s].reshape(BLK, count)
                back_mid = mid[r, s].reshape(BLK, count)
                back = dot(square(ce[m][:, 0, slot, r]), back_mid, 1, 0)
                back = (back * slope[r, s].astype(jnp.float32)).astype(jnp.bfloat16)
                part = dot(active[r, s], back_mid, 1, 1).astype(jnp.bfloat16)
                ref[at, :, 2, slot, r] = part.reshape(ndp, rows, BLK)
                part = dot(p, back, 1, 1).astype(jnp.bfloat16)
                ref[at, :, 1, slot, r] = part.reshape(ndp, rows, BLK)
                first = dot(square(ab[m][:, 1, slot, r]), back, 1, 0).astype(jnp.bfloat16)
                spread[r, :, s] = first.reshape(tiles)
        for m in range(nb):
            d = f ^ m
            x = x_ref[:, d, lo:hi, :].reshape(count, BLK)
            ref, at = grads(m)
            total = 0.0
            for r in range(2):
                back = spread[r, d].reshape(BLK, count)
                total = total + dot(back, square(ab[m][:, 0, slot, r]), 0, 1)
                part = dot(x, back, 0, 1).astype(jnp.bfloat16)
                ref[at, :, 0, slot, r] = part.reshape(ndp, rows, BLK)
            gin_ref[:, d, lo:hi, :] = total.astype(jnp.bfloat16).reshape(ndp, hi - lo, BLK)


def on_chip(kernel, outs, scratch, inputs):
    in_specs = [pl.BlockSpec(memory_space=pltpu.SMEM)]
    in_specs += [pl.BlockSpec(memory_space=pltpu.VMEM)] * (len(inputs) - 1)
    return pl.pallas_call(
        kernel,
        out_shape=[jax.ShapeDtypeStruct(shape, jnp.bfloat16) for shape in outs],
        in_specs=in_specs,
        out_specs=[pl.BlockSpec(memory_space=pltpu.VMEM)] * len(outs),
        scratch_shapes=[pltpu.VMEM(shape, jnp.bfloat16) for shape in scratch],
        compiler_params=pltpu.CompilerParams(vmem_limit_bytes=56 * 2**20),
    )(*inputs)


def token_plan(tokens, grad_out, weight_a, weight_b, weight_c, weight_e):
    ndp, nb = lax.axis_size("dp"), lax.axis_size("bfly")
    blocks, rows, _ = weight_a.shape
    parts, count = 2 * blocks, tokens.shape[0]
    dealt_a = weight_a.reshape(blocks, rows, 2, BLK).transpose(0, 2, 1, 3).reshape(parts, rows, BLK)
    dealt_e = weight_e.reshape(parts, rows, BLK)
    seat = lax.axis_index("bfly").astype(jnp.int32).reshape(1)

    def weights_in(first, second):
        both = jnp.stack([deal_weight(first), deal_weight(second)], axis=1)
        return gather_bfly(exchange(both, "dp"))

    everyone = ("dp", "bfly")
    ab = weights_in(dealt_a, weight_b)
    ce = weights_in(weight_c, dealt_e)
    x = exchange(deal_tokens(tokens), everyone).reshape(ndp, nb, -1, BLK)
    g = exchange(deal_tokens(grad_out), everyone).reshape(ndp, nb, -1, BLK)

    own, mid = count * ndp // nb, count * ndp // nb // 2
    saved = []
    for t in (own, mid):
        tiled, whole = (2, nb, nb, BLK // nb, t), (2, nb, BLK, t)
        saved += [tiled, whole, whole, tiled]
    out, *kept = on_chip(forward_kernel, [x.shape] + saved, [], [seat, x] + ab + ce)
    output = undeal_tokens(exchange(out.reshape(ndp * nb, -1, BLK), everyone), count)
    grad_shape = (2, ndp, 4, 2, 2, rows, BLK)
    gin, keep, send = on_chip(
        backward_kernel,
        [x.shape, grad_shape, grad_shape],
        [saved[0], saved[0], saved[4], saved[4]],
        [seat, x, g] + ab + ce + kept,
    )
    grad_in = undeal_tokens(exchange(gin.reshape(ndp * nb, -1, BLK), everyone), count)
    got = exchange(scatter_bfly(keep, send), "dp").astype(jnp.float32)
    got = got.reshape(ndp // 2, 2, 4, 2, 2, rows, BLK)

    def own_rows(which):
        mid = got[:, 0, which, 1] + got[:, 1, which, 1]
        return jnp.stack([got[:, 0, which, 0], mid, got[:, 1, which, 0]], axis=1)

    grad_a = own_rows(0).reshape(blocks, 2, rows, BLK).transpose(0, 2, 1, 3)
    return (
        output,
        grad_in,
        grad_a.reshape(weight_a.shape),
        own_rows(1).reshape(weight_b.shape),
        own_rows(2).reshape(weight_c.shape),
        own_rows(3).reshape(weight_e.shape),
    )


def per_device(tokens, grad_out, weight_a, weight_b, weight_c, weight_e):
    ndp, nb = lax.axis_size("dp"), lax.axis_size("bfly")
    fits = nb == 4 and ndp % 2 == 0 and 2 * weight_a.shape[0] == 3 * ndp
    fits = fits and tokens.shape[0] % (32 * nb) == 0 and weight_a.shape[1] * ndp == BLK
    fits = fits and weight_a.shape[2] == 2 * BLK and weight_e.shape[1] == 2 * weight_a.shape[1]
    plan = token_plan if fits else any_mesh
    return plan(tokens, grad_out, weight_a, weight_b, weight_c, weight_e)


def solution(mesh):
    in_specs = (P("dp", "bfly"),) * 2 + (P("bfly", "dp", None),) * 4
    return jax.shard_map(
        per_device, mesh=mesh, in_specs=in_specs, out_specs=in_specs, check_vma=False
    )
```

time: 375 us -> 392 us (1.045)
  blocking collectives: 0 us -> 42.5 us
  Pallas kernels: 0 us -> 37.4 us
  starting transfers between devices: 54.8 us -> 31.7 us
  matrix products: 23 us -> 0 us
  other arithmetic: 31.7 us -> 18.7 us
  waiting for transfers between devices: 211 us -> 220 us
  local copies, waits for them, and re-layouts: 47.8 us -> 39.4 us
    ppermute x12 -> x8, waiting for transfers between devices: 67.4 us -> 122 us  [xor_permute(): return lax.ppermute(x, 'bfly', [(i, i ^ mask) for i in range(n)])]
    all_to_all x10 -> x6, waiting for transfers between devices: 143 us -> 98.4 us  [exchange(): return lax.all_to_all(x, axes, split_axis=0, concat_axis=0, tiled=True)]
    all_to_all x0 -> x1, blocking collectives: none -> 42.5 us  [exchange(): return lax.all_to_all(x, axes, split_axis=0, concat_axis=0, tiled=True)]
    pallas_call x0 -> x2, Pallas kernels: none -> 37.4 us  [on_chip(): pl.pallas_call(kernel, out_shape=[jax.ShapeDtypeStruct(shape, jnp.bfloat1...]
    dot_general x24 -> x0, matrix products: 23 us -> none  [mm(): return jnp.einsum(spec, a, b, preferred_element_type=jnp.float32)]
    all_to_all x10 -> x6, starting transfers between devices: 47.3 us -> 27.1 us  [exchange(): return lax.all_to_all(x, axes, split_axis=0, concat_axis=0, tiled=True)]
    another operation x16 -> x4, other arithmetic: 13.1 us -> 0.28 us  [own_rows(): return jnp.stack([got[:, 0, which, 0], mid, got[:, 1, which, 0]], axis=1)]
    unnamed x76 -> x20, local copies, waits for them, and re-layouts: 19.8 us -> 12.5 us
  transfers between devices with their start and end apart: 22 -> 14, of which waited for: 11 -> 8; matrix products, arithmetic and copies ran while one was open for 18% -> 12% of each run, Pallas kernels for 0% -> 4%
where the time goes in v2:
time: 392 us; the launch traced here: 391 us
  waiting for transfers between devices  220 us (56%)
  blocking collectives  42.5 us (11%)
  local copies, waits for them, and re-layouts  39.4 us (10%)
  Pallas kernels  37.4 us (10%)
  starting transfers between devices  31.7 us (8%)
  other arithmetic  18.7 us (5%)
    ppermute x8, waiting for transfers between devices, xor_permute(): return lax.ppermute(x, 'bfly', [(i, i ^ mask) for i in range(n)])  122 us
    all_to_all x6, waiting for transfers between devices, exchange(): return lax.all_to_all(x, axes, split_axis=0, concat_axis=0, tiled=True)  98.4 us
    all_to_all x1, blocking collectives, exchange(): return lax.all_to_all(x, axes, split_axis=0, concat_axis=0, tiled=True)  42.5 us
    pallas_call x2, Pallas kernels, on_chip(): pl.pallas_call(kernel, out_shape=[jax.ShapeDtypeStruct(shape, jnp.bfloat1...  37.4 us
    all_to_all x6, starting transfers between devices, exchange(): return lax.all_to_all(x, axes, split_axis=0, concat_axis=0, tiled=True)  27.1 us
    unnamed x20, local copies, waits for them, and re-layouts  12.5 us
    slice x4, local copies, waits for them, and re-layouts, deal_tokens(): view[:, :, 0::2].reshape(nb, count // nb, ndp, BLK).transpose(2, 0, 1, 3)  8.35 us
    convert_element_type x2, other arithmetic, add(): return (x.astype(jnp.float32) + y.astype(jnp.float32)).astype(jnp.bfloat16)  7.96 us
  transfers between devices with their start and end apart: 14, of which 8 were waited for; matrix products, arithmetic and copies ran while one was open for 12% of the time, Pallas kernels for 4%

profile of v2, /device:TPU:0, one launch (start us, length us, event | category | flops | bytes accessed | tf_op | source)
XLA Modules:
  0.0 391.0 jit_solution(15198866843595046788)
XLA Ops:
  4.1 7.4 %all-to-all-start.1 = ((bf16[8,2,2,2,32,256]{5,4,3,2,1,0:T(8,128)(2,1)}), bf16[8,2,2,2,32,256]{5,4,3,2,1,0:T(8,128)(2,1)S(1)}, u32[]{:S(2)}, u32[]{:S(2)}) async-start(bf16[8,2,2,2,32,256]{5,4,3,2,1,0:T(8,128)(2,1)} %maximum_maximum_fusion), calls=%async_computation.1 | async-start | bytes 2097152 | tf_op jit(solution)/shard_map/all_to_all | solution.py:86
  12.8 24.5 %all-to-all-done.1.refs_0_ = bf16[8,2,2,2,32,256]{5,4,3,2,1,0:T(8,128)(2,1)S(1)} async-done(((bf16[8,2,2,2,32,256]{5,4,3,2,1,0:T(8,128)(2,1)}), bf16[8,2,2,2,32,256]{5,4,3,2,1,0:T(8,128)(2,1)S(1)}, u32[]{:S(2)}, u32[]{:S(2)}) %all-to-all-start.1) | async-done | bytes 1048608 | tf_op jit(solution)/shard_map/all_to_all | solution.py:86
  37.3 3.6 all-to-all-start.2
  40.9 2.6 copy.63
  44.5 2.3 slice.130
  49.3 2.3 pad_maximum_fusion
  51.6 15.2 %all-to-all-done.2.refs_4_ = bf16[8,2,2,2,32,256]{5,4,3,2,1,0:T(8,128)(2,1)S(1)} async-done(((bf16[8,2,2,2,32,256]{5,4,3,2,1,0:T(8,128)(2,1)}), bf16[8,2,2,2,32,256]{5,4,3,2,1,0:T(8,128)(2,1)S(1)}, u32[]{:S(2)}, u32[]{:S(2)}) %all-to-all-start.2) | async-done | bytes 1048608 | tf_op jit(solution)/shard_map/all_to_all | solution.py:86
  67.8 3.7 all-to-all-start
  71.5 2.6 copy.69
  75.1 2.3 slice.148
  78.4 2.3 copy.70
  80.7 2.5 pad_maximum_fusion.1
  83.3 25.9 %all-to-all-done = bf16[32,96,256]{2,1,0:T(8,128)(2,1)S(1)} async-done(((bf16[32,96,256]{2,1,0:T(8,128)(2,1)}), bf16[32,96,256]{2,1,0:T(8,128)(2,1)S(1)}, u32[]{:S(2)}, u32[]{:S(2)}) %all-to-all-start) | async-done | bytes 1572896 | tf_op jit(solution)/shard_map/all_to_all | solution.py:86
  109.2 4.1 %all-to-all-start.4 = ((bf16[32,96,256]{2,1,0:T(8,128)(2,1)}), bf16[32,96,256]{2,1,0:T(8,128)(2,1)}, u32[]{:S(2)}, u32[]{:S(2)}) async-start(bf16[32,96,256]{2,1,0:T(8,128)(2,1)} %pad_maximum_fusion.1), calls=%async_computation.4 | async-start | bytes 3145728 | tf_op jit(solution)/shard_map/all_to_all | solution.py:86
  113.3 1.8 collective-permute-start.1
  115.9 39.9 %collective-permute-done.1.refs_2_ = bf16[8,2,2,2,32,256]{5,4,3,2,1,0:T(8,128)(2,1)} collective-permute-done((bf16[8,2,2,2,32,256]{5,4,3,2,1,0:T(8,128)(2,1)S(1)}, bf16[8,2,2,2,32,256]{5,4,3,2,1,0:T(8,128)(2,1)}, u32[]{:S(2)}, u32[]{:S(2)}) %collective-permute-start.1) | collective-permute-done | bytes 1048608 | tf_op jit(solution)/shard_map/ppermute | solution.py:82
  155.8 22.0 %collective-permute-done.4.refs_6_ = bf16[8,2,2,2,32,256]{5,4,3,2,1,0:T(8,128)(2,1)} collective-permute-done((bf16[8,2,2,2,32,256]{5,4,3,2,1,0:T(8,128)(2,1)}, bf16[8,2,2,2,32,256]{5,4,3,2,1,0:T(8,128)(2,1)}, u32[]{:S(2)}, u32[]{:S(2)}) %collective-permute-start.4) | collective-permute-done | bytes 1048608 | tf_op jit(solution)/shard_map/ppermute | solution.py:82
  177.8 3.0 collective-permute-done.5.refs_7_
  180.8 16.6 %shard_map.109 = (bf16[8,4,96,256]{3,2,1,0:T(8,128)(2,1)}, bf16[2,4,4,64,512]{4,3,2,1,0:T(8,128)(2,1)}, bf16[2,4,256,512]{3,2,1,0:T(8,128)(2,1)}, bf16[2,4,256,5...) custom-call(s32[1]{0:T(128)} %bitcast.f_ref, ...), custom_call_target="tpu_custom_call" | custom-call | tf_op jit(solution)/shard_map/pallas_call | solution.py:233
  197.4 20.8 %shard_map.110 = (bf16[8,4,96,256]{3,2,1,0:T(8,128)(2,1)}, bf16[2,8,4,2,2,32,256]{6,5,4,3,2,1,0:T(8,128)(2,1)}, bf16[2,8,4,2,2,32,256]{6,5,4,3,2,1,0:T(8,128)(2,1)}) custom-call(s32[1]{0:T(128)} %bitcast.f_ref, bf16[8,4,96,256]{3,2,1,0:T(8,128)(2,1)} %bitcast.146, bf16[8,4,96,256]{3,2,1,0:T(8,128)(2,1)} %bitcast.35.g_ref, ...), custom_call_target="tpu_custom_call" | custom-call | tf_op jit(solution)/shard_map/pallas_call | solution.py:233
  218.4 42.5 %all_to_all.35 = bf16[32,96,256]{2,1,0:T(8,128)(2,1)} all-to-all(bf16[32,96,256]{2,1,0:T(8,128)(2,1)S(1)} %bitcast.163), channel_id=1, replica_groups=mesh['dp'=8,'bfly'=4] {'dp','bfly'}, dimensions={0} | all-to-all | bytes 3145728 | tf_op jit(solution)/shard_map/all_to_all | solution.py:86
  260.9 3.1 all-to-all-start.5
  263.9 5.6 %add_convert_fusion = bf16[2,8,4,2,2,32,256]{6,5,4,3,2,1,0:T(8,128)(2,1)S(1)} fusion(bf16[2,8,4,2,2,32,256]{6,5,4,3,2,1,0:T(8,128)(2,1)} %collective-permute-done.6, bf16[2,8,4,2,2,32,256]{6,5,4,3,2,1,0:T(8,128)(2,1)} %get-tuple-element.28), kind=kLoop, calls=%fused_computation | loop fusion | flops 8388608 | bytes 12582912 | tf_op jit(solution)/shard_map/convert_element_type | solution.py:103
  269.9 1.8 collective-permute-start.7
  271.7 57.1 %collective-permute-done.7 = bf16[8,4,2,2,32,256]{5,4,3,2,1,0:T(8,128)(2,1)S(1)} collective-permute-done((bf16[8,4,2,2,32,256]{5,4,3,2,1,0:T(8,128)(2,1)S(1)}, bf16[8,4,2,2,32,256]{5,4,3,2,1,0:T(8,128)(2,1)S(1)}, u32[]{:S(2)}, u32[]{:S(2)}) %collective-permute-start.7) | collective-permute-done | bytes 2097184 | tf_op jit(solution)/shard_map/ppermute | solution.py:82
  328.8 2.4 fusion
  332.3 5.3 %all-to-all-start.6 = ((bf16[8,4,2,2,32,256]{5,4,3,2,1,0:T(8,128)(2,1)}), bf16[8,4,2,2,32,256]{5,4,3,2,1,0:T(8,128)(2,1)S(1)}, u32[]{:S(2)}, u32[]{:S(2)}) async-start(bf16[8,4,2,2,32,256]{5,4,3,2,1,0:T(8,128)(2,1)} %fusion), calls=%async_computation.6 | async-start | bytes 4194304 | tf_op jit(solution)/shard_map/all_to_all | solution.py:86
  340.3 2.6 copy.68
  342.9 2.6 copy.91
  348.1 2.6 copy.73
  350.7 2.6 copy.92
  353.3 32.8 %all-to-all-done.6 = bf16[8,4,2,2,32,256]{5,4,3,2,1,0:T(8,128)(2,1)S(1)} async-done(((bf16[8,4,2,2,32,256]{5,4,3,2,1,0:T(8,128)(2,1)}), bf16[8,4,2,2,32,256]{5,4,3,2,1,0:T(8,128)(2,1)S(1)}, u32[]{:S(2)}, u32[]{:S(2)}) %all-to-all-start.6) | async-done | bytes 2097184 | tf_op jit(solution)/shard_map/all_to_all | solution.py:86
  (69 shorter events, 23.9 us)
Async XLA Ops:
  3.0 8.5 %copy-start.6 = (bf16[12,64,256]{2,1,0:T(8,128)(2,1)S(1)}, bf16[12,64,256]{2,1,0:T(8,128)(2,1)}, u32[]{:S(2)}) copy-start(bf16[12,64,256]{2,1,0:T(8,128)(2,1)} %param.11) | copy-start | bytes 1179652
  4.1 7.5 %copy-start.7 = (bf16[24,32,256]{2,1,0:T(8,128)(2,1)S(1)}, bf16[24,32,256]{2,1,0:T(8,128)(2,1)}, u32[]{:S(2)}) copy-start(bf16[24,32,256]{2,1,0:T(8,128)(2,1)} %param.10) | copy-start | bytes 1179652
  4.1 33.2 %all-to-all-start.1 = ((bf16[8,2,2,2,32,256]{5,4,3,2,1,0:T(8,128)(2,1)}), bf16[8,2,2,2,32,256]{5,4,3,2,1,0:T(8,128)(2,1)S(1)}, u32[]{:S(2)}, u32[]{:S(2)}) async-start(bf16[8,2,2,2,32,256]{5,4,3,2,1,0:T(8,128)(2,1)} %maximum_maximum_fusion), calls=%async_computation.1 | async-start | bytes 2097152 | tf_op jit(solution)/shard_map/all_to_all | solution.py:86
  37.3 78.1 %copy-start.1 = (bf16[8,2,2,2,32,256]{5,4,3,2,1,0:T(8,128)(2,1)}, bf16[8,2,2,2,32,256]{5,4,3,2,1,0:T(8,128)(2,1)S(1)}, u32[]{:S(2)}) copy-start(bf16[8,2,2,2,32,256]{5,4,3,2,1,0:T(8,128)(2,1)S(1)} %all-to-all-done.1.refs_0_) | copy-start | bytes 3145732
  37.3 29.5 %all-to-all-start.2 = ((bf16[8,2,2,2,32,256]{5,4,3,2,1,0:T(8,128)(2,1)}), bf16[8,2,2,2,32,256]{5,4,3,2,1,0:T(8,128)(2,1)S(1)}, u32[]{:S(2)}, u32[]{:S(2)}) async-start(bf16[8,2,2,2,32,256]{5,4,3,2,1,0:T(8,128)(2,1)} %maximum_maximum_fusion.1), calls=%async_computation.2 | async-start | bytes 2097152 | tf_op jit(solution)/shard_map/all_to_all | solution.py:86
  66.8 1.0 copy-start.2
  67.8 41.4 %all-to-all-start = ((bf16[32,96,256]{2,1,0:T(8,128)(2,1)}), bf16[32,96,256]{2,1,0:T(8,128)(2,1)S(1)}, u32[]{:S(2)}, u32[]{:S(2)}) async-start(bf16[32,96,256]{2,1,0:T(8,128)(2,1)} %pad_maximum_fusion), calls=%async_computation | async-start | bytes 3145728 | tf_op jit(solution)/shard_map/all_to_all | solution.py:86
  78.4 2.3 copy-start.4
  109.2 71.5 %copy-start = (bf16[32,96,256]{2,1,0:T(8,128)(2,1)}, bf16[32,96,256]{2,1,0:T(8,128)(2,1)S(1)}, u32[]{:S(2)}) copy-start(bf16[32,96,256]{2,1,0:T(8,128)(2,1)S(1)} %all-to-all-done) | copy-start | bytes 4718596
  109.2 88.2 %all-to-all-start.4 = ((bf16[32,96,256]{2,1,0:T(8,128)(2,1)}), bf16[32,96,256]{2,1,0:T(8,128)(2,1)}, u32[]{:S(2)}, u32[]{:S(2)}) async-start(bf16[32,96,256]{2,1,0:T(8,128)(2,1)} %pad_maximum_fusion.1), calls=%async_computation.4 | async-start | bytes 3145728 | tf_op jit(solution)/shard_map/all_to_all | solution.py:86
  113.3 42.5 %collective-permute-start.1 = (bf16[8,2,2,2,32,256]{5,4,3,2,1,0:T(8,128)(2,1)S(1)}, bf16[8,2,2,2,32,256]{5,4,3,2,1,0:T(8,128)(2,1)}, u32[]{:S(2)}, u32[]{:S(2)}) collective-permute-start(bf16[8,2,2,2,32,256]{5,4,3,2,1,0:T(8,128)(2,1)S(1)} %all-to-all-done.1.refs_0_), channel_id=1, source_target_pairs={{0,2},{1,3},{2,0},{3,1},{4,6},{5,7},{6,4},{7,5},{8,10},{9,11},{10,... | collective-permute-start | bytes 3145736 | tf_op jit(solution)/shard_map/ppermute | solution.py:82
  115.0 62.7 %collective-permute-start.4 = (bf16[8,2,2,2,32,256]{5,4,3,2,1,0:T(8,128)(2,1)}, bf16[8,2,2,2,32,256]{5,4,3,2,1,0:T(8,128)(2,1)}, u32[]{:S(2)}, u32[]{:S(2)}) collective-permute-start(bf16[8,2,2,2,32,256]{5,4,3,2,1,0:T(8,128)(2,1)} %copy-done.2), channel_id=1, source_target_pairs={{0,2},{1,3},{2,0},{3,1},{4,6},{5,7},{6,4},{7,5},{8,10},{9,11},{10,... | collective-permute-start | bytes 3145736 | tf_op jit(solution)/shard_map/ppermute | solution.py:82
  115.4 62.4 %collective-permute-start = (bf16[8,2,2,2,32,256]{5,4,3,2,1,0:T(8,128)(2,1)S(1)}, bf16[8,2,2,2,32,256]{5,4,3,2,1,0:T(8,128)(2,1)}, u32[]{:S(2)}, u32[]{:S(2)}) collective-permute-start(bf16[8,2,2,2,32,256]{5,4,3,2,1,0:T(8,128)(2,1)S(1)} %all-to-all-done.1.refs_0_), channel_id=1, source_target_pairs={{0,1},{1,0},{2,3},{3,2},{4,5},{5,4},{6,7},{7,6},{8,9},{9,8},{10,11... | collective-permute-start | bytes 3145736 | tf_op jit(solution)/shard_map/ppermute | solution.py:82
  115.4 62.4 %collective-permute-start.3 = (bf16[8,2,2,2,32,256]{5,4,3,2,1,0:T(8,128)(2,1)}, bf16[8,2,2,2,32,256]{5,4,3,2,1,0:T(8,128)(2,1)}, u32[]{:S(2)}, u32[]{:S(2)}) collective-permute-start(bf16[8,2,2,2,32,256]{5,4,3,2,1,0:T(8,128)(2,1)} %copy-done.2), channel_id=1, source_target_pairs={{0,1},{1,0},{2,3},{3,2},{4,5},{5,4},{6,7},{7,6},{8,9},{9,8},{10,11... | collective-permute-start | bytes 3145736 | tf_op jit(solution)/shard_map/ppermute | solution.py:82
  155.8 22.0 %collective-permute-start.2 = (bf16[8,2,2,2,32,256]{5,4,3,2,1,0:T(8,128)(2,1)}, bf16[8,2,2,2,32,256]{5,4,3,2,1,0:T(8,128)(2,1)}, u32[]{:S(2)}, u32[]{:S(2)}) collective-permute-start(bf16[8,2,2,2,32,256]{5,4,3,2,1,0:T(8,128)(2,1)} %collective-permute-done.1.refs_2_), channel_id=1, source_target_pairs={{0,1},{1,0},{2,3},{3,2},{4,5},{5,4},{6,7},{7,6},{8,9},{9,8},{10,11... | collective-permute-start | bytes 3145736 | tf_op jit(solution)/shard_map/ppermute | solution.py:82
  177.7 3.0 collective-permute-start.5
  197.4 21.0 %copy-start.5 = (bf16[8,4,96,256]{3,2,1,0:T(8,128)(2,1)S(1)}, bf16[8,4,96,256]{3,2,1,0:T(8,128)(2,1)}, u32[]{:S(2)}) copy-start(bf16[8,4,96,256]{3,2,1,0:T(8,128)(2,1)} %get-tuple-element.18) | copy-start | bytes 4718596
  218.2 45.7 %collective-permute-start.6 = (bf16[2,8,4,2,2,32,256]{6,5,4,3,2,1,0:T(8,128)(2,1)}, bf16[2,8,4,2,2,32,256]{6,5,4,3,2,1,0:T(8,128)(2,1)}, u32[]{:S(2)}, u32[]{:S(2)}) collective-permute-start(bf16[2,8,4,2,2,32,256]{6,5,4,3,2,1,0:T(8,128)(2,1)} %get-tuple-element.29), channel_id=1, source_target_pairs={{0,1},{1,0},{2,3},{3,2},{4,5},{5,4},{6,7},{7,6},{8,9},{9,8},{10,11... | collective-permute-start | bytes 12582920 | tf_op jit(solution)/shard_map/ppermute | solution.py:82
  260.9 70.3 %all-to-all-start.5 = ((bf16[32,96,256]{2,1,0:T(8,128)(2,1)}), bf16[32,96,256]{2,1,0:T(8,128)(2,1)S(1)}, u32[]{:S(2)}, u32[]{:S(2)}) async-start(bf16[32,96,256]{2,1,0:T(8,128)(2,1)} %bitcast.36), calls=%async_computation.5 | async-start | bytes 3145728 | tf_op jit(solution)/shard_map/all_to_all | solution.py:86
  269.9 58.9 %collective-permute-start.7 = (bf16[8,4,2,2,32,256]{5,4,3,2,1,0:T(8,128)(2,1)S(1)}, bf16[8,4,2,2,32,256]{5,4,3,2,1,0:T(8,128)(2,1)S(1)}, u32[]{:S(2)}, u32[]{:S(2)}) collective-permute-start(bf16[8,4,2,2,32,256]{5,4,3,2,1,0:T(8,128)(2,1)S(1)} %slice_bitcast_fusion), channel_id=1, source_target_pairs={{0,2},{1,3},{2,0},{3,1},{4,6},{5,7},{6,4},{7,5},{8,10},{9,11},{10,... | collective-permute-start | bytes 6291464 | tf_op jit(solution)/shard_map/ppermute | solution.py:82
  331.1 1.2 copy-start.3
  332.3 53.8 %all-to-all-start.6 = ((bf16[8,4,2,2,32,256]{5,4,3,2,1,0:T(8,128)(2,1)}), bf16[8,4,2,2,32,256]{5,4,3,2,1,0:T(8,128)(2,1)S(1)}, u32[]{:S(2)}, u32[]{:S(2)}) async-start(bf16[8,4,2,2,32,256]{5,4,3,2,1,0:T(8,128)(2,1)} %fusion), calls=%async_computation.6 | async-start | bytes 4194304 | tf_op jit(solution)/shard_map/all_to_all | solution.py:86
  337.6 1.2 slice-start.2
  337.6 1.4 slice-start.3
  345.5 1.2 slice-start
  345.5 1.4 slice-start.1

commit v3 on v2

--- a/solution.py
+++ b/solution.py
@@ -1,3 +1,5 @@
+import math
+
 import jax
 import jax.numpy as jnp
 from jax import lax
@@ -94,18 +96,16 @@
     return jnp.stack([own, mid], axis=2).reshape((pairs * 2, 2) + sets.shape[2:])
 
 
-def gather_bfly(w):
-    across = xor_permute(w, 2)
+def gather_bfly(w, across):
     return [w, xor_permute(w, 1), across, xor_permute(across, 1)]
+
+
+def after(x, *earlier):
+    return lax.optimization_barrier((x,) + earlier)[0]
 
 
 def add(x, y):
     return (x.astype(jnp.float32) + y.astype(jnp.float32)).astype(jnp.bfloat16)
-
-
-def scatter_bfly(keep, send):
-    half = add(keep, xor_permute(send, 1))
-    return add(half[0], xor_permute(half[1], 2))
 
 
 def deal_tokens(x):
@@ -227,7 +227,7 @@
             gin_ref[:, d, lo:hi, :] = total.astype(jnp.bfloat16).reshape(ndp, hi - lo, BLK)
 
 
-def on_chip(kernel, outs, scratch, inputs):
+def on_chip(kernel, products, outs, scratch, inputs):
     in_specs = [pl.BlockSpec(memory_space=pltpu.SMEM)]
     in_specs += [pl.BlockSpec(memory_space=pltpu.VMEM)] * (len(inputs) - 1)
     return pl.pallas_call(
@@ -236,6 +236,11 @@
         in_specs=in_specs,
         out_specs=[pl.BlockSpec(memory_space=pltpu.VMEM)] * len(outs),
         scratch_shapes=[pltpu.VMEM(shape, jnp.bfloat16) for shape in scratch],
+        cost_estimate=pl.CostEstimate(
+            flops=products * 2 * BLK * BLK,
+            transcendentals=0,
+            bytes_accessed=sum(x.size for x in inputs) * 2 + sum(map(math.prod, outs)) * 2,
+        ),
         compiler_params=pltpu.CompilerParams(vmem_limit_bytes=56 * 2**20),
     )(*inputs)
 
@@ -248,32 +253,40 @@
     dealt_e = weight_e.reshape(parts, rows, BLK)
     seat = lax.axis_index("bfly").astype(jnp.int32).reshape(1)
 
-    def weights_in(first, second):
-        both = jnp.stack([deal_weight(first), deal_weight(second)], axis=1)
-        return gather_bfly(exchange(both, "dp"))
+    def pack(first, second):
+        return jnp.stack([deal_weight(first), deal_weight(second)], axis=1)
 
     everyone = ("dp", "bfly")
-    ab = weights_in(dealt_a, weight_b)
-    ce = weights_in(weight_c, dealt_e)
-    x = exchange(deal_tokens(tokens), everyone).reshape(ndp, nb, -1, BLK)
-    g = exchange(deal_tokens(grad_out), everyone).reshape(ndp, nb, -1, BLK)
+    shape = (ndp, nb, -1, BLK)
+    ab = exchange(pack(dealt_a, weight_b), "dp")
+    ab_across = xor_permute(ab, 2)
+    ce = exchange(after(pack(weight_c, dealt_e), ab), "dp")
+    ce_across = xor_permute(ce, 2)
+    x = exchange(after(deal_tokens(tokens), ab_across, ce), everyone)
+    g = exchange(after(deal_tokens(grad_out), ce_across, x), everyone).reshape(shape)
+    x = x.reshape(shape)
+    ab, ce = gather_bfly(ab, ab_across), gather_bfly(ce, ce_across)
 
     own, mid = count * ndp // nb, count * ndp // nb // 2
     saved = []
     for t in (own, mid):
         tiled, whole = (2, nb, nb, BLK // nb, t), (2, nb, BLK, t)
         saved += [tiled, whole, whole, tiled]
-    out, *kept = on_chip(forward_kernel, [x.shape] + saved, [], [seat, x] + ab + ce)
-    output = undeal_tokens(exchange(out.reshape(ndp * nb, -1, BLK), everyone), count)
+    products = 2 * nb * (own + mid)
+    out, *kept = on_chip(forward_kernel, 4 * products, [x.shape] + saved, [], [seat, x] + ab + ce)
+    out = exchange(out.reshape(ndp * nb, -1, BLK), everyone)
     grad_shape = (2, ndp, 4, 2, 2, rows, BLK)
     gin, keep, send = on_chip(
         backward_kernel,
+        8 * products,
         [x.shape, grad_shape, grad_shape],
         [saved[0], saved[0], saved[4], saved[4]],
         [seat, x, g] + ab + ce + kept,
     )
-    grad_in = undeal_tokens(exchange(gin.reshape(ndp * nb, -1, BLK), everyone), count)
-    got = exchange(scatter_bfly(keep, send), "dp").astype(jnp.float32)
+    half = add(keep, xor_permute(send, 1))
+    gin = exchange(after(gin.reshape(ndp * nb, -1, BLK), half, out), everyone)
+    dealt = add(half[0], xor_permute(half[1], 2))
+    got = exchange(after(dealt, gin), "dp").astype(jnp.float32)
     got = got.reshape(ndp // 2, 2, 4, 2, 2, rows, BLK)
 
     def own_rows(which):
@@ -282,8 +295,8 @@
 
     grad_a = own_rows(0).reshape(blocks, 2, rows, BLK).transpose(0, 2, 1, 3)
     return (
-        output,
-        grad_in,
+        undeal_tokens(out, count),
+        undeal_tokens(gin, count),
         grad_a.reshape(weight_a.shape),
         own_rows(1).reshape(weight_b.shape),
         own_rows(2).reshape(weight_c.shape),

time: 392 us -> 351 us (0.90)
  blocking collectives: 42.5 us -> 0 us
  local copies, waits for them, and re-layouts: 39.4 us -> 30.1 us
  starting transfers between devices: 31.7 us -> 40.4 us
    all_to_all x1 -> x0, blocking collectives: 42.5 us -> none  [exchange(): return lax.all_to_all(x, axes, split_axis=0, concat_axis=0, tiled=True)]
    all_to_all x6 -> x7, starting transfers between devices: 27.1 us -> 34.1 us  [exchange(): return lax.all_to_all(x, axes, split_axis=0, concat_axis=0, tiled=True)]
    slice x4, local copies, waits for them, and re-layouts: 8.35 us -> 3.17 us  [deal_tokens(): view[:, :, 0::2].reshape(nb, count // nb, ndp, BLK).transpose(2, 0, 1, 3)]
    unnamed x20 -> x24, local copies, waits for them, and re-layouts: 12.5 us -> 9.87 us
    all_to_all x6 -> x7, waiting for transfers between devices: 98.4 us -> 98 us  [exchange(): return lax.all_to_all(x, axes, split_axis=0, concat_axis=0, tiled=True)]
  transfers between devices with their start and end apart: 14 -> 15, of which waited for: 8 -> 13; matrix products, arithmetic and copies ran while one was open for 12% -> 11% of each run, Pallas kernels for 4% -> 5%
where the time goes in v3:
time: 351 us; the launch traced here: 350 us
  waiting for transfers between devices  221 us (63%)
  starting transfers between devices  40.4 us (12%)
  Pallas kernels  37.3 us (11%)
  local copies, waits for them, and re-layouts  30.1 us (9%)
  other arithmetic  19.7 us (6%)
    ppermute x8, waiting for transfers between devices, xor_permute(): return lax.ppermute(x, 'bfly', [(i, i ^ mask) for i in range(n)])  123 us
    all_to_all x7, waiting for transfers between devices, exchange(): return lax.all_to_all(x, axes, split_axis=0, concat_axis=0, tiled=True)  98 us
    pallas_call x2, Pallas kernels, on_chip(): pl.pallas_call(kernel, out_shape=[jax.ShapeDtypeStruct(shape, jnp.bfloat1...  37.3 us
    all_to_all x7, starting transfers between devices, exchange(): return lax.all_to_all(x, axes, split_axis=0, concat_axis=0, tiled=True)  34.1 us
    convert_element_type x2, other arithmetic, add(): return (x.astype(jnp.float32) + y.astype(jnp.float32)).astype(jnp.bfloat16)  10.3 us
    unnamed x24, local copies, waits for them, and re-layouts  9.87 us
  transfers between devices with their start and end apart: 15, of which 13 were waited for; matrix products, arithmetic and copies ran while one was open for 11% of the time, Pallas kernels for 5%

profile of v3, /device:TPU:0, one launch (start us, length us, event | category | flops | bytes accessed | tf_op | source)
XLA Modules:
  0.0 349.7 jit_solution(15410851075289252849)
XLA Ops:
  3.1 7.4 %all-to-all-start = ((bf16[8,2,2,2,32,256]{5,4,3,2,1,0:T(8,128)(2,1)}), bf16[8,2,2,2,32,256]{5,4,3,2,1,0:T(8,128)(2,1)}, u32[]{:S(2)}, u32[]{:S(2)}) async-start(bf16[8,2,2,2,32,256]{5,4,3,2,1,0:T(8,128)(2,1)} %maximum_maximum_fusion), calls=%async_computation | async-start | bytes 2097152 | tf_op jit(solution)/shard_map/all_to_all | solution.py:88
  11.8 24.6 %all-to-all-done.refs_0_ = bf16[8,2,2,2,32,256]{5,4,3,2,1,0:T(8,128)(2,1)} async-done(((bf16[8,2,2,2,32,256]{5,4,3,2,1,0:T(8,128)(2,1)}), bf16[8,2,2,2,32,256]{5,4,3,2,1,0:T(8,128)(2,1)}, u32[]{:S(2)}, u32[]{:S(2)}) %all-to-all-start) | async-done | bytes 1048608 | tf_op jit(solution)/shard_map/all_to_all | solution.py:88
  36.4 4.2 %all-to-all-start.1 = ((bf16[8,2,2,2,32,256]{5,4,3,2,1,0:T(8,128)(2,1)}), bf16[8,2,2,2,32,256]{5,4,3,2,1,0:T(8,128)(2,1)}, u32[]{:S(2)}, u32[]{:S(2)}) async-start(bf16[8,2,2,2,32,256]{5,4,3,2,1,0:T(8,128)(2,1)} %maximum_maximum_fusion.1), calls=%async_computation.1 | async-start | bytes 2097152 | tf_op jit(solution)/shard_map/all_to_all | solution.py:88
  40.7 1.6 collective-permute-start
  45.0 20.1 %collective-permute-done.refs_2_ = bf16[8,2,2,2,32,256]{5,4,3,2,1,0:T(8,128)(2,1)} collective-permute-done((bf16[8,2,2,2,32,256]{5,4,3,2,1,0:T(8,128)(2,1)}, bf16[8,2,2,2,32,256]{5,4,3,2,1,0:T(8,128)(2,1)}, u32[]{:S(2)}, u32[]{:S(2)}) %collective-permute-start) | collective-permute-done | bytes 1048608 | tf_op jit(solution)/shard_map/ppermute | solution.py:84
  66.3 4.6 %all-to-all-start.2 = ((bf16[32,96,256]{2,1,0:T(8,128)(2,1)}), bf16[32,96,256]{2,1,0:T(8,128)(2,1)S(1)}, u32[]{:S(2)}, u32[]{:S(2)}) async-start(bf16[32,96,256]{2,1,0:T(8,128)(2,1)} %pad_maximum_fusion), calls=%async_computation.2 | async-start | bytes 3145728 | tf_op jit(solution)/shard_map/all_to_all | solution.py:88
  70.9 1.8 collective-permute-start.4
  72.7 1.7 copy.69
  76.3 1.5 copy.70
  78.8 2.3 pad_maximum_fusion.1
  81.2 32.0 %collective-permute-done.4.refs_6_ = bf16[8,2,2,2,32,256]{5,4,3,2,1,0:T(8,128)(2,1)} collective-permute-done((bf16[8,2,2,2,32,256]{5,4,3,2,1,0:T(8,128)(2,1)}, bf16[8,2,2,2,32,256]{5,4,3,2,1,0:T(8,128)(2,1)}, u32[]{:S(2)}, u32[]{:S(2)}) %collective-permute-start.4) | collective-permute-done | bytes 1048608 | tf_op jit(solution)/shard_map/ppermute | solution.py:84
  113.1 4.8 %all-to-all-start.4 = ((bf16[32,96,256]{2,1,0:T(8,128)(2,1)}), bf16[32,96,256]{2,1,0:T(8,128)(2,1)S(1)}, u32[]{:S(2)}, u32[]{:S(2)}) async-start(bf16[32,96,256]{2,1,0:T(8,128)(2,1)} %pad_maximum_fusion.1), calls=%async_computation.4 | async-start | bytes 3145728 | tf_op jit(solution)/shard_map/all_to_all | solution.py:88
  119.0 2.0 collective-permute-done.1.refs_1_
  122.5 1.5 collective-permute-done.3.refs_5_
  125.5 16.6 %shard_map.109 = (bf16[8,4,96,256]{3,2,1,0:T(8,128)(2,1)}, bf16[2,4,4,64,512]{4,3,2,1,0:T(8,128)(2,1)}, bf16[2,4,256,512]{3,2,1,0:T(8,128)(2,1)}, bf16[2,4,256,5...) custom-call(s32[1]{0:T(128)} %bitcast.f_ref, ...), custom_call_target="tpu_custom_call" | custom-call | flops 3221225472 | bytes 24117250 | tf_op jit(solution)/shard_map/pallas_call | solution.py:233
  142.1 13.4 %all-to-all-done.4 = bf16[32,96,256]{2,1,0:T(8,128)(2,1)S(1)} async-done(((bf16[32,96,256]{2,1,0:T(8,128)(2,1)}), bf16[32,96,256]{2,1,0:T(8,128)(2,1)S(1)}, u32[]{:S(2)}, u32[]{:S(2)}) %all-to-all-start.4) | async-done | bytes 1572896 | tf_op jit(solution)/shard_map/all_to_all | solution.py:88
  156.6 20.7 %shard_map.110 = (bf16[8,4,96,256]{3,2,1,0:T(8,128)(2,1)}, bf16[2,8,4,2,2,32,256]{6,5,4,3,2,1,0:T(8,128)(2,1)}, bf16[2,8,4,2,2,32,256]{6,5,4,3,2,1,0:T(8,128)(2,1)}) custom-call(s32[1]{0:T(128)} %bitcast.f_ref, bf16[8,4,96,256]{3,2,1,0:T(8,128)(2,1)} %bitcast.157, bf16[8,4,96,256]{3,2,1,0:T(8,128)(2,1)} %bitcast.158, ...), custom_call_target="tpu_custom_call" | custom-call | flops 6442450944 | bytes 34078720 | tf_op jit(solution)/shard_map/pallas_call | solution.py:233
  177.3 3.9 %all-to-all-start.3 = ((bf16[32,96,256]{2,1,0:T(8,128)(2,1)}), bf16[32,96,256]{2,1,0:T(8,128)(2,1)S(1)}, u32[]{:S(2)}, u32[]{:S(2)}) async-start(bf16[32,96,256]{2,1,0:T(8,128)(2,1)} %bitcast.22), calls=%async_computation.3 | async-start | bytes 3145728 | tf_op jit(solution)/shard_map/all_to_all | solution.py:88
  181.2 3.6 %collective-permute-done.6 = bf16[2,8,4,2,2,32,256]{6,5,4,3,2,1,0:T(8,128)(2,1)} collective-permute-done((bf16[2,8,4,2,2,32,256]{6,5,4,3,2,1,0:T(8,128)(2,1)}, bf16[2,8,4,2,2,32,256]{6,5,4,3,2,1,0:T(8,128)(2,1)}, u32[]{:S(2)}, u32[]{:S(2)}) %collective-permute-start.6) | collective-permute-done | bytes 4194336 | tf_op jit(solution)/shard_map/ppermute | solution.py:84
  184.8 8.0 %add_convert_fusion = bf16[2,8,4,2,2,32,256]{6,5,4,3,2,1,0:T(8,128)(2,1)} fusion(bf16[2,8,4,2,2,32,256]{6,5,4,3,2,1,0:T(8,128)(2,1)} %collective-permute-done.6, bf16[2,8,4,2,2,32,256]{6,5,4,3,2,1,0:T(8,128)(2,1)} %get-tuple-element.36), kind=kLoop, calls=%fused_computation | loop fusion | flops 8388608 | bytes 12582912 | tf_op jit(solution)/shard_map/convert_element_type | solution.py:108
  192.8 26.1 %all-to-all-done.3 = bf16[32,96,256]{2,1,0:T(8,128)(2,1)S(1)} async-done(((bf16[32,96,256]{2,1,0:T(8,128)(2,1)}), bf16[32,96,256]{2,1,0:T(8,128)(2,1)S(1)}, u32[]{:S(2)}, u32[]{:S(2)}) %all-to-all-start.3) | async-done | bytes 1572896 | tf_op jit(solution)/shard_map/all_to_all | solution.py:88
  218.9 3.8 %all-to-all-start.5 = ((bf16[32,96,256]{2,1,0:T(8,128)(2,1)}), bf16[32,96,256]{2,1,0:T(8,128)(2,1)S(1)}, u32[]{:S(2)}, u32[]{:S(2)}) async-start(bf16[32,96,256]{2,1,0:T(8,128)(2,1)} %bitcast.164), calls=%async_computation.5 | async-start | bytes 3145728 | tf_op jit(solution)/shard_map/all_to_all | solution.py:88
  222.7 1.9 slice_bitcast_fusion
  224.7 1.8 collective-permute-start.7
  226.5 60.9 %collective-permute-done.7 = bf16[8,4,2,2,32,256]{5,4,3,2,1,0:T(8,128)(2,1)S(1)} collective-permute-done((bf16[8,4,2,2,32,256]{5,4,3,2,1,0:T(8,128)(2,1)S(1)}, bf16[8,4,2,2,32,256]{5,4,3,2,1,0:T(8,128)(2,1)S(1)}, u32[]{:S(2)}, u32[]{:S(2)}) %collective-permute-start.7) | collective-permute-done | bytes 2097184 | tf_op jit(solution)/shard_map/ppermute | solution.py:84
  287.4 2.3 fusion
  290.8 5.5 %all-to-all-start.6 = ((bf16[8,4,2,2,32,256]{5,4,3,2,1,0:T(8,128)(2,1)}), bf16[8,4,2,2,32,256]{5,4,3,2,1,0:T(8,128)(2,1)S(1)}, u32[]{:S(2)}, u32[]{:S(2)}) async-start(bf16[8,4,2,2,32,256]{5,4,3,2,1,0:T(8,128)(2,1)} %fusion), calls=%async_computation.6 | async-start | bytes 4194304 | tf_op jit(solution)/shard_map/all_to_all | solution.py:88
  299.0 2.6 copy.68
  301.6 2.6 copy.91
  306.8 2.6 copy.73
  309.4 2.6 copy.92
  312.0 32.8 %all-to-all-done.6 = bf16[8,4,2,2,32,256]{5,4,3,2,1,0:T(8,128)(2,1)S(1)} async-done(((bf16[8,4,2,2,32,256]{5,4,3,2,1,0:T(8,128)(2,1)}), bf16[8,4,2,2,32,256]{5,4,3,2,1,0:T(8,128)(2,1)S(1)}, u32[]{:S(2)}, u32[]{:S(2)}) %all-to-all-start.6) | async-done | bytes 2097184 | tf_op jit(solution)/shard_map/all_to_all | solution.py:88
  (74 shorter events, 27.0 us)
Async XLA Ops:
  0.6 1.3 copy-start.7
  2.0 8.5 %copy-start.8 = (bf16[24,32,256]{2,1,0:T(8,128)(2,1)S(1)}, bf16[24,32,256]{2,1,0:T(8,128)(2,1)}, u32[]{:S(2)}) copy-start(bf16[24,32,256]{2,1,0:T(8,128)(2,1)} %param.10) | copy-start | bytes 1179652
  3.1 7.5 %copy-start.9 = (bf16[12,64,256]{2,1,0:T(8,128)(2,1)S(1)}, bf16[12,64,256]{2,1,0:T(8,128)(2,1)}, u32[]{:S(2)}) copy-start(bf16[12,64,256]{2,1,0:T(8,128)(2,1)} %param.11) | copy-start | bytes 1179652
  3.1 33.3 %all-to-all-start = ((bf16[8,2,2,2,32,256]{5,4,3,2,1,0:T(8,128)(2,1)}), bf16[8,2,2,2,32,256]{5,4,3,2,1,0:T(8,128)(2,1)}, u32[]{:S(2)}, u32[]{:S(2)}) async-start(bf16[8,2,2,2,32,256]{5,4,3,2,1,0:T(8,128)(2,1)} %maximum_maximum_fusion), calls=%async_computation | async-start | bytes 2097152 | tf_op jit(solution)/shard_map/all_to_all | solution.py:88
  10.7 31.5 %copy-start.6 = (bf16[256,3072]{1,0:T(8,128)(2,1)S(1)}, bf16[256,3072]{1,0:T(8,128)(2,1)}, u32[]{:S(2)}) copy-start(bf16[256,3072]{1,0:T(8,128)(2,1)} %param.6) | copy-start | bytes 4718596
  36.4 29.9 %all-to-all-start.1 = ((bf16[8,2,2,2,32,256]{5,4,3,2,1,0:T(8,128)(2,1)}), bf16[8,2,2,2,32,256]{5,4,3,2,1,0:T(8,128)(2,1)}, u32[]{:S(2)}, u32[]{:S(2)}) async-start(bf16[8,2,2,2,32,256]{5,4,3,2,1,0:T(8,128)(2,1)} %maximum_maximum_fusion.1), calls=%async_computation.1 | async-start | bytes 2097152 | tf_op jit(solution)/shard_map/all_to_all | solution.py:88
  40.7 24.5 %collective-permute-start = (bf16[8,2,2,2,32,256]{5,4,3,2,1,0:T(8,128)(2,1)}, bf16[8,2,2,2,32,256]{5,4,3,2,1,0:T(8,128)(2,1)}, u32[]{:S(2)}, u32[]{:S(2)}) collective-permute-start(bf16[8,2,2,2,32,256]{5,4,3,2,1,0:T(8,128)(2,1)} %all-to-all-done.refs_0_), channel_id=1, source_target_pairs={{0,2},{1,3},{2,0},{3,1},{4,6},{5,7},{6,4},{7,5},{8,10},{9,11},{10,... | collective-permute-start | bytes 3145736 | tf_op jit(solution)/shard_map/ppermute | solution.py:84
  66.3 46.9 %all-to-all-start.2 = ((bf16[32,96,256]{2,1,0:T(8,128)(2,1)}), bf16[32,96,256]{2,1,0:T(8,128)(2,1)S(1)}, u32[]{:S(2)}, u32[]{:S(2)}) async-start(bf16[32,96,256]{2,1,0:T(8,128)(2,1)} %pad_maximum_fusion), calls=%async_computation.2 | async-start | bytes 3145728 | tf_op jit(solution)/shard_map/all_to_all | solution.py:88
  70.9 42.3 %collective-permute-start.4 = (bf16[8,2,2,2,32,256]{5,4,3,2,1,0:T(8,128)(2,1)}, bf16[8,2,2,2,32,256]{5,4,3,2,1,0:T(8,128)(2,1)}, u32[]{:S(2)}, u32[]{:S(2)}) collective-permute-start(bf16[8,2,2,2,32,256]{5,4,3,2,1,0:T(8,128)(2,1)} %all-to-all-done.1.refs_4_), channel_id=1, source_target_pairs={{0,2},{1,3},{2,0},{3,1},{4,6},{5,7},{6,4},{7,5},{8,10},{9,11},{10,... | collective-permute-start | bytes 3145736 | tf_op jit(solution)/shard_map/ppermute | solution.py:84
  76.3 1.5 copy-start.5
  113.1 12.3 %copy-start.3 = (bf16[32,96,256]{2,1,0:T(8,128)(2,1)}, bf16[32,96,256]{2,1,0:T(8,128)(2,1)S(1)}, u32[]{:S(2)}) copy-start(bf16[32,96,256]{2,1,0:T(8,128)(2,1)S(1)} %all-to-all-done.2) | copy-start | bytes 4718596
  113.1 42.3 %all-to-all-start.4 = ((bf16[32,96,256]{2,1,0:T(8,128)(2,1)}), bf16[32,96,256]{2,1,0:T(8,128)(2,1)S(1)}, u32[]{:S(2)}, u32[]{:S(2)}) async-start(bf16[32,96,256]{2,1,0:T(8,128)(2,1)} %pad_maximum_fusion.1), calls=%async_computation.4 | async-start | bytes 3145728 | tf_op jit(solution)/shard_map/all_to_all | solution.py:88
  117.9 3.1 collective-permute-start.1
  118.2 4.3 %collective-permute-start.2 = (bf16[8,2,2,2,32,256]{5,4,3,2,1,0:T(8,128)(2,1)}, bf16[8,2,2,2,32,256]{5,4,3,2,1,0:T(8,128)(2,1)}, u32[]{:S(2)}, u32[]{:S(2)}) collective-permute-start(bf16[8,2,2,2,32,256]{5,4,3,2,1,0:T(8,128)(2,1)} %collective-permute-done.refs_2_), channel_id=1, source_target_pairs={{0,1},{1,0},{2,3},{3,2},{4,5},{5,4},{6,7},{7,6},{8,9},{9,8},{10,11... | collective-permute-start | bytes 3145736 | tf_op jit(solution)/shard_map/ppermute | solution.py:84
  118.5 5.5 %collective-permute-start.3 = (bf16[8,2,2,2,32,256]{5,4,3,2,1,0:T(8,128)(2,1)}, bf16[8,2,2,2,32,256]{5,4,3,2,1,0:T(8,128)(2,1)}, u32[]{:S(2)}, u32[]{:S(2)}) collective-permute-start(bf16[8,2,2,2,32,256]{5,4,3,2,1,0:T(8,128)(2,1)} %all-to-all-done.1.refs_4_), channel_id=1, source_target_pairs={{0,1},{1,0},{2,3},{3,2},{4,5},{5,4},{6,7},{7,6},{8,9},{9,8},{10,11... | collective-permute-start | bytes 3145736 | tf_op jit(solution)/shard_map/ppermute | solution.py:84
  118.7 6.7 %collective-permute-start.5 = (bf16[8,2,2,2,32,256]{5,4,3,2,1,0:T(8,128)(2,1)}, bf16[8,2,2,2,32,256]{5,4,3,2,1,0:T(8,128)(2,1)}, u32[]{:S(2)}, u32[]{:S(2)}) collective-permute-start(bf16[8,2,2,2,32,256]{5,4,3,2,1,0:T(8,128)(2,1)} %collective-permute-done.4.refs_6_), channel_id=1, source_target_pairs={{0,1},{1,0},{2,3},{3,2},{4,5},{5,4},{6,7},{7,6},{8,9},{9,8},{10,11... | collective-permute-start | bytes 3145736 | tf_op jit(solution)/shard_map/ppermute | solution.py:84
  155.5 1.1 copy-start.4
  177.3 7.5 %collective-permute-start.6 = (bf16[2,8,4,2,2,32,256]{6,5,4,3,2,1,0:T(8,128)(2,1)}, bf16[2,8,4,2,2,32,256]{6,5,4,3,2,1,0:T(8,128)(2,1)}, u32[]{:S(2)}, u32[]{:S(2)}) collective-permute-start(bf16[2,8,4,2,2,32,256]{6,5,4,3,2,1,0:T(8,128)(2,1)} %get-tuple-element.37), channel_id=1, source_target_pairs={{0,1},{1,0},{2,3},{3,2},{4,5},{5,4},{6,7},{7,6},{8,9},{9,8},{10,11... | collective-permute-start | bytes 12582920 | tf_op jit(solution)/shard_map/ppermute | solution.py:84
  177.3 41.6 %all-to-all-start.3 = ((bf16[32,96,256]{2,1,0:T(8,128)(2,1)}), bf16[32,96,256]{2,1,0:T(8,128)(2,1)S(1)}, u32[]{:S(2)}, u32[]{:S(2)}) async-start(bf16[32,96,256]{2,1,0:T(8,128)(2,1)} %bitcast.22), calls=%async_computation.3 | async-start | bytes 3145728 | tf_op jit(solution)/shard_map/all_to_all | solution.py:88
  218.9 5.7 %copy-start.1 = (bf16[32,96,256]{2,1,0:T(8,128)(2,1)}, bf16[32,96,256]{2,1,0:T(8,128)(2,1)S(1)}, u32[]{:S(2)}) copy-start(bf16[32,96,256]{2,1,0:T(8,128)(2,1)S(1)} %all-to-all-done.3) | copy-start | bytes 4718596
  218.9 70.7 %all-to-all-start.5 = ((bf16[32,96,256]{2,1,0:T(8,128)(2,1)}), bf16[32,96,256]{2,1,0:T(8,128)(2,1)S(1)}, u32[]{:S(2)}, u32[]{:S(2)}) async-start(bf16[32,96,256]{2,1,0:T(8,128)(2,1)} %bitcast.164), calls=%async_computation.5 | async-start | bytes 3145728 | tf_op jit(solution)/shard_map/all_to_all | solution.py:88
  222.7 64.7 %copy-start = (bf16[2,8,4,2,2,32,256]{6,5,4,3,2,1,0:T(8,128)(2,1)S(1)}, bf16[2,8,4,2,2,32,256]{6,5,4,3,2,1,0:T(8,128)(2,1)}, u32[]{:S(2)}) copy-start(bf16[2,8,4,2,2,32,256]{6,5,4,3,2,1,0:T(8,128)(2,1)} %add_convert_fusion) | copy-start | bytes 12582916
  224.7 62.7 %collective-permute-start.7 = (bf16[8,4,2,2,32,256]{5,4,3,2,1,0:T(8,128)(2,1)S(1)}, bf16[8,4,2,2,32,256]{5,4,3,2,1,0:T(8,128)(2,1)S(1)}, u32[]{:S(2)}, u32[]{:S(2)}) collective-permute-start(bf16[8,4,2,2,32,256]{5,4,3,2,1,0:T(8,128)(2,1)S(1)} %slice_bitcast_fusion), channel_id=1, source_target_pairs={{0,2},{1,3},{2,0},{3,1},{4,6},{5,7},{6,4},{7,5},{8,10},{9,11},{10,... | collective-permute-start | bytes 6291464 | tf_op jit(solution)/shard_map/ppermute | solution.py:84
  289.7 1.1 copy-start.2
  290.8 53.9 %all-to-all-start.6 = ((bf16[8,4,2,2,32,256]{5,4,3,2,1,0:T(8,128)(2,1)}), bf16[8,4,2,2,32,256]{5,4,3,2,1,0:T(8,128)(2,1)S(1)}, u32[]{:S(2)}, u32[]{:S(2)}) async-start(bf16[8,4,2,2,32,256]{5,4,3,2,1,0:T(8,128)(2,1)} %fusion), calls=%async_computation.6 | async-start | bytes 4194304 | tf_op jit(solution)/shard_map/all_to_all | solution.py:88
  296.3 1.2 slice-start.1
  296.3 1.4 slice-start
  304.2 1.2 slice-start.3
  304.2 1.4 slice-start.2

commit v4 on v3

--- a/solution.py
+++ b/solution.py
@@ -79,9 +79,8 @@
     return (rows(output), rows(back_input)) + grads
 
 
-def xor_permute(x, mask):
-    n = lax.axis_size("bfly")
-    return lax.ppermute(x, "bfly", [(i, i ^ mask) for i in range(n)])
+def xor_permute(x, mask, axis="bfly"):
+    return lax.ppermute(x, axis, [(i, i ^ mask) for i in range(lax.axis_size(axis))])
 
 
 def exchange(x, axes):
@@ -92,8 +91,8 @@
     pairs = lax.axis_size("dp") // 2
     sets = w.reshape(pairs, 3, 2, w.shape[1], w.shape[2])
     own = jnp.stack([sets[:, 0], sets[:, 2]], axis=1)
-    mid = jnp.stack([sets[:, 1], sets[:, 1]], axis=1)
-    return jnp.stack([own, mid], axis=2).reshape((pairs * 2, 2) + sets.shape[2:])
+    mid = sets[:, 1][:, :, None]
+    return jnp.concatenate([own, mid], axis=2).reshape((pairs * 2, 3) + sets.shape[3:])
 
 
 def gather_bfly(w, across):
@@ -140,90 +139,122 @@
     return pl.ds(r * (part // 2), part // 2)
 
 
-def forward_kernel(f_ref, x_ref, *refs):
-    ab, ce, (out_ref,), saved = refs[:4], refs[4:8], refs[8:9], (refs[9:13], refs[13:17])
+def weight_of(slot, w, v):
+    def get(m, which, r):
+        if slot == 0:
+            return square(w[m][:, which, r])
+        return square(v[m][:, which] if r else w[m][:, which, 2])
+
+    return get
+
+
+def wide_weight(slot, w, e_ref, y):
+    def get(m, r):
+        if slot == 0:
+            return square(w[m][half_src(e_ref.shape[1], r), 3, :2])
+        return square(e_ref[m, half_src(e_ref.shape[1], r ^ y)])
+
+    return get
+
+
+def join_halves(w, v, e_ref, y):
+    for m in range(len(w)):
+        e_ref[m, :, y] = w[m][:, 3, 2]
+        e_ref[m, :, 1 - y] = v[m][:, 3]
+
+
+def forward_kernel(seat_ref, x_ref, *refs):
+    w, v, (out_ref,), saved, e_ref = refs[:4], refs[4:8], refs[8:9], (refs[9:13], refs[13:17]), refs[17]
     ndp, nb, all_rows, _ = x_ref.shape
     own_rows = 2 * all_rows // 3
-    f = f_ref[0]
+    f, y = seat_ref[0], seat_ref[1]
+    join_halves(w, v, e_ref, y)
     for slot, (lo, hi) in enumerate(((0, own_rows), (own_rows, all_rows))):
         perm, active, slope, ret = saved[slot]
+        weight, wide = weight_of(slot, w, v), wide_weight(slot, w, e_ref, y)
         count = ndp * (hi - lo)
         tiles = (nb, BLK // nb, count)
         for m in range(nb):
             d = f ^ m
             x = x_ref[:, d, lo:hi, :].reshape(count, BLK)
             for r in range(2):
-                spread = dot(square(ab[m][:, 0, slot, r]), x, 0, 1).astype(jnp.bfloat16)
+                spread = dot(weight(m, 0, r), x, 0, 1).astype(jnp.bfloat16)
                 perm[r, :, d] = spread.reshape(tiles)
         for m in range(nb):
             s = f ^ m
             for r in range(2):
                 p = perm[r, s].reshape(BLK, count)
-                value, grade = gelu_pair(dot(square(ab[m][:, 1, slot, r]), p, 0, 0))
+                value, grade = gelu_pair(dot(weight(m, 1, r), p, 0, 0))
                 value = value.astype(jnp.bfloat16)
                 active[r, s] = value
                 slope[r, s] = grade.astype(jnp.bfloat16)
-                narrowed = dot(square(ce[m][:, 0, slot, r]), value, 0, 0).astype(jnp.bfloat16)
+                narrowed = dot(weight(m, 2, r), value, 0, 0).astype(jnp.bfloat16)
                 ret[r, :, s] = narrowed.reshape(tiles)
         for m in range(nb):
             d = f ^ m
             total = 0.0
             for r in range(2):
-                e = square(ce[m][half_src(ndp, r), 1, slot])
-                total = total + dot(ret[r, d].reshape(BLK, count), e, 0, 0)
+                total = total + dot(ret[r, d].reshape(BLK, count), wide(m, r), 0, 0)
             out_ref[:, d, lo:hi, :] = total.astype(jnp.bfloat16).reshape(ndp, hi - lo, BLK)
 
 
-def backward_kernel(f_ref, x_ref, g_ref, *refs):
-    ab, ce, saved = refs[:4], refs[4:8], (refs[8:12], refs[12:16])
-    gin_ref, keep_ref, send_ref = refs[16:19]
-    scratch = (refs[19:21], refs[21:23])
+def backward_kernel(seat_ref, x_ref, g_ref, *refs):
+    w, v, saved = refs[:4], refs[4:8], (refs[8:12], refs[12:16])
+    gin_ref, own_keep, own_send, mid_keep, mid_send = refs[16:21]
+    scratch, e_ref = (refs[21:23], refs[23:25]), refs[25]
     ndp, nb, all_rows, _ = x_ref.shape
     own_rows = 2 * all_rows // 3
     rows = BLK // ndp
-    f = f_ref[0]
-
-    def grads(m):
-        return (send_ref if m % 2 else keep_ref), m // 2
+    f, y = seat_ref[0], seat_ref[1]
+    join_halves(w, v, e_ref, y)
+
+    def store(slot, m, which, r, part):
+        ref = ((own_keep, own_send), (mid_keep, mid_send))[slot][m % 2]
+        if slot == 0:
+            ref[m // 2, :, which, r] = part.astype(jnp.bfloat16).reshape(ndp, rows, BLK)
+        else:
+            ref[r, m // 2, :, which] = part.astype(jnp.bfloat16).reshape(ndp, rows, BLK)
+
+    def store_wide(slot, m, r, part):
+        ref = ((own_keep, own_send), (mid_keep, mid_send))[slot][m % 2]
+        part = part.astype(jnp.bfloat16).reshape(ndp // 2, 2, rows, BLK)
+        if slot == 0:
+            ref[m // 2, half_src(ndp, r), 3] = part
+        else:
+            ref[y, m // 2, half_src(ndp, r ^ y), 3] = part[:, 0]
+            ref[1 - y, m // 2, half_src(ndp, r ^ y), 3] = part[:, 1]
 
     for slot, (lo, hi) in enumerate(((0, own_rows), (own_rows, all_rows))):
         perm, active, slope, ret = saved[slot]
         mid, spread = scratch[slot]
+        weight, wide = weight_of(slot, w, v), wide_weight(slot, w, e_ref, y)
         count = ndp * (hi - lo)
         tiles = (nb, BLK // nb, count)
         for m in range(nb):
             d = f ^ m
             g = g_ref[:, d, lo:hi, :].reshape(count, BLK)
-            ref, at = grads(m)
-            for r in range(2):
-                e = square(ce[m][half_src(ndp, r), 1, slot])
-                mid[r, :, d] = dot(e, g, 1, 1).astype(jnp.bfloat16).reshape(tiles)
-                part = dot(ret[r, d].reshape(BLK, count), g, 1, 0).astype(jnp.bfloat16)
-                ref[at, half_src(ndp, r), 3, slot] = part.reshape(ndp // 2, 2, rows, BLK)
+            for r in range(2):
+                mid[r, :, d] = dot(wide(m, r), g, 1, 1).astype(jnp.bfloat16).reshape(tiles)
+                store_wide(slot, m, r, dot(ret[r, d].reshape(BLK, count), g, 1, 0))
         for m in range(nb):
             s = f ^ m
-            ref, at = grads(m)
             for r in range(2):
                 p = perm[r, s].reshape(BLK, count)
                 back_mid = mid[r, s].reshape(BLK, count)
-                back = dot(square(ce[m][:, 0, slot, r]), back_mid, 1, 0)
+                back = dot(weight(m, 2, r), back_mid, 1, 0)
                 back = (back * slope[r, s].astype(jnp.float32)).astype(jnp.bfloat16)
-                part = dot(active[r, s], back_mid, 1, 1).astype(jnp.bfloat16)
-                ref[at, :, 2, slot, r] = part.reshape(ndp, rows, BLK)
-                part = dot(p, back, 1, 1).astype(jnp.bfloat16)
-                ref[at, :, 1, slot, r] = part.reshape(ndp, rows, BLK)
-                first = dot(square(ab[m][:, 1, slot, r]), back, 1, 0).astype(jnp.bfloat16)
+                store(slot, m, 2, r, dot(active[r, s], back_mid, 1, 1))
+                store(slot, m, 1, r, dot(p, back, 1, 1))
+                first = dot(weight(m, 1, r), back, 1, 0).astype(jnp.bfloat16)
                 spread[r, :, s] = first.reshape(tiles)
         for m in range(nb):
             d = f ^ m
             x = x_ref[:, d, lo:hi, :].reshape(count, BLK)
-            ref, at = grads(m)
             total = 0.0
             for r in range(2):
                 back = spread[r, d].reshape(BLK, count)
-                total = total + dot(back, square(ab[m][:, 0, slot, r]), 0, 1)
-                part = dot(x, back, 0, 1).astype(jnp.bfloat16)
-                ref[at, :, 0, slot, r] = part.reshape(ndp, rows, BLK)
+                total = total + dot(back, weight(m, 0, r), 0, 1)
+                store(slot, m, 0, r, dot(x, back, 0, 1))
             gin_ref[:, d, lo:hi, :] = total.astype(jnp.bfloat16).reshape(ndp, hi - lo, BLK)
 
 
@@ -251,47 +282,51 @@
     parts, count = 2 * blocks, tokens.shape[0]
     dealt_a = weight_a.reshape(blocks, rows, 2, BLK).transpose(0, 2, 1, 3).reshape(parts, rows, BLK)
     dealt_e = weight_e.reshape(parts, rows, BLK)
-    seat = lax.axis_index("bfly").astype(jnp.int32).reshape(1)
-
-    def pack(first, second):
-        return jnp.stack([deal_weight(first), deal_weight(second)], axis=1)
+    seat = jnp.stack([lax.axis_index("bfly"), lax.axis_index("dp") % 2]).astype(jnp.int32)
 
     everyone = ("dp", "bfly")
     shape = (ndp, nb, -1, BLK)
-    ab = exchange(pack(dealt_a, weight_b), "dp")
-    ab_across = xor_permute(ab, 2)
-    ce = exchange(after(pack(weight_c, dealt_e), ab), "dp")
-    ce_across = xor_permute(ce, 2)
-    x = exchange(after(deal_tokens(tokens), ab_across, ce), everyone)
-    g = exchange(after(deal_tokens(grad_out), ce_across, x), everyone).reshape(shape)
+    dealt = [deal_weight(w) for w in (dealt_a, weight_b, weight_c, dealt_e)]
+    w = exchange(jnp.stack(dealt, axis=1), "dp")
+    across = xor_permute(w, 2)
+    v = xor_permute(w[:, :, 2], 1, "dp")
+    x = exchange(after(deal_tokens(tokens), w), everyone)
+    g = exchange(after(deal_tokens(grad_out), x), everyone).reshape(shape)
     x = x.reshape(shape)
-    ab, ce = gather_bfly(ab, ab_across), gather_bfly(ce, ce_across)
+    weights = gather_bfly(w, across) + gather_bfly(v, xor_permute(across[:, :, 2], 1, "dp"))
 
     own, mid = count * ndp // nb, count * ndp // nb // 2
     saved = []
     for t in (own, mid):
         tiled, whole = (2, nb, nb, BLK // nb, t), (2, nb, BLK, t)
         saved += [tiled, whole, whole, tiled]
+    halves = (nb, ndp, 2, rows, BLK)
     products = 2 * nb * (own + mid)
-    out, *kept = on_chip(forward_kernel, 4 * products, [x.shape] + saved, [], [seat, x] + ab + ce)
+    out, *kept = on_chip(
+        forward_kernel, 4 * products, [x.shape] + saved, [halves], [seat, x] + weights
+    )
     out = exchange(out.reshape(ndp * nb, -1, BLK), everyone)
-    grad_shape = (2, ndp, 4, 2, 2, rows, BLK)
-    gin, keep, send = on_chip(
+    own_shape, mid_shape = (2, ndp, 4, 2, rows, BLK), (2, 2, ndp, 4, rows, BLK)
+    gin, own_keep, own_send, mid_keep, mid_send = on_chip(
         backward_kernel,
         8 * products,
-        [x.shape, grad_shape, grad_shape],
-        [saved[0], saved[0], saved[4], saved[4]],
-        [seat, x, g] + ab + ce + kept,
-    )
-    half = add(keep, xor_permute(send, 1))
-    gin = exchange(after(gin.reshape(ndp * nb, -1, BLK), half, out), everyone)
-    dealt = add(half[0], xor_permute(half[1], 2))
+        [x.shape, own_shape, own_shape, mid_shape, mid_shape],
+        [saved[0], saved[0], saved[4], saved[4], halves],
+        [seat, x, g] + weights + kept,
+    )
+    mid = add(mid_keep, xor_permute(mid_send, 1))
+    own = add(own_keep, xor_permute(own_send, 1))
+    mid = add(mid[0], xor_permute(mid[1], 1, "dp"))
+    gin = exchange(after(gin.reshape(ndp * nb, -1, BLK), out), everyone)
+    own = add(own[0], xor_permute(own[1], 2))
+    mid = add(mid[0], xor_permute(mid[1], 2))
+    dealt = jnp.concatenate([own, mid[:, :, None]], axis=2)
     got = exchange(after(dealt, gin), "dp").astype(jnp.float32)
-    got = got.reshape(ndp // 2, 2, 4, 2, 2, rows, BLK)
+    got = got.reshape(ndp // 2, 2, 4, 3, rows, BLK)
 
     def own_rows(which):
-        mid = got[:, 0, which, 1] + got[:, 1, which, 1]
-        return jnp.stack([got[:, 0, which, 0], mid, got[:, 1, which, 0]], axis=1)
+        mid = jnp.stack([got[:, 0, which, 2], got[:, 1, which, 2]], axis=1)
+        return jnp.stack([got[:, 0, which, :2], mid, got[:, 1, which, :2]], axis=1)
 
     grad_a = own_rows(0).reshape(blocks, 2, rows, BLK).transpose(0, 2, 1, 3)
     return (

time: 351 us -> 323 us (0.920)
  waiting for transfers between devices: 221 us -> 190 us
  local copies, waits for them, and re-layouts: 30.1 us -> 38.8 us
    ppermute x8 -> x12, waiting for transfers between devices: 123 us -> 91.2 us  [xor_permute(): lax.ppermute(x, axis, [(i, i ^ mask) for i in range(lax.axis_size(axis))])]
    all_to_all x7 -> x6, starting transfers between devices: 34.1 us -> 27.3 us  [exchange(): return lax.all_to_all(x, axes, split_axis=0, concat_axis=0, tiled=True)]
    ppermute x0 -> x2, local copies, waits for them, and re-layouts: none -> 5.5 us  [xor_permute(): lax.ppermute(x, axis, [(i, i ^ mask) for i in range(lax.axis_size(axis))])]
    convert_element_type x2 -> x4, other arithmetic: 10.3 us -> 6.57 us  [add(): return (x.astype(jnp.float32) + y.astype(jnp.float32)).astype(jnp.bfloat16)]
    ppermute x8 -> x12, starting transfers between devices: 6.31 us -> 9.58 us  [xor_permute(): lax.ppermute(x, axis, [(i, i ^ mask) for i in range(lax.axis_size(axis))])]
    unnamed x24 -> x28, local copies, waits for them, and re-layouts: 9.87 us -> 10.5 us
    all_to_all x7 -> x6, waiting for transfers between devices: 98 us -> 98.7 us  [exchange(): return lax.all_to_all(x, axes, split_axis=0, concat_axis=0, tiled=True)]
  transfers between devices with their start and end apart: 15 -> 18, of which waited for: 13 -> 9; matrix products, arithmetic and copies ran while one was open for 11% -> 13% of each run, Pallas kernels for 5% -> 12%
where the time goes in v4:
time: 323 us; the launch traced here: 322 us
  waiting for transfers between devices  190 us (59%)
  local copies, waits for them, and re-layouts  38.8 us (12%)
  Pallas kernels  37.7 us (12%)
  starting transfers between devices  36.9 us (11%)
  other arithmetic  17.3 us (5%)
    all_to_all x6, waiting for transfers between devices, exchange(): return lax.all_to_all(x, axes, split_axis=0, concat_axis=0, tiled=True)  98.7 us
    ppermute x12, waiting for transfers between devices, xor_permute(): lax.ppermute(x, axis, [(i, i ^ mask) for i in range(lax.axis_size(axis))])  91.2 us
    pallas_call x2, Pallas kernels, on_chip(): pl.pallas_call(kernel, out_shape=[jax.ShapeDtypeStruct(shape, jnp.bfloat1...  37.7 us
    all_to_all x6, starting transfers between devices, exchange(): return lax.all_to_all(x, axes, split_axis=0, concat_axis=0, tiled=True)  27.3 us
    unnamed x28, local copies, waits for them, and re-layouts  10.5 us
    ppermute x12, starting transfers between devices, xor_permute(): lax.ppermute(x, axis, [(i, i ^ mask) for i in range(lax.axis_size(axis))])  9.58 us
    convert_element_type x4, other arithmetic, add(): return (x.astype(jnp.float32) + y.astype(jnp.float32)).astype(jnp.bfloat16)  6.57 us
  transfers between devices with their start and end apart: 18, of which 9 were waited for; matrix products, arithmetic and copies ran while one was open for 13% of the time, Pallas kernels for 12%

profile of v4, /device:TPU:0, one launch (start us, length us, event | category | flops | bytes accessed | tf_op | source)
XLA Modules:
  0.0 321.7 jit_solution(15054447632010483327)
XLA Ops:
  4.3 7.3 %all-to-all-start = ((bf16[8,4,3,32,256]{4,3,1,2,0:T(8,128)(2,1)}), bf16[8,4,3,32,256]{4,3,1,2,0:T(8,128)(2,1)S(1)}, u32[]{:S(2)}, u32[]{:S(2)}) async-start(bf16[8,4,3,32,256]{4,3,1,2,0:T(8,128)(2,1)} %maximum_maximum_fusion), calls=%async_computation | async-start | bytes 3145728 | tf_op jit(solution)/shard_map/all_to_all | solution.py:87
  11.5 1.7 copy.148
  17.7 2.3 pad_maximum_fusion
  20.0 28.6 %all-to-all-done = bf16[8,4,3,32,256]{4,3,1,2,0:T(8,128)(2,1)S(1)} async-done(((bf16[8,4,3,32,256]{4,3,1,2,0:T(8,128)(2,1)}), bf16[8,4,3,32,256]{4,3,1,2,0:T(8,128)(2,1)S(1)}, u32[]{:S(2)}, u32[]{:S(2)}) %all-to-all-start) | async-done | bytes 1572896 | tf_op jit(solution)/shard_map/all_to_all | solution.py:87
  48.5 3.8 %all-to-all-start.1 = ((bf16[32,96,256]{2,1,0:T(8,128)(2,1)}), bf16[32,96,256]{2,1,0:T(8,128)(2,1)}, u32[]{:S(2)}, u32[]{:S(2)}) async-start(bf16[32,96,256]{2,1,0:T(8,128)(2,1)} %pad_maximum_fusion), calls=%async_computation.1 | async-start | bytes 3145728 | tf_op jit(solution)/shard_map/all_to_all | solution.py:87
  53.6 1.7 collective-permute-start.1
  55.3 1.7 copy.165
  61.5 2.3 pad_maximum_fusion.1
  63.8 26.4 %all-to-all-done.1 = bf16[32,96,256]{2,1,0:T(8,128)(2,1)} async-done(((bf16[32,96,256]{2,1,0:T(8,128)(2,1)}), bf16[32,96,256]{2,1,0:T(8,128)(2,1)}, u32[]{:S(2)}, u32[]{:S(2)}) %all-to-all-start.1) | async-done | bytes 1572896 | tf_op jit(solution)/shard_map/all_to_all | solution.py:87
  90.2 3.8 %all-to-all-start.3 = ((bf16[32,96,256]{2,1,0:T(8,128)(2,1)}), bf16[32,96,256]{2,1,0:T(8,128)(2,1)S(1)}, u32[]{:S(2)}, u32[]{:S(2)}) async-start(bf16[32,96,256]{2,1,0:T(8,128)(2,1)} %pad_maximum_fusion.1), calls=%async_computation.3 | async-start | bytes 3145728 | tf_op jit(solution)/shard_map/all_to_all | solution.py:87
  94.1 21.2 %collective-permute-done.1 = bf16[8,4,3,32,256]{4,3,1,0,2:T(8,128)(2,1)} collective-permute-done((bf16[8,4,3,32,256]{4,3,1,0,2:T(8,128)(2,1)}, bf16[8,4,3,32,256]{4,3,1,0,2:T(8,128)(2,1)}, u32[]{:S(2)}, u32[]{:S(2)}) %collective-permute-start.1) | collective-permute-done | bytes 1572896 | tf_op jit(solution)/shard_map/ppermute | solution.py:83
  117.2 1.9 collective-permute-start.3
  120.4 14.3 %collective-permute-done.3.refs_4_ = bf16[8,4,32,256]{3,2,1,0:T(8,128)(2,1)S(1)} collective-permute-done((bf16[8,4,32,256]{3,2,1,0:T(8,128)(2,1)S(1)}, bf16[8,4,32,256]{3,2,1,0:T(8,128)(2,1)S(1)}, u32[]{:S(2)}, u32[]{:S(2)}) %collective-permute-start.3) | collective-permute-done | bytes 524320 | tf_op jit(solution)/shard_map/ppermute | solution.py:83
  134.7 11.1 %collective-permute-done.5.refs_6_ = bf16[8,4,32,256]{3,2,1,0:T(8,128)(2,1)S(1)} collective-permute-done((bf16[8,4,32,256]{3,2,1,0:T(8,128)(2,1)S(1)}, bf16[8,4,32,256]{3,2,1,0:T(8,128)(2,1)S(1)}, u32[]{:S(2)}, u32[]{:S(2)}) %collective-permute-start.5) | collective-permute-done | bytes 524320 | tf_op jit(solution)/shard_map/ppermute | solution.py:83
  146.5 2.7 copy.161.refs_2_
  149.2 2.8 copy.162.refs_3_
  152.8 17.2 %shard_map.109 = (bf16[8,4,96,256]{3,2,1,0:T(8,128)(2,1)}, bf16[2,4,4,64,512]{4,3,2,1,0:T(8,128)(2,1)}, bf16[2,4,256,512]{3,2,1,0:T(8,128)(2,1)}, bf16[2,4,256,5...) custom-call(s32[2]{0:T(128)} %pad_add_fusion.seat_ref, ...), custom_call_target="tpu_custom_call" | custom-call | flops 3221225472 | bytes 24117252 | tf_op jit(solution)/shard_map/pallas_call | solution.py:264
  171.2 3.8 %all-to-all-start.2 = ((bf16[32,96,256]{2,1,0:T(8,128)(2,1)}), bf16[32,96,256]{2,1,0:T(8,128)(2,1)S(1)}, u32[]{:S(2)}, u32[]{:S(2)}) async-start(bf16[32,96,256]{2,1,0:T(8,128)(2,1)} %bitcast.187), calls=%async_computation.2 | async-start | bytes 3145728 | tf_op jit(solution)/shard_map/all_to_all | solution.py:87
  175.0 20.6 %shard_map.110 = (bf16[8,4,96,256]{3,2,1,0:T(8,128)(2,1)}, bf16[2,8,4,2,32,256]{5,4,3,2,1,0:T(8,128)(2,1)}, bf16[2,8,4,2,32,256]{5,4,3,2,1,0:T(8,128)(2,1)}, bf1...) custom-call(s32[2]{0:T(128)} %pad_add_fusion.seat_ref, bf16[8,4,96,256]{3,2,1,0:T(8,128)(2,1)} %bitcast.24.x_ref, ...), custom_call_target="tpu_custom_call" | custom-call | flops 6442450944 | bytes 34078724 | tf_op jit(solution)/shard_map/pallas_call | solution.py:264
  196.2 16.4 %all-to-all-done.2 = bf16[32,96,256]{2,1,0:T(8,128)(2,1)S(1)} async-done(((bf16[32,96,256]{2,1,0:T(8,128)(2,1)}), bf16[32,96,256]{2,1,0:T(8,128)(2,1)S(1)}, u32[]{:S(2)}, u32[]{:S(2)}) %all-to-all-start.2) | async-done | bytes 1572896 | tf_op jit(solution)/shard_map/all_to_all | solution.py:87
  212.6 4.0 %all-to-all-start.4 = ((bf16[32,96,256]{2,1,0:T(8,128)(2,1)}), bf16[32,96,256]{2,1,0:T(8,128)(2,1)S(1)}, u32[]{:S(2)}, u32[]{:S(2)}) async-start(bf16[32,96,256]{2,1,0:T(8,128)(2,1)} %bitcast.186), calls=%async_computation.4 | async-start | bytes 3145728 | tf_op jit(solution)/shard_map/all_to_all | solution.py:87
  216.6 3.2 %add_convert_fusion = bf16[2,2,8,4,32,256]{5,4,3,2,1,0:T(8,128)(2,1)S(1)} fusion(bf16[2,2,8,4,32,256]{5,4,3,2,1,0:T(8,128)(2,1)} %collective-permute-done.9, bf16[2,2,8,4,32,256]{5,4,3,2,1,0:T(8,128)(2,1)} %get-tuple-element.39), kind=kLoop, calls=%fused_computation | loop fusion | flops 4194304 | bytes 6291456 | tf_op jit(solution)/shard_map/convert_element_type | solution.py:107
  219.9 1.6 collective-permute-start.10
  221.5 2.5 add_convert_fusion.1
  225.7 32.8 %collective-permute-done.10 = bf16[2,8,4,32,256]{4,3,2,1,0:T(8,128)(2,1)S(1)} collective-permute-done((bf16[2,8,4,32,256]{4,3,2,1,0:T(8,128)(2,1)S(1)}, bf16[2,8,4,32,256]{4,3,2,1,0:T(8,128)(2,1)S(1)}, u32[]{:S(2)}, u32[]{:S(2)}) %collective-permute-start.10) | collective-permute-done | bytes 1048608 | tf_op jit(solution)/shard_map/ppermute | solution.py:83
  260.9 11.7 %collective-permute-done.11 = bf16[8,4,32,256]{3,2,1,0:T(8,128)(2,1)S(1)} collective-permute-done((bf16[8,4,32,256]{3,2,1,0:T(8,128)(2,1)S(1)}, bf16[8,4,32,256]{3,2,1,0:T(8,128)(2,1)S(1)}, u32[]{:S(2)}, u32[]{:S(2)}) %collective-permute-start.11) | collective-permute-done | bytes 524320 | tf_op jit(solution)/shard_map/ppermute | solution.py:83
  274.2 4.6 %all-to-all-start.5 = ((bf16[8,4,3,32,256]{4,3,2,1,0:T(8,128)(2,1)}), bf16[8,4,3,32,256]{4,3,2,1,0:T(8,128)(2,1)}, u32[]{:S(2)}, u32[]{:S(2)}) async-start(bf16[8,4,3,32,256]{4,3,2,1,0:T(8,128)(2,1)} %pad_maximum_fusion.2), calls=%async_computation.5 | async-start | bytes 3145728 | tf_op jit(solution)/shard_map/all_to_all | solution.py:87
  280.1 1.6 copy.164
  281.7 2.6 copy.191
  286.3 1.7 copy.192
  288.0 27.3 %all-to-all-done.5 = bf16[8,4,3,32,256]{4,3,2,1,0:T(8,128)(2,1)} async-done(((bf16[8,4,3,32,256]{4,3,2,1,0:T(8,128)(2,1)}), bf16[8,4,3,32,256]{4,3,2,1,0:T(8,128)(2,1)}, u32[]{:S(2)}, u32[]{:S(2)}) %all-to-all-start.5) | async-done | bytes 1572896 | tf_op jit(solution)/shard_map/all_to_all | solution.py:87
  315.3 1.8 convert.4
  (97 shorter events, 33.5 us)
Async XLA Ops:
  0.6 1.3 copy-start.9
  0.6 1.3 copy-start.10
  1.8 1.0 copy-start.11
  4.3 44.3 %all-to-all-start = ((bf16[8,4,3,32,256]{4,3,1,2,0:T(8,128)(2,1)}), bf16[8,4,3,32,256]{4,3,1,2,0:T(8,128)(2,1)S(1)}, u32[]{:S(2)}, u32[]{:S(2)}) async-start(bf16[8,4,3,32,256]{4,3,1,2,0:T(8,128)(2,1)} %maximum_maximum_fusion), calls=%async_computation | async-start | bytes 3145728 | tf_op jit(solution)/shard_map/all_to_all | solution.py:87
  15.1 1.5 copy-start.4
  48.5 41.7 %all-to-all-start.1 = ((bf16[32,96,256]{2,1,0:T(8,128)(2,1)}), bf16[32,96,256]{2,1,0:T(8,128)(2,1)}, u32[]{:S(2)}, u32[]{:S(2)}) async-start(bf16[32,96,256]{2,1,0:T(8,128)(2,1)} %pad_maximum_fusion), calls=%async_computation.1 | async-start | bytes 3145728 | tf_op jit(solution)/shard_map/all_to_all | solution.py:87
  53.6 61.7 %collective-permute-start.1 = (bf16[8,4,3,32,256]{4,3,1,0,2:T(8,128)(2,1)}, bf16[8,4,3,32,256]{4,3,1,0,2:T(8,128)(2,1)}, u32[]{:S(2)}, u32[]{:S(2)}) collective-permute-start(bf16[8,4,3,32,256]{4,3,1,0,2:T(8,128)(2,1)} %copy.158), channel_id=1, source_target_pairs={{0,2},{1,3},{2,0},{3,1},{4,6},{5,7},{6,4},{7,5},{8,10},{9,11},{10,... | collective-permute-start | bytes 4718600 | tf_op jit(solution)/shard_map/ppermute | solution.py:83
  58.9 1.5 copy-start.5
  90.2 79.8 %all-to-all-start.3 = ((bf16[32,96,256]{2,1,0:T(8,128)(2,1)}), bf16[32,96,256]{2,1,0:T(8,128)(2,1)S(1)}, u32[]{:S(2)}, u32[]{:S(2)}) async-start(bf16[32,96,256]{2,1,0:T(8,128)(2,1)} %pad_maximum_fusion.1), calls=%async_computation.3 | async-start | bytes 3145728 | tf_op jit(solution)/shard_map/all_to_all | solution.py:87
  115.3 33.9 %collective-permute-start.2 = (bf16[8,4,3,32,256]{4,3,1,0,2:T(8,128)(2,1)}, bf16[8,4,3,32,256]{4,3,1,0,2:T(8,128)(2,1)}, u32[]{:S(2)}, u32[]{:S(2)}) collective-permute-start(bf16[8,4,3,32,256]{4,3,1,0,2:T(8,128)(2,1)} %collective-permute-done.1), channel_id=1, source_target_pairs={{0,1},{1,0},{2,3},{3,2},{4,5},{5,4},{6,7},{7,6},{8,9},{9,8},{10,11... | collective-permute-start | bytes 4718600 | tf_op jit(solution)/shard_map/ppermute | solution.py:83
  116.6 35.4 %collective-permute-start = (bf16[8,4,3,32,256]{4,3,2,1,0:T(8,128)(2,1)}, bf16[8,4,3,32,256]{4,3,2,1,0:T(8,128)(2,1)}, u32[]{:S(2)}, u32[]{:S(2)}) collective-permute-start(bf16[8,4,3,32,256]{4,3,2,1,0:T(8,128)(2,1)} %copy.160.refs_0_), channel_id=1, source_target_pairs={{0,1},{1,0},{2,3},{3,2},{4,5},{5,4},{6,7},{7,6},{8,9},{9,8},{10,11... | collective-permute-start | bytes 4718600 | tf_op jit(solution)/shard_map/ppermute | solution.py:83
  117.2 17.5 %collective-permute-start.3 = (bf16[8,4,32,256]{3,2,1,0:T(8,128)(2,1)S(1)}, bf16[8,4,32,256]{3,2,1,0:T(8,128)(2,1)S(1)}, u32[]{:S(2)}, u32[]{:S(2)}) collective-permute-start(bf16[8,4,32,256]{3,2,1,0:T(8,128)(2,1)S(1)} %slice_bitcast_fusion.7), channel_id=1, source_target_pairs={{0,4},{4,0},{8,12},{12,8},{16,20},{20,16},{24,28},{28,24},{1,5},{5... | collective-permute-start | bytes 1572872 | tf_op jit(solution)/shard_map/ppermute | solution.py:83
  120.2 25.6 %collective-permute-start.5 = (bf16[8,4,32,256]{3,2,1,0:T(8,128)(2,1)S(1)}, bf16[8,4,32,256]{3,2,1,0:T(8,128)(2,1)S(1)}, u32[]{:S(2)}, u32[]{:S(2)}) collective-permute-start(bf16[8,4,32,256]{3,2,1,0:T(8,128)(2,1)S(1)} %slice_bitcast_fusion.6), channel_id=1, source_target_pairs={{0,4},{4,0},{8,12},{12,8},{16,20},{20,16},{24,28},{28,24},{1,5},{5... | collective-permute-start | bytes 1572872 | tf_op jit(solution)/shard_map/ppermute | solution.py:83
  134.7 14.6 %copy-start.6 = (bf16[8,4,32,256]{3,2,1,0:T(8,128)(2,1)}, bf16[8,4,32,256]{3,2,1,0:T(8,128)(2,1)S(1)}, u32[]{:S(2)}) copy-start(bf16[8,4,32,256]{3,2,1,0:T(8,128)(2,1)S(1)} %collective-permute-done.3.refs_4_) | copy-start | bytes 1572868
  134.7 17.3 %collective-permute-start.4 = (bf16[8,4,32,256]{3,2,1,0:T(8,128)(2,1)S(1)}, bf16[8,4,32,256]{3,2,1,0:T(8,128)(2,1)S(1)}, u32[]{:S(2)}, u32[]{:S(2)}) collective-permute-start(bf16[8,4,32,256]{3,2,1,0:T(8,128)(2,1)S(1)} %collective-permute-done.3.refs_4_), channel_id=1, source_target_pairs={{0,1},{1,0},{2,3},{3,2},{4,5},{5,4},{6,7},{7,6},{8,9},{9,8},{10,11... | collective-permute-start | bytes 1572872 | tf_op jit(solution)/shard_map/ppermute | solution.py:83
  145.8 3.4 %copy-start.7 = (bf16[8,4,32,256]{3,2,1,0:T(8,128)(2,1)}, bf16[8,4,32,256]{3,2,1,0:T(8,128)(2,1)S(1)}, u32[]{:S(2)}) copy-start(bf16[8,4,32,256]{3,2,1,0:T(8,128)(2,1)S(1)} %collective-permute-done.5.refs_6_) | copy-start | bytes 1572868
  145.8 6.2 %collective-permute-start.6 = (bf16[8,4,32,256]{3,2,1,0:T(8,128)(2,1)S(1)}, bf16[8,4,32,256]{3,2,1,0:T(8,128)(2,1)}, u32[]{:S(2)}, u32[]{:S(2)}) collective-permute-start(bf16[8,4,32,256]{3,2,1,0:T(8,128)(2,1)S(1)} %collective-permute-done.5.refs_6_), channel_id=1, source_target_pairs={{0,1},{1,0},{2,3},{3,2},{4,5},{5,4},{6,7},{7,6},{8,9},{9,8},{10,11... | collective-permute-start | bytes 1572872 | tf_op jit(solution)/shard_map/ppermute | solution.py:83
  152.0 0.8 copy-start.8
  170.0 1.2 copy-start.2
  171.2 41.4 %all-to-all-start.2 = ((bf16[32,96,256]{2,1,0:T(8,128)(2,1)}), bf16[32,96,256]{2,1,0:T(8,128)(2,1)S(1)}, u32[]{:S(2)}, u32[]{:S(2)}) async-start(bf16[32,96,256]{2,1,0:T(8,128)(2,1)} %bitcast.187), calls=%async_computation.2 | async-start | bytes 3145728 | tf_op jit(solution)/shard_map/all_to_all | solution.py:87
  195.6 21.0 %collective-permute-start.9 = (bf16[2,2,8,4,32,256]{5,4,3,2,1,0:T(8,128)(2,1)}, bf16[2,2,8,4,32,256]{5,4,3,2,1,0:T(8,128)(2,1)}, u32[]{:S(2)}, u32[]{:S(2)}) collective-permute-start(bf16[2,2,8,4,32,256]{5,4,3,2,1,0:T(8,128)(2,1)} %get-tuple-element.40), channel_id=1, source_target_pairs={{0,1},{1,0},{2,3},{3,2},{4,5},{5,4},{6,7},{7,6},{8,9},{9,8},{10,11... | collective-permute-start | bytes 6291464 | tf_op jit(solution)/shard_map/ppermute | solution.py:83
  195.7 25.8 %collective-permute-start.7 = (bf16[2,8,4,2,32,256]{5,4,3,2,1,0:T(8,128)(2,1)}, bf16[2,8,4,2,32,256]{5,4,3,2,1,0:T(8,128)(2,1)}, u32[]{:S(2)}, u32[]{:S(2)}) collective-permute-start(bf16[2,8,4,2,32,256]{5,4,3,2,1,0:T(8,128)(2,1)} %get-tuple-element.38), channel_id=1, source_target_pairs={{0,1},{1,0},{2,3},{3,2},{4,5},{5,4},{6,7},{7,6},{8,9},{9,8},{10,11... | collective-permute-start | bytes 6291464 | tf_op jit(solution)/shard_map/ppermute | solution.py:83
  212.6 66.2 %copy-start = (bf16[32,96,256]{2,1,0:T(8,128)(2,1)}, bf16[32,96,256]{2,1,0:T(8,128)(2,1)S(1)}, u32[]{:S(2)}) copy-start(bf16[32,96,256]{2,1,0:T(8,128)(2,1)S(1)} %all-to-all-done.2) | copy-start | bytes 4718596
  212.6 61.6 %all-to-all-start.4 = ((bf16[32,96,256]{2,1,0:T(8,128)(2,1)}), bf16[32,96,256]{2,1,0:T(8,128)(2,1)S(1)}, u32[]{:S(2)}, u32[]{:S(2)}) async-start(bf16[32,96,256]{2,1,0:T(8,128)(2,1)} %bitcast.186), calls=%async_computation.4 | async-start | bytes 3145728 | tf_op jit(solution)/shard_map/all_to_all | solution.py:87
  219.8 1.7 copy-start.3
  219.9 38.6 %collective-permute-start.10 = (bf16[2,8,4,32,256]{4,3,2,1,0:T(8,128)(2,1)S(1)}, bf16[2,8,4,32,256]{4,3,2,1,0:T(8,128)(2,1)S(1)}, u32[]{:S(2)}, u32[]{:S(2)}) collective-permute-start(bf16[2,8,4,32,256]{4,3,2,1,0:T(8,128)(2,1)S(1)} %slice_bitcast_fusion), channel_id=1, source_target_pairs={{0,4},{4,0},{8,12},{12,8},{16,20},{20,16},{24,28},{28,24},{1,5},{5... | collective-permute-start | bytes 3145736 | tf_op jit(solution)/shard_map/ppermute | solution.py:83
  224.1 36.4 %collective-permute-start.8 = (bf16[8,4,2,32,256]{4,3,2,1,0:T(8,128)(2,1)S(1)}, bf16[8,4,2,32,256]{4,3,2,1,0:T(8,128)(2,1)S(1)}, u32[]{:S(2)}, u32[]{:S(2)}) collective-permute-start(bf16[8,4,2,32,256]{4,3,2,1,0:T(8,128)(2,1)S(1)} %slice_bitcast_fusion.2), channel_id=1, source_target_pairs={{0,2},{1,3},{2,0},{3,1},{4,6},{5,7},{6,4},{7,5},{8,10},{9,11},{10,... | collective-permute-start | bytes 3145736 | tf_op jit(solution)/shard_map/ppermute | solution.py:83
  259.0 13.7 %collective-permute-start.11 = (bf16[8,4,32,256]{3,2,1,0:T(8,128)(2,1)S(1)}, bf16[8,4,32,256]{3,2,1,0:T(8,128)(2,1)S(1)}, u32[]{:S(2)}, u32[]{:S(2)}) collective-permute-start(bf16[8,4,32,256]{3,2,1,0:T(8,128)(2,1)S(1)} %slice_bitcast_fusion.4), channel_id=1, source_target_pairs={{0,2},{1,3},{2,0},{3,1},{4,6},{5,7},{6,4},{7,5},{8,10},{9,11},{10,... | collective-permute-start | bytes 1572872 | tf_op jit(solution)/shard_map/ppermute | solution.py:83
  274.2 10.1 %copy-start.1 = (bf16[32,96,256]{2,1,0:T(8,128)(2,1)}, bf16[32,96,256]{2,1,0:T(8,128)(2,1)S(1)}, u32[]{:S(2)}) copy-start(bf16[32,96,256]{2,1,0:T(8,128)(2,1)S(1)} %all-to-all-done.4) | copy-start | bytes 4718596
  274.2 41.1 %all-to-all-start.5 = ((bf16[8,4,3,32,256]{4,3,2,1,0:T(8,128)(2,1)}), bf16[8,4,3,32,256]{4,3,2,1,0:T(8,128)(2,1)}, u32[]{:S(2)}, u32[]{:S(2)}) async-start(bf16[8,4,3,32,256]{4,3,2,1,0:T(8,128)(2,1)} %pad_maximum_fusion.2), calls=%async_computation.5 | async-start | bytes 3145728 | tf_op jit(solution)/shard_map/all_to_all | solution.py:87
  278.9 1.0 slice-start
  284.3 1.0 slice-start.1

commit v5 on v4

--- a/solution.py
+++ b/solution.py
@@ -142,8 +142,8 @@
 def weight_of(slot, w, v):
     def get(m, which, r):
         if slot == 0:
-            return square(w[m][:, which, r])
-        return square(v[m][:, which] if r else w[m][:, which, 2])
+            return square(w[which // 2][m][:, which % 2, r])
+        return square(v[m][r, :, which])
 
     return get
 
@@ -151,24 +151,25 @@
 def wide_weight(slot, w, e_ref, y):
     def get(m, r):
         if slot == 0:
-            return square(w[m][half_src(e_ref.shape[1], r), 3, :2])
+            return square(w[1][m][half_src(e_ref.shape[1], r), 1])
         return square(e_ref[m, half_src(e_ref.shape[1], r ^ y)])
 
     return get
 
 
-def join_halves(w, v, e_ref, y):
-    for m in range(len(w)):
-        e_ref[m, :, y] = w[m][:, 3, 2]
-        e_ref[m, :, 1 - y] = v[m][:, 3]
+def join_halves(v, e_ref, y):
+    for m in range(len(v)):
+        e_ref[m, :, y] = v[m][0, :, 3]
+        e_ref[m, :, 1 - y] = v[m][1, :, 3]
 
 
 def forward_kernel(seat_ref, x_ref, *refs):
-    w, v, (out_ref,), saved, e_ref = refs[:4], refs[4:8], refs[8:9], (refs[9:13], refs[13:17]), refs[17]
+    w, v, out_ref, saved = (refs[:4], refs[4:8]), refs[8:12], refs[12], (refs[13:17], refs[17:21])
+    e_ref = refs[21]
     ndp, nb, all_rows, _ = x_ref.shape
     own_rows = 2 * all_rows // 3
     f, y = seat_ref[0], seat_ref[1]
-    join_halves(w, v, e_ref, y)
+    join_halves(v, e_ref, y)
     for slot, (lo, hi) in enumerate(((0, own_rows), (own_rows, all_rows))):
         perm, active, slope, ret = saved[slot]
         weight, wide = weight_of(slot, w, v), wide_weight(slot, w, e_ref, y)
@@ -199,14 +200,14 @@
 
 
 def backward_kernel(seat_ref, x_ref, g_ref, *refs):
-    w, v, saved = refs[:4], refs[4:8], (refs[8:12], refs[12:16])
-    gin_ref, own_keep, own_send, mid_keep, mid_send = refs[16:21]
-    scratch, e_ref = (refs[21:23], refs[23:25]), refs[25]
+    w, v, saved = (refs[:4], refs[4:8]), refs[8:12], (refs[12:16], refs[16:20])
+    gin_ref, own_keep, own_send, mid_keep, mid_send = refs[20:25]
+    scratch, e_ref = (refs[25:27], refs[27:29]), refs[29]
     ndp, nb, all_rows, _ = x_ref.shape
     own_rows = 2 * all_rows // 3
     rows = BLK // ndp
     f, y = seat_ref[0], seat_ref[1]
-    join_halves(w, v, e_ref, y)
+    join_halves(v, e_ref, y)
 
     def store(slot, m, which, r, part):
         ref = ((own_keep, own_send), (mid_keep, mid_send))[slot][m % 2]
@@ -288,12 +289,19 @@
     shape = (ndp, nb, -1, BLK)
     dealt = [deal_weight(w) for w in (dealt_a, weight_b, weight_c, dealt_e)]
     w = exchange(jnp.stack(dealt, axis=1), "dp")
-    across = xor_permute(w, 2)
-    v = xor_permute(w[:, :, 2], 1, "dp")
+    parts_in = (w[:, :, 2], w[:, :2, :2], w[:, 2:, :2])
+    mid_across, ab_across, ce_across = (xor_permute(part, 2) for part in parts_in)
     x = exchange(after(deal_tokens(tokens), w), everyone)
-    g = exchange(after(deal_tokens(grad_out), x), everyone).reshape(shape)
+    mid_swapped = xor_permute(parts_in[0], 1, "dp")
+    g = after(deal_tokens(grad_out), x, mid_across, ab_across, mid_swapped)
+    g = exchange(g, everyone).reshape(shape)
     x = x.reshape(shape)
-    weights = gather_bfly(w, across) + gather_bfly(v, xor_permute(across[:, :, 2], 1, "dp"))
+    both = [
+        jnp.stack([parts_in[0], mid_swapped]),
+        jnp.stack([mid_across, xor_permute(mid_across, 1, "dp")]),
+    ]
+    weights = gather_bfly(parts_in[1], ab_across) + gather_bfly(parts_in[2], ce_across)
+    weights += gather_bfly(*both)
 
     own, mid = count * ndp // nb, count * ndp // nb // 2
     saved = []
@@ -314,10 +322,10 @@
         [saved[0], saved[0], saved[4], saved[4], halves],
         [seat, x, g] + weights + kept,
     )
-    mid = add(mid_keep, xor_permute(mid_send, 1))
-    own = add(own_keep, xor_permute(own_send, 1))
+    half_mid = mid = add(mid_keep, xor_permute(mid_send, 1))
+    half_own = own = add(own_keep, xor_permute(own_send, 1))
     mid = add(mid[0], xor_permute(mid[1], 1, "dp"))
-    gin = exchange(after(gin.reshape(ndp * nb, -1, BLK), out), everyone)
+    gin = exchange(after(gin.reshape(ndp * nb, -1, BLK), out, half_mid, half_own), everyone)
     own = add(own[0], xor_permute(own[1], 2))
     mid = add(mid[0], xor_permute(mid[1], 2))
     dealt = jnp.concatenate([own, mid[:, :, None]], axis=2)

time: 323 us -> 308 us (0.954)
  waiting for transfers between devices: 190 us -> 168 us
  starting transfers between devices: 36.9 us -> 43.5 us
    all_to_all x6, waiting for transfers between devices: 98.7 us -> 62.4 us  [exchange(): return lax.all_to_all(x, axes, split_axis=0, concat_axis=0, tiled=True)]
    ppermute x12 -> x16, waiting for transfers between devices: 91.2 us -> 106 us  [xor_permute(): lax.ppermute(x, axis, [(i, i ^ mask) for i in range(lax.axis_size(axis))])]
    ppermute x2 -> x0, local copies, waits for them, and re-layouts: 5.5 us -> none  [xor_permute(): lax.ppermute(x, axis, [(i, i ^ mask) for i in range(lax.axis_size(axis))])]
    another operation x0 -> x2, other arithmetic: none -> 3.48 us  [the longest x1 2.18 us: token_plan(): jnp.stack([mid_across, xor_permute(mid_across, 1, 'dp')])]
    ppermute x12 -> x16, starting transfers between devices: 9.58 us -> 13 us  [xor_permute(): lax.ppermute(x, axis, [(i, i ^ mask) for i in range(lax.axis_size(axis))])]
    unnamed x28 -> x30, local copies, waits for them, and re-layouts: 10.5 us -> 12.6 us
  transfers between devices with their start and end apart: 18 -> 22, of which waited for: 9 -> 12; matrix products, arithmetic and copies ran while one was open for 13% -> 14% of each run, Pallas kernels for 12% -> 12%
where the time goes in v5:
time: 308 us; the launch traced here: 307 us
  waiting for transfers between devices  168 us (55%)
  starting transfers between devices  43.5 us (14%)
  Pallas kernels  37.8 us (12%)
  local copies, waits for them, and re-layouts  36.8 us (12%)
  other arithmetic  20.1 us (7%)
    ppermute x16, waiting for transfers between devices, xor_permute(): lax.ppermute(x, axis, [(i, i ^ mask) for i in range(lax.axis_size(axis))])  106 us
    all_to_all x6, waiting for transfers between devices, exchange(): return lax.all_to_all(x, axes, split_axis=0, concat_axis=0, tiled=True)  62.4 us
    pallas_call x2, Pallas kernels, on_chip(): pl.pallas_call(kernel, out_shape=[jax.ShapeDtypeStruct(shape, jnp.bfloat1...  37.8 us
    all_to_all x6, starting transfers between devices, exchange(): return lax.all_to_all(x, axes, split_axis=0, concat_axis=0, tiled=True)  30.5 us
    ppermute x16, starting transfers between devices, xor_permute(): lax.ppermute(x, axis, [(i, i ^ mask) for i in range(lax.axis_size(axis))])  13 us
    unnamed x30, local copies, waits for them, and re-layouts  12.6 us
  transfers between devices with their start and end apart: 22, of which 12 were waited for; matrix products, arithmetic and copies ran while one was open for 14% of the time, Pallas kernels for 12%

profile of v5, /device:TPU:0, one launch (start us, length us, event | category | flops | bytes accessed | tf_op | source)
XLA Modules:
  0.0 307.2 jit_solution(4705029848430845796)
XLA Ops:
  4.3 7.3 %all-to-all-start = ((bf16[8,4,3,32,256]{4,3,1,2,0:T(8,128)(2,1)}), bf16[8,4,3,32,256]{4,3,1,2,0:T(8,128)(2,1)S(1)}, u32[]{:S(2)}, u32[]{:S(2)}) async-start(bf16[8,4,3,32,256]{4,3,1,2,0:T(8,128)(2,1)} %maximum_maximum_fusion), calls=%async_computation | async-start | bytes 3145728 | tf_op jit(solution)/shard_map/all_to_all | solution.py:87
  11.5 1.7 copy.172
  15.1 1.5 copy.173
  17.7 2.3 pad_maximum_fusion
  20.0 28.6 %all-to-all-done = bf16[8,4,3,32,256]{4,3,1,2,0:T(8,128)(2,1)S(1)} async-done(((bf16[8,4,3,32,256]{4,3,1,2,0:T(8,128)(2,1)}), bf16[8,4,3,32,256]{4,3,1,2,0:T(8,128)(2,1)S(1)}, u32[]{:S(2)}, u32[]{:S(2)}) %all-to-all-start) | async-done | bytes 1572896 | tf_op jit(solution)/shard_map/all_to_all | solution.py:87
  48.5 3.7 %all-to-all-start.1 = ((bf16[32,96,256]{2,1,0:T(8,128)(2,1)}), bf16[32,96,256]{2,1,0:T(8,128)(2,1)S(1)}, u32[]{:S(2)}, u32[]{:S(2)}) async-start(bf16[32,96,256]{2,1,0:T(8,128)(2,1)} %pad_maximum_fusion), calls=%async_computation.1 | async-start | bytes 3145728 | tf_op jit(solution)/shard_map/all_to_all | solution.py:87
  53.3 1.8 collective-permute-start.8
  58.8 1.7 copy.186
  62.4 1.5 copy.187
  65.0 2.3 pad_maximum_fusion.1
  67.3 14.4 %collective-permute-done.8 = bf16[8,4,32,256]{3,2,1,0:T(8,128)(2,1)} collective-permute-done((bf16[8,4,32,256]{3,2,1,0:T(8,128)(2,1)}, bf16[8,4,32,256]{3,2,1,0:T(8,128)(2,1)}, u32[]{:S(2)}, u32[]{:S(2)}) %collective-permute-start.8) | collective-permute-done | bytes 524320 | tf_op jit(solution)/shard_map/ppermute | solution.py:83
  81.6 12.9 %collective-permute-done.1.refs_2_ = bf16[8,2,2,32,256]{4,3,2,1,0:T(8,128)(2,1)} collective-permute-done((bf16[8,2,2,32,256]{4,3,2,1,0:T(8,128)(2,1)}, bf16[8,2,2,32,256]{4,3,2,1,0:T(8,128)(2,1)}, u32[]{:S(2)}, u32[]{:S(2)}) %collective-permute-start.1) | collective-permute-done | bytes 524320 | tf_op jit(solution)/shard_map/ppermute | solution.py:83
  95.6 4.7 %all-to-all-start.3 = ((bf16[32,96,256]{2,1,0:T(8,128)(2,1)}), bf16[32,96,256]{2,1,0:T(8,128)(2,1)S(1)}, u32[]{:S(2)}, u32[]{:S(2)}) async-start(bf16[32,96,256]{2,1,0:T(8,128)(2,1)} %pad_maximum_fusion.1), calls=%async_computation.3 | async-start | bytes 3145728 | tf_op jit(solution)/shard_map/all_to_all | solution.py:87
  100.4 1.7 collective-permute-start.9
  103.2 1.5 collective-permute-start.4
  106.3 22.2 %collective-permute-done.9 = bf16[8,4,32,256]{3,2,1,0:T(8,128)(2,1)S(1)} collective-permute-done((bf16[8,4,32,256]{3,2,1,0:T(8,128)(2,1)}, bf16[8,4,32,256]{3,2,1,0:T(8,128)(2,1)S(1)}, u32[]{:S(2)}, u32[]{:S(2)}) %collective-permute-start.9) | collective-permute-done | bytes 524320 | tf_op jit(solution)/shard_map/ppermute | solution.py:83
  128.5 2.2 pad_maximum_fusion.4.refs_10_
  132.7 2.0 collective-permute-done.3.refs_5_
  136.0 17.3 %shard_map.109 = (bf16[8,4,96,256]{3,2,1,0:T(8,128)(2,1)}, bf16[2,4,4,64,512]{4,3,2,1,0:T(8,128)(2,1)}, bf16[2,4,256,512]{3,2,1,0:T(8,128)(2,1)}, bf16[2,4,256,5...) custom-call(s32[2]{0:T(128)} %pad_add_fusion.seat_ref, ...), custom_call_target="tpu_custom_call" | custom-call | flops 3221225472 | bytes 24117252 | tf_op jit(solution)/shard_map/pallas_call | solution.py:265
  154.5 6.1 %all-to-all-start.2 = ((bf16[32,96,256]{2,1,0:T(8,128)(2,1)}), bf16[32,96,256]{2,1,0:T(8,128)(2,1)}, u32[]{:S(2)}, u32[]{:S(2)}) async-start(bf16[32,96,256]{2,1,0:T(8,128)(2,1)} %bitcast.195), calls=%async_computation.2 | async-start | bytes 3145728 | tf_op jit(solution)/shard_map/all_to_all | solution.py:87
  160.5 20.5 %shard_map.110 = (bf16[8,4,96,256]{3,2,1,0:T(8,128)(2,1)}, bf16[2,8,4,2,32,256]{5,4,3,2,1,0:T(8,128)(2,1)}, bf16[2,8,4,2,32,256]{5,4,3,2,1,0:T(8,128)(2,1)}, bf1...) custom-call(s32[2]{0:T(128)} %pad_add_fusion.seat_ref, bf16[8,4,96,256]{3,2,1,0:T(8,128)(2,1)} %bitcast.183, ...), custom_call_target="tpu_custom_call" | custom-call | flops 6442450944 | bytes 34078724 | tf_op jit(solution)/shard_map/pallas_call | solution.py:265
  181.6 3.9 %collective-permute-done.11 = bf16[2,2,8,4,32,256]{5,4,3,2,1,0:T(8,128)(2,1)S(1)} collective-permute-done((bf16[2,2,8,4,32,256]{5,4,3,2,1,0:T(8,128)(2,1)}, bf16[2,2,8,4,32,256]{5,4,3,2,1,0:T(8,128)(2,1)S(1)}, u32[]{:S(2)}, u32[]{:S(2)}) %collective-permute-start.11) | collective-permute-done | bytes 2097184 | tf_op jit(solution)/shard_map/ppermute | solution.py:83
  185.4 4.0 %add_convert_fusion.1 = bf16[2,2,8,4,32,256]{5,4,3,2,1,0:T(8,128)(2,1)} fusion(bf16[2,2,8,4,32,256]{5,4,3,2,1,0:T(8,128)(2,1)S(1)} %collective-permute-done.11, bf16[2,2,8,4,32,256]{5,4,3,2,1,0:T(8,128)(2,1)} %get-tuple-element.36), kind=kLoop, calls=%fused_computation.1 | loop fusion | flops 4194304 | bytes 6291456 | tf_op jit(solution)/shard_map/convert_element_type | solution.py:107
  190.6 7.5 %all-to-all-done.2 = bf16[32,96,256]{2,1,0:T(8,128)(2,1)} async-done(((bf16[32,96,256]{2,1,0:T(8,128)(2,1)}), bf16[32,96,256]{2,1,0:T(8,128)(2,1)}, u32[]{:S(2)}, u32[]{:S(2)}) %all-to-all-start.2) | async-done | bytes 1572896 | tf_op jit(solution)/shard_map/all_to_all | solution.py:87
  198.1 4.1 %all-to-all-start.4 = ((bf16[32,96,256]{2,1,0:T(8,128)(2,1)}), bf16[32,96,256]{2,1,0:T(8,128)(2,1)}, u32[]{:S(2)}, u32[]{:S(2)}) async-start(bf16[32,96,256]{2,1,0:T(8,128)(2,1)} %bitcast.194), calls=%async_computation.4 | async-start | bytes 3145728 | tf_op jit(solution)/shard_map/all_to_all | solution.py:87
  206.8 37.2 %collective-permute-done.14 = bf16[2,8,4,32,256]{4,3,2,1,0:T(8,128)(2,1)S(1)} collective-permute-done((bf16[2,8,4,32,256]{4,3,2,1,0:T(8,128)(2,1)S(1)}, bf16[2,8,4,32,256]{4,3,2,1,0:T(8,128)(2,1)S(1)}, u32[]{:S(2)}, u32[]{:S(2)}) %collective-permute-start.14) | collective-permute-done | bytes 1048608 | tf_op jit(solution)/shard_map/ppermute | solution.py:83
  246.5 11.7 %collective-permute-done.15 = bf16[8,4,32,256]{3,2,1,0:T(8,128)(2,1)S(1)} collective-permute-done((bf16[8,4,32,256]{3,2,1,0:T(8,128)(2,1)S(1)}, bf16[8,4,32,256]{3,2,1,0:T(8,128)(2,1)S(1)}, u32[]{:S(2)}, u32[]{:S(2)}) %collective-permute-start.15) | collective-permute-done | bytes 524320 | tf_op jit(solution)/shard_map/ppermute | solution.py:83
  259.7 4.6 %all-to-all-start.5 = ((bf16[8,4,3,32,256]{4,3,2,1,0:T(8,128)(2,1)}), bf16[8,4,3,32,256]{4,3,2,1,0:T(8,128)(2,1)}, u32[]{:S(2)}, u32[]{:S(2)}) async-start(bf16[8,4,3,32,256]{4,3,2,1,0:T(8,128)(2,1)} %pad_maximum_fusion.2), calls=%async_computation.5 | async-start | bytes 3145728 | tf_op jit(solution)/shard_map/all_to_all | solution.py:87
  267.7 1.7 copy.209
  272.8 1.7 copy.210
  274.5 26.3 %all-to-all-done.5 = bf16[8,4,3,32,256]{4,3,2,1,0:T(8,128)(2,1)} async-done(((bf16[8,4,3,32,256]{4,3,2,1,0:T(8,128)(2,1)}), bf16[8,4,3,32,256]{4,3,2,1,0:T(8,128)(2,1)}, u32[]{:S(2)}, u32[]{:S(2)}) %all-to-all-start.5) | async-done | bytes 1572896 | tf_op jit(solution)/shard_map/all_to_all | solution.py:87
  300.8 1.8 convert.4
  (103 shorter events, 43.7 us)
Async XLA Ops:
  0.6 1.3 copy-start.9
  0.6 1.3 copy-start.10
  4.3 44.3 %all-to-all-start = ((bf16[8,4,3,32,256]{4,3,1,2,0:T(8,128)(2,1)}), bf16[8,4,3,32,256]{4,3,1,2,0:T(8,128)(2,1)S(1)}, u32[]{:S(2)}, u32[]{:S(2)}) async-start(bf16[8,4,3,32,256]{4,3,1,2,0:T(8,128)(2,1)} %maximum_maximum_fusion), calls=%async_computation | async-start | bytes 3145728 | tf_op jit(solution)/shard_map/all_to_all | solution.py:87
  15.1 1.5 copy-start.5
  48.5 46.0 %all-to-all-start.1 = ((bf16[32,96,256]{2,1,0:T(8,128)(2,1)}), bf16[32,96,256]{2,1,0:T(8,128)(2,1)S(1)}, u32[]{:S(2)}, u32[]{:S(2)}) async-start(bf16[32,96,256]{2,1,0:T(8,128)(2,1)} %pad_maximum_fusion), calls=%async_computation.1 | async-start | bytes 3145728 | tf_op jit(solution)/shard_map/all_to_all | solution.py:87
  53.3 28.3 %collective-permute-start.8 = (bf16[8,4,32,256]{3,2,1,0:T(8,128)(2,1)}, bf16[8,4,32,256]{3,2,1,0:T(8,128)(2,1)}, u32[]{:S(2)}, u32[]{:S(2)}) collective-permute-start(bf16[8,4,32,256]{3,2,1,0:T(8,128)(2,1)} %get-tuple-element.77), channel_id=1, source_target_pairs={{0,2},{1,3},{2,0},{3,1},{4,6},{5,7},{6,4},{7,5},{8,10},{9,11},{10,... | collective-permute-start | bytes 1572872 | tf_op jit(solution)/shard_map/ppermute | solution.py:83
  55.1 26.6 %collective-permute-start.6 = (bf16[8,4,32,256]{3,2,1,0:T(8,128)(2,1)}, bf16[8,4,32,256]{3,2,1,0:T(8,128)(2,1)}, u32[]{:S(2)}, u32[]{:S(2)}) collective-permute-start(bf16[8,4,32,256]{3,2,1,0:T(8,128)(2,1)} %get-tuple-element.77), channel_id=1, source_target_pairs={{0,4},{4,0},{8,12},{12,8},{16,20},{20,16},{24,28},{28,24},{1,5},{5... | collective-permute-start | bytes 1572872 | tf_op jit(solution)/shard_map/ppermute | solution.py:83
  58.3 36.2 %collective-permute-start.1 = (bf16[8,2,2,32,256]{4,3,2,1,0:T(8,128)(2,1)}, bf16[8,2,2,32,256]{4,3,2,1,0:T(8,128)(2,1)}, u32[]{:S(2)}, u32[]{:S(2)}) collective-permute-start(bf16[8,2,2,32,256]{4,3,2,1,0:T(8,128)(2,1)} %copy.214.refs_0_), channel_id=1, source_target_pairs={{0,2},{1,3},{2,0},{3,1},{4,6},{5,7},{6,4},{7,5},{8,10},{9,11},{10,... | collective-permute-start | bytes 1572872 | tf_op jit(solution)/shard_map/ppermute | solution.py:83
  62.4 1.5 copy-start.6
  94.5 1.1 copy-start.1
  95.6 57.7 %all-to-all-start.3 = ((bf16[32,96,256]{2,1,0:T(8,128)(2,1)}), bf16[32,96,256]{2,1,0:T(8,128)(2,1)S(1)}, u32[]{:S(2)}, u32[]{:S(2)}) async-start(bf16[32,96,256]{2,1,0:T(8,128)(2,1)} %pad_maximum_fusion.1), calls=%async_computation.3 | async-start | bytes 3145728 | tf_op jit(solution)/shard_map/all_to_all | solution.py:87
  100.4 28.1 %collective-permute-start.9 = (bf16[8,4,32,256]{3,2,1,0:T(8,128)(2,1)}, bf16[8,4,32,256]{3,2,1,0:T(8,128)(2,1)S(1)}, u32[]{:S(2)}, u32[]{:S(2)}) collective-permute-start(bf16[8,4,32,256]{3,2,1,0:T(8,128)(2,1)} %collective-permute-done.8), channel_id=1, source_target_pairs={{0,4},{4,0},{8,12},{12,8},{16,20},{20,16},{24,28},{28,24},{1,5},{5... | collective-permute-start | bytes 1572872 | tf_op jit(solution)/shard_map/ppermute | solution.py:83
  102.1 29.2 %collective-permute-start = (bf16[8,2,2,32,256]{4,3,2,1,0:T(8,128)(2,1)}, bf16[8,2,2,32,256]{4,3,2,1,0:T(8,128)(2,1)S(1)}, u32[]{:S(2)}, u32[]{:S(2)}) collective-permute-start(bf16[8,2,2,32,256]{4,3,2,1,0:T(8,128)(2,1)} %copy.214.refs_0_), channel_id=1, source_target_pairs={{0,1},{1,0},{2,3},{3,2},{4,5},{5,4},{6,7},{7,6},{8,9},{9,8},{10,11... | collective-permute-start | bytes 1572872 | tf_op jit(solution)/shard_map/ppermute | solution.py:83
  103.1 27.6 %copy-start.7 = (bf16[8,2,2,32,256]{4,3,2,1,0:T(8,128)(2,1)}, bf16[8,2,2,32,256]{4,3,2,1,0:T(8,128)(2,1)S(1)}, u32[]{:S(2)}) copy-start(bf16[8,2,2,32,256]{4,3,2,1,0:T(8,128)(2,1)S(1)} %copy.215.refs_4_) | copy-start | bytes 1572868
  103.2 28.2 %collective-permute-start.4 = (bf16[8,2,2,32,256]{4,3,2,1,0:T(8,128)(2,1)S(1)}, bf16[8,2,2,32,256]{4,3,2,1,0:T(8,128)(2,1)}, u32[]{:S(2)}, u32[]{:S(2)}) collective-permute-start(bf16[8,2,2,32,256]{4,3,2,1,0:T(8,128)(2,1)S(1)} %copy.215.refs_4_), channel_id=1, source_target_pairs={{0,2},{1,3},{2,0},{3,1},{4,6},{5,7},{6,4},{7,5},{8,10},{9,11},{10,... | collective-permute-start | bytes 1572872 | tf_op jit(solution)/shard_map/ppermute | solution.py:83
  106.0 30.0 %copy-start.3 = (bf16[2,8,4,32,256]{4,3,2,1,0:T(8,128)(2,1)}, bf16[2,8,4,32,256]{4,3,2,1,0:T(8,128)(2,1)S(1)}, u32[]{:S(2)}) copy-start(bf16[2,8,4,32,256]{4,3,2,1,0:T(8,128)(2,1)S(1)} %pad_maximum_fusion.3.refs_8_) | copy-start | bytes 3145732
  106.0 30.0 %collective-permute-start.7 = (bf16[2,8,4,32,256]{4,3,2,1,0:T(8,128)(2,1)S(1)}, bf16[2,8,4,32,256]{4,3,2,1,0:T(8,128)(2,1)}, u32[]{:S(2)}, u32[]{:S(2)}) collective-permute-start(bf16[2,8,4,32,256]{4,3,2,1,0:T(8,128)(2,1)S(1)} %pad_maximum_fusion.3.refs_8_), channel_id=1, source_target_pairs={{0,1},{1,0},{2,3},{3,2},{4,5},{5,4},{6,7},{7,6},{8,9},{9,8},{10,11... | collective-permute-start | bytes 3145736 | tf_op jit(solution)/shard_map/ppermute | solution.py:83
  130.7 5.3 %collective-permute-start.10 = (bf16[2,8,4,32,256]{4,3,2,1,0:T(8,128)(2,1)}, bf16[2,8,4,32,256]{4,3,2,1,0:T(8,128)(2,1)}, u32[]{:S(2)}, u32[]{:S(2)}) collective-permute-start(bf16[2,8,4,32,256]{4,3,2,1,0:T(8,128)(2,1)} %pad_maximum_fusion.4.refs_10_), channel_id=1, source_target_pairs={{0,1},{1,0},{2,3},{3,2},{4,5},{5,4},{6,7},{7,6},{8,9},{9,8},{10,11... | collective-permute-start | bytes 3145736 | tf_op jit(solution)/shard_map/ppermute | solution.py:83
  130.7 3.9 %collective-permute-start.3 = (bf16[8,2,2,32,256]{4,3,2,1,0:T(8,128)(2,1)S(1)}, bf16[8,2,2,32,256]{4,3,2,1,0:T(8,128)(2,1)}, u32[]{:S(2)}, u32[]{:S(2)}) collective-permute-start(bf16[8,2,2,32,256]{4,3,2,1,0:T(8,128)(2,1)S(1)} %copy.215.refs_4_), channel_id=1, source_target_pairs={{0,1},{1,0},{2,3},{3,2},{4,5},{5,4},{6,7},{7,6},{8,9},{9,8},{10,11... | collective-permute-start | bytes 1572872 | tf_op jit(solution)/shard_map/ppermute | solution.py:83
  131.2 4.0 %collective-permute-start.2 = (bf16[8,2,2,32,256]{4,3,2,1,0:T(8,128)(2,1)}, bf16[8,2,2,32,256]{4,3,2,1,0:T(8,128)(2,1)}, u32[]{:S(2)}, u32[]{:S(2)}) collective-permute-start(bf16[8,2,2,32,256]{4,3,2,1,0:T(8,128)(2,1)} %collective-permute-done.1.refs_2_), channel_id=1, source_target_pairs={{0,1},{1,0},{2,3},{3,2},{4,5},{5,4},{6,7},{7,6},{8,9},{9,8},{10,11... | collective-permute-start | bytes 1572872 | tf_op jit(solution)/shard_map/ppermute | solution.py:83
  132.0 3.9 %collective-permute-start.5 = (bf16[8,2,2,32,256]{4,3,2,1,0:T(8,128)(2,1)}, bf16[8,2,2,32,256]{4,3,2,1,0:T(8,128)(2,1)}, u32[]{:S(2)}, u32[]{:S(2)}) collective-permute-start(bf16[8,2,2,32,256]{4,3,2,1,0:T(8,128)(2,1)} %collective-permute-done.4.refs_6_), channel_id=1, source_target_pairs={{0,1},{1,0},{2,3},{3,2},{4,5},{5,4},{6,7},{7,6},{8,9},{9,8},{10,11... | collective-permute-start | bytes 1572872 | tf_op jit(solution)/shard_map/ppermute | solution.py:83
  153.3 1.2 copy-start.2
  154.5 43.6 %all-to-all-start.2 = ((bf16[32,96,256]{2,1,0:T(8,128)(2,1)}), bf16[32,96,256]{2,1,0:T(8,128)(2,1)}, u32[]{:S(2)}, u32[]{:S(2)}) async-start(bf16[32,96,256]{2,1,0:T(8,128)(2,1)} %bitcast.195), calls=%async_computation.2 | async-start | bytes 3145728 | tf_op jit(solution)/shard_map/all_to_all | solution.py:87
  181.0 4.4 %collective-permute-start.11 = (bf16[2,2,8,4,32,256]{5,4,3,2,1,0:T(8,128)(2,1)}, bf16[2,2,8,4,32,256]{5,4,3,2,1,0:T(8,128)(2,1)S(1)}, u32[]{:S(2)}, u32[]{:S(2)}) collective-permute-start(bf16[2,2,8,4,32,256]{5,4,3,2,1,0:T(8,128)(2,1)} %get-tuple-element.37), channel_id=1, source_target_pairs={{0,1},{1,0},{2,3},{3,2},{4,5},{5,4},{6,7},{7,6},{8,9},{9,8},{10,11... | collective-permute-start | bytes 6291464 | tf_op jit(solution)/shard_map/ppermute | solution.py:83
  181.1 8.4 %collective-permute-start.12 = (bf16[2,8,4,2,32,256]{5,4,3,2,1,0:T(8,128)(2,1)}, bf16[2,8,4,2,32,256]{5,4,3,2,1,0:T(8,128)(2,1)S(1)}, u32[]{:S(2)}, u32[]{:S(2)}) collective-permute-start(bf16[2,8,4,2,32,256]{5,4,3,2,1,0:T(8,128)(2,1)} %get-tuple-element.39), channel_id=1, source_target_pairs={{0,1},{1,0},{2,3},{3,2},{4,5},{5,4},{6,7},{7,6},{8,9},{9,8},{10,11... | collective-permute-start | bytes 6291464 | tf_op jit(solution)/shard_map/ppermute | solution.py:83
  185.4 4.0 %copy-start.4 = (bf16[2,8,4,2,32,256]{5,4,3,2,1,0:T(8,128)(2,1)S(1)}, bf16[2,8,4,2,32,256]{5,4,3,2,1,0:T(8,128)(2,1)}, u32[]{:S(2)}) copy-start(bf16[2,8,4,2,32,256]{5,4,3,2,1,0:T(8,128)(2,1)} %get-tuple-element.38) | copy-start | bytes 6291460
  198.1 61.6 %all-to-all-start.4 = ((bf16[32,96,256]{2,1,0:T(8,128)(2,1)}), bf16[32,96,256]{2,1,0:T(8,128)(2,1)}, u32[]{:S(2)}, u32[]{:S(2)}) async-start(bf16[32,96,256]{2,1,0:T(8,128)(2,1)} %bitcast.194), calls=%async_computation.4 | async-start | bytes 3145728 | tf_op jit(solution)/shard_map/all_to_all | solution.py:87
  202.2 41.8 %copy-start = (bf16[2,2,8,4,32,256]{5,4,3,2,1,0:T(8,128)(2,1)S(1)}, bf16[2,2,8,4,32,256]{5,4,3,2,1,0:T(8,128)(2,1)}, u32[]{:S(2)}) copy-start(bf16[2,2,8,4,32,256]{5,4,3,2,1,0:T(8,128)(2,1)} %add_convert_fusion.1) | copy-start | bytes 6291460
  203.7 40.3 %collective-permute-start.14 = (bf16[2,8,4,32,256]{4,3,2,1,0:T(8,128)(2,1)S(1)}, bf16[2,8,4,32,256]{4,3,2,1,0:T(8,128)(2,1)S(1)}, u32[]{:S(2)}, u32[]{:S(2)}) collective-permute-start(bf16[2,8,4,32,256]{4,3,2,1,0:T(8,128)(2,1)S(1)} %slice_bitcast_fusion), channel_id=1, source_target_pairs={{0,4},{4,0},{8,12},{12,8},{16,20},{20,16},{24,28},{28,24},{1,5},{5... | collective-permute-start | bytes 3145736 | tf_op jit(solution)/shard_map/ppermute | solution.py:83
  205.3 40.7 %collective-permute-start.13 = (bf16[8,4,2,32,256]{4,3,2,1,0:T(8,128)(2,1)S(1)}, bf16[8,4,2,32,256]{4,3,2,1,0:T(8,128)(2,1)S(1)}, u32[]{:S(2)}, u32[]{:S(2)}) collective-permute-start(bf16[8,4,2,32,256]{4,3,2,1,0:T(8,128)(2,1)S(1)} %slice_bitcast_fusion.2), channel_id=1, source_target_pairs={{0,2},{1,3},{2,0},{3,1},{4,6},{5,7},{6,4},{7,5},{8,10},{9,11},{10,... | collective-permute-start | bytes 3145736 | tf_op jit(solution)/shard_map/ppermute | solution.py:83
  244.5 13.7 %collective-permute-start.15 = (bf16[8,4,32,256]{3,2,1,0:T(8,128)(2,1)S(1)}, bf16[8,4,32,256]{3,2,1,0:T(8,128)(2,1)S(1)}, u32[]{:S(2)}, u32[]{:S(2)}) collective-permute-start(bf16[8,4,32,256]{3,2,1,0:T(8,128)(2,1)S(1)} %slice_bitcast_fusion.4), channel_id=1, source_target_pairs={{0,2},{1,3},{2,0},{3,1},{4,6},{5,7},{6,4},{7,5},{8,10},{9,11},{10,... | collective-permute-start | bytes 1572872 | tf_op jit(solution)/shard_map/ppermute | solution.py:83
  259.7 41.1 %all-to-all-start.5 = ((bf16[8,4,3,32,256]{4,3,2,1,0:T(8,128)(2,1)}), bf16[8,4,3,32,256]{4,3,2,1,0:T(8,128)(2,1)}, u32[]{:S(2)}, u32[]{:S(2)}) async-start(bf16[8,4,3,32,256]{4,3,2,1,0:T(8,128)(2,1)} %pad_maximum_fusion.2), calls=%async_computation.5 | async-start | bytes 3145728 | tf_op jit(solution)/shard_map/all_to_all | solution.py:87
  (2 other events, 1.8 us)

commit v6 on v5

--- a/solution.py
+++ b/solution.py
@@ -1,3 +1,4 @@
+import functools
 import math
 
 import jax
@@ -139,131 +140,137 @@
     return pl.ds(r * (part // 2), part // 2)
 
 
-def weight_of(slot, w, v):
-    def get(m, which, r):
+def readers(slot, refs, y):
+    if slot == 0:
+        pairs = (refs[:4], refs[4:8])
+        half = refs[0].shape[0] // 2
+
+        def weight(m, which, r):
+            return square(pairs[which // 2][m][:, which % 2, r])
+
+        def wide(m, r):
+            return square(pairs[1][m][r * half : (r + 1) * half, 1])
+
+        return weight, wide, refs[8:]
+
+    halves, e_ref, half = (refs[:4], refs[4:8]), refs[-1], refs[0].shape[0] // 2
+    for m in range(4):
+        e_ref[m, :, y] = halves[0][m][:, 3]
+        e_ref[m, :, 1 - y] = halves[1][m][:, 3]
+
+    def shared(m, which, r):
+        return square(halves[r][m][:, which])
+
+    def wide_shared(m, r):
+        return square(e_ref[m, pl.ds((r ^ y) * half, half)])
+
+    return shared, wide_shared, refs[8:-1]
+
+
+def slot_rows(slot, x_ref):
+    own = 2 * x_ref.shape[2] // 3
+    return (0, own) if slot == 0 else (own, x_ref.shape[2])
+
+
+def forward_kernel(slot, seat_ref, x_ref, *refs):
+    ndp, nb = x_ref.shape[:2]
+    f, y = seat_ref[0], seat_ref[1]
+    weight, wide, refs = readers(slot, refs, y)
+    lo, hi = slot_rows(slot, x_ref)
+    if slot == 1:
+        refs[1][:, :, :lo, :] = refs[0][...]
+        refs = refs[1:]
+    out_ref, perm, active, slope, ret = refs
+    count = ndp * (hi - lo)
+    tiles = (nb, BLK // nb, count)
+    for m in range(nb):
+        d = f ^ m
+        x = x_ref[:, d, lo:hi, :].reshape(count, BLK)
+        for r in range(2):
+            spread = dot(weight(m, 0, r), x, 0, 1).astype(jnp.bfloat16)
+            perm[r, :, d] = spread.reshape(tiles)
+    for m in range(nb):
+        s = f ^ m
+        for r in range(2):
+            p = perm[r, s].reshape(BLK, count)
+            value, grade = gelu_pair(dot(weight(m, 1, r), p, 0, 0))
+            value = value.astype(jnp.bfloat16)
+            active[r, s] = value
+            slope[r, s] = grade.astype(jnp.bfloat16)
+            narrowed = dot(weight(m, 2, r), value, 0, 0).astype(jnp.bfloat16)
+            ret[r, :, s] = narrowed.reshape(tiles)
+    for m in range(nb):
+        d = f ^ m
+        total = 0.0
+        for r in range(2):
+            total = total + dot(ret[r, d].reshape(BLK, count), wide(m, r), 0, 0)
+        out_ref[:, d, lo:hi, :] = total.astype(jnp.bfloat16).reshape(ndp, hi - lo, BLK)
+
+
+def backward_kernel(slot, seat_ref, x_ref, g_ref, *refs):
+    ndp, nb = x_ref.shape[:2]
+    rows, half = BLK // ndp, ndp // 2
+    f, y = seat_ref[0], seat_ref[1]
+    weight, wide, refs = readers(slot, refs, y)
+    (perm, active, slope, ret), refs = refs[:4], refs[4:]
+    lo, hi = slot_rows(slot, x_ref)
+    if slot == 1:
+        refs[1][:, :, :lo, :] = refs[0][...]
+        refs = refs[1:]
+    gin_ref, keep_ref, send_ref, mid, spread = refs
+
+    def store(m, which, r, part):
+        ref = (keep_ref, send_ref)[m % 2]
+        part = part.astype(jnp.bfloat16).reshape(ndp, rows, BLK)
         if slot == 0:
-            return square(w[which // 2][m][:, which % 2, r])
-        return square(v[m][r, :, which])
-
-    return get
-
-
-def wide_weight(slot, w, e_ref, y):
-    def get(m, r):
+            ref[m // 2, :, which, r] = part
+        else:
+            ref[r, m // 2, :, which] = part
+
+    def store_wide(m, r, part):
+        ref = (keep_ref, send_ref)[m % 2]
+        part = part.astype(jnp.bfloat16).reshape(half, 2, rows, BLK)
         if slot == 0:
-            return square(w[1][m][half_src(e_ref.shape[1], r), 1])
-        return square(e_ref[m, half_src(e_ref.shape[1], r ^ y)])
-
-    return get
-
-
-def join_halves(v, e_ref, y):
-    for m in range(len(v)):
-        e_ref[m, :, y] = v[m][0, :, 3]
-        e_ref[m, :, 1 - y] = v[m][1, :, 3]
-
-
-def forward_kernel(seat_ref, x_ref, *refs):
-    w, v, out_ref, saved = (refs[:4], refs[4:8]), refs[8:12], refs[12], (refs[13:17], refs[17:21])
-    e_ref = refs[21]
-    ndp, nb, all_rows, _ = x_ref.shape
-    own_rows = 2 * all_rows // 3
-    f, y = seat_ref[0], seat_ref[1]
-    join_halves(v, e_ref, y)
-    for slot, (lo, hi) in enumerate(((0, own_rows), (own_rows, all_rows))):
-        perm, active, slope, ret = saved[slot]
-        weight, wide = weight_of(slot, w, v), wide_weight(slot, w, e_ref, y)
-        count = ndp * (hi - lo)
-        tiles = (nb, BLK // nb, count)
-        for m in range(nb):
-            d = f ^ m
-            x = x_ref[:, d, lo:hi, :].reshape(count, BLK)
-            for r in range(2):
-                spread = dot(weight(m, 0, r), x, 0, 1).astype(jnp.bfloat16)
-                perm[r, :, d] = spread.reshape(tiles)
-        for m in range(nb):
-            s = f ^ m
-            for r in range(2):
-                p = perm[r, s].reshape(BLK, count)
-                value, grade = gelu_pair(dot(weight(m, 1, r), p, 0, 0))
-                value = value.astype(jnp.bfloat16)
-                active[r, s] = value
-                slope[r, s] = grade.astype(jnp.bfloat16)
-                narrowed = dot(weight(m, 2, r), value, 0, 0).astype(jnp.bfloat16)
-                ret[r, :, s] = narrowed.reshape(tiles)
-        for m in range(nb):
-            d = f ^ m
-            total = 0.0
-            for r in range(2):
-                total = total + dot(ret[r, d].reshape(BLK, count), wide(m, r), 0, 0)
-            out_ref[:, d, lo:hi, :] = total.astype(jnp.bfloat16).reshape(ndp, hi - lo, BLK)
-
-
-def backward_kernel(seat_ref, x_ref, g_ref, *refs):
-    w, v, saved = (refs[:4], refs[4:8]), refs[8:12], (refs[12:16], refs[16:20])
-    gin_ref, own_keep, own_send, mid_keep, mid_send = refs[20:25]
-    scratch, e_ref = (refs[25:27], refs[27:29]), refs[29]
-    ndp, nb, all_rows, _ = x_ref.shape
-    own_rows = 2 * all_rows // 3
-    rows = BLK // ndp
-    f, y = seat_ref[0], seat_ref[1]
-    join_halves(v, e_ref, y)
-
-    def store(slot, m, which, r, part):
-        ref = ((own_keep, own_send), (mid_keep, mid_send))[slot][m % 2]
-        if slot == 0:
-            ref[m // 2, :, which, r] = part.astype(jnp.bfloat16).reshape(ndp, rows, BLK)
+            ref[m // 2, r * half : (r + 1) * half, 3] = part
         else:
-            ref[r, m // 2, :, which] = part.astype(jnp.bfloat16).reshape(ndp, rows, BLK)
-
-    def store_wide(slot, m, r, part):
-        ref = ((own_keep, own_send), (mid_keep, mid_send))[slot][m % 2]
-        part = part.astype(jnp.bfloat16).reshape(ndp // 2, 2, rows, BLK)
-        if slot == 0:
-            ref[m // 2, half_src(ndp, r), 3] = part
-        else:
-            ref[y, m // 2, half_src(ndp, r ^ y), 3] = part[:, 0]
-            ref[1 - y, m // 2, half_src(ndp, r ^ y), 3] = part[:, 1]
-
-    for slot, (lo, hi) in enumerate(((0, own_rows), (own_rows, all_rows))):
-        perm, active, slope, ret = saved[slot]
-        mid, spread = scratch[slot]
-        weight, wide = weight_of(slot, w, v), wide_weight(slot, w, e_ref, y)
-        count = ndp * (hi - lo)
-        tiles = (nb, BLK // nb, count)
-        for m in range(nb):
-            d = f ^ m
-            g = g_ref[:, d, lo:hi, :].reshape(count, BLK)
-            for r in range(2):
-                mid[r, :, d] = dot(wide(m, r), g, 1, 1).astype(jnp.bfloat16).reshape(tiles)
-                store_wide(slot, m, r, dot(ret[r, d].reshape(BLK, count), g, 1, 0))
-        for m in range(nb):
-            s = f ^ m
-            for r in range(2):
-                p = perm[r, s].reshape(BLK, count)
-                back_mid = mid[r, s].reshape(BLK, count)
-                back = dot(weight(m, 2, r), back_mid, 1, 0)
-                back = (back * slope[r, s].astype(jnp.float32)).astype(jnp.bfloat16)
-                store(slot, m, 2, r, dot(active[r, s], back_mid, 1, 1))
-                store(slot, m, 1, r, dot(p, back, 1, 1))
-                first = dot(weight(m, 1, r), back, 1, 0).astype(jnp.bfloat16)
-                spread[r, :, s] = first.reshape(tiles)
-        for m in range(nb):
-            d = f ^ m
-            x = x_ref[:, d, lo:hi, :].reshape(count, BLK)
-            total = 0.0
-            for r in range(2):
-                back = spread[r, d].reshape(BLK, count)
-                total = total + dot(back, weight(m, 0, r), 0, 1)
-                store(slot, m, 0, r, dot(x, back, 0, 1))
-            gin_ref[:, d, lo:hi, :] = total.astype(jnp.bfloat16).reshape(ndp, hi - lo, BLK)
-
-
-def on_chip(kernel, products, outs, scratch, inputs):
+            ref[y, m // 2, pl.ds((r ^ y) * half, half), 3] = part[:, 0]
+            ref[1 - y, m // 2, pl.ds((r ^ y) * half, half), 3] = part[:, 1]
+
+    count = ndp * (hi - lo)
+    tiles = (nb, BLK // nb, count)
+    for m in range(nb):
+        d = f ^ m
+        g = g_ref[:, d, lo:hi, :].reshape(count, BLK)
+        for r in range(2):
+            mid[r, :, d] = dot(wide(m, r), g, 1, 1).astype(jnp.bfloat16).reshape(tiles)
+            store_wide(m, r, dot(ret[r, d].reshape(BLK, count), g, 1, 0))
+    for m in range(nb):
+        s = f ^ m
+        for r in range(2):
+            p = perm[r, s].reshape(BLK, count)
+            back_mid = mid[r, s].reshape(BLK, count)
+            back = dot(weight(m, 2, r), back_mid, 1, 0)
+            back = (back * slope[r, s].astype(jnp.float32)).astype(jnp.bfloat16)
+            store(m, 2, r, dot(active[r, s], back_mid, 1, 1))
+            store(m, 1, r, dot(p, back, 1, 1))
+            first = dot(weight(m, 1, r), back, 1, 0).astype(jnp.bfloat16)
+            spread[r, :, s] = first.reshape(tiles)
+    for m in range(nb):
+        d = f ^ m
+        x = x_ref[:, d, lo:hi, :].reshape(count, BLK)
+        total = 0.0
+        for r in range(2):
+            back = spread[r, d].reshape(BLK, count)
+            total = total + dot(back, weight(m, 0, r), 0, 1)
+            store(m, 0, r, dot(x, back, 0, 1))
+        gin_ref[:, d, lo:hi, :] = total.astype(jnp.bfloat16).reshape(ndp, hi - lo, BLK)
+
+
+def on_chip(kernel, slot, products, outs, scratch, inputs):
     in_specs = [pl.BlockSpec(memory_space=pltpu.SMEM)]
     in_specs += [pl.BlockSpec(memory_space=pltpu.VMEM)] * (len(inputs) - 1)
     return pl.pallas_call(
-        kernel,
+        functools.partial(kernel, slot),
         out_shape=[jax.ShapeDtypeStruct(shape, jnp.bfloat16) for shape in outs],
         in_specs=in_specs,
         out_specs=[pl.BlockSpec(memory_space=pltpu.VMEM)] * len(outs),
@@ -296,32 +303,38 @@
     g = after(deal_tokens(grad_out), x, mid_across, ab_across, mid_swapped)
     g = exchange(g, everyone).reshape(shape)
     x = x.reshape(shape)
-    both = [
-        jnp.stack([parts_in[0], mid_swapped]),
-        jnp.stack([mid_across, xor_permute(mid_across, 1, "dp")]),
+    swapped_across = xor_permute(mid_across, 1, "dp")
+    weights = [
+        gather_bfly(parts_in[1], ab_across) + gather_bfly(parts_in[2], ce_across),
+        gather_bfly(parts_in[0], mid_across) + [mid_swapped, xor_permute(mid_swapped, 1)],
     ]
-    weights = gather_bfly(parts_in[1], ab_across) + gather_bfly(parts_in[2], ce_across)
-    weights += gather_bfly(*both)
-
-    own, mid = count * ndp // nb, count * ndp // nb // 2
-    saved = []
-    for t in (own, mid):
-        tiled, whole = (2, nb, nb, BLK // nb, t), (2, nb, BLK, t)
-        saved += [tiled, whole, whole, tiled]
-    halves = (nb, ndp, 2, rows, BLK)
-    products = 2 * nb * (own + mid)
-    out, *kept = on_chip(
-        forward_kernel, 4 * products, [x.shape] + saved, [halves], [seat, x] + weights
-    )
-    out = exchange(out.reshape(ndp * nb, -1, BLK), everyone)
-    own_shape, mid_shape = (2, ndp, 4, 2, rows, BLK), (2, 2, ndp, 4, rows, BLK)
-    gin, own_keep, own_send, mid_keep, mid_send = on_chip(
-        backward_kernel,
-        8 * products,
-        [x.shape, own_shape, own_shape, mid_shape, mid_shape],
-        [saved[0], saved[0], saved[4], saved[4], halves],
-        [seat, x, g] + weights + kept,
-    )
+
+    counts = (count * ndp // nb, count * ndp // nb // 2)
+    rows_shape = ((ndp, nb, count // nb, BLK), x.shape)
+    grad_shapes = ((2, ndp, 4, 2, rows, BLK), (2, 2, ndp, 4, rows, BLK))
+    joined = ([], [(nb, ndp, 2, rows, BLK)])
+    tiled = [(2, nb, nb, BLK // nb, t) for t in counts]
+    whole = [(2, nb, BLK, t) for t in counts]
+    out, gin, kept, grads = [], [], [], []
+    for slot, t in enumerate(counts):
+        shapes = [rows_shape[slot], tiled[slot], whole[slot], whole[slot], tiled[slot]]
+        inputs = [seat, x] + weights[slot] + out
+        first, *rest = on_chip(forward_kernel, slot, 8 * nb * t, shapes, joined[slot], inputs)
+        out = [first]
+        kept.append(rest)
+        if slot == 0:
+            last = after(swapped_across, first)
+            weights[1] += [last, xor_permute(last, 1)]
+    out = exchange(out[0].reshape(ndp * nb, -1, BLK), everyone)
+    for slot, t in enumerate(counts):
+        shapes = [rows_shape[slot], grad_shapes[slot], grad_shapes[slot]]
+        scratch = [tiled[slot], tiled[slot]] + joined[slot]
+        inputs = [seat, x, g] + weights[slot] + kept[slot] + gin
+        first, *rest = on_chip(backward_kernel, slot, 16 * nb * t, shapes, scratch, inputs)
+        gin = [first]
+        grads.append(rest)
+    gin = gin[0]
+    (own_keep, own_send), (mid_keep, mid_send) = grads
     half_mid = mid = add(mid_keep, xor_permute(mid_send, 1))
     half_own = own = add(own_keep, xor_permute(own_send, 1))
     mid = add(mid[0], xor_permute(mid[1], 1, "dp"))

time: 308 us -> 309 us (level)
  Pallas kernels: 37.8 us -> 42.5 us
  other arithmetic: 20.1 us -> 16.5 us
    pallas_call x2 -> x4, Pallas kernels: 37.8 us -> 42.5 us  [on_chip(): pl.pallas_call(functools.partial(kernel, slot), out_shape=[jax.ShapeDtype...]
    another operation x2 -> x0, other arithmetic: 3.48 us -> none  [the longest x1 2.18 us: token_plan(): jnp.stack([mid_across, xor_permute(mid_across, 1, 'dp')])]
    unnamed x30 -> x40, local copies, waits for them, and re-layouts: 12.6 us -> 14.2 us
    ppermute x16 -> x18, waiting for transfers between devices: 106 us -> 107 us  [xor_permute(): lax.ppermute(x, axis, [(i, i ^ mask) for i in range(lax.axis_size(axis))])]
    ppermute x16 -> x18, starting transfers between devices: 13 us -> 12.7 us  [xor_permute(): lax.ppermute(x, axis, [(i, i ^ mask) for i in range(lax.axis_size(axis))])]
  transfers between devices with their start and end apart: 22 -> 24, of which waited for: 12 -> 10; matrix products, arithmetic and copies ran while one was open for 14% -> 13% of each run, Pallas kernels for 12% -> 14%
where the time goes in v6:
time: 309 us; the launch traced here: 308 us
  waiting for transfers between devices  168 us (54%)
  Pallas kernels  42.5 us (14%)
  starting transfers between devices  41.6 us (13%)
  local copies, waits for them, and re-layouts  37.9 us (12%)
  other arithmetic  16.5 us (5%)
    ppermute x18, waiting for transfers between devices, xor_permute(): lax.ppermute(x, axis, [(i, i ^ mask) for i in range(lax.axis_size(axis))])  107 us
    all_to_all x6, waiting for transfers between devices, exchange(): return lax.all_to_all(x, axes, split_axis=0, concat_axis=0, tiled=True)  61.5 us
    pallas_call x4, Pallas kernels, on_chip(): pl.pallas_call(functools.partial(kernel, slot), out_shape=[jax.ShapeDtype...  42.5 us
    all_to_all x6, starting transfers between devices, exchange(): return lax.all_to_all(x, axes, split_axis=0, concat_axis=0, tiled=True)  28.9 us
    unnamed x40, local copies, waits for them, and re-layouts  14.2 us
    ppermute x18, starting transfers between devices, xor_permute(): lax.ppermute(x, axis, [(i, i ^ mask) for i in range(lax.axis_size(axis))])  12.7 us
  transfers between devices with their start and end apart: 24, of which 10 were waited for; matrix products, arithmetic and copies ran while one was open for 13% of the time, Pallas kernels for 14%

profile of v6, /device:TPU:0, one launch (start us, length us, event | category | flops | bytes accessed | tf_op | source)
XLA Modules:
  0.0 308.0 jit_solution(7387941789451143010)
XLA Ops:
  4.3 7.3 %all-to-all-start = ((bf16[8,4,3,32,256]{4,3,1,2,0:T(8,128)(2,1)}), bf16[8,4,3,32,256]{4,3,1,2,0:T(8,128)(2,1)S(1)}, u32[]{:S(2)}, u32[]{:S(2)}) async-start(bf16[8,4,3,32,256]{4,3,1,2,0:T(8,128)(2,1)} %maximum_maximum_fusion), calls=%async_computation | async-start | bytes 3145728 | tf_op jit(solution)/shard_map/all_to_all | solution.py:88
  11.5 1.7 copy.172
  17.7 2.3 pad_maximum_fusion
  20.0 28.6 %all-to-all-done = bf16[8,4,3,32,256]{4,3,1,2,0:T(8,128)(2,1)S(1)} async-done(((bf16[8,4,3,32,256]{4,3,1,2,0:T(8,128)(2,1)}), bf16[8,4,3,32,256]{4,3,1,2,0:T(8,128)(2,1)S(1)}, u32[]{:S(2)}, u32[]{:S(2)}) %all-to-all-start) | async-done | bytes 1572896 | tf_op jit(solution)/shard_map/all_to_all | solution.py:88
  48.5 3.7 %all-to-all-start.1 = ((bf16[32,96,256]{2,1,0:T(8,128)(2,1)}), bf16[32,96,256]{2,1,0:T(8,128)(2,1)S(1)}, u32[]{:S(2)}, u32[]{:S(2)}) async-start(bf16[32,96,256]{2,1,0:T(8,128)(2,1)} %pad_maximum_fusion), calls=%async_computation.1 | async-start | bytes 3145728 | tf_op jit(solution)/shard_map/all_to_all | solution.py:88
  53.9 1.8 collective-permute-start.7
  56.8 1.8 collective-permute-start.3
  58.6 1.7 copy.186
  64.7 2.3 pad_maximum_fusion.1
  67.1 14.6 %collective-permute-done.7.refs_2_ = bf16[8,2,2,32,256]{4,3,2,1,0:T(8,128)(2,1)} collective-permute-done((bf16[8,2,2,32,256]{4,3,2,1,0:T(8,128)(2,1)}, bf16[8,2,2,32,256]{4,3,2,1,0:T(8,128)(2,1)}, u32[]{:S(2)}, u32[]{:S(2)}) %collective-permute-start.7) | collective-permute-done | bytes 524320 | tf_op jit(solution)/shard_map/ppermute | solution.py:84
  81.6 12.9 %collective-permute-done.1.refs_2_ = bf16[8,4,32,256]{3,2,1,0:T(8,128)(2,1)} collective-permute-done((bf16[8,4,32,256]{3,2,1,0:T(8,128)(2,1)}, bf16[8,4,32,256]{3,2,1,0:T(8,128)(2,1)}, u32[]{:S(2)}, u32[]{:S(2)}) %collective-permute-start.1) | collective-permute-done | bytes 524320 | tf_op jit(solution)/shard_map/ppermute | solution.py:84
  95.6 4.7 %all-to-all-start.3 = ((bf16[32,96,256]{2,1,0:T(8,128)(2,1)}), bf16[32,96,256]{2,1,0:T(8,128)(2,1)S(1)}, u32[]{:S(2)}, u32[]{:S(2)}) async-start(bf16[32,96,256]{2,1,0:T(8,128)(2,1)} %pad_maximum_fusion.1), calls=%async_computation.3 | async-start | bytes 3145728 | tf_op jit(solution)/shard_map/all_to_all | solution.py:88
  101.5 1.7 collective-permute-start.10
  103.7 25.5 %collective-permute-done.10.refs_6_ = bf16[8,2,2,32,256]{4,3,2,1,0:T(8,128)(2,1)} collective-permute-done((bf16[8,2,2,32,256]{4,3,2,1,0:T(8,128)(2,1)S(1)}, bf16[8,2,2,32,256]{4,3,2,1,0:T(8,128)(2,1)}, u32[]{:S(2)}, u32[]{:S(2)}) %collective-permute-start.10) | collective-permute-done | bytes 524320 | tf_op jit(solution)/shard_map/ppermute | solution.py:84
  131.5 10.9 %shard_map.109 = (bf16[8,4,64,256]{3,2,1,0:T(8,128)(2,1)}, bf16[2,4,4,64,512]{4,3,2,1,0:T(8,128)(2,1)}, bf16[2,4,256,512]{3,2,1,0:T(8,128)(2,1)}, bf16[2,4,256,5...) custom-call(s32[2]{0:T(128)} %pad_add_fusion.seat_ref, bf16[8,4,96,256]{3,2,1,0:T(8,128)(2,1)} %bitcast.170, ...), custom_call_target="tpu_custom_call" | custom-call | flops 2147483648 | bytes 15204356 | tf_op jit(solution)/shard_map/pallas_call | solution.py:272
  142.4 2.9 collective-permute-done.5.refs_6_
  145.4 1.8 collective-permute-done.12.refs_7_
  148.1 7.6 %shard_map.110 = (bf16[8,4,96,256]{3,2,1,0:T(8,128)(2,1)}, bf16[2,4,4,64,256]{4,3,2,1,0:T(8,128)(2,1)}, bf16[2,4,256,256]{3,2,1,0:T(8,128)(2,1)}, bf16[2,4,256,2...) custom-call(s32[2]{0:T(128)} %pad_add_fusion.seat_ref, bf16[8,4,96,256]{3,2,1,0:T(8,128)(2,1)} %bitcast.171, ...), custom_call_target="tpu_custom_call" | custom-call | flops 1073741824 | bytes 12582916 | tf_op jit(solution)/shard_map/pallas_call | solution.py:272
  156.8 4.4 %all-to-all-start.2 = ((bf16[32,96,256]{2,1,0:T(8,128)(2,1)}), bf16[32,96,256]{2,1,0:T(8,128)(2,1)}, u32[]{:S(2)}, u32[]{:S(2)}) async-start(bf16[32,96,256]{2,1,0:T(8,128)(2,1)} %bitcast.192), calls=%async_computation.2 | async-start | bytes 3145728 | tf_op jit(solution)/shard_map/all_to_all | solution.py:88
  161.3 13.1 %shard_map.111 = (bf16[8,4,64,256]{3,2,1,0:T(8,128)(2,1)}, bf16[2,8,4,2,32,256]{5,4,3,2,1,0:T(8,128)(2,1)}, bf16[2,8,4,2,32,256]{5,4,3,2,1,0:T(8,128)(2,1)}) custom-call(s32[2]{0:T(128)} %pad_add_fusion.seat_ref, bf16[8,4,96,256]{3,2,1,0:T(8,128)(2,1)} %bitcast.172, bf16[8,4,96,256]{3,2,1,0:T(8,128)(2,1)} %bitcast.174, ...), custom_call_target="tpu_custom_call" | custom-call | flops 4294967296 | bytes 20971524 | tf_op jit(solution)/shard_map/pallas_call | solution.py:272
  174.4 10.9 %shard_map.112 = (bf16[8,4,96,256]{3,2,1,0:T(8,128)(2,1)}, bf16[2,2,8,4,32,256]{5,4,3,2,1,0:T(8,128)(2,1)}, bf16[2,2,8,4,32,256]{5,4,3,2,1,0:T(8,128)(2,1)}) custom-call(s32[2]{0:T(128)} %pad_add_fusion.seat_ref, bf16[8,4,96,256]{3,2,1,0:T(8,128)(2,1)} %bitcast.173, bf16[8,4,96,256]{3,2,1,0:T(8,128)(2,1)} %bitcast.175, ...), custom_call_target="tpu_custom_call" | custom-call | flops 2147483648 | bytes 18350084 | tf_op jit(solution)/shard_map/pallas_call | solution.py:272
  187.2 2.7 add_convert_fusion
  189.9 2.3 add_convert_fusion.1
  192.2 6.6 %all-to-all-done.2 = bf16[32,96,256]{2,1,0:T(8,128)(2,1)} async-done(((bf16[32,96,256]{2,1,0:T(8,128)(2,1)}), bf16[32,96,256]{2,1,0:T(8,128)(2,1)}, u32[]{:S(2)}, u32[]{:S(2)}) %all-to-all-start.2) | async-done | bytes 1572896 | tf_op jit(solution)/shard_map/all_to_all | solution.py:88
  198.8 4.1 %all-to-all-start.4 = ((bf16[32,96,256]{2,1,0:T(8,128)(2,1)}), bf16[32,96,256]{2,1,0:T(8,128)(2,1)}, u32[]{:S(2)}, u32[]{:S(2)}) async-start(bf16[32,96,256]{2,1,0:T(8,128)(2,1)} %bitcast.191), calls=%async_computation.4 | async-start | bytes 3145728 | tf_op jit(solution)/shard_map/all_to_all | solution.py:88
  207.4 37.3 %collective-permute-done.16 = bf16[2,8,4,32,256]{4,3,2,1,0:T(8,128)(2,1)S(1)} collective-permute-done((bf16[2,8,4,32,256]{4,3,2,1,0:T(8,128)(2,1)S(1)}, bf16[2,8,4,32,256]{4,3,2,1,0:T(8,128)(2,1)S(1)}, u32[]{:S(2)}, u32[]{:S(2)}) %collective-permute-start.16) | collective-permute-done | bytes 1048608 | tf_op jit(solution)/shard_map/ppermute | solution.py:84
  247.2 11.7 %collective-permute-done.17 = bf16[8,4,32,256]{3,2,1,0:T(8,128)(2,1)S(1)} collective-permute-done((bf16[8,4,32,256]{3,2,1,0:T(8,128)(2,1)S(1)}, bf16[8,4,32,256]{3,2,1,0:T(8,128)(2,1)S(1)}, u32[]{:S(2)}, u32[]{:S(2)}) %collective-permute-start.17) | collective-permute-done | bytes 524320 | tf_op jit(solution)/shard_map/ppermute | solution.py:84
  260.5 4.6 %all-to-all-start.5 = ((bf16[8,4,3,32,256]{4,3,2,1,0:T(8,128)(2,1)}), bf16[8,4,3,32,256]{4,3,2,1,0:T(8,128)(2,1)}, u32[]{:S(2)}, u32[]{:S(2)}) async-start(bf16[8,4,3,32,256]{4,3,2,1,0:T(8,128)(2,1)} %pad_maximum_fusion.2), calls=%async_computation.5 | async-start | bytes 3145728 | tf_op jit(solution)/shard_map/all_to_all | solution.py:88
  268.4 1.7 copy.209
  273.5 1.7 copy.210
  275.3 26.3 %all-to-all-done.5 = bf16[8,4,3,32,256]{4,3,2,1,0:T(8,128)(2,1)} async-done(((bf16[8,4,3,32,256]{4,3,2,1,0:T(8,128)(2,1)}), bf16[8,4,3,32,256]{4,3,2,1,0:T(8,128)(2,1)}, u32[]{:S(2)}, u32[]{:S(2)}) %all-to-all-start.5) | async-done | bytes 1572896 | tf_op jit(solution)/shard_map/all_to_all | solution.py:88
  301.6 1.8 convert.4
  (117 shorter events, 43.7 us)
Async XLA Ops:
  4.3 44.3 %all-to-all-start = ((bf16[8,4,3,32,256]{4,3,1,2,0:T(8,128)(2,1)}), bf16[8,4,3,32,256]{4,3,1,2,0:T(8,128)(2,1)S(1)}, u32[]{:S(2)}, u32[]{:S(2)}) async-start(bf16[8,4,3,32,256]{4,3,1,2,0:T(8,128)(2,1)} %maximum_maximum_fusion), calls=%async_computation | async-start | bytes 3145728 | tf_op jit(solution)/shard_map/all_to_all | solution.py:88
  48.5 46.0 %all-to-all-start.1 = ((bf16[32,96,256]{2,1,0:T(8,128)(2,1)}), bf16[32,96,256]{2,1,0:T(8,128)(2,1)S(1)}, u32[]{:S(2)}, u32[]{:S(2)}) async-start(bf16[32,96,256]{2,1,0:T(8,128)(2,1)} %pad_maximum_fusion), calls=%async_computation.1 | async-start | bytes 3145728 | tf_op jit(solution)/shard_map/all_to_all | solution.py:88
  53.9 27.7 %collective-permute-start.7 = (bf16[8,2,2,32,256]{4,3,2,1,0:T(8,128)(2,1)}, bf16[8,2,2,32,256]{4,3,2,1,0:T(8,128)(2,1)}, u32[]{:S(2)}, u32[]{:S(2)}) collective-permute-start(bf16[8,2,2,32,256]{4,3,2,1,0:T(8,128)(2,1)} %copy.215.refs_0_), channel_id=1, source_target_pairs={{0,2},{1,3},{2,0},{3,1},{4,6},{5,7},{6,4},{7,5},{8,10},{9,11},{10,... | collective-permute-start | bytes 1572872 | tf_op jit(solution)/shard_map/ppermute | solution.py:84
  56.6 37.9 %collective-permute-start.1 = (bf16[8,4,32,256]{3,2,1,0:T(8,128)(2,1)}, bf16[8,4,32,256]{3,2,1,0:T(8,128)(2,1)}, u32[]{:S(2)}, u32[]{:S(2)}) collective-permute-start(bf16[8,4,32,256]{3,2,1,0:T(8,128)(2,1)} %slice_bitcast_fusion.6.refs_0_), channel_id=1, source_target_pairs={{0,2},{1,3},{2,0},{3,1},{4,6},{5,7},{6,4},{7,5},{8,10},{9,11},{10,... | collective-permute-start | bytes 1572872 | tf_op jit(solution)/shard_map/ppermute | solution.py:84
  56.8 37.7 %collective-permute-start.3 = (bf16[8,4,32,256]{3,2,1,0:T(8,128)(2,1)}, bf16[8,4,32,256]{3,2,1,0:T(8,128)(2,1)}, u32[]{:S(2)}, u32[]{:S(2)}) collective-permute-start(bf16[8,4,32,256]{3,2,1,0:T(8,128)(2,1)} %slice_bitcast_fusion.6.refs_0_), channel_id=1, source_target_pairs={{0,4},{4,0},{8,12},{12,8},{16,20},{20,16},{24,28},{28,24},{1,5},{5... | collective-permute-start | bytes 1572872 | tf_op jit(solution)/shard_map/ppermute | solution.py:84
  95.6 60.0 %all-to-all-start.3 = ((bf16[32,96,256]{2,1,0:T(8,128)(2,1)}), bf16[32,96,256]{2,1,0:T(8,128)(2,1)S(1)}, u32[]{:S(2)}, u32[]{:S(2)}) async-start(bf16[32,96,256]{2,1,0:T(8,128)(2,1)} %pad_maximum_fusion.1), calls=%async_computation.3 | async-start | bytes 3145728 | tf_op jit(solution)/shard_map/all_to_all | solution.py:88
  101.5 29.5 %copy-start.13 = (bf16[8,2,2,32,256]{4,3,2,1,0:T(8,128)(2,1)}, bf16[8,2,2,32,256]{4,3,2,1,0:T(8,128)(2,1)S(1)}, u32[]{:S(2)}) copy-start(bf16[8,2,2,32,256]{4,3,2,1,0:T(8,128)(2,1)S(1)} %copy.216.refs_4_) | copy-start | bytes 1572868
  101.5 27.7 %collective-permute-start.10 = (bf16[8,2,2,32,256]{4,3,2,1,0:T(8,128)(2,1)S(1)}, bf16[8,2,2,32,256]{4,3,2,1,0:T(8,128)(2,1)}, u32[]{:S(2)}, u32[]{:S(2)}) collective-permute-start(bf16[8,2,2,32,256]{4,3,2,1,0:T(8,128)(2,1)S(1)} %copy.216.refs_4_), channel_id=1, source_target_pairs={{0,2},{1,3},{2,0},{3,1},{4,6},{5,7},{6,4},{7,5},{8,10},{9,11},{10,... | collective-permute-start | bytes 1572872 | tf_op jit(solution)/shard_map/ppermute | solution.py:84
  103.2 27.6 %collective-permute-start.6 = (bf16[8,2,2,32,256]{4,3,2,1,0:T(8,128)(2,1)}, bf16[8,2,2,32,256]{4,3,2,1,0:T(8,128)(2,1)}, u32[]{:S(2)}, u32[]{:S(2)}) collective-permute-start(bf16[8,2,2,32,256]{4,3,2,1,0:T(8,128)(2,1)} %copy.215.refs_0_), channel_id=1, source_target_pairs={{0,1},{1,0},{2,3},{3,2},{4,5},{5,4},{6,7},{7,6},{8,9},{9,8},{10,11... | collective-permute-start | bytes 1572872 | tf_op jit(solution)/shard_map/ppermute | solution.py:84
  103.2 27.8 %collective-permute-start.9 = (bf16[8,2,2,32,256]{4,3,2,1,0:T(8,128)(2,1)S(1)}, bf16[8,2,2,32,256]{4,3,2,1,0:T(8,128)(2,1)}, u32[]{:S(2)}, u32[]{:S(2)}) collective-permute-start(bf16[8,2,2,32,256]{4,3,2,1,0:T(8,128)(2,1)S(1)} %copy.216.refs_4_), channel_id=1, source_target_pairs={{0,1},{1,0},{2,3},{3,2},{4,5},{5,4},{6,7},{7,6},{8,9},{9,8},{10,11... | collective-permute-start | bytes 1572872 | tf_op jit(solution)/shard_map/ppermute | solution.py:84
  103.7 27.6 %collective-permute-start.8 = (bf16[8,2,2,32,256]{4,3,2,1,0:T(8,128)(2,1)}, bf16[8,2,2,32,256]{4,3,2,1,0:T(8,128)(2,1)}, u32[]{:S(2)}, u32[]{:S(2)}) collective-permute-start(bf16[8,2,2,32,256]{4,3,2,1,0:T(8,128)(2,1)} %collective-permute-done.7.refs_2_), channel_id=1, source_target_pairs={{0,1},{1,0},{2,3},{3,2},{4,5},{5,4},{6,7},{7,6},{8,9},{9,8},{10,11... | collective-permute-start | bytes 1572872 | tf_op jit(solution)/shard_map/ppermute | solution.py:84
  129.2 2.3 collective-permute-start.11
  129.2 16.1 %collective-permute-start.5 = (bf16[8,4,32,256]{3,2,1,0:T(8,128)(2,1)}, bf16[8,4,32,256]{3,2,1,0:T(8,128)(2,1)S(1)}, u32[]{:S(2)}, u32[]{:S(2)}) collective-permute-start(bf16[8,4,32,256]{3,2,1,0:T(8,128)(2,1)} %collective-permute-done.1.refs_2_), channel_id=1, source_target_pairs={{0,4},{4,0},{8,12},{12,8},{16,20},{20,16},{24,28},{28,24},{1,5},{5... | collective-permute-start | bytes 1572872 | tf_op jit(solution)/shard_map/ppermute | solution.py:84
  130.8 14.5 %collective-permute-start = (bf16[8,4,32,256]{3,2,1,0:T(8,128)(2,1)}, bf16[8,4,32,256]{3,2,1,0:T(8,128)(2,1)S(1)}, u32[]{:S(2)}, u32[]{:S(2)}) collective-permute-start(bf16[8,4,32,256]{3,2,1,0:T(8,128)(2,1)} %slice_bitcast_fusion.6.refs_0_), channel_id=1, source_target_pairs={{0,1},{1,0},{2,3},{3,2},{4,5},{5,4},{6,7},{7,6},{8,9},{9,8},{10,11... | collective-permute-start | bytes 1572872 | tf_op jit(solution)/shard_map/ppermute | solution.py:84
  131.0 14.3 %collective-permute-start.2 = (bf16[8,4,32,256]{3,2,1,0:T(8,128)(2,1)}, bf16[8,4,32,256]{3,2,1,0:T(8,128)(2,1)S(1)}, u32[]{:S(2)}, u32[]{:S(2)}) collective-permute-start(bf16[8,4,32,256]{3,2,1,0:T(8,128)(2,1)} %collective-permute-done.1.refs_2_), channel_id=1, source_target_pairs={{0,1},{1,0},{2,3},{3,2},{4,5},{5,4},{6,7},{7,6},{8,9},{9,8},{10,11... | collective-permute-start | bytes 1572872 | tf_op jit(solution)/shard_map/ppermute | solution.py:84
  131.3 14.1 %collective-permute-start.4 = (bf16[8,4,32,256]{3,2,1,0:T(8,128)(2,1)}, bf16[8,4,32,256]{3,2,1,0:T(8,128)(2,1)S(1)}, u32[]{:S(2)}, u32[]{:S(2)}) collective-permute-start(bf16[8,4,32,256]{3,2,1,0:T(8,128)(2,1)} %collective-permute-done.3.refs_4_), channel_id=1, source_target_pairs={{0,1},{1,0},{2,3},{3,2},{4,5},{5,4},{6,7},{7,6},{8,9},{9,8},{10,11... | collective-permute-start | bytes 1572872 | tf_op jit(solution)/shard_map/ppermute | solution.py:84
  145.3 1.9 copy-start.8
  145.3 1.9 collective-permute-start.12
  145.3 1.9 copy-start.9
  145.3 1.9 copy-start.10
  145.4 1.9 copy-start.11
  156.8 42.0 %all-to-all-start.2 = ((bf16[32,96,256]{2,1,0:T(8,128)(2,1)}), bf16[32,96,256]{2,1,0:T(8,128)(2,1)}, u32[]{:S(2)}, u32[]{:S(2)}) async-start(bf16[32,96,256]{2,1,0:T(8,128)(2,1)} %bitcast.192), calls=%async_computation.2 | async-start | bytes 3145728 | tf_op jit(solution)/shard_map/all_to_all | solution.py:88
  174.4 11.4 %collective-permute-start.14 = (bf16[2,8,4,2,32,256]{5,4,3,2,1,0:T(8,128)(2,1)}, bf16[2,8,4,2,32,256]{5,4,3,2,1,0:T(8,128)(2,1)S(1)}, u32[]{:S(2)}, u32[]{:S(2)}) collective-permute-start(bf16[2,8,4,2,32,256]{5,4,3,2,1,0:T(8,128)(2,1)} %get-tuple-element.45), channel_id=1, source_target_pairs={{0,1},{1,0},{2,3},{3,2},{4,5},{5,4},{6,7},{7,6},{8,9},{9,8},{10,11... | collective-permute-start | bytes 6291464 | tf_op jit(solution)/shard_map/ppermute | solution.py:84
  174.4 12.8 %copy-start.3 = (bf16[2,8,4,2,32,256]{5,4,3,2,1,0:T(8,128)(2,1)S(1)}, bf16[2,8,4,2,32,256]{5,4,3,2,1,0:T(8,128)(2,1)}, u32[]{:S(2)}) copy-start(bf16[2,8,4,2,32,256]{5,4,3,2,1,0:T(8,128)(2,1)} %get-tuple-element.44) | copy-start | bytes 6291460
  185.3 4.6 %collective-permute-start.13 = (bf16[2,2,8,4,32,256]{5,4,3,2,1,0:T(8,128)(2,1)}, bf16[2,2,8,4,32,256]{5,4,3,2,1,0:T(8,128)(2,1)S(1)}, u32[]{:S(2)}, u32[]{:S(2)}) collective-permute-start(bf16[2,2,8,4,32,256]{5,4,3,2,1,0:T(8,128)(2,1)} %get-tuple-element.43), channel_id=1, source_target_pairs={{0,1},{1,0},{2,3},{3,2},{4,5},{5,4},{6,7},{7,6},{8,9},{9,8},{10,11... | collective-permute-start | bytes 6291464 | tf_op jit(solution)/shard_map/ppermute | solution.py:84
  187.2 2.7 copy-start.4
  198.8 61.6 %all-to-all-start.4 = ((bf16[32,96,256]{2,1,0:T(8,128)(2,1)}), bf16[32,96,256]{2,1,0:T(8,128)(2,1)}, u32[]{:S(2)}, u32[]{:S(2)}) async-start(bf16[32,96,256]{2,1,0:T(8,128)(2,1)} %bitcast.191), calls=%async_computation.4 | async-start | bytes 3145728 | tf_op jit(solution)/shard_map/all_to_all | solution.py:88
  204.3 40.5 %copy-start.1 = (bf16[2,2,8,4,32,256]{5,4,3,2,1,0:T(8,128)(2,1)S(1)}, bf16[2,2,8,4,32,256]{5,4,3,2,1,0:T(8,128)(2,1)}, u32[]{:S(2)}) copy-start(bf16[2,2,8,4,32,256]{5,4,3,2,1,0:T(8,128)(2,1)} %add_convert_fusion.1) | copy-start | bytes 6291460
  204.3 40.5 %collective-permute-start.16 = (bf16[2,8,4,32,256]{4,3,2,1,0:T(8,128)(2,1)S(1)}, bf16[2,8,4,32,256]{4,3,2,1,0:T(8,128)(2,1)S(1)}, u32[]{:S(2)}, u32[]{:S(2)}) collective-permute-start(bf16[2,8,4,32,256]{4,3,2,1,0:T(8,128)(2,1)S(1)} %slice_bitcast_fusion), channel_id=1, source_target_pairs={{0,4},{4,0},{8,12},{12,8},{16,20},{20,16},{24,28},{28,24},{1,5},{5... | collective-permute-start | bytes 3145736 | tf_op jit(solution)/shard_map/ppermute | solution.py:84
  205.9 40.9 %collective-permute-start.15 = (bf16[8,4,2,32,256]{4,3,2,1,0:T(8,128)(2,1)S(1)}, bf16[8,4,2,32,256]{4,3,2,1,0:T(8,128)(2,1)S(1)}, u32[]{:S(2)}, u32[]{:S(2)}) collective-permute-start(bf16[8,4,2,32,256]{4,3,2,1,0:T(8,128)(2,1)S(1)} %slice_bitcast_fusion.2), channel_id=1, source_target_pairs={{0,2},{1,3},{2,0},{3,1},{4,6},{5,7},{6,4},{7,5},{8,10},{9,11},{10,... | collective-permute-start | bytes 3145736 | tf_op jit(solution)/shard_map/ppermute | solution.py:84
  245.3 13.7 %collective-permute-start.17 = (bf16[8,4,32,256]{3,2,1,0:T(8,128)(2,1)S(1)}, bf16[8,4,32,256]{3,2,1,0:T(8,128)(2,1)S(1)}, u32[]{:S(2)}, u32[]{:S(2)}) collective-permute-start(bf16[8,4,32,256]{3,2,1,0:T(8,128)(2,1)S(1)} %slice_bitcast_fusion.4), channel_id=1, source_target_pairs={{0,2},{1,3},{2,0},{3,1},{4,6},{5,7},{6,4},{7,5},{8,10},{9,11},{10,... | collective-permute-start | bytes 1572872 | tf_op jit(solution)/shard_map/ppermute | solution.py:84
  260.5 41.1 %all-to-all-start.5 = ((bf16[8,4,3,32,256]{4,3,2,1,0:T(8,128)(2,1)}), bf16[8,4,3,32,256]{4,3,2,1,0:T(8,128)(2,1)}, u32[]{:S(2)}, u32[]{:S(2)}) async-start(bf16[8,4,3,32,256]{4,3,2,1,0:T(8,128)(2,1)} %pad_maximum_fusion.2), calls=%async_computation.5 | async-start | bytes 3145728 | tf_op jit(solution)/shard_map/all_to_all | solution.py:88
  (9 other events, 11.3 us)

commit v7 on v4

--- a/solution.py
+++ b/solution.py
@@ -142,8 +142,9 @@
 def weight_of(slot, w, v):
     def get(m, which, r):
         if slot == 0:
-            return square(w[m][:, which, r])
-        return square(v[m][:, which] if r else w[m][:, which, 2])
+            return square(w[which // 2][m][:, r, which % 2])
+        ref = w[which // 2][m] if r == 0 else v[which // 2][m]
+        return square(ref[:, 2 if r == 0 else 0, which % 2])
 
     return get
 
@@ -151,20 +152,25 @@
 def wide_weight(slot, w, e_ref, y):
     def get(m, r):
         if slot == 0:
-            return square(w[m][half_src(e_ref.shape[1], r), 3, :2])
+            return square(w[1][m][half_src(e_ref.shape[1], r), :2, 1])
         return square(e_ref[m, half_src(e_ref.shape[1], r ^ y)])
 
     return get
 
 
 def join_halves(w, v, e_ref, y):
-    for m in range(len(w)):
-        e_ref[m, :, y] = w[m][:, 3, 2]
-        e_ref[m, :, 1 - y] = v[m][:, 3]
+    for m in range(4):
+        e_ref[m, :, y] = w[1][m][:, 2, 1]
+        e_ref[m, :, 1 - y] = v[1][m][:, 0, 1]
+
+
+def weight_refs(refs):
+    return (refs[:4], refs[4:8]), (refs[8:12], refs[12:16]), refs[16:]
 
 
 def forward_kernel(seat_ref, x_ref, *refs):
-    w, v, (out_ref,), saved, e_ref = refs[:4], refs[4:8], refs[8:9], (refs[9:13], refs[13:17]), refs[17]
+    w, v, (out_ref, *refs) = weight_refs(refs)
+    saved, e_ref = (refs[:4], refs[4:8]), refs[8]
     ndp, nb, all_rows, _ = x_ref.shape
     own_rows = 2 * all_rows // 3
     f, y = seat_ref[0], seat_ref[1]
@@ -199,9 +205,10 @@
 
 
 def backward_kernel(seat_ref, x_ref, g_ref, *refs):
-    w, v, saved = refs[:4], refs[4:8], (refs[8:12], refs[12:16])
-    gin_ref, own_keep, own_send, mid_keep, mid_send = refs[16:21]
-    scratch, e_ref = (refs[21:23], refs[23:25]), refs[25]
+    w, v, refs = weight_refs(refs)
+    saved = refs[:4], refs[4:8]
+    gin_ref, own_keep, own_send, mid_keep, mid_send = refs[8:13]
+    scratch, e_ref = (refs[13:15], refs[15:17]), refs[17]
     ndp, nb, all_rows, _ = x_ref.shape
     own_rows = 2 * all_rows // 3
     rows = BLK // ndp
@@ -211,7 +218,7 @@
     def store(slot, m, which, r, part):
         ref = ((own_keep, own_send), (mid_keep, mid_send))[slot][m % 2]
         if slot == 0:
-            ref[m // 2, :, which, r] = part.astype(jnp.bfloat16).reshape(ndp, rows, BLK)
+            ref[m // 2, :, r, which] = part.astype(jnp.bfloat16).reshape(ndp, rows, BLK)
         else:
             ref[r, m // 2, :, which] = part.astype(jnp.bfloat16).reshape(ndp, rows, BLK)
 
@@ -219,7 +226,7 @@
         ref = ((own_keep, own_send), (mid_keep, mid_send))[slot][m % 2]
         part = part.astype(jnp.bfloat16).reshape(ndp // 2, 2, rows, BLK)
         if slot == 0:
-            ref[m // 2, half_src(ndp, r), 3] = part
+            ref[m // 2, half_src(ndp, r), :, 3] = part
         else:
             ref[y, m // 2, half_src(ndp, r ^ y), 3] = part[:, 0]
             ref[1 - y, m // 2, half_src(ndp, r ^ y), 3] = part[:, 1]
@@ -259,6 +266,7 @@
 
 
 def on_chip(kernel, products, outs, scratch, inputs):
+    cells = sum(x.size for x in inputs) + sum(map(math.prod, outs + scratch))
     in_specs = [pl.BlockSpec(memory_space=pltpu.SMEM)]
     in_specs += [pl.BlockSpec(memory_space=pltpu.VMEM)] * (len(inputs) - 1)
     return pl.pallas_call(
@@ -272,7 +280,7 @@
             transcendentals=0,
             bytes_accessed=sum(x.size for x in inputs) * 2 + sum(map(math.prod, outs)) * 2,
         ),
-        compiler_params=pltpu.CompilerParams(vmem_limit_bytes=56 * 2**20),
+        compiler_params=pltpu.CompilerParams(vmem_limit_bytes=2 * cells + 6 * 2**20),
     )(*inputs)
 
 
@@ -286,14 +294,20 @@
 
     everyone = ("dp", "bfly")
     shape = (ndp, nb, -1, BLK)
-    dealt = [deal_weight(w) for w in (dealt_a, weight_b, weight_c, dealt_e)]
-    w = exchange(jnp.stack(dealt, axis=1), "dp")
-    across = xor_permute(w, 2)
-    v = xor_permute(w[:, :, 2], 1, "dp")
-    x = exchange(after(deal_tokens(tokens), w), everyone)
-    g = exchange(after(deal_tokens(grad_out), x), everyone).reshape(shape)
+    def deal(first, second):
+        return jnp.stack([deal_weight(first), deal_weight(second)], axis=2)
+
+    def halves(w):
+        swapped = xor_permute(w[:, 2:], 1, "dp")
+        return w, xor_permute(w, 2), swapped, xor_permute(swapped, 2)
+
+    ab = halves(exchange(deal(dealt_a, weight_b), "dp"))
+    ce = halves(exchange(after(deal(weight_c, dealt_e), ab[0]), "dp"))
+    x = exchange(after(deal_tokens(tokens), ce[0], ab[1], ab[3]), everyone)
+    g = exchange(after(deal_tokens(grad_out), x, ce[1], ce[3]), everyone).reshape(shape)
     x = x.reshape(shape)
-    weights = gather_bfly(w, across) + gather_bfly(v, xor_permute(across[:, :, 2], 1, "dp"))
+    weights = gather_bfly(*ab[:2]) + gather_bfly(*ce[:2])
+    weights += gather_bfly(*ab[2:]) + gather_bfly(*ce[2:])
 
     own, mid = count * ndp // nb, count * ndp // nb // 2
     saved = []
@@ -306,7 +320,7 @@
         forward_kernel, 4 * products, [x.shape] + saved, [halves], [seat, x] + weights
     )
     out = exchange(out.reshape(ndp * nb, -1, BLK), everyone)
-    own_shape, mid_shape = (2, ndp, 4, 2, rows, BLK), (2, 2, ndp, 4, rows, BLK)
+    own_shape, mid_shape = (2, ndp, 2, 4, rows, BLK), (2, 2, ndp, 4, rows, BLK)
     gin, own_keep, own_send, mid_keep, mid_send = on_chip(
         backward_kernel,
         8 * products,
@@ -314,19 +328,19 @@
         [saved[0], saved[0], saved[4], saved[4], halves],
         [seat, x, g] + weights + kept,
     )
-    mid = add(mid_keep, xor_permute(mid_send, 1))
-    own = add(own_keep, xor_permute(own_send, 1))
+    half_mid = mid = add(mid_keep, xor_permute(mid_send, 1))
+    half_own = own = add(own_keep, xor_permute(own_send, 1))
     mid = add(mid[0], xor_permute(mid[1], 1, "dp"))
-    gin = exchange(after(gin.reshape(ndp * nb, -1, BLK), out), everyone)
+    gin = exchange(after(gin.reshape(ndp * nb, -1, BLK), out, half_mid, half_own), everyone)
     own = add(own[0], xor_permute(own[1], 2))
     mid = add(mid[0], xor_permute(mid[1], 2))
-    dealt = jnp.concatenate([own, mid[:, :, None]], axis=2)
+    dealt = jnp.concatenate([own, mid[:, None]], axis=1)
     got = exchange(after(dealt, gin), "dp").astype(jnp.float32)
-    got = got.reshape(ndp // 2, 2, 4, 3, rows, BLK)
+    got = got.reshape(ndp // 2, 2, 3, 4, rows, BLK)
 
     def own_rows(which):
-        mid = jnp.stack([got[:, 0, which, 2], got[:, 1, which, 2]], axis=1)
-        return jnp.stack([got[:, 0, which, :2], mid, got[:, 1, which, :2]], axis=1)
+        mid = jnp.stack([got[:, 0, 2, which], got[:, 1, 2, which]], axis=1)
+        return jnp.stack([got[:, 0, :2, which], mid, got[:, 1, :2, which]], axis=1)
 
     grad_a = own_rows(0).reshape(blocks, 2, rows, BLK).transpose(0, 2, 1, 3)
     return (

time: 323 us -> 307 us (0.950)
  waiting for transfers between devices: 190 us -> 147 us
  local copies, waits for them, and re-layouts: 38.8 us -> 58.9 us
  starting transfers between devices: 36.9 us -> 51.5 us
  Pallas kernels: 37.7 us -> 30 us
    all_to_all x6 -> x7, waiting for transfers between devices: 98.7 us -> 52.2 us  [exchange(): return lax.all_to_all(x, axes, split_axis=0, concat_axis=0, tiled=True)]
    unnamed x28 -> x64, local copies, waits for them, and re-layouts: 10.5 us -> 30.4 us
    ppermute x12 -> x19, starting transfers between devices: 9.58 us -> 17.4 us  [xor_permute(): lax.ppermute(x, axis, [(i, i ^ mask) for i in range(lax.axis_size(axis))])]
    pallas_call x2, Pallas kernels: 37.7 us -> 30 us  [on_chip(): pl.pallas_call(kernel, out_shape=[jax.ShapeDtypeStruct(shape, jnp.bfloat1...]
    all_to_all x6 -> x7, starting transfers between devices: 27.3 us -> 34.1 us  [exchange(): return lax.all_to_all(x, axes, split_axis=0, concat_axis=0, tiled=True)]
    ppermute x2 -> x0, local copies, waits for them, and re-layouts: 5.5 us -> none  [xor_permute(): lax.ppermute(x, axis, [(i, i ^ mask) for i in range(lax.axis_size(axis))])]
    slice x4, local copies, waits for them, and re-layouts: 5.15 us -> 9.11 us  [deal_tokens(): view[:, :, 0::2].reshape(nb, count // nb, ndp, BLK).transpose(2, 0, 1, 3)]
    ppermute x12 -> x19, waiting for transfers between devices: 91.2 us -> 94.6 us  [xor_permute(): lax.ppermute(x, axis, [(i, i ^ mask) for i in range(lax.axis_size(axis))])]
  transfers between devices with their start and end apart: 18 -> 26, of which waited for: 9 -> 14; matrix products, arithmetic and copies ran while one was open for 13% -> 15% of each run, Pallas kernels for 12% -> 10%
where the time goes in v7:
time: 307 us; the launch traced here: 306 us
  waiting for transfers between devices  147 us (48%)
  local copies, waits for them, and re-layouts  58.9 us (19%)
  starting transfers between devices  51.5 us (17%)
  Pallas kernels  30 us (10%)
  other arithmetic  17.3 us (6%)
    ppermute x19, waiting for transfers between devices, xor_permute(): lax.ppermute(x, axis, [(i, i ^ mask) for i in range(lax.axis_size(axis))])  94.6 us
    all_to_all x7, waiting for transfers between devices, exchange(): return lax.all_to_all(x, axes, split_axis=0, concat_axis=0, tiled=True)  52.2 us
    all_to_all x7, starting transfers between devices, exchange(): return lax.all_to_all(x, axes, split_axis=0, concat_axis=0, tiled=True)  34.1 us
    unnamed x64, local copies, waits for them, and re-layouts  30.4 us
    pallas_call x2, Pallas kernels, on_chip(): pl.pallas_call(kernel, out_shape=[jax.ShapeDtypeStruct(shape, jnp.bfloat1...  30 us
    ppermute x19, starting transfers between devices, xor_permute(): lax.ppermute(x, axis, [(i, i ^ mask) for i in range(lax.axis_size(axis))])  17.4 us
    slice x4, local copies, waits for them, and re-layouts, deal_tokens(): view[:, :, 0::2].reshape(nb, count // nb, ndp, BLK).transpose(2, 0, 1, 3)  9.11 us
  transfers between devices with their start and end apart: 26, of which 14 were waited for; matrix products, arithmetic and copies ran while one was open for 15% of the time, Pallas kernels for 10%

profile of v7, /device:TPU:0, one launch (start us, length us, event | category | flops | bytes accessed | tf_op | source)
XLA Modules:
  0.0 305.6 jit_solution(14133978097599437606)
XLA Ops:
  3.0 7.3 %all-to-all-start = ((bf16[8,3,2,32,256]{4,3,2,1,0:T(8,128)(2,1)}), bf16[8,3,2,32,256]{4,3,2,1,0:T(8,128)(2,1)S(1)}, u32[]{:S(2)}, u32[]{:S(2)}) async-start(bf16[8,3,2,32,256]{4,3,2,1,0:T(8,128)(2,1)} %maximum_maximum_fusion.1), calls=%async_computation | async-start | bytes 1572864 | tf_op jit(solution)/shard_map/all_to_all | solution.py:87
  11.4 19.1 %all-to-all-done.refs_0_ = bf16[8,3,2,32,256]{4,3,2,1,0:T(8,128)(2,1)S(1)} async-done(((bf16[8,3,2,32,256]{4,3,2,1,0:T(8,128)(2,1)}), bf16[8,3,2,32,256]{4,3,2,1,0:T(8,128)(2,1)S(1)}, u32[]{:S(2)}, u32[]{:S(2)}) %all-to-all-start) | async-done | bytes 786464 | tf_op jit(solution)/shard_map/all_to_all | solution.py:87
  30.5 3.6 %all-to-all-start.1 = ((bf16[8,3,2,32,256]{4,3,2,1,0:T(8,128)(2,1)}), bf16[8,3,2,32,256]{4,3,2,1,0:T(8,128)(2,1)S(1)}, u32[]{:S(2)}, u32[]{:S(2)}) async-start(bf16[8,3,2,32,256]{4,3,2,1,0:T(8,128)(2,1)} %maximum_maximum_fusion), calls=%async_computation.1 | async-start | bytes 1572864 | tf_op jit(solution)/shard_map/all_to_all | solution.py:87
  35.6 2.0 collective-permute-start.1
  37.6 12.6 %collective-permute-done.1.refs_8_ = bf16[8,1,2,32,256]{4,3,2,1,0:T(8,128)(2,1)S(1)} collective-permute-done((bf16[8,1,2,32,256]{4,3,2,1,0:T(8,128)(2,1)S(1)}, bf16[8,1,2,32,256]{4,3,2,1,0:T(8,128)(2,1)S(1)}, u32[]{:S(2)}, u32[]{:S(2)}) %collective-permute-start.1) | collective-permute-done | bytes 262176 | tf_op jit(solution)/shard_map/ppermute | solution.py:83
  51.6 2.6 copy.70
  55.3 2.3 slice.144
  57.5 2.3 copy.71
  60.8 2.7 pad_maximum_fusion
  64.4 4.1 %all-to-all-start.2 = ((bf16[32,96,256]{2,1,0:T(8,128)(2,1)}), bf16[32,96,256]{2,1,0:T(8,128)(2,1)S(1)}, u32[]{:S(2)}, u32[]{:S(2)}) async-start(bf16[32,96,256]{2,1,0:T(8,128)(2,1)} %pad_maximum_fusion), calls=%async_computation.2 | async-start | bytes 3145728 | tf_op jit(solution)/shard_map/all_to_all | solution.py:87
  71.9 17.2 %collective-permute-done.10.refs_12_ = bf16[8,1,2,32,256]{4,3,2,1,0:T(8,128)(2,1)} collective-permute-done((bf16[8,1,2,32,256]{4,3,2,1,0:T(8,128)(2,1)S(1)}, bf16[8,1,2,32,256]{4,3,2,1,0:T(8,128)(2,1)}, u32[]{:S(2)}, u32[]{:S(2)}) %collective-permute-start.10) | collective-permute-done | bytes 262176 | tf_op jit(solution)/shard_map/ppermute | solution.py:83
  89.1 2.1 collective-permute-start.12
  91.2 2.6 copy.79
  95.7 2.3 slice.164
  98.0 2.3 copy.80
  100.2 2.0 copy.81
  102.3 2.7 pad_maximum_fusion.1
  104.9 5.9 %collective-permute-done.12.refs_14_ = bf16[8,1,2,32,256]{4,3,2,1,0:T(8,128)(2,1)} collective-permute-done((bf16[8,1,2,32,256]{4,3,2,1,0:T(8,128)(2,1)}, bf16[8,1,2,32,256]{4,3,2,1,0:T(8,128)(2,1)}, u32[]{:S(2)}, u32[]{:S(2)}) %collective-permute-start.12) | collective-permute-done | bytes 262176 | tf_op jit(solution)/shard_map/ppermute | solution.py:83
  110.8 4.9 %all-to-all-start.4 = ((bf16[32,96,256]{2,1,0:T(8,128)(2,1)}), bf16[32,96,256]{2,1,0:T(8,128)(2,1)}, u32[]{:S(2)}, u32[]{:S(2)}) async-start(bf16[32,96,256]{2,1,0:T(8,128)(2,1)} %pad_maximum_fusion.1), calls=%async_computation.4 | async-start | bytes 3145728 | tf_op jit(solution)/shard_map/all_to_all | solution.py:87
  116.9 2.3 collective-permute-done.8.refs_9_
  120.0 2.4 collective-permute-done.9.refs_11_
  131.1 11.2 %shard_map.109 = (bf16[8,4,96,256]{3,2,1,0:T(8,128)(2,1)S(1)}, bf16[2,4,4,64,512]{4,3,2,1,0:T(8,128)(2,1)S(1)}, bf16[2,4,256,512]{3,2,1,0:T(8,128)(2,1)S(1)}, bf...) custom-call(s32[2]{0:T(128)S(1)} %pad_add_fusion.seat_ref, ...), custom_call_target="tpu_custom_call" | custom-call | flops 3221225472 | bytes 24117252 | tf_op jit(solution)/shard_map/pallas_call | solution.py:272
  153.3 5.6 %all-to-all-start.3 = ((bf16[32,96,256]{2,1,0:T(8,128)(2,1)}), bf16[32,96,256]{2,1,0:T(8,128)(2,1)}, u32[]{:S(2)}, u32[]{:S(2)}) async-start(bf16[32,96,256]{2,1,0:T(8,128)(2,1)} %bitcast.164), calls=%async_computation.3 | async-start | bytes 3145728 | tf_op jit(solution)/shard_map/all_to_all | solution.py:87
  161.8 18.7 %shard_map.110 = (bf16[8,4,96,256]{3,2,1,0:T(8,128)(2,1)}, bf16[2,8,2,4,32,256]{5,4,3,2,1,0:T(8,128)(2,1)}, bf16[2,8,2,4,32,256]{5,4,3,2,1,0:T(8,128)(2,1)}, bf1...) custom-call(s32[2]{0:T(128)S(1)} %pad_add_fusion.seat_ref, bf16[8,4,96,256]{3,2,1,0:T(8,128)(2,1)} %bitcast.163, ...), custom_call_target="tpu_custom_call" | custom-call | flops 6442450944 | bytes 34078724 | tf_op jit(solution)/shard_map/pallas_call | solution.py:272
  181.1 3.9 %collective-permute-done.14 = bf16[2,2,8,4,32,256]{5,4,3,2,1,0:T(8,128)(2,1)S(1)} collective-permute-done((bf16[2,2,8,4,32,256]{5,4,3,2,1,0:T(8,128)(2,1)}, bf16[2,2,8,4,32,256]{5,4,3,2,1,0:T(8,128)(2,1)S(1)}, u32[]{:S(2)}, u32[]{:S(2)}) %collective-permute-start.14) | collective-permute-done | bytes 2097184 | tf_op jit(solution)/shard_map/ppermute | solution.py:83
  185.0 4.0 %add_convert_fusion.1 = bf16[2,2,8,4,32,256]{5,4,3,2,1,0:T(8,128)(2,1)} fusion(bf16[2,2,8,4,32,256]{5,4,3,2,1,0:T(8,128)(2,1)S(1)} %collective-permute-done.14, bf16[2,2,8,4,32,256]{5,4,3,2,1,0:T(8,128)(2,1)} %get-tuple-element.38), kind=kLoop, calls=%fused_computation.1 | loop fusion | flops 4194304 | bytes 6291456 | tf_op jit(solution)/shard_map/convert_element_type | solution.py:107
  190.0 6.5 %all-to-all-done.3 = bf16[32,96,256]{2,1,0:T(8,128)(2,1)} async-done(((bf16[32,96,256]{2,1,0:T(8,128)(2,1)}), bf16[32,96,256]{2,1,0:T(8,128)(2,1)}, u32[]{:S(2)}, u32[]{:S(2)}) %all-to-all-start.3) | async-done | bytes 1572896 | tf_op jit(solution)/shard_map/all_to_all | solution.py:87
  196.5 4.1 %all-to-all-start.5 = ((bf16[32,96,256]{2,1,0:T(8,128)(2,1)}), bf16[32,96,256]{2,1,0:T(8,128)(2,1)}, u32[]{:S(2)}, u32[]{:S(2)}) async-start(bf16[32,96,256]{2,1,0:T(8,128)(2,1)} %bitcast.180), calls=%async_computation.5 | async-start | bytes 3145728 | tf_op jit(solution)/shard_map/all_to_all | solution.py:87
  205.2 37.2 %collective-permute-done.17 = bf16[2,8,4,32,256]{4,3,2,1,0:T(8,128)(2,1)S(1)} collective-permute-done((bf16[2,8,4,32,256]{4,3,2,1,0:T(8,128)(2,1)S(1)}, bf16[2,8,4,32,256]{4,3,2,1,0:T(8,128)(2,1)S(1)}, u32[]{:S(2)}, u32[]{:S(2)}) %collective-permute-start.17) | collective-permute-done | bytes 1048608 | tf_op jit(solution)/shard_map/ppermute | solution.py:83
  244.8 11.7 %collective-permute-done.18 = bf16[8,4,32,256]{3,2,1,0:T(8,128)(2,1)S(1)} collective-permute-done((bf16[8,4,32,256]{3,2,1,0:T(8,128)(2,1)S(1)}, bf16[8,4,32,256]{3,2,1,0:T(8,128)(2,1)S(1)}, u32[]{:S(2)}, u32[]{:S(2)}) %collective-permute-start.18) | collective-permute-done | bytes 524320 | tf_op jit(solution)/shard_map/ppermute | solution.py:83
  258.1 4.6 %all-to-all-start.6 = ((bf16[8,3,4,32,256]{4,3,2,1,0:T(8,128)(2,1)}), bf16[8,3,4,32,256]{4,3,2,1,0:T(8,128)(2,1)}, u32[]{:S(2)}, u32[]{:S(2)}) async-start(bf16[8,3,4,32,256]{4,3,2,1,0:T(8,128)(2,1)} %pad_maximum_fusion.2), calls=%async_computation.6 | async-start | bytes 3145728 | tf_op jit(solution)/shard_map/all_to_all | solution.py:87
  272.9 26.3 %all-to-all-done.6 = bf16[8,3,4,32,256]{4,3,2,1,0:T(8,128)(2,1)} async-done(((bf16[8,3,4,32,256]{4,3,2,1,0:T(8,128)(2,1)}), bf16[8,3,4,32,256]{4,3,2,1,0:T(8,128)(2,1)}, u32[]{:S(2)}, u32[]{:S(2)}) %all-to-all-start.6) | async-done | bytes 1572896 | tf_op jit(solution)/shard_map/all_to_all | solution.py:87
  (144 shorter events, 65.6 us)
Async XLA Ops:
  1.9 8.3 %copy-start.28 = (bf16[24,32,256]{2,1,0:T(8,128)(2,1)S(1)}, bf16[24,32,256]{2,1,0:T(8,128)(2,1)}, u32[]{:S(2)}) copy-start(bf16[24,32,256]{2,1,0:T(8,128)(2,1)} %param.10) | copy-start | bytes 1179652
  2.0 8.3 %copy-start.29 = (bf16[12,64,256]{2,1,0:T(8,128)(2,1)S(1)}, bf16[12,64,256]{2,1,0:T(8,128)(2,1)}, u32[]{:S(2)}) copy-start(bf16[12,64,256]{2,1,0:T(8,128)(2,1)} %param.11) | copy-start | bytes 1179652
  3.0 27.5 %all-to-all-start = ((bf16[8,3,2,32,256]{4,3,2,1,0:T(8,128)(2,1)}), bf16[8,3,2,32,256]{4,3,2,1,0:T(8,128)(2,1)S(1)}, u32[]{:S(2)}, u32[]{:S(2)}) async-start(bf16[8,3,2,32,256]{4,3,2,1,0:T(8,128)(2,1)} %maximum_maximum_fusion.1), calls=%async_computation | async-start | bytes 1572864 | tf_op jit(solution)/shard_map/all_to_all | solution.py:87
  30.5 33.0 %all-to-all-start.1 = ((bf16[8,3,2,32,256]{4,3,2,1,0:T(8,128)(2,1)}), bf16[8,3,2,32,256]{4,3,2,1,0:T(8,128)(2,1)S(1)}, u32[]{:S(2)}, u32[]{:S(2)}) async-start(bf16[8,3,2,32,256]{4,3,2,1,0:T(8,128)(2,1)} %maximum_maximum_fusion), calls=%async_computation.1 | async-start | bytes 1572864 | tf_op jit(solution)/shard_map/all_to_all | solution.py:87
  34.0 29.5 %collective-permute-start = (bf16[8,3,2,32,256]{4,3,2,1,0:T(8,128)(2,1)S(1)}, bf16[8,3,2,32,256]{4,3,2,1,0:T(8,128)(2,1)S(1)}, u32[]{:S(2)}, u32[]{:S(2)}) collective-permute-start(bf16[8,3,2,32,256]{4,3,2,1,0:T(8,128)(2,1)S(1)} %all-to-all-done.refs_0_), channel_id=1, source_target_pairs={{0,2},{1,3},{2,0},{3,1},{4,6},{5,7},{6,4},{7,5},{8,10},{9,11},{10,... | collective-permute-start | bytes 2359304 | tf_op jit(solution)/shard_map/ppermute | solution.py:83
  35.6 14.6 %collective-permute-start.1 = (bf16[8,1,2,32,256]{4,3,2,1,0:T(8,128)(2,1)S(1)}, bf16[8,1,2,32,256]{4,3,2,1,0:T(8,128)(2,1)S(1)}, u32[]{:S(2)}, u32[]{:S(2)}) collective-permute-start(bf16[8,1,2,32,256]{4,3,2,1,0:T(8,128)(2,1)S(1)} %slice.205), channel_id=1, source_target_pairs={{0,4},{4,0},{8,12},{12,8},{16,20},{20,16},{24,28},{28,24},{1,5},{5... | collective-permute-start | bytes 786440 | tf_op jit(solution)/shard_map/ppermute | solution.py:83
  50.2 13.2 %collective-permute-start.2 = (bf16[8,1,2,32,256]{4,3,2,1,0:T(8,128)(2,1)S(1)}, bf16[8,1,2,32,256]{4,3,2,1,0:T(8,128)(2,1)S(1)}, u32[]{:S(2)}, u32[]{:S(2)}) collective-permute-start(bf16[8,1,2,32,256]{4,3,2,1,0:T(8,128)(2,1)S(1)} %collective-permute-done.1.refs_8_), channel_id=1, source_target_pairs={{0,2},{1,3},{2,0},{3,1},{4,6},{5,7},{6,4},{7,5},{8,10},{9,11},{10,... | collective-permute-start | bytes 786440 | tf_op jit(solution)/shard_map/ppermute | solution.py:83
  64.4 46.4 %all-to-all-start.2 = ((bf16[32,96,256]{2,1,0:T(8,128)(2,1)}), bf16[32,96,256]{2,1,0:T(8,128)(2,1)S(1)}, u32[]{:S(2)}, u32[]{:S(2)}) async-start(bf16[32,96,256]{2,1,0:T(8,128)(2,1)} %pad_maximum_fusion), calls=%async_computation.2 | async-start | bytes 3145728 | tf_op jit(solution)/shard_map/all_to_all | solution.py:87
  68.5 42.3 %collective-permute-start.6 = (bf16[8,3,2,32,256]{4,3,2,1,0:T(8,128)(2,1)S(1)}, bf16[8,3,2,32,256]{4,3,2,1,0:T(8,128)(2,1)}, u32[]{:S(2)}, u32[]{:S(2)}) collective-permute-start(bf16[8,3,2,32,256]{4,3,2,1,0:T(8,128)(2,1)S(1)} %all-to-all-done.1.refs_4_), channel_id=1, source_target_pairs={{0,2},{1,3},{2,0},{3,1},{4,6},{5,7},{6,4},{7,5},{8,10},{9,11},{10,... | collective-permute-start | bytes 2359304 | tf_op jit(solution)/shard_map/ppermute | solution.py:83
  70.4 18.7 %collective-permute-start.10 = (bf16[8,1,2,32,256]{4,3,2,1,0:T(8,128)(2,1)S(1)}, bf16[8,1,2,32,256]{4,3,2,1,0:T(8,128)(2,1)}, u32[]{:S(2)}, u32[]{:S(2)}) collective-permute-start(bf16[8,1,2,32,256]{4,3,2,1,0:T(8,128)(2,1)S(1)} %slice.206), channel_id=1, source_target_pairs={{0,4},{4,0},{8,12},{12,8},{16,20},{20,16},{24,28},{28,24},{1,5},{5... | collective-permute-start | bytes 786440 | tf_op jit(solution)/shard_map/ppermute | solution.py:83
  89.1 21.7 %collective-permute-start.12 = (bf16[8,1,2,32,256]{4,3,2,1,0:T(8,128)(2,1)}, bf16[8,1,2,32,256]{4,3,2,1,0:T(8,128)(2,1)}, u32[]{:S(2)}, u32[]{:S(2)}) collective-permute-start(bf16[8,1,2,32,256]{4,3,2,1,0:T(8,128)(2,1)} %collective-permute-done.10.refs_12_), channel_id=1, source_target_pairs={{0,2},{1,3},{2,0},{3,1},{4,6},{5,7},{6,4},{7,5},{8,10},{9,11},{10,... | collective-permute-start | bytes 786440 | tf_op jit(solution)/shard_map/ppermute | solution.py:83
  110.8 31.5 %copy-start = (bf16[32,96,256]{2,1,0:T(8,128)(2,1)}, bf16[32,96,256]{2,1,0:T(8,128)(2,1)S(1)}, u32[]{:S(2)}) copy-start(bf16[32,96,256]{2,1,0:T(8,128)(2,1)S(1)} %all-to-all-done.2) | copy-start | bytes 4718596
  110.8 42.5 %all-to-all-start.4 = ((bf16[32,96,256]{2,1,0:T(8,128)(2,1)}), bf16[32,96,256]{2,1,0:T(8,128)(2,1)}, u32[]{:S(2)}, u32[]{:S(2)}) async-start(bf16[32,96,256]{2,1,0:T(8,128)(2,1)} %pad_maximum_fusion.1), calls=%async_computation.4 | async-start | bytes 3145728 | tf_op jit(solution)/shard_map/all_to_all | solution.py:87
  115.7 7.5 %collective-permute-start.3 = (bf16[8,3,2,32,256]{4,3,2,1,0:T(8,128)(2,1)S(1)}, bf16[8,3,2,32,256]{4,3,2,1,0:T(8,128)(2,1)S(1)}, u32[]{:S(2)}, u32[]{:S(2)}) collective-permute-start(bf16[8,3,2,32,256]{4,3,2,1,0:T(8,128)(2,1)S(1)} %all-to-all-done.refs_0_), channel_id=1, source_target_pairs={{0,1},{1,0},{2,3},{3,2},{4,5},{5,4},{6,7},{7,6},{8,9},{9,8},{10,11... | collective-permute-start | bytes 2359304 | tf_op jit(solution)/shard_map/ppermute | solution.py:83
  115.8 3.4 %collective-permute-start.8 = (bf16[8,1,2,32,256]{4,3,2,1,0:T(8,128)(2,1)S(1)}, bf16[8,1,2,32,256]{4,3,2,1,0:T(8,128)(2,1)S(1)}, u32[]{:S(2)}, u32[]{:S(2)}) collective-permute-start(bf16[8,1,2,32,256]{4,3,2,1,0:T(8,128)(2,1)S(1)} %collective-permute-done.1.refs_8_), channel_id=1, source_target_pairs={{0,1},{1,0},{2,3},{3,2},{4,5},{5,4},{6,7},{7,6},{8,9},{9,8},{10,11... | collective-permute-start | bytes 786440 | tf_op jit(solution)/shard_map/ppermute | solution.py:83
  116.3 8.3 %collective-permute-start.4 = (bf16[8,3,2,32,256]{4,3,2,1,0:T(8,128)(2,1)}, bf16[8,3,2,32,256]{4,3,2,1,0:T(8,128)(2,1)}, u32[]{:S(2)}, u32[]{:S(2)}) collective-permute-start(bf16[8,3,2,32,256]{4,3,2,1,0:T(8,128)(2,1)} %copy-done.10), channel_id=1, source_target_pairs={{0,1},{1,0},{2,3},{3,2},{4,5},{5,4},{6,7},{7,6},{8,9},{9,8},{10,11... | collective-permute-start | bytes 2359304 | tf_op jit(solution)/shard_map/ppermute | solution.py:83
  116.4 9.6 %collective-permute-start.5 = (bf16[8,3,2,32,256]{4,3,2,1,0:T(8,128)(2,1)S(1)}, bf16[8,3,2,32,256]{4,3,2,1,0:T(8,128)(2,1)}, u32[]{:S(2)}, u32[]{:S(2)}) collective-permute-start(bf16[8,3,2,32,256]{4,3,2,1,0:T(8,128)(2,1)S(1)} %all-to-all-done.1.refs_4_), channel_id=1, source_target_pairs={{0,1},{1,0},{2,3},{3,2},{4,5},{5,4},{6,7},{7,6},{8,9},{9,8},{10,11... | collective-permute-start | bytes 2359304 | tf_op jit(solution)/shard_map/ppermute | solution.py:83
  116.8 9.2 %collective-permute-start.7 = (bf16[8,3,2,32,256]{4,3,2,1,0:T(8,128)(2,1)}, bf16[8,3,2,32,256]{4,3,2,1,0:T(8,128)(2,1)}, u32[]{:S(2)}, u32[]{:S(2)}) collective-permute-start(bf16[8,3,2,32,256]{4,3,2,1,0:T(8,128)(2,1)} %collective-permute-done.6.refs_6_), channel_id=1, source_target_pairs={{0,1},{1,0},{2,3},{3,2},{4,5},{5,4},{6,7},{7,6},{8,9},{9,8},{10,11... | collective-permute-start | bytes 2359304 | tf_op jit(solution)/shard_map/ppermute | solution.py:83
  119.9 2.5 collective-permute-start.9
  123.1 1.9 collective-permute-start.11
  124.1 1.9 collective-permute-start.13
  153.3 5.6 %copy-start.12 = (bf16[8,3,2,32,256]{4,3,2,1,0:T(8,128)(2,1)S(1)}, bf16[8,3,2,32,256]{4,3,2,1,0:T(8,128)(2,1)}, u32[]{:S(2)}) copy-start(bf16[8,3,2,32,256]{4,3,2,1,0:T(8,128)(2,1)} %copy-done.10) | copy-start | bytes 2359300
  153.3 5.6 %copy-start.15 = (bf16[8,3,2,32,256]{4,3,2,1,0:T(8,128)(2,1)S(1)}, bf16[8,3,2,32,256]{4,3,2,1,0:T(8,128)(2,1)}, u32[]{:S(2)}) copy-start(bf16[8,3,2,32,256]{4,3,2,1,0:T(8,128)(2,1)} %copy-done.13) | copy-start | bytes 2359300
  153.3 43.2 %all-to-all-start.3 = ((bf16[32,96,256]{2,1,0:T(8,128)(2,1)}), bf16[32,96,256]{2,1,0:T(8,128)(2,1)}, u32[]{:S(2)}, u32[]{:S(2)}) async-start(bf16[32,96,256]{2,1,0:T(8,128)(2,1)} %bitcast.164), calls=%async_computation.3 | async-start | bytes 3145728 | tf_op jit(solution)/shard_map/all_to_all | solution.py:87
  180.5 4.4 %collective-permute-start.14 = (bf16[2,2,8,4,32,256]{5,4,3,2,1,0:T(8,128)(2,1)}, bf16[2,2,8,4,32,256]{5,4,3,2,1,0:T(8,128)(2,1)S(1)}, u32[]{:S(2)}, u32[]{:S(2)}) collective-permute-start(bf16[2,2,8,4,32,256]{5,4,3,2,1,0:T(8,128)(2,1)} %get-tuple-element.39), channel_id=1, source_target_pairs={{0,1},{1,0},{2,3},{3,2},{4,5},{5,4},{6,7},{7,6},{8,9},{9,8},{10,11... | collective-permute-start | bytes 6291464 | tf_op jit(solution)/shard_map/ppermute | solution.py:83
  180.6 8.4 %collective-permute-start.15 = (bf16[2,8,2,4,32,256]{5,4,3,2,1,0:T(8,128)(2,1)}, bf16[2,8,2,4,32,256]{5,4,3,2,1,0:T(8,128)(2,1)S(1)}, u32[]{:S(2)}, u32[]{:S(2)}) collective-permute-start(bf16[2,8,2,4,32,256]{5,4,3,2,1,0:T(8,128)(2,1)} %get-tuple-element.41), channel_id=1, source_target_pairs={{0,1},{1,0},{2,3},{3,2},{4,5},{5,4},{6,7},{7,6},{8,9},{9,8},{10,11... | collective-permute-start | bytes 6291464 | tf_op jit(solution)/shard_map/ppermute | solution.py:83
  196.5 61.6 %all-to-all-start.5 = ((bf16[32,96,256]{2,1,0:T(8,128)(2,1)}), bf16[32,96,256]{2,1,0:T(8,128)(2,1)}, u32[]{:S(2)}, u32[]{:S(2)}) async-start(bf16[32,96,256]{2,1,0:T(8,128)(2,1)} %bitcast.180), calls=%async_computation.5 | async-start | bytes 3145728 | tf_op jit(solution)/shard_map/all_to_all | solution.py:87
  200.6 41.8 %copy-start.25 = (bf16[2,2,8,4,32,256]{5,4,3,2,1,0:T(8,128)(2,1)S(1)}, bf16[2,2,8,4,32,256]{5,4,3,2,1,0:T(8,128)(2,1)}, u32[]{:S(2)}) copy-start(bf16[2,2,8,4,32,256]{5,4,3,2,1,0:T(8,128)(2,1)} %add_convert_fusion.1) | copy-start | bytes 6291460
  202.1 40.3 %collective-permute-start.17 = (bf16[2,8,4,32,256]{4,3,2,1,0:T(8,128)(2,1)S(1)}, bf16[2,8,4,32,256]{4,3,2,1,0:T(8,128)(2,1)S(1)}, u32[]{:S(2)}, u32[]{:S(2)}) collective-permute-start(bf16[2,8,4,32,256]{4,3,2,1,0:T(8,128)(2,1)S(1)} %slice_bitcast_fusion), channel_id=1, source_target_pairs={{0,4},{4,0},{8,12},{12,8},{16,20},{20,16},{24,28},{28,24},{1,5},{5... | collective-permute-start | bytes 3145736 | tf_op jit(solution)/shard_map/ppermute | solution.py:83
  203.7 40.7 %collective-permute-start.16 = (bf16[8,2,4,32,256]{4,3,2,1,0:T(8,128)(2,1)S(1)}, bf16[8,2,4,32,256]{4,3,2,1,0:T(8,128)(2,1)S(1)}, u32[]{:S(2)}, u32[]{:S(2)}) collective-permute-start(bf16[8,2,4,32,256]{4,3,2,1,0:T(8,128)(2,1)S(1)} %slice_bitcast_fusion.2), channel_id=1, source_target_pairs={{0,2},{1,3},{2,0},{3,1},{4,6},{5,7},{6,4},{7,5},{8,10},{9,11},{10,... | collective-permute-start | bytes 3145736 | tf_op jit(solution)/shard_map/ppermute | solution.py:83
  242.9 13.7 %collective-permute-start.18 = (bf16[8,4,32,256]{3,2,1,0:T(8,128)(2,1)S(1)}, bf16[8,4,32,256]{3,2,1,0:T(8,128)(2,1)S(1)}, u32[]{:S(2)}, u32[]{:S(2)}) collective-permute-start(bf16[8,4,32,256]{3,2,1,0:T(8,128)(2,1)S(1)} %slice_bitcast_fusion.4), channel_id=1, source_target_pairs={{0,2},{1,3},{2,0},{3,1},{4,6},{5,7},{6,4},{7,5},{8,10},{9,11},{10,... | collective-permute-start | bytes 1572872 | tf_op jit(solution)/shard_map/ppermute | solution.py:83
  258.1 41.1 %all-to-all-start.6 = ((bf16[8,3,4,32,256]{4,3,2,1,0:T(8,128)(2,1)}), bf16[8,3,4,32,256]{4,3,2,1,0:T(8,128)(2,1)}, u32[]{:S(2)}, u32[]{:S(2)}) async-start(bf16[8,3,4,32,256]{4,3,2,1,0:T(8,128)(2,1)} %pad_maximum_fusion.2), calls=%async_computation.6 | async-start | bytes 3145728 | tf_op jit(solution)/shard_map/all_to_all | solution.py:87
  (24 other events, 27.8 us)

commit v8 on v7

--- a/solution.py
+++ b/solution.py
@@ -204,16 +204,53 @@
             out_ref[:, d, lo:hi, :] = total.astype(jnp.bfloat16).reshape(ndp, hi - lo, BLK)
 
 
-def backward_kernel(seat_ref, x_ref, g_ref, *refs):
-    w, v, refs = weight_refs(refs)
-    saved = refs[:4], refs[4:8]
-    gin_ref, own_keep, own_send, mid_keep, mid_send = refs[8:13]
-    scratch, e_ref = (refs[13:15], refs[15:17]), refs[17]
-    ndp, nb, all_rows, _ = x_ref.shape
+class Streamed:
+    def __init__(self, sources, targets, sems, order):
+        self.targets, self.waiting = targets, {}
+        for i in order:
+            self.waiting[i] = pltpu.make_async_copy(sources[i], targets[i], sems.at[i])
+            self.waiting[i].start()
+
+    def get(self, i):
+        if i in self.waiting:
+            self.waiting.pop(i).wait()
+        return self.targets[i]
+
+
+class Lookup:
+    def __init__(self, streamed, indices):
+        self.streamed, self.indices = streamed, indices
+
+    def __getitem__(self, at):
+        return self.streamed.get(self.indices[at])
+
+
+BACKWARD_ORDER = (
+    (1, 6, 21, 7, 8, 9, 2, 18, 19, 20, 3, 4, 5, 0) + tuple(range(14, 18)) + (25,) + tuple(range(10, 14)) + (22, 23, 24)
+)
+
+
+def backward_kernel(seat_ref, *refs):
+    count_in = len(BACKWARD_ORDER)
+    sources, refs = refs[:count_in], refs[count_in:]
+    results, refs = refs[:9], refs[9:]
+    targets, refs = refs[:count_in], refs[count_in:]
+    staged, refs = refs[:5], refs[5:]
+    scratch, (e_ref, in_sems, out_sems) = (refs[:2], refs[2:4]), refs[4:]
+    streamed = Streamed(sources, targets, in_sems, BACKWARD_ORDER)
+    at = [Lookup(streamed, range(i, i + 4)) for i in range(2, 26, 4)]
+    w, v, saved = at[:2], at[2:4], at[4:]
+    gin_ref, own_keep, own_send, mid_keep, mid_send = staged
+    sent = []
+
+    def send(source, target):
+        sent.append(pltpu.make_async_copy(source, target, out_sems.at[len(sent)]))
+        sent[-1].start()
+
+    ndp, nb, all_rows, _ = targets[0].shape
     own_rows = 2 * all_rows // 3
     rows = BLK // ndp
     f, y = seat_ref[0], seat_ref[1]
-    join_halves(w, v, e_ref, y)
 
     def store(slot, m, which, r, part):
         ref = ((own_keep, own_send), (mid_keep, mid_send))[slot][m % 2]
@@ -232,55 +269,71 @@
             ref[1 - y, m // 2, half_src(ndp, r ^ y), 3] = part[:, 1]
 
     for slot, (lo, hi) in enumerate(((0, own_rows), (own_rows, all_rows))):
-        perm, active, slope, ret = saved[slot]
+        perm, active, slope, ret = range(4)
         mid, spread = scratch[slot]
+        if slot == 1:
+            join_halves(w, v, e_ref, y)
         weight, wide = weight_of(slot, w, v), wide_weight(slot, w, e_ref, y)
         count = ndp * (hi - lo)
         tiles = (nb, BLK // nb, count)
         for m in range(nb):
             d = f ^ m
-            g = g_ref[:, d, lo:hi, :].reshape(count, BLK)
+            g = streamed.get(1)[:, d, lo:hi, :].reshape(count, BLK)
             for r in range(2):
                 mid[r, :, d] = dot(wide(m, r), g, 1, 1).astype(jnp.bfloat16).reshape(tiles)
-                store_wide(slot, m, r, dot(ret[r, d].reshape(BLK, count), g, 1, 0))
+                store_wide(slot, m, r, dot(saved[slot][ret][r, d].reshape(BLK, count), g, 1, 0))
         for m in range(nb):
             s = f ^ m
             for r in range(2):
-                p = perm[r, s].reshape(BLK, count)
+                p = saved[slot][perm][r, s].reshape(BLK, count)
                 back_mid = mid[r, s].reshape(BLK, count)
                 back = dot(weight(m, 2, r), back_mid, 1, 0)
-                back = (back * slope[r, s].astype(jnp.float32)).astype(jnp.bfloat16)
-                store(slot, m, 2, r, dot(active[r, s], back_mid, 1, 1))
+                back = (back * saved[slot][slope][r, s].astype(jnp.float32)).astype(jnp.bfloat16)
+                store(slot, m, 2, r, dot(saved[slot][active][r, s], back_mid, 1, 1))
                 store(slot, m, 1, r, dot(p, back, 1, 1))
                 first = dot(weight(m, 1, r), back, 1, 0).astype(jnp.bfloat16)
                 spread[r, :, s] = first.reshape(tiles)
         for m in range(nb):
             d = f ^ m
-            x = x_ref[:, d, lo:hi, :].reshape(count, BLK)
+            x = streamed.get(0)[:, d, lo:hi, :].reshape(count, BLK)
             total = 0.0
             for r in range(2):
                 back = spread[r, d].reshape(BLK, count)
                 total = total + dot(back, weight(m, 0, r), 0, 1)
                 store(slot, m, 0, r, dot(x, back, 0, 1))
             gin_ref[:, d, lo:hi, :] = total.astype(jnp.bfloat16).reshape(ndp, hi - lo, BLK)
-
-
-def on_chip(kernel, products, outs, scratch, inputs):
-    cells = sum(x.size for x in inputs) + sum(map(math.prod, outs + scratch))
-    in_specs = [pl.BlockSpec(memory_space=pltpu.SMEM)]
-    in_specs += [pl.BlockSpec(memory_space=pltpu.VMEM)] * (len(inputs) - 1)
+        if slot == 0:
+            send(own_keep, results[1])
+            send(own_send.at[0], results[2])
+            send(own_send.at[1], results[3])
+    send(mid_keep, results[4])
+    for i in range(4):
+        send(mid_send.at[i // 2, i % 2], results[5 + i])
+    send(gin_ref, results[0])
+    for copy in sent:
+        copy.wait()
+
+
+def on_chip(kernel, products, outs, scratch, inputs, results=None):
+    streamed = results is not None
+    space = pl.ANY if streamed else pltpu.VMEM
+    staged = [x.shape for x in inputs[1:]] + outs if streamed else []
+    outs = results or outs
+    sems = [pltpu.SemaphoreType.DMA((n,)) for n in (len(inputs) - 1, len(outs))]
     return pl.pallas_call(
         kernel,
         out_shape=[jax.ShapeDtypeStruct(shape, jnp.bfloat16) for shape in outs],
-        in_specs=in_specs,
-        out_specs=[pl.BlockSpec(memory_space=pltpu.VMEM)] * len(outs),
-        scratch_shapes=[pltpu.VMEM(shape, jnp.bfloat16) for shape in scratch],
+        in_specs=[pl.BlockSpec(memory_space=pltpu.SMEM)]
+        + [pl.BlockSpec(memory_space=space)] * (len(inputs) - 1),
+        out_specs=[pl.BlockSpec(memory_space=space)] * len(outs),
+        scratch_shapes=[pltpu.VMEM(shape, jnp.bfloat16) for shape in staged + scratch]
+        + (sems if streamed else []),
         cost_estimate=pl.CostEstimate(
             flops=products * 2 * BLK * BLK,
             transcendentals=0,
             bytes_accessed=sum(x.size for x in inputs) * 2 + sum(map(math.prod, outs)) * 2,
         ),
-        compiler_params=pltpu.CompilerParams(vmem_limit_bytes=2 * cells + 6 * 2**20),
+        compiler_params=pltpu.CompilerParams(vmem_limit_bytes=56 * 2**20),
     )(*inputs)
 
 
@@ -321,19 +374,28 @@
     )
     out = exchange(out.reshape(ndp * nb, -1, BLK), everyone)
     own_shape, mid_shape = (2, ndp, 2, 4, rows, BLK), (2, 2, ndp, 4, rows, BLK)
-    gin, own_keep, own_send, mid_keep, mid_send = on_chip(
+    gin, own_keep, *sends = on_chip(
         backward_kernel,
         8 * products,
         [x.shape, own_shape, own_shape, mid_shape, mid_shape],
         [saved[0], saved[0], saved[4], saved[4], halves],
         [seat, x, g] + weights + kept,
-    )
-    half_mid = mid = add(mid_keep, xor_permute(mid_send, 1))
-    half_own = own = add(own_keep, xor_permute(own_send, 1))
-    mid = add(mid[0], xor_permute(mid[1], 1, "dp"))
-    gin = exchange(after(gin.reshape(ndp * nb, -1, BLK), out, half_mid, half_own), everyone)
-    own = add(own[0], xor_permute(own[1], 2))
-    mid = add(mid[0], xor_permute(mid[1], 2))
+        [x.shape, own_shape] + [own_shape[1:]] * 2 + [mid_shape] + [mid_shape[2:]] * 4,
+    )
+    mid_keep = sends.pop(2)
+    far = add(mid_keep[1, 1], xor_permute(sends[5], 1))
+    own_far = add(own_keep[1], xor_permute(sends[1], 1))
+    far = add(add(mid_keep[0, 1], xor_permute(sends[3], 1)), xor_permute(far, 1, "dp"))
+    own_near = add(own_keep[0], xor_permute(sends[0], 1))
+    near = add(mid_keep[1, 0], xor_permute(sends[4], 1))
+    part = ndp // 2
+    own_first = add(own_near[:part], xor_permute(own_far[:part], 2))
+    gin = exchange(after(gin.reshape(ndp * nb, -1, BLK), out, far, own_first), everyone)
+    own_last = add(own_near[part:], xor_permute(after(own_far[part:], own_first), 2))
+    own = jnp.concatenate([own_first, own_last], axis=0)
+    near = xor_permute(near, 1, "dp")
+    near = add(add(mid_keep[0, 0], xor_permute(sends[2], 1)), near)
+    mid = add(near, xor_permute(far, 2))
     dealt = jnp.concatenate([own, mid[:, None]], axis=1)
     got = exchange(after(dealt, gin), "dp").astype(jnp.float32)
     got = got.reshape(ndp // 2, 2, 3, 4, rows, BLK)

time: 307 us -> 302 us (0.984)
  local copies, waits for them, and re-layouts: 58.9 us -> 31.7 us
  waiting for transfers between devices: 147 us -> 157 us
  Pallas kernels: 30 us -> 35.5 us
  starting transfers between devices: 51.5 us -> 55.6 us
    unnamed x64 -> x44, local copies, waits for them, and re-layouts: 30.4 us -> 10.9 us
    all_to_all x7, waiting for transfers between devices: 52.2 us -> 59.3 us  [exchange(): return lax.all_to_all(x, axes, split_axis=0, concat_axis=0, tiled=True)]
    pallas_call x2, Pallas kernels: 30 us -> 35.5 us  [on_chip(): pl.pallas_call(kernel, out_shape=[jax.ShapeDtypeStruct(shape, jnp.bfloat1...]
    slice x4, local copies, waits for them, and re-layouts: 9.11 us -> 5.15 us  [deal_tokens(): view[:, :, 0::2].reshape(nb, count // nb, ndp, BLK).transpose(2, 0, 1, 3)]
    ppermute x19 -> x25, starting transfers between devices: 17.4 us -> 21.1 us  [xor_permute(): lax.ppermute(x, axis, [(i, i ^ mask) for i in range(lax.axis_size(axis))])]
    ppermute x19 -> x25, waiting for transfers between devices: 94.6 us -> 97.9 us  [xor_permute(): lax.ppermute(x, axis, [(i, i ^ mask) for i in range(lax.axis_size(axis))])]
    convert_element_type x4 -> x5, other arithmetic: 5.88 us -> 7.14 us  [add(): return (x.astype(jnp.float32) + y.astype(jnp.float32)).astype(jnp.bfloat16)]
  transfers between devices with their start and end apart: 26 -> 32, of which waited for: 14 -> 17; matrix products, arithmetic and copies ran while one was open for 15% -> 13% of each run, Pallas kernels for 10% -> 12%
where the time goes in v8:
time: 302 us; the launch traced here: 301 us
  waiting for transfers between devices  157 us (52%)
  starting transfers between devices  55.6 us (18%)
  Pallas kernels  35.5 us (12%)
  local copies, waits for them, and re-layouts  31.7 us (10%)
  other arithmetic  19.6 us (6%)
    ppermute x25, waiting for transfers between devices, xor_permute(): lax.ppermute(x, axis, [(i, i ^ mask) for i in range(lax.axis_size(axis))])  97.9 us
    all_to_all x7, waiting for transfers between devices, exchange(): return lax.all_to_all(x, axes, split_axis=0, concat_axis=0, tiled=True)  59.3 us
    pallas_call x2, Pallas kernels, on_chip(): pl.pallas_call(kernel, out_shape=[jax.ShapeDtypeStruct(shape, jnp.bfloat1...  35.5 us
    all_to_all x7, starting transfers between devices, exchange(): return lax.all_to_all(x, axes, split_axis=0, concat_axis=0, tiled=True)  34.4 us
    ppermute x25, starting transfers between devices, xor_permute(): lax.ppermute(x, axis, [(i, i ^ mask) for i in range(lax.axis_size(axis))])  21.1 us
    unnamed x44, local copies, waits for them, and re-layouts  10.9 us
    convert_element_type x5, other arithmetic, add(): return (x.astype(jnp.float32) + y.astype(jnp.float32)).astype(jnp.bfloat16)  7.14 us
  transfers between devices with their start and end apart: 32, of which 17 were waited for; matrix products, arithmetic and copies ran while one was open for 13% of the time, Pallas kernels for 12%

profile of v8, /device:TPU:0, one launch (start us, length us, event | category | flops | bytes accessed | tf_op | source)
XLA Modules:
  0.0 300.7 jit_solution(14501466640622905622)
XLA Ops:
  3.0 7.4 %all-to-all-start = ((bf16[8,3,2,32,256]{4,3,2,1,0:T(8,128)(2,1)}), bf16[8,3,2,32,256]{4,3,2,1,0:T(8,128)(2,1)S(1)}, u32[]{:S(2)}, u32[]{:S(2)}) async-start(bf16[8,3,2,32,256]{4,3,2,1,0:T(8,128)(2,1)} %maximum_maximum_fusion.1), calls=%async_computation | async-start | bytes 1572864 | tf_op jit(solution)/shard_map/all_to_all | solution.py:87
  11.5 19.1 %all-to-all-done.refs_0_.refs_2_ = bf16[8,3,2,32,256]{4,3,2,1,0:T(8,128)(2,1)S(1)} async-done(((bf16[8,3,2,32,256]{4,3,2,1,0:T(8,128)(2,1)}), bf16[8,3,2,32,256]{4,3,2,1,0:T(8,128)(2,1)S(1)}, u32[]{:S(2)}, u32[]{:S(2)}) %all-to-all-start) | async-done | bytes 786464 | tf_op jit(solution)/shard_map/all_to_all | solution.py:87
  30.6 3.6 %all-to-all-start.1 = ((bf16[8,3,2,32,256]{4,3,2,1,0:T(8,128)(2,1)}), bf16[8,3,2,32,256]{4,3,2,1,0:T(8,128)(2,1)S(1)}, u32[]{:S(2)}, u32[]{:S(2)}) async-start(bf16[8,3,2,32,256]{4,3,2,1,0:T(8,128)(2,1)} %maximum_maximum_fusion), calls=%async_computation.1 | async-start | bytes 1572864 | tf_op jit(solution)/shard_map/all_to_all | solution.py:87
  35.7 2.0 collective-permute-start.1
  37.7 12.6 %collective-permute-done.1.refs_8_.refs_10_ = bf16[8,1,2,32,256]{4,3,2,1,0:T(8,128)(2,1)S(1)} collective-permute-done((bf16[8,1,2,32,256]{4,3,2,1,0:T(8,128)(2,1)S(1)}, bf16[8,1,2,32,256]{4,3,2,1,0:T(8,128)(2,1)S(1)}, u32[]{:S(2)}, u32[]{:S(2)}) %collective-permute-start.1) | collective-permute-done | bytes 262176 | tf_op jit(solution)/shard_map/ppermute | solution.py:83
  57.9 2.3 pad_maximum_fusion
  61.1 4.6 %all-to-all-start.2 = ((bf16[32,96,256]{2,1,0:T(8,128)(2,1)}), bf16[32,96,256]{2,1,0:T(8,128)(2,1)S(1)}, u32[]{:S(2)}, u32[]{:S(2)}) async-start(bf16[32,96,256]{2,1,0:T(8,128)(2,1)} %pad_maximum_fusion), calls=%async_computation.2 | async-start | bytes 3145728 | tf_op jit(solution)/shard_map/all_to_all | solution.py:87
  65.7 1.8 collective-permute-start.6
  70.0 16.2 %collective-permute-done.10.refs_12_.refs_14_ = bf16[8,1,2,32,256]{4,3,2,1,0:T(8,128)(2,1)} collective-permute-done((bf16[8,1,2,32,256]{4,3,2,1,0:T(8,128)(2,1)S(1)}, bf16[8,1,2,32,256]{4,3,2,1,0:T(8,128)(2,1)}, u32[]{:S(2)}, u32[]{:S(2)}) %collective-permute-start.10) | collective-permute-done | bytes 262176 | tf_op jit(solution)/shard_map/ppermute | solution.py:83
  86.3 2.1 collective-permute-start.12
  94.5 2.3 pad_maximum_fusion.1
  96.8 11.1 %collective-permute-done.12.refs_14_.refs_16_ = bf16[8,1,2,32,256]{4,3,2,1,0:T(8,128)(2,1)} collective-permute-done((bf16[8,1,2,32,256]{4,3,2,1,0:T(8,128)(2,1)}, bf16[8,1,2,32,256]{4,3,2,1,0:T(8,128)(2,1)}, u32[]{:S(2)}, u32[]{:S(2)}) %collective-permute-start.12) | collective-permute-done | bytes 262176 | tf_op jit(solution)/shard_map/ppermute | solution.py:83
  109.1 4.7 %all-to-all-start.4 = ((bf16[32,96,256]{2,1,0:T(8,128)(2,1)}), bf16[32,96,256]{2,1,0:T(8,128)(2,1)S(1)}, u32[]{:S(2)}, u32[]{:S(2)}) async-start(bf16[32,96,256]{2,1,0:T(8,128)(2,1)} %pad_maximum_fusion.1), calls=%async_computation.4 | async-start | bytes 3145728 | tf_op jit(solution)/shard_map/all_to_all | solution.py:87
  115.0 2.0 collective-permute-done.8.refs_9_.refs_11_
  117.4 2.4 collective-permute-done.9.refs_11_.refs_13_
  122.1 17.3 %shard_map.109 = (bf16[8,4,96,256]{3,2,1,0:T(8,128)(2,1)}, bf16[2,4,4,64,512]{4,3,2,1,0:T(8,128)(2,1)}, bf16[2,4,256,512]{3,2,1,0:T(8,128)(2,1)}, bf16[2,4,256,5...) custom-call(s32[2]{0:T(128)} %pad_add_fusion.seat_ref, ...), custom_call_target="tpu_custom_call" | custom-call | flops 3221225472 | bytes 24117252 | tf_op jit(solution)/shard_map/pallas_call | solution.py:323
  139.4 12.1 %all-to-all-done.4 = bf16[32,96,256]{2,1,0:T(8,128)(2,1)S(1)} async-done(((bf16[32,96,256]{2,1,0:T(8,128)(2,1)}), bf16[32,96,256]{2,1,0:T(8,128)(2,1)S(1)}, u32[]{:S(2)}, u32[]{:S(2)}) %all-to-all-start.4) | async-done | bytes 1572896 | tf_op jit(solution)/shard_map/all_to_all | solution.py:87
  152.6 4.0 %all-to-all-start.3 = ((bf16[32,96,256]{2,1,0:T(8,128)(2,1)}), bf16[32,96,256]{2,1,0:T(8,128)(2,1)S(1)}, u32[]{:S(2)}, u32[]{:S(2)}) async-start(bf16[32,96,256]{2,1,0:T(8,128)(2,1)} %bitcast.178), calls=%async_computation.3 | async-start | bytes 3145728 | tf_op jit(solution)/shard_map/all_to_all | solution.py:87
  156.6 18.2 %shard_map.110 = (bf16[8,4,96,256]{3,2,1,0:T(8,128)(2,1)}, bf16[2,8,2,4,32,256]{5,4,3,2,1,0:T(8,128)(2,1)}, bf16[8,2,4,32,256]{4,3,2,1,0:T(8,128)(2,1)}, bf16[8,...) custom-call(s32[2]{0:T(128)} %pad_add_fusion.seat_ref, ...), custom_call_target="tpu_custom_call" | custom-call | flops 6442450944 | bytes 34078724 | tf_op jit(solution)/shard_map/pallas_call | solution.py:323
  176.1 3.8 %collective-permute-done.15 = bf16[8,4,32,256]{3,2,1,0:T(8,128)(2,1)S(1)} collective-permute-done((bf16[8,4,32,256]{3,2,1,0:T(8,128)(2,1)}, bf16[8,4,32,256]{3,2,1,0:T(8,128)(2,1)S(1)}, u32[]{:S(2)}, u32[]{:S(2)}) %collective-permute-start.15) | collective-permute-done | bytes 524320 | tf_op jit(solution)/shard_map/ppermute | solution.py:83
  180.7 2.5 fusion.2
  183.2 1.8 collective-permute-start.16
  188.6 10.8 %collective-permute-done.16 = bf16[8,4,32,256]{3,2,1,0:T(8,128)(2,1)S(1)} collective-permute-done((bf16[8,4,32,256]{3,2,1,0:T(8,128)(2,1)S(1)}, bf16[8,4,32,256]{3,2,1,0:T(8,128)(2,1)S(1)}, u32[]{:S(2)}, u32[]{:S(2)}) %collective-permute-start.16) | collective-permute-done | bytes 524320 | tf_op jit(solution)/shard_map/ppermute | solution.py:83
  199.4 2.4 add_convert_fusion.4
  203.1 4.7 %all-to-all-start.5 = ((bf16[32,96,256]{2,1,0:T(8,128)(2,1)}), bf16[32,96,256]{2,1,0:T(8,128)(2,1)S(1)}, u32[]{:S(2)}, u32[]{:S(2)}) async-start(bf16[32,96,256]{2,1,0:T(8,128)(2,1)} %bitcast.177), calls=%async_computation.5 | async-start | bytes 3145728 | tf_op jit(solution)/shard_map/all_to_all | solution.py:87
  211.8 24.3 %collective-permute-done.23 = bf16[8,4,32,256]{3,2,1,0:T(8,128)(2,1)S(1)} collective-permute-done((bf16[8,4,32,256]{3,2,1,0:T(8,128)(2,1)}, bf16[8,4,32,256]{3,2,1,0:T(8,128)(2,1)S(1)}, u32[]{:S(2)}, u32[]{:S(2)}) %collective-permute-start.23) | collective-permute-done | bytes 524320 | tf_op jit(solution)/shard_map/ppermute | solution.py:83
  238.5 11.5 %collective-permute-done.20 = bf16[4,2,4,32,256]{4,3,2,1,0:T(8,128)(2,1)S(1)} collective-permute-done((bf16[4,2,4,32,256]{4,3,2,1,0:T(8,128)(2,1)}, bf16[4,2,4,32,256]{4,3,2,1,0:T(8,128)(2,1)S(1)}, u32[]{:S(2)}, u32[]{:S(2)}) %collective-permute-start.20) | collective-permute-done | bytes 524320 | tf_op jit(solution)/shard_map/ppermute | solution.py:83
  251.5 5.5 %all-to-all-start.6 = ((bf16[8,3,4,32,256]{4,3,2,1,0:T(8,128)(2,1)}), bf16[8,3,4,32,256]{4,3,2,1,0:T(8,128)(2,1)}, u32[]{:S(2)}, u32[]{:S(2)}) async-start(bf16[8,3,4,32,256]{4,3,2,1,0:T(8,128)(2,1)} %pad_maximum_fusion.2), calls=%async_computation.6 | async-start | bytes 3145728 | tf_op jit(solution)/shard_map/all_to_all | solution.py:87
  259.9 2.6 copy.102
  264.5 1.7 copy.103
  266.2 28.1 %all-to-all-done.6 = bf16[8,3,4,32,256]{4,3,2,1,0:T(8,128)(2,1)} async-done(((bf16[8,3,4,32,256]{4,3,2,1,0:T(8,128)(2,1)}), bf16[8,3,4,32,256]{4,3,2,1,0:T(8,128)(2,1)}, u32[]{:S(2)}, u32[]{:S(2)}) %all-to-all-start.6) | async-done | bytes 1572896 | tf_op jit(solution)/shard_map/all_to_all | solution.py:87
  294.3 1.8 convert.7
  (137 shorter events, 52.2 us)
Async XLA Ops:
  3.0 27.6 %all-to-all-start = ((bf16[8,3,2,32,256]{4,3,2,1,0:T(8,128)(2,1)}), bf16[8,3,2,32,256]{4,3,2,1,0:T(8,128)(2,1)S(1)}, u32[]{:S(2)}, u32[]{:S(2)}) async-start(bf16[8,3,2,32,256]{4,3,2,1,0:T(8,128)(2,1)} %maximum_maximum_fusion.1), calls=%async_computation | async-start | bytes 1572864 | tf_op jit(solution)/shard_map/all_to_all | solution.py:87
  30.6 29.6 %all-to-all-start.1 = ((bf16[8,3,2,32,256]{4,3,2,1,0:T(8,128)(2,1)}), bf16[8,3,2,32,256]{4,3,2,1,0:T(8,128)(2,1)S(1)}, u32[]{:S(2)}, u32[]{:S(2)}) async-start(bf16[8,3,2,32,256]{4,3,2,1,0:T(8,128)(2,1)} %maximum_maximum_fusion), calls=%async_computation.1 | async-start | bytes 1572864 | tf_op jit(solution)/shard_map/all_to_all | solution.py:87
  34.1 26.1 %collective-permute-start = (bf16[8,3,2,32,256]{4,3,2,1,0:T(8,128)(2,1)S(1)}, bf16[8,3,2,32,256]{4,3,2,1,0:T(8,128)(2,1)}, u32[]{:S(2)}, u32[]{:S(2)}) collective-permute-start(bf16[8,3,2,32,256]{4,3,2,1,0:T(8,128)(2,1)S(1)} %all-to-all-done.refs_0_.refs_2_), channel_id=1, source_target_pairs={{0,2},{1,3},{2,0},{3,1},{4,6},{5,7},{6,4},{7,5},{8,10},{9,11},{10,... | collective-permute-start | bytes 2359304 | tf_op jit(solution)/shard_map/ppermute | solution.py:83
  35.7 14.6 %collective-permute-start.1 = (bf16[8,1,2,32,256]{4,3,2,1,0:T(8,128)(2,1)S(1)}, bf16[8,1,2,32,256]{4,3,2,1,0:T(8,128)(2,1)S(1)}, u32[]{:S(2)}, u32[]{:S(2)}) collective-permute-start(bf16[8,1,2,32,256]{4,3,2,1,0:T(8,128)(2,1)S(1)} %slice.221), channel_id=1, source_target_pairs={{0,4},{4,0},{8,12},{12,8},{16,20},{20,16},{24,28},{28,24},{1,5},{5... | collective-permute-start | bytes 786440 | tf_op jit(solution)/shard_map/ppermute | solution.py:83
  50.3 9.8 %collective-permute-start.2 = (bf16[8,1,2,32,256]{4,3,2,1,0:T(8,128)(2,1)S(1)}, bf16[8,1,2,32,256]{4,3,2,1,0:T(8,128)(2,1)}, u32[]{:S(2)}, u32[]{:S(2)}) collective-permute-start(bf16[8,1,2,32,256]{4,3,2,1,0:T(8,128)(2,1)S(1)} %collective-permute-done.1.refs_8_.refs_10_), channel_id=1, source_target_pairs={{0,2},{1,3},{2,0},{3,1},{4,6},{5,7},{6,4},{7,5},{8,10},{9,11},{10,... | collective-permute-start | bytes 786440 | tf_op jit(solution)/shard_map/ppermute | solution.py:83
  61.1 46.9 %all-to-all-start.2 = ((bf16[32,96,256]{2,1,0:T(8,128)(2,1)}), bf16[32,96,256]{2,1,0:T(8,128)(2,1)S(1)}, u32[]{:S(2)}, u32[]{:S(2)}) async-start(bf16[32,96,256]{2,1,0:T(8,128)(2,1)} %pad_maximum_fusion), calls=%async_computation.2 | async-start | bytes 3145728 | tf_op jit(solution)/shard_map/all_to_all | solution.py:87
  65.7 42.3 %collective-permute-start.6 = (bf16[8,3,2,32,256]{4,3,2,1,0:T(8,128)(2,1)}, bf16[8,3,2,32,256]{4,3,2,1,0:T(8,128)(2,1)}, u32[]{:S(2)}, u32[]{:S(2)}) collective-permute-start(bf16[8,3,2,32,256]{4,3,2,1,0:T(8,128)(2,1)} %copy-done.5), channel_id=1, source_target_pairs={{0,2},{1,3},{2,0},{3,1},{4,6},{5,7},{6,4},{7,5},{8,10},{9,11},{10,... | collective-permute-start | bytes 2359304 | tf_op jit(solution)/shard_map/ppermute | solution.py:83
  68.5 17.8 %collective-permute-start.10 = (bf16[8,1,2,32,256]{4,3,2,1,0:T(8,128)(2,1)S(1)}, bf16[8,1,2,32,256]{4,3,2,1,0:T(8,128)(2,1)}, u32[]{:S(2)}, u32[]{:S(2)}) collective-permute-start(bf16[8,1,2,32,256]{4,3,2,1,0:T(8,128)(2,1)S(1)} %slice.222), channel_id=1, source_target_pairs={{0,4},{4,0},{8,12},{12,8},{16,20},{20,16},{24,28},{28,24},{1,5},{5... | collective-permute-start | bytes 786440 | tf_op jit(solution)/shard_map/ppermute | solution.py:83
  86.3 21.7 %collective-permute-start.12 = (bf16[8,1,2,32,256]{4,3,2,1,0:T(8,128)(2,1)}, bf16[8,1,2,32,256]{4,3,2,1,0:T(8,128)(2,1)}, u32[]{:S(2)}, u32[]{:S(2)}) collective-permute-start(bf16[8,1,2,32,256]{4,3,2,1,0:T(8,128)(2,1)} %collective-permute-done.10.refs_12_.refs_14_), channel_id=1, source_target_pairs={{0,2},{1,3},{2,0},{3,1},{4,6},{5,7},{6,4},{7,5},{8,10},{9,11},{10,... | collective-permute-start | bytes 786440 | tf_op jit(solution)/shard_map/ppermute | solution.py:83
  109.1 42.3 %all-to-all-start.4 = ((bf16[32,96,256]{2,1,0:T(8,128)(2,1)}), bf16[32,96,256]{2,1,0:T(8,128)(2,1)S(1)}, u32[]{:S(2)}, u32[]{:S(2)}) async-start(bf16[32,96,256]{2,1,0:T(8,128)(2,1)} %pad_maximum_fusion.1), calls=%async_computation.4 | async-start | bytes 3145728 | tf_op jit(solution)/shard_map/all_to_all | solution.py:87
  113.9 6.1 %collective-permute-start.3 = (bf16[8,3,2,32,256]{4,3,2,1,0:T(8,128)(2,1)}, bf16[8,3,2,32,256]{4,3,2,1,0:T(8,128)(2,1)S(1)}, u32[]{:S(2)}, u32[]{:S(2)}) collective-permute-start(bf16[8,3,2,32,256]{4,3,2,1,0:T(8,128)(2,1)} %copy-done.4), channel_id=1, source_target_pairs={{0,1},{1,0},{2,3},{3,2},{4,5},{5,4},{6,7},{7,6},{8,9},{9,8},{10,11... | collective-permute-start | bytes 2359304 | tf_op jit(solution)/shard_map/ppermute | solution.py:83
  114.0 3.0 %collective-permute-start.8 = (bf16[8,1,2,32,256]{4,3,2,1,0:T(8,128)(2,1)S(1)}, bf16[8,1,2,32,256]{4,3,2,1,0:T(8,128)(2,1)S(1)}, u32[]{:S(2)}, u32[]{:S(2)}) collective-permute-start(bf16[8,1,2,32,256]{4,3,2,1,0:T(8,128)(2,1)S(1)} %collective-permute-done.1.refs_8_.refs_10_), channel_id=1, source_target_pairs={{0,1},{1,0},{2,3},{3,2},{4,5},{5,4},{6,7},{7,6},{8,9},{9,8},{10,11... | collective-permute-start | bytes 786440 | tf_op jit(solution)/shard_map/ppermute | solution.py:83
  114.4 6.5 %collective-permute-start.4 = (bf16[8,3,2,32,256]{4,3,2,1,0:T(8,128)(2,1)}, bf16[8,3,2,32,256]{4,3,2,1,0:T(8,128)(2,1)S(1)}, u32[]{:S(2)}, u32[]{:S(2)}) collective-permute-start(bf16[8,3,2,32,256]{4,3,2,1,0:T(8,128)(2,1)} %collective-permute-done.refs_2_.refs_4_), channel_id=1, source_target_pairs={{0,1},{1,0},{2,3},{3,2},{4,5},{5,4},{6,7},{7,6},{8,9},{9,8},{10,11... | collective-permute-start | bytes 2359304 | tf_op jit(solution)/shard_map/ppermute | solution.py:83
  114.5 7.5 %collective-permute-start.5 = (bf16[8,3,2,32,256]{4,3,2,1,0:T(8,128)(2,1)}, bf16[8,3,2,32,256]{4,3,2,1,0:T(8,128)(2,1)}, u32[]{:S(2)}, u32[]{:S(2)}) collective-permute-start(bf16[8,3,2,32,256]{4,3,2,1,0:T(8,128)(2,1)} %copy-done.5), channel_id=1, source_target_pairs={{0,1},{1,0},{2,3},{3,2},{4,5},{5,4},{6,7},{7,6},{8,9},{9,8},{10,11... | collective-permute-start | bytes 2359304 | tf_op jit(solution)/shard_map/ppermute | solution.py:83
  115.0 7.1 %collective-permute-start.7 = (bf16[8,3,2,32,256]{4,3,2,1,0:T(8,128)(2,1)}, bf16[8,3,2,32,256]{4,3,2,1,0:T(8,128)(2,1)}, u32[]{:S(2)}, u32[]{:S(2)}) collective-permute-start(bf16[8,3,2,32,256]{4,3,2,1,0:T(8,128)(2,1)} %collective-permute-done.6.refs_6_.refs_8_), channel_id=1, source_target_pairs={{0,1},{1,0},{2,3},{3,2},{4,5},{5,4},{6,7},{7,6},{8,9},{9,8},{10,11... | collective-permute-start | bytes 2359304 | tf_op jit(solution)/shard_map/ppermute | solution.py:83
  117.1 2.8 collective-permute-start.9
  119.8 1.9 collective-permute-start.11
  120.0 2.1 collective-permute-start.13
  152.6 50.5 %all-to-all-start.3 = ((bf16[32,96,256]{2,1,0:T(8,128)(2,1)}), bf16[32,96,256]{2,1,0:T(8,128)(2,1)S(1)}, u32[]{:S(2)}, u32[]{:S(2)}) async-start(bf16[32,96,256]{2,1,0:T(8,128)(2,1)} %bitcast.178), calls=%async_computation.3 | async-start | bytes 3145728 | tf_op jit(solution)/shard_map/all_to_all | solution.py:87
  174.8 10.3 %collective-permute-start.17 = (bf16[8,2,4,32,256]{4,3,2,1,0:T(8,128)(2,1)}, bf16[8,2,4,32,256]{4,3,2,1,0:T(8,128)(2,1)S(1)}, u32[]{:S(2)}, u32[]{:S(2)}) collective-permute-start(bf16[8,2,4,32,256]{4,3,2,1,0:T(8,128)(2,1)} %get-tuple-element.47), channel_id=1, source_target_pairs={{0,1},{1,0},{2,3},{3,2},{4,5},{5,4},{6,7},{7,6},{8,9},{9,8},{10,11... | collective-permute-start | bytes 3145736 | tf_op jit(solution)/shard_map/ppermute | solution.py:83
  175.1 9.9 %collective-permute-start.18 = (bf16[8,2,4,32,256]{4,3,2,1,0:T(8,128)(2,1)}, bf16[8,2,4,32,256]{4,3,2,1,0:T(8,128)(2,1)S(1)}, u32[]{:S(2)}, u32[]{:S(2)}) collective-permute-start(bf16[8,2,4,32,256]{4,3,2,1,0:T(8,128)(2,1)} %get-tuple-element.48), channel_id=1, source_target_pairs={{0,1},{1,0},{2,3},{3,2},{4,5},{5,4},{6,7},{7,6},{8,9},{9,8},{10,11... | collective-permute-start | bytes 3145736 | tf_op jit(solution)/shard_map/ppermute | solution.py:83
  175.3 4.6 %collective-permute-start.15 = (bf16[8,4,32,256]{3,2,1,0:T(8,128)(2,1)}, bf16[8,4,32,256]{3,2,1,0:T(8,128)(2,1)S(1)}, u32[]{:S(2)}, u32[]{:S(2)}) collective-permute-start(bf16[8,4,32,256]{3,2,1,0:T(8,128)(2,1)} %get-tuple-element.45), channel_id=1, source_target_pairs={{0,1},{1,0},{2,3},{3,2},{4,5},{5,4},{6,7},{7,6},{8,9},{9,8},{10,11... | collective-permute-start | bytes 1572872 | tf_op jit(solution)/shard_map/ppermute | solution.py:83
  175.6 5.1 %collective-permute-start.22 = (bf16[8,4,32,256]{3,2,1,0:T(8,128)(2,1)}, bf16[8,4,32,256]{3,2,1,0:T(8,128)(2,1)S(1)}, u32[]{:S(2)}, u32[]{:S(2)}) collective-permute-start(bf16[8,4,32,256]{3,2,1,0:T(8,128)(2,1)} %get-tuple-element.52), channel_id=1, source_target_pairs={{0,1},{1,0},{2,3},{3,2},{4,5},{5,4},{6,7},{7,6},{8,9},{9,8},{10,11... | collective-permute-start | bytes 1572872 | tf_op jit(solution)/shard_map/ppermute | solution.py:83
  175.9 12.7 %collective-permute-start.14 = (bf16[8,4,32,256]{3,2,1,0:T(8,128)(2,1)}, bf16[8,4,32,256]{3,2,1,0:T(8,128)(2,1)S(1)}, u32[]{:S(2)}, u32[]{:S(2)}) collective-permute-start(bf16[8,4,32,256]{3,2,1,0:T(8,128)(2,1)} %get-tuple-element.44), channel_id=1, source_target_pairs={{0,1},{1,0},{2,3},{3,2},{4,5},{5,4},{6,7},{7,6},{8,9},{9,8},{10,11... | collective-permute-start | bytes 1572872 | tf_op jit(solution)/shard_map/ppermute | solution.py:83
  183.2 16.2 %collective-permute-start.16 = (bf16[8,4,32,256]{3,2,1,0:T(8,128)(2,1)S(1)}, bf16[8,4,32,256]{3,2,1,0:T(8,128)(2,1)S(1)}, u32[]{:S(2)}, u32[]{:S(2)}) collective-permute-start(bf16[8,4,32,256]{3,2,1,0:T(8,128)(2,1)S(1)} %get-tuple-element.83), channel_id=1, source_target_pairs={{0,4},{4,0},{8,12},{12,8},{16,20},{20,16},{24,28},{28,24},{1,5},{5... | collective-permute-start | bytes 1572872 | tf_op jit(solution)/shard_map/ppermute | solution.py:83
  187.1 15.0 %collective-permute-start.19 = (bf16[4,2,4,32,256]{4,3,2,1,0:T(8,128)(2,1)S(1)}, bf16[4,2,4,32,256]{4,3,2,1,0:T(8,128)(2,1)S(1)}, u32[]{:S(2)}, u32[]{:S(2)}) collective-permute-start(bf16[4,2,4,32,256]{4,3,2,1,0:T(8,128)(2,1)S(1)} %get-tuple-element.87), channel_id=1, source_target_pairs={{0,2},{1,3},{2,0},{3,1},{4,6},{5,7},{6,4},{7,5},{8,10},{9,11},{10,... | collective-permute-start | bytes 1572872 | tf_op jit(solution)/shard_map/ppermute | solution.py:83
  203.1 48.4 %all-to-all-start.5 = ((bf16[32,96,256]{2,1,0:T(8,128)(2,1)}), bf16[32,96,256]{2,1,0:T(8,128)(2,1)S(1)}, u32[]{:S(2)}, u32[]{:S(2)}) async-start(bf16[32,96,256]{2,1,0:T(8,128)(2,1)} %bitcast.177), calls=%async_computation.5 | async-start | bytes 3145728 | tf_op jit(solution)/shard_map/all_to_all | solution.py:87
  207.8 4.0 %collective-permute-start.21 = (bf16[8,4,32,256]{3,2,1,0:T(8,128)(2,1)}, bf16[8,4,32,256]{3,2,1,0:T(8,128)(2,1)S(1)}, u32[]{:S(2)}, u32[]{:S(2)}) collective-permute-start(bf16[8,4,32,256]{3,2,1,0:T(8,128)(2,1)} %get-tuple-element.51), channel_id=1, source_target_pairs={{0,1},{1,0},{2,3},{3,2},{4,5},{5,4},{6,7},{7,6},{8,9},{9,8},{10,11... | collective-permute-start | bytes 1572872 | tf_op jit(solution)/shard_map/ppermute | solution.py:83
  208.1 28.0 %collective-permute-start.23 = (bf16[8,4,32,256]{3,2,1,0:T(8,128)(2,1)}, bf16[8,4,32,256]{3,2,1,0:T(8,128)(2,1)S(1)}, u32[]{:S(2)}, u32[]{:S(2)}) collective-permute-start(bf16[8,4,32,256]{3,2,1,0:T(8,128)(2,1)} %get-tuple-element.82), channel_id=1, source_target_pairs={{0,4},{4,0},{8,12},{12,8},{16,20},{20,16},{24,28},{28,24},{1,5},{5... | collective-permute-start | bytes 1572872 | tf_op jit(solution)/shard_map/ppermute | solution.py:83
  209.8 27.3 %collective-permute-start.24 = (bf16[8,4,32,256]{3,2,1,0:T(8,128)(2,1)}, bf16[8,4,32,256]{3,2,1,0:T(8,128)(2,1)S(1)}, u32[]{:S(2)}, u32[]{:S(2)}) collective-permute-start(bf16[8,4,32,256]{3,2,1,0:T(8,128)(2,1)} %add_convert_fusion.4), channel_id=1, source_target_pairs={{0,2},{1,3},{2,0},{3,1},{4,6},{5,7},{6,4},{7,5},{8,10},{9,11},{10,... | collective-permute-start | bytes 1572872 | tf_op jit(solution)/shard_map/ppermute | solution.py:83
  211.3 38.7 %collective-permute-start.20 = (bf16[4,2,4,32,256]{4,3,2,1,0:T(8,128)(2,1)}, bf16[4,2,4,32,256]{4,3,2,1,0:T(8,128)(2,1)S(1)}, u32[]{:S(2)}, u32[]{:S(2)}) collective-permute-start(bf16[4,2,4,32,256]{4,3,2,1,0:T(8,128)(2,1)} %get-tuple-element.50), channel_id=1, source_target_pairs={{0,2},{1,3},{2,0},{3,1},{4,6},{5,7},{6,4},{7,5},{8,10},{9,11},{10,... | collective-permute-start | bytes 1572872 | tf_op jit(solution)/shard_map/ppermute | solution.py:83
  251.5 42.8 %all-to-all-start.6 = ((bf16[8,3,4,32,256]{4,3,2,1,0:T(8,128)(2,1)}), bf16[8,3,4,32,256]{4,3,2,1,0:T(8,128)(2,1)}, u32[]{:S(2)}, u32[]{:S(2)}) async-start(bf16[8,3,4,32,256]{4,3,2,1,0:T(8,128)(2,1)} %pad_maximum_fusion.2), calls=%async_computation.6 | async-start | bytes 3145728 | tf_op jit(solution)/shard_map/all_to_all | solution.py:87
  (22 other events, 286.7 us)

commit v9 on v8

--- a/solution.py
+++ b/solution.py
@@ -1,3 +1,4 @@
+import functools
 import math
 
 import jax
@@ -139,28 +140,28 @@
     return pl.ds(r * (part // 2), part // 2)
 
 
-def weight_of(slot, w, v):
+def weight_of(slot, w, v, shared):
     def get(m, which, r):
         if slot == 0:
             return square(w[which // 2][m][:, r, which % 2])
         ref = w[which // 2][m] if r == 0 else v[which // 2][m]
-        return square(ref[:, 2 if r == 0 else 0, which % 2])
+        return square(ref[:, shared if r == 0 else 0, which % 2])
 
     return get
 
 
-def wide_weight(slot, w, e_ref, y):
+def wide_weight(slot, w, e_ref, y, ndp):
     def get(m, r):
         if slot == 0:
-            return square(w[1][m][half_src(e_ref.shape[1], r), :2, 1])
-        return square(e_ref[m, half_src(e_ref.shape[1], r ^ y)])
+            return square(w[1][m][half_src(ndp, r), :2, 1])
+        return square(e_ref[m, half_src(ndp, r ^ y)])
 
     return get
 
 
-def join_halves(w, v, e_ref, y):
+def join_halves(w, v, e_ref, y, shared):
     for m in range(4):
-        e_ref[m, :, y] = w[1][m][:, 2, 1]
+        e_ref[m, :, y] = w[1][m][:, shared, 1]
         e_ref[m, :, 1 - y] = v[1][m][:, 0, 1]
 
 
@@ -174,10 +175,10 @@
     ndp, nb, all_rows, _ = x_ref.shape
     own_rows = 2 * all_rows // 3
     f, y = seat_ref[0], seat_ref[1]
-    join_halves(w, v, e_ref, y)
+    join_halves(w, v, e_ref, y, 2)
     for slot, (lo, hi) in enumerate(((0, own_rows), (own_rows, all_rows))):
         perm, active, slope, ret = saved[slot]
-        weight, wide = weight_of(slot, w, v), wide_weight(slot, w, e_ref, y)
+        weight, wide = weight_of(slot, w, v, 2), wide_weight(slot, w, e_ref, y, ndp)
         count = ndp * (hi - lo)
         tiles = (nb, BLK // nb, count)
         for m in range(nb):
@@ -226,108 +227,131 @@
 
 
 BACKWARD_ORDER = (
-    (1, 6, 21, 7, 8, 9, 2, 18, 19, 20, 3, 4, 5, 0) + tuple(range(14, 18)) + (25,) + tuple(range(10, 14)) + (22, 23, 24)
+    (1, 6, 13, 7, 8, 9, 2, 10, 11, 12, 3, 4, 5, 0),
+    (1, 6, 14, 7, 15, 8, 16, 9, 17, 21, 2, 18, 19, 20, 3, 4, 5, 10, 11, 12, 13, 0, 22),
 )
 
 
-def backward_kernel(seat_ref, *refs):
-    count_in = len(BACKWARD_ORDER)
-    sources, refs = refs[:count_in], refs[count_in:]
-    results, refs = refs[:9], refs[9:]
+def backward_kernel(slot, seat_ref, *refs):
+    order = BACKWARD_ORDER[slot]
+    count_in, count_out = len(order), 6 if slot else 4
+    sources, refs = list(refs[:count_in]), refs[count_in:]
+    results, refs = refs[:count_out], refs[count_out:]
     targets, refs = refs[:count_in], refs[count_in:]
-    staged, refs = refs[:5], refs[5:]
-    scratch, (e_ref, in_sems, out_sems) = (refs[:2], refs[2:4]), refs[4:]
-    streamed = Streamed(sources, targets, in_sems, BACKWARD_ORDER)
-    at = [Lookup(streamed, range(i, i + 4)) for i in range(2, 26, 4)]
-    w, v, saved = at[:2], at[2:4], at[4:]
-    gin_ref, own_keep, own_send, mid_keep, mid_send = staged
+    (gin_ref, keep, send_ref, mid, spread), refs = refs[:5], refs[5:]
+    e_ref = refs[0] if slot else None
+    in_sems, out_sems = refs[-2:]
+
+    ndp, nb, all_rows, _ = sources[0].shape
+    lo, hi = (2 * all_rows // 3, all_rows) if slot else (0, 2 * all_rows // 3)
+    for i in range(2):
+        sources[i] = sources[i].at[:, :, lo:hi]
+    for i in range(2, 10):
+        sources[i] = sources[i].at[:, 2:] if slot else sources[i].at[:, :2]
+    streamed = Streamed(sources, targets, in_sems, order)
+    at = [Lookup(streamed, range(i, i + 4)) for i in range(2, 22, 4)]
+    w, v = at[:2], at[2:4] if slot else None
+    perm, active, slope, ret = (
+        functools.partial(streamed.get, (18 if slot else 10) + i) for i in range(4)
+    )
     sent = []
 
     def send(source, target):
         sent.append(pltpu.make_async_copy(source, target, out_sems.at[len(sent)]))
         sent[-1].start()
 
-    ndp, nb, all_rows, _ = targets[0].shape
-    own_rows = 2 * all_rows // 3
-    rows = BLK // ndp
+    rows, half = BLK // ndp, ndp // 2
     f, y = seat_ref[0], seat_ref[1]
 
-    def store(slot, m, which, r, part):
-        ref = ((own_keep, own_send), (mid_keep, mid_send))[slot][m % 2]
+    def store(m, which, r, part):
+        ref = (keep, send_ref)[m % 2]
+        part = part.astype(jnp.bfloat16).reshape(ndp, rows, BLK)
         if slot == 0:
-            ref[m // 2, :, r, which] = part.astype(jnp.bfloat16).reshape(ndp, rows, BLK)
+            ref[m // 2, :, r, which] = part
         else:
-            ref[r, m // 2, :, which] = part.astype(jnp.bfloat16).reshape(ndp, rows, BLK)
-
-    def store_wide(slot, m, r, part):
-        ref = ((own_keep, own_send), (mid_keep, mid_send))[slot][m % 2]
-        part = part.astype(jnp.bfloat16).reshape(ndp // 2, 2, rows, BLK)
+            ref[r, m // 2, :, which] = part
+
+    def store_wide(m, r, part):
+        ref = (keep, send_ref)[m % 2]
+        part = part.astype(jnp.bfloat16).reshape(half, 2, rows, BLK)
         if slot == 0:
             ref[m // 2, half_src(ndp, r), :, 3] = part
         else:
             ref[y, m // 2, half_src(ndp, r ^ y), 3] = part[:, 0]
             ref[1 - y, m // 2, half_src(ndp, r ^ y), 3] = part[:, 1]
 
-    for slot, (lo, hi) in enumerate(((0, own_rows), (own_rows, all_rows))):
-        perm, active, slope, ret = range(4)
-        mid, spread = scratch[slot]
-        if slot == 1:
-            join_halves(w, v, e_ref, y)
-        weight, wide = weight_of(slot, w, v), wide_weight(slot, w, e_ref, y)
-        count = ndp * (hi - lo)
-        tiles = (nb, BLK // nb, count)
-        for m in range(nb):
-            d = f ^ m
-            g = streamed.get(1)[:, d, lo:hi, :].reshape(count, BLK)
-            for r in range(2):
-                mid[r, :, d] = dot(wide(m, r), g, 1, 1).astype(jnp.bfloat16).reshape(tiles)
-                store_wide(slot, m, r, dot(saved[slot][ret][r, d].reshape(BLK, count), g, 1, 0))
-        for m in range(nb):
-            s = f ^ m
-            for r in range(2):
-                p = saved[slot][perm][r, s].reshape(BLK, count)
-                back_mid = mid[r, s].reshape(BLK, count)
-                back = dot(weight(m, 2, r), back_mid, 1, 0)
-                back = (back * saved[slot][slope][r, s].astype(jnp.float32)).astype(jnp.bfloat16)
-                store(slot, m, 2, r, dot(saved[slot][active][r, s], back_mid, 1, 1))
-                store(slot, m, 1, r, dot(p, back, 1, 1))
-                first = dot(weight(m, 1, r), back, 1, 0).astype(jnp.bfloat16)
-                spread[r, :, s] = first.reshape(tiles)
-        for m in range(nb):
-            d = f ^ m
-            x = streamed.get(0)[:, d, lo:hi, :].reshape(count, BLK)
-            total = 0.0
-            for r in range(2):
-                back = spread[r, d].reshape(BLK, count)
-                total = total + dot(back, weight(m, 0, r), 0, 1)
-                store(slot, m, 0, r, dot(x, back, 0, 1))
-            gin_ref[:, d, lo:hi, :] = total.astype(jnp.bfloat16).reshape(ndp, hi - lo, BLK)
-        if slot == 0:
-            send(own_keep, results[1])
-            send(own_send.at[0], results[2])
-            send(own_send.at[1], results[3])
-    send(mid_keep, results[4])
-    for i in range(4):
-        send(mid_send.at[i // 2, i % 2], results[5 + i])
-    send(gin_ref, results[0])
+    if slot:
+        join_halves(w, v, e_ref, y, 0)
+    weight, wide = weight_of(slot, w, v, 0), wide_weight(slot, w, e_ref, y, ndp)
+    count = ndp * (hi - lo)
+    tiles = (nb, BLK // nb, count)
+    for m in range(nb):
+        d = f ^ m
+        g = streamed.get(1)[:, d].reshape(count, BLK)
+        for r in range(2):
+            mid[r, :, d] = dot(wide(m, r), g, 1, 1).astype(jnp.bfloat16).reshape(tiles)
+            store_wide(m, r, dot(ret()[r, d].reshape(BLK, count), g, 1, 0))
+    for m in range(nb):
+        s = f ^ m
+        for r in range(2):
+            p = perm()[r, s].reshape(BLK, count)
+            back_mid = mid[r, s].reshape(BLK, count)
+            back = dot(weight(m, 2, r), back_mid, 1, 0)
+            back = (back * slope()[r, s].astype(jnp.float32)).astype(jnp.bfloat16)
+            store(m, 2, r, dot(active()[r, s], back_mid, 1, 1))
+            store(m, 1, r, dot(p, back, 1, 1))
+            first = dot(weight(m, 1, r), back, 1, 0).astype(jnp.bfloat16)
+            spread[r, :, s] = first.reshape(tiles)
+    for m in range(nb):
+        d = f ^ m
+        x = streamed.get(0)[:, d].reshape(count, BLK)
+        total = 0.0
+        for r in range(2):
+            back = spread[r, d].reshape(BLK, count)
+            total = total + dot(back, weight(m, 0, r), 0, 1)
+            store(m, 0, r, dot(x, back, 0, 1))
+        gin_ref[:, d] = total.astype(jnp.bfloat16).reshape(ndp, hi - lo, BLK)
+    send(keep, results[1])
+    if slot == 0:
+        send(send_ref.at[0], results[2])
+        send(send_ref.at[1], results[3])
+        send(gin_ref, results[0])
+    else:
+        for i in range(4):
+            send(send_ref.at[i // 2, i % 2], results[2 + i])
+        send(streamed.get(22), results[0].at[:, :, :lo])
+        send(gin_ref, results[0].at[:, :, lo:])
     for copy in sent:
         copy.wait()
 
 
-def on_chip(kernel, products, outs, scratch, inputs, results=None):
-    streamed = results is not None
-    space = pl.ANY if streamed else pltpu.VMEM
-    staged = [x.shape for x in inputs[1:]] + outs if streamed else []
-    outs = results or outs
-    sems = [pltpu.SemaphoreType.DMA((n,)) for n in (len(inputs) - 1, len(outs))]
+def grads_kernel(got_ref, a_ref, b_ref, c_ref, e_ref):
+    pairs = got_ref.shape[0] // 2
+    rows = got_ref.shape[3]
+    for which, ref in enumerate((a_ref, b_ref, c_ref, e_ref)):
+        for place in range(6):
+            owner, part = ((0, 0), (0, 1), (0, 2), (1, 2), (1, 0), (1, 1))[place]
+            for i in range(pairs):
+                value = got_ref[2 * i + owner, part, which].astype(jnp.float32)
+                if which == 0:
+                    ref[3 * i + place // 2, :, (place % 2) * BLK : (place % 2 + 1) * BLK] = value
+                elif which == 3:
+                    ref[3 * i + place // 2, (place % 2) * rows : (place % 2 + 1) * rows, :] = value
+                else:
+                    ref[6 * i + place] = value
+
+
+def on_chip(kernel, products, outs, scratch, inputs, targets=None):
+    space = pltpu.VMEM if targets is None else pl.ANY
+    sems = [pltpu.SemaphoreType.DMA((n,)) for n in (len(inputs) - 1, len(outs) + 1)]
     return pl.pallas_call(
         kernel,
         out_shape=[jax.ShapeDtypeStruct(shape, jnp.bfloat16) for shape in outs],
         in_specs=[pl.BlockSpec(memory_space=pltpu.SMEM)]
         + [pl.BlockSpec(memory_space=space)] * (len(inputs) - 1),
         out_specs=[pl.BlockSpec(memory_space=space)] * len(outs),
-        scratch_shapes=[pltpu.VMEM(shape, jnp.bfloat16) for shape in staged + scratch]
-        + (sems if streamed else []),
+        scratch_shapes=[pltpu.VMEM(shape, jnp.bfloat16) for shape in (targets or []) + scratch]
+        + (sems if targets else []),
         cost_estimate=pl.CostEstimate(
             flops=products * 2 * BLK * BLK,
             transcendentals=0,
@@ -350,14 +374,14 @@
     def deal(first, second):
         return jnp.stack([deal_weight(first), deal_weight(second)], axis=2)
 
-    def halves(w):
-        swapped = xor_permute(w[:, 2:], 1, "dp")
-        return w, xor_permute(w, 2), swapped, xor_permute(swapped, 2)
-
-    ab = halves(exchange(deal(dealt_a, weight_b), "dp"))
-    ce = halves(exchange(after(deal(weight_c, dealt_e), ab[0]), "dp"))
-    x = exchange(after(deal_tokens(tokens), ce[0], ab[1], ab[3]), everyone)
-    g = exchange(after(deal_tokens(grad_out), x, ce[1], ce[3]), everyone).reshape(shape)
+    def with_halves(w):
+        across = xor_permute(w, 2)
+        return (w, across) + tuple(xor_permute(part[:, 2:], 1, "dp") for part in (w, across))
+
+    ab = with_halves(exchange(deal(dealt_a, weight_b), "dp"))
+    ce = with_halves(exchange(after(deal(weight_c, dealt_e), ab[0]), "dp"))
+    x = exchange(after(deal_tokens(tokens), ce[0], *ab[1:]), everyone)
+    g = exchange(after(deal_tokens(grad_out), x, *ce[1:]), everyone).reshape(shape)
     x = x.reshape(shape)
     weights = gather_bfly(*ab[:2]) + gather_bfly(*ce[:2])
     weights += gather_bfly(*ab[2:]) + gather_bfly(*ce[2:])
@@ -374,45 +398,47 @@
     )
     out = exchange(out.reshape(ndp * nb, -1, BLK), everyone)
     own_shape, mid_shape = (2, ndp, 2, 4, rows, BLK), (2, 2, ndp, 4, rows, BLK)
-    gin, own_keep, *sends = on_chip(
-        backward_kernel,
-        8 * products,
-        [x.shape, own_shape, own_shape, mid_shape, mid_shape],
-        [saved[0], saved[0], saved[4], saved[4], halves],
-        [seat, x, g] + weights + kept,
-        [x.shape, own_shape] + [own_shape[1:]] * 2 + [mid_shape] + [mid_shape[2:]] * 4,
-    )
-    mid_keep = sends.pop(2)
-    far = add(mid_keep[1, 1], xor_permute(sends[5], 1))
-    own_far = add(own_keep[1], xor_permute(sends[1], 1))
-    far = add(add(mid_keep[0, 1], xor_permute(sends[3], 1)), xor_permute(far, 1, "dp"))
-    own_near = add(own_keep[0], xor_permute(sends[0], 1))
-    near = add(mid_keep[1, 0], xor_permute(sends[4], 1))
+    weight_shape = (ndp, 1, 2, rows, BLK)
+    own_rows, mid_rows = ((ndp, nb, t // ndp, BLK) for t in (own, mid))
+    gin, own_keep, *own_sends = on_chip(
+        functools.partial(backward_kernel, 0),
+        16 * nb * own,
+        [own_rows, own_shape] + [own_shape[1:]] * 2,
+        [own_rows, own_shape, own_shape] + [saved[0]] * 2,
+        [seat, x, g] + weights[:8] + kept[:4],
+        [own_rows] * 2 + [(ndp, 2) + weight_shape[2:]] * 8 + saved[:4],
+    )
+    gin, mid_keep, *mid_sends = on_chip(
+        functools.partial(backward_kernel, 1),
+        16 * nb * mid,
+        [x.shape, mid_shape] + [mid_shape[2:]] * 4,
+        [mid_rows, mid_shape, mid_shape] + [saved[4]] * 2 + [halves],
+        [seat, x, g] + weights + kept[4:] + [gin],
+        [mid_rows] * 2 + [weight_shape] * 16 + saved[4:] + [own_rows],
+    )
+    own_far = add(own_keep[1], xor_permute(own_sends[1], 1))
+    far = add(mid_keep[1, 1], after(xor_permute(mid_sends[3], 1), own_far))
+    far = add(add(mid_keep[0, 1], xor_permute(mid_sends[1], 1)), xor_permute(far, 1, "dp"))
+    own_near = add(own_keep[0], xor_permute(own_sends[0], 1))
+    near = add(mid_keep[1, 0], xor_permute(mid_sends[2], 1))
     part = ndp // 2
     own_first = add(own_near[:part], xor_permute(own_far[:part], 2))
     gin = exchange(after(gin.reshape(ndp * nb, -1, BLK), out, far, own_first), everyone)
     own_last = add(own_near[part:], xor_permute(after(own_far[part:], own_first), 2))
     own = jnp.concatenate([own_first, own_last], axis=0)
     near = xor_permute(near, 1, "dp")
-    near = add(add(mid_keep[0, 0], xor_permute(sends[2], 1)), near)
+    near = add(add(mid_keep[0, 0], xor_permute(mid_sends[0], 1)), near)
     mid = add(near, xor_permute(far, 2))
     dealt = jnp.concatenate([own, mid[:, None]], axis=1)
-    got = exchange(after(dealt, gin), "dp").astype(jnp.float32)
-    got = got.reshape(ndp // 2, 2, 3, 4, rows, BLK)
-
-    def own_rows(which):
-        mid = jnp.stack([got[:, 0, 2, which], got[:, 1, 2, which]], axis=1)
-        return jnp.stack([got[:, 0, :2, which], mid, got[:, 1, :2, which]], axis=1)
-
-    grad_a = own_rows(0).reshape(blocks, 2, rows, BLK).transpose(0, 2, 1, 3)
-    return (
-        undeal_tokens(out, count),
-        undeal_tokens(gin, count),
-        grad_a.reshape(weight_a.shape),
-        own_rows(1).reshape(weight_b.shape),
-        own_rows(2).reshape(weight_c.shape),
-        own_rows(3).reshape(weight_e.shape),
-    )
+    got = exchange(after(dealt, gin), "dp")
+    grads = pl.pallas_call(
+        grads_kernel,
+        out_shape=[
+            jax.ShapeDtypeStruct(w.shape, jnp.float32)
+            for w in (weight_a, weight_b, weight_c, weight_e)
+        ],
+    )(got)
+    return (undeal_tokens(out, count), undeal_tokens(gin, count), *grads)
 
 
 def per_device(tokens, grad_out, weight_a, weight_b, weight_c, weight_e):

time: 302 us -> 305 us (level)
  Pallas kernels: 35.5 us -> 43.5 us
  waiting for transfers between devices: 157 us -> 162 us
  other arithmetic: 19.6 us -> 14.8 us
  local copies, waits for them, and re-layouts: 31.7 us -> 28 us
    pallas_call x2 -> x3, Pallas kernels: 35.5 us -> 40.4 us  [on_chip(): pl.pallas_call(kernel, out_shape=[jax.ShapeDtypeStruct(shape, jnp.bfloat1...]
    ppermute x25, waiting for transfers between devices: 97.9 us -> 103 us  [xor_permute(): lax.ppermute(x, axis, [(i, i ^ mask) for i in range(lax.axis_size(axis))])]
    another operation x5 -> x0, local copies, waits for them, and re-layouts: 3.16 us -> none  [the longest x4 3.05 us: own_rows(): return jnp.stack([got[:, 0, :2, which], mid, got[:, 1, :2, which]], axis=1)]
    pallas_call x0 -> x1, Pallas kernels: none -> 3.12 us  [token_plan(): pl.pallas_call(grads_kernel, out_shape=[jax.ShapeDtypeStruct(w.shape, jnp...]
    unnamed x44 -> x46, local copies, waits for them, and re-layouts: 10.9 us -> 11.1 us
  transfers between devices with their start and end apart: 32 -> 32, of which waited for: 17 -> 13; matrix products, arithmetic and copies ran while one was open for 13% -> 12% of each run, Pallas kernels for 12% -> 13%
where the time goes in v9:
time: 305 us; the launch traced here: 304 us
  waiting for transfers between devices  162 us (53%)
  starting transfers between devices  54.6 us (18%)
  Pallas kernels  43.5 us (14%)
  local copies, waits for them, and re-layouts  28 us (9%)
  other arithmetic  14.8 us (5%)
    ppermute x25, waiting for transfers between devices, xor_permute(): lax.ppermute(x, axis, [(i, i ^ mask) for i in range(lax.axis_size(axis))])  103 us
    all_to_all x7, waiting for transfers between devices, exchange(): return lax.all_to_all(x, axes, split_axis=0, concat_axis=0, tiled=True)  59.7 us
    pallas_call x3, Pallas kernels, on_chip(): pl.pallas_call(kernel, out_shape=[jax.ShapeDtypeStruct(shape, jnp.bfloat1...  40.4 us
    all_to_all x7, starting transfers between devices, exchange(): return lax.all_to_all(x, axes, split_axis=0, concat_axis=0, tiled=True)  34.6 us
    ppermute x25, starting transfers between devices, xor_permute(): lax.ppermute(x, axis, [(i, i ^ mask) for i in range(lax.axis_size(axis))])  20 us
    unnamed x46, local copies, waits for them, and re-layouts  11.1 us
  transfers between devices with their start and end apart: 32, of which 13 were waited for; matrix products, arithmetic and copies ran while one was open for 12% of the time, Pallas kernels for 13%

profile of v9, /device:TPU:0, one launch (start us, length us, event | category | flops | bytes accessed | tf_op | source)
XLA Modules:
  0.0 304.3 jit_solution(12126350928564005830)
XLA Ops:
  3.0 7.4 %all-to-all-start = ((bf16[8,3,2,32,256]{4,3,2,1,0:T(8,128)(2,1)}), bf16[8,3,2,32,256]{4,3,2,1,0:T(8,128)(2,1)S(1)}, u32[]{:S(2)}, u32[]{:S(2)}) async-start(bf16[8,3,2,32,256]{4,3,2,1,0:T(8,128)(2,1)} %maximum_maximum_fusion.1), calls=%async_computation | async-start | bytes 1572864 | tf_op jit(solution)/shard_map/all_to_all | solution.py:88
  11.5 19.1 %all-to-all-done.refs_0_.refs_2_ = bf16[8,3,2,32,256]{4,3,2,1,0:T(8,128)(2,1)S(1)} async-done(((bf16[8,3,2,32,256]{4,3,2,1,0:T(8,128)(2,1)}), bf16[8,3,2,32,256]{4,3,2,1,0:T(8,128)(2,1)S(1)}, u32[]{:S(2)}, u32[]{:S(2)}) %all-to-all-start) | async-done | bytes 786464 | tf_op jit(solution)/shard_map/all_to_all | solution.py:88
  30.6 3.6 %all-to-all-start.1 = ((bf16[8,3,2,32,256]{4,3,2,1,0:T(8,128)(2,1)}), bf16[8,3,2,32,256]{4,3,2,1,0:T(8,128)(2,1)S(1)}, u32[]{:S(2)}, u32[]{:S(2)}) async-start(bf16[8,3,2,32,256]{4,3,2,1,0:T(8,128)(2,1)} %maximum_maximum_fusion), calls=%async_computation.1 | async-start | bytes 1572864 | tf_op jit(solution)/shard_map/all_to_all | solution.py:88
  36.4 2.0 collective-permute-start.1
  38.4 14.9 %collective-permute-done.refs_2_.refs_4_ = bf16[8,3,2,32,256]{4,3,2,1,0:T(8,128)(2,1)S(1)} collective-permute-done((bf16[8,3,2,32,256]{4,3,2,1,0:T(8,128)(2,1)S(1)}, bf16[8,3,2,32,256]{4,3,2,1,0:T(8,128)(2,1)S(1)}, u32[]{:S(2)}, u32[]{:S(2)}) %collective-permute-start) | collective-permute-done | bytes 786464 | tf_op jit(solution)/shard_map/ppermute | solution.py:84
  54.3 1.7 collective-permute-start.2
  56.0 1.7 copy.37
  61.8 5.3 %all-to-all-start.2 = ((bf16[32,96,256]{2,1,0:T(8,128)(2,1)}), bf16[32,96,256]{2,1,0:T(8,128)(2,1)S(1)}, u32[]{:S(2)}, u32[]{:S(2)}) async-start(bf16[32,96,256]{2,1,0:T(8,128)(2,1)} %pad_maximum_fusion), calls=%async_computation.2 | async-start | bytes 3145728 | tf_op jit(solution)/shard_map/all_to_all | solution.py:88
  67.1 1.8 collective-permute-start.6
  71.1 32.5 %collective-permute-done.6.refs_6_.refs_8_ = bf16[8,3,2,32,256]{4,3,2,1,0:T(8,128)(2,1)S(1)} collective-permute-done((bf16[8,3,2,32,256]{4,3,2,1,0:T(8,128)(2,1)S(1)}, bf16[8,3,2,32,256]{4,3,2,1,0:T(8,128)(2,1)S(1)}, u32[]{:S(2)}, u32[]{:S(2)}) %collective-permute-start.6) | collective-permute-done | bytes 786464 | tf_op jit(solution)/shard_map/ppermute | solution.py:84
  106.1 1.7 copy.46
  112.3 2.3 pad_maximum_fusion.1
  115.8 3.9 %all-to-all-start.4 = ((bf16[32,96,256]{2,1,0:T(8,128)(2,1)}), bf16[32,96,256]{2,1,0:T(8,128)(2,1)S(1)}, u32[]{:S(2)}, u32[]{:S(2)}) async-start(bf16[32,96,256]{2,1,0:T(8,128)(2,1)} %pad_maximum_fusion.1), calls=%async_computation.4 | async-start | bytes 3145728 | tf_op jit(solution)/shard_map/all_to_all | solution.py:88
  120.8 2.3 collective-permute-done.8.refs_9_.refs_11_
  124.0 1.6 collective-permute-done.9.refs_11_.refs_13_
  127.5 17.3 %shard_map.109 = (bf16[8,4,96,256]{3,2,1,0:T(8,128)(2,1)}, bf16[2,4,4,64,512]{4,3,2,1,0:T(8,128)(2,1)}, bf16[2,4,256,512]{3,2,1,0:T(8,128)(2,1)}, bf16[2,4,256,5...) custom-call(s32[2]{0:T(128)} %pad_add_fusion.seat_ref, ...), custom_call_target="tpu_custom_call" | custom-call | flops 3221225472 | bytes 24117252 | tf_op jit(solution)/shard_map/pallas_call | solution.py:347
  144.8 12.5 %all-to-all-done.4 = bf16[32,96,256]{2,1,0:T(8,128)(2,1)S(1)} async-done(((bf16[32,96,256]{2,1,0:T(8,128)(2,1)}), bf16[32,96,256]{2,1,0:T(8,128)(2,1)S(1)}, u32[]{:S(2)}, u32[]{:S(2)}) %all-to-all-start.4) | async-done | bytes 1572896 | tf_op jit(solution)/shard_map/all_to_all | solution.py:88
  158.5 4.0 %all-to-all-start.3 = ((bf16[32,96,256]{2,1,0:T(8,128)(2,1)}), bf16[32,96,256]{2,1,0:T(8,128)(2,1)S(1)}, u32[]{:S(2)}, u32[]{:S(2)}) async-start(bf16[32,96,256]{2,1,0:T(8,128)(2,1)} %bitcast.101), calls=%async_computation.3 | async-start | bytes 3145728 | tf_op jit(solution)/shard_map/all_to_all | solution.py:88
  162.4 12.4 %shard_map.110 = (bf16[8,4,64,256]{3,2,1,0:T(8,128)(2,1)}, bf16[2,8,2,4,32,256]{5,4,3,2,1,0:T(8,128)(2,1)}, bf16[8,2,4,32,256]{4,3,2,1,0:T(8,128)(2,1)}, bf16[8,2,4,32,256]{4,3,2,1,0:T(8,128)(2,1)}) custom-call(s32[2]{0:T(128)} %pad_add_fusion.seat_ref, bf16[8,4,96,256]{3,2,1,0:T(8,128)(2,1)} %bitcast.82, bf16[8,4,96,256]{3,2,1,0:T(8,128)(2,1)} %bitcast.84, ...), custom_call_target="tpu_custom_call" | custom-call | flops 4294967296 | bytes 23068676 | tf_op jit(solution)/shard_map/pallas_call | solution.py:347
  175.4 10.7 %shard_map.111 = (bf16[8,4,96,256]{3,2,1,0:T(8,128)(2,1)}, bf16[2,2,8,4,32,256]{5,4,3,2,1,0:T(8,128)(2,1)}, bf16[8,4,32,256]{3,2,1,0:T(8,128)(2,1)}, bf16[8,4,32...) custom-call(s32[2]{0:T(128)} %pad_add_fusion.seat_ref, ...), custom_call_target="tpu_custom_call" | custom-call | flops 2147483648 | bytes 22544388 | tf_op jit(solution)/shard_map/pallas_call | solution.py:347
  188.9 1.7 collective-permute-start.19
  193.2 11.9 %collective-permute-done.19 = bf16[4,2,4,32,256]{4,3,2,1,0:T(8,128)(2,1)S(1)} collective-permute-done((bf16[4,2,4,32,256]{4,3,2,1,0:T(8,128)(2,1)S(1)}, bf16[4,2,4,32,256]{4,3,2,1,0:T(8,128)(2,1)S(1)}, u32[]{:S(2)}, u32[]{:S(2)}) %collective-permute-start.19) | collective-permute-done | bytes 524320 | tf_op jit(solution)/shard_map/ppermute | solution.py:84
  208.3 5.1 %all-to-all-start.5 = ((bf16[32,96,256]{2,1,0:T(8,128)(2,1)}), bf16[32,96,256]{2,1,0:T(8,128)(2,1)S(1)}, u32[]{:S(2)}, u32[]{:S(2)}) async-start(bf16[32,96,256]{2,1,0:T(8,128)(2,1)} %bitcast.100), calls=%async_computation.5 | async-start | bytes 3145728 | tf_op jit(solution)/shard_map/all_to_all | solution.py:88
  213.4 1.8 collective-permute-start.20
  217.3 25.5 %collective-permute-done.20 = bf16[4,2,4,32,256]{4,3,2,1,0:T(8,128)(2,1)S(1)} collective-permute-done((bf16[4,2,4,32,256]{4,3,2,1,0:T(8,128)(2,1)}, bf16[4,2,4,32,256]{4,3,2,1,0:T(8,128)(2,1)S(1)}, u32[]{:S(2)}, u32[]{:S(2)}) %collective-permute-start.20) | collective-permute-done | bytes 524320 | tf_op jit(solution)/shard_map/ppermute | solution.py:84
  244.0 11.6 %collective-permute-done.24 = bf16[8,4,32,256]{3,2,1,0:T(8,128)(2,1)S(1)} collective-permute-done((bf16[8,4,32,256]{3,2,1,0:T(8,128)(2,1)}, bf16[8,4,32,256]{3,2,1,0:T(8,128)(2,1)S(1)}, u32[]{:S(2)}, u32[]{:S(2)}) %collective-permute-start.24) | collective-permute-done | bytes 524320 | tf_op jit(solution)/shard_map/ppermute | solution.py:84
  258.3 5.5 %all-to-all-start.6 = ((bf16[8,3,4,32,256]{4,3,2,1,0:T(8,128)(2,1)}), bf16[8,3,4,32,256]{4,3,2,1,0:T(8,128)(2,1)}, u32[]{:S(2)}, u32[]{:S(2)}) async-start(bf16[8,3,4,32,256]{4,3,2,1,0:T(8,128)(2,1)} %pad_maximum_fusion.2), calls=%async_computation.6 | async-start | bytes 3145728 | tf_op jit(solution)/shard_map/all_to_all | solution.py:88
  265.1 1.6 copy.45
  266.7 2.6 copy.51
  271.3 1.7 copy.52
  273.0 28.1 %all-to-all-done.6.got_ref = bf16[8,3,4,32,256]{4,3,2,1,0:T(8,128)(2,1)} async-done(((bf16[8,3,4,32,256]{4,3,2,1,0:T(8,128)(2,1)}), bf16[8,3,4,32,256]{4,3,2,1,0:T(8,128)(2,1)}, u32[]{:S(2)}, u32[]{:S(2)}) %all-to-all-start.6) | async-done | bytes 1572896 | tf_op jit(solution)/shard_map/all_to_all | solution.py:88
  301.2 3.1 %shard_map.112 = (f32[12,32,512]{2,1,0:T(8,128)}, f32[24,32,256]{2,1,0:T(8,128)}, f32[24,32,256]{2,1,0:T(8,128)}, f32[12,64,256]{2,1,0:T(8,128)}) custom-call(bf16[8,3,4,32,256]{4,3,2,1,0:T(8,128)(2,1)} %all-to-all-done.6.got_ref), custom_call_target="tpu_custom_call" | custom-call | tf_op jit(solution)/shard_map/pallas_call | solution.py:434
  (129 shorter events, 44.4 us)
Async XLA Ops:
  3.0 27.6 %all-to-all-start = ((bf16[8,3,2,32,256]{4,3,2,1,0:T(8,128)(2,1)}), bf16[8,3,2,32,256]{4,3,2,1,0:T(8,128)(2,1)S(1)}, u32[]{:S(2)}, u32[]{:S(2)}) async-start(bf16[8,3,2,32,256]{4,3,2,1,0:T(8,128)(2,1)} %maximum_maximum_fusion.1), calls=%async_computation | async-start | bytes 1572864 | tf_op jit(solution)/shard_map/all_to_all | solution.py:88
  30.6 31.2 %all-to-all-start.1 = ((bf16[8,3,2,32,256]{4,3,2,1,0:T(8,128)(2,1)}), bf16[8,3,2,32,256]{4,3,2,1,0:T(8,128)(2,1)S(1)}, u32[]{:S(2)}, u32[]{:S(2)}) async-start(bf16[8,3,2,32,256]{4,3,2,1,0:T(8,128)(2,1)} %maximum_maximum_fusion), calls=%async_computation.1 | async-start | bytes 1572864 | tf_op jit(solution)/shard_map/all_to_all | solution.py:88
  34.1 19.2 %collective-permute-start = (bf16[8,3,2,32,256]{4,3,2,1,0:T(8,128)(2,1)S(1)}, bf16[8,3,2,32,256]{4,3,2,1,0:T(8,128)(2,1)S(1)}, u32[]{:S(2)}, u32[]{:S(2)}) collective-permute-start(bf16[8,3,2,32,256]{4,3,2,1,0:T(8,128)(2,1)S(1)} %all-to-all-done.refs_0_.refs_2_), channel_id=1, source_target_pairs={{0,2},{1,3},{2,0},{3,1},{4,6},{5,7},{6,4},{7,5},{8,10},{9,11},{10,... | collective-permute-start | bytes 2359304 | tf_op jit(solution)/shard_map/ppermute | solution.py:84
  36.4 25.4 %collective-permute-start.1 = (bf16[8,1,2,32,256]{4,3,2,1,0:T(8,128)(2,1)}, bf16[8,1,2,32,256]{4,3,2,1,0:T(8,128)(2,1)S(1)}, u32[]{:S(2)}, u32[]{:S(2)}) collective-permute-start(bf16[8,1,2,32,256]{4,3,2,1,0:T(8,128)(2,1)} %slice.165), channel_id=1, source_target_pairs={{0,4},{4,0},{8,12},{12,8},{16,20},{20,16},{24,28},{28,24},{1,5},{5... | collective-permute-start | bytes 786440 | tf_op jit(solution)/shard_map/ppermute | solution.py:84
  54.3 7.5 %collective-permute-start.2 = (bf16[8,1,2,32,256]{4,3,2,1,0:T(8,128)(2,1)}, bf16[8,1,2,32,256]{4,3,2,1,0:T(8,128)(2,1)}, u32[]{:S(2)}, u32[]{:S(2)}) collective-permute-start(bf16[8,1,2,32,256]{4,3,2,1,0:T(8,128)(2,1)} %slice.166), channel_id=1, source_target_pairs={{0,4},{4,0},{8,12},{12,8},{16,20},{20,16},{24,28},{28,24},{1,5},{5... | collective-permute-start | bytes 786440 | tf_op jit(solution)/shard_map/ppermute | solution.py:84
  61.8 52.8 %all-to-all-start.2 = ((bf16[32,96,256]{2,1,0:T(8,128)(2,1)}), bf16[32,96,256]{2,1,0:T(8,128)(2,1)S(1)}, u32[]{:S(2)}, u32[]{:S(2)}) async-start(bf16[32,96,256]{2,1,0:T(8,128)(2,1)} %pad_maximum_fusion), calls=%async_computation.2 | async-start | bytes 3145728 | tf_op jit(solution)/shard_map/all_to_all | solution.py:88
  67.1 36.6 %collective-permute-start.6 = (bf16[8,3,2,32,256]{4,3,2,1,0:T(8,128)(2,1)S(1)}, bf16[8,3,2,32,256]{4,3,2,1,0:T(8,128)(2,1)S(1)}, u32[]{:S(2)}, u32[]{:S(2)}) collective-permute-start(bf16[8,3,2,32,256]{4,3,2,1,0:T(8,128)(2,1)S(1)} %all-to-all-done.1.refs_4_.refs_6_), channel_id=1, source_target_pairs={{0,2},{1,3},{2,0},{3,1},{4,6},{5,7},{6,4},{7,5},{8,10},{9,11},{10,... | collective-permute-start | bytes 2359304 | tf_op jit(solution)/shard_map/ppermute | solution.py:84
  69.7 45.0 %collective-permute-start.10 = (bf16[8,1,2,32,256]{4,3,2,1,0:T(8,128)(2,1)}, bf16[8,1,2,32,256]{4,3,2,1,0:T(8,128)(2,1)}, u32[]{:S(2)}, u32[]{:S(2)}) collective-permute-start(bf16[8,1,2,32,256]{4,3,2,1,0:T(8,128)(2,1)} %slice.167), channel_id=1, source_target_pairs={{0,4},{4,0},{8,12},{12,8},{16,20},{20,16},{24,28},{28,24},{1,5},{5... | collective-permute-start | bytes 786440 | tf_op jit(solution)/shard_map/ppermute | solution.py:84
  104.7 9.9 %collective-permute-start.12 = (bf16[8,1,2,32,256]{4,3,2,1,0:T(8,128)(2,1)}, bf16[8,1,2,32,256]{4,3,2,1,0:T(8,128)(2,1)}, u32[]{:S(2)}, u32[]{:S(2)}) collective-permute-start(bf16[8,1,2,32,256]{4,3,2,1,0:T(8,128)(2,1)} %slice.168), channel_id=1, source_target_pairs={{0,4},{4,0},{8,12},{12,8},{16,20},{20,16},{24,28},{28,24},{1,5},{5... | collective-permute-start | bytes 786440 | tf_op jit(solution)/shard_map/ppermute | solution.py:84
  115.8 41.5 %all-to-all-start.4 = ((bf16[32,96,256]{2,1,0:T(8,128)(2,1)}), bf16[32,96,256]{2,1,0:T(8,128)(2,1)S(1)}, u32[]{:S(2)}, u32[]{:S(2)}) async-start(bf16[32,96,256]{2,1,0:T(8,128)(2,1)} %pad_maximum_fusion.1), calls=%async_computation.4 | async-start | bytes 3145728 | tf_op jit(solution)/shard_map/all_to_all | solution.py:88
  119.7 3.6 %collective-permute-start.3 = (bf16[8,3,2,32,256]{4,3,2,1,0:T(8,128)(2,1)}, bf16[8,3,2,32,256]{4,3,2,1,0:T(8,128)(2,1)S(1)}, u32[]{:S(2)}, u32[]{:S(2)}) collective-permute-start(bf16[8,3,2,32,256]{4,3,2,1,0:T(8,128)(2,1)} %copy-done.2), channel_id=1, source_target_pairs={{0,1},{1,0},{2,3},{3,2},{4,5},{5,4},{6,7},{7,6},{8,9},{9,8},{10,11... | collective-permute-start | bytes 2359304 | tf_op jit(solution)/shard_map/ppermute | solution.py:84
  119.8 6.6 %collective-permute-start.4 = (bf16[8,3,2,32,256]{4,3,2,1,0:T(8,128)(2,1)}, bf16[8,3,2,32,256]{4,3,2,1,0:T(8,128)(2,1)S(1)}, u32[]{:S(2)}, u32[]{:S(2)}) collective-permute-start(bf16[8,3,2,32,256]{4,3,2,1,0:T(8,128)(2,1)} %copy-done.6), channel_id=1, source_target_pairs={{0,1},{1,0},{2,3},{3,2},{4,5},{5,4},{6,7},{7,6},{8,9},{9,8},{10,11... | collective-permute-start | bytes 2359304 | tf_op jit(solution)/shard_map/ppermute | solution.py:84
  120.2 2.9 collective-permute-start.8
  120.3 6.5 %collective-permute-start.5 = (bf16[8,3,2,32,256]{4,3,2,1,0:T(8,128)(2,1)}, bf16[8,3,2,32,256]{4,3,2,1,0:T(8,128)(2,1)}, u32[]{:S(2)}, u32[]{:S(2)}) collective-permute-start(bf16[8,3,2,32,256]{4,3,2,1,0:T(8,128)(2,1)} %copy-done.3), channel_id=1, source_target_pairs={{0,1},{1,0},{2,3},{3,2},{4,5},{5,4},{6,7},{7,6},{8,9},{9,8},{10,11... | collective-permute-start | bytes 2359304 | tf_op jit(solution)/shard_map/ppermute | solution.py:84
  120.7 6.7 %collective-permute-start.7 = (bf16[8,3,2,32,256]{4,3,2,1,0:T(8,128)(2,1)}, bf16[8,3,2,32,256]{4,3,2,1,0:T(8,128)(2,1)}, u32[]{:S(2)}, u32[]{:S(2)}) collective-permute-start(bf16[8,3,2,32,256]{4,3,2,1,0:T(8,128)(2,1)} %copy-done.7), channel_id=1, source_target_pairs={{0,1},{1,0},{2,3},{3,2},{4,5},{5,4},{6,7},{7,6},{8,9},{9,8},{10,11... | collective-permute-start | bytes 2359304 | tf_op jit(solution)/shard_map/ppermute | solution.py:84
  123.1 2.5 collective-permute-start.9
  123.9 3.0 collective-permute-start.11
  125.6 1.9 collective-permute-start.13
  158.5 49.9 %all-to-all-start.3 = ((bf16[32,96,256]{2,1,0:T(8,128)(2,1)}), bf16[32,96,256]{2,1,0:T(8,128)(2,1)S(1)}, u32[]{:S(2)}, u32[]{:S(2)}) async-start(bf16[32,96,256]{2,1,0:T(8,128)(2,1)} %bitcast.101), calls=%async_computation.3 | async-start | bytes 3145728 | tf_op jit(solution)/shard_map/all_to_all | solution.py:88
  174.9 12.1 %collective-permute-start.16 = (bf16[8,2,4,32,256]{4,3,2,1,0:T(8,128)(2,1)}, bf16[8,2,4,32,256]{4,3,2,1,0:T(8,128)(2,1)S(1)}, u32[]{:S(2)}, u32[]{:S(2)}) collective-permute-start(bf16[8,2,4,32,256]{4,3,2,1,0:T(8,128)(2,1)} %get-tuple-element.54), channel_id=1, source_target_pairs={{0,1},{1,0},{2,3},{3,2},{4,5},{5,4},{6,7},{7,6},{8,9},{9,8},{10,11... | collective-permute-start | bytes 3145736 | tf_op jit(solution)/shard_map/ppermute | solution.py:84
  175.2 11.8 %collective-permute-start.18 = (bf16[8,2,4,32,256]{4,3,2,1,0:T(8,128)(2,1)}, bf16[8,2,4,32,256]{4,3,2,1,0:T(8,128)(2,1)S(1)}, u32[]{:S(2)}, u32[]{:S(2)}) collective-permute-start(bf16[8,2,4,32,256]{4,3,2,1,0:T(8,128)(2,1)} %get-tuple-element.56), channel_id=1, source_target_pairs={{0,1},{1,0},{2,3},{3,2},{4,5},{5,4},{6,7},{7,6},{8,9},{9,8},{10,11... | collective-permute-start | bytes 3145736 | tf_op jit(solution)/shard_map/ppermute | solution.py:84
  186.2 4.4 %collective-permute-start.15 = (bf16[8,4,32,256]{3,2,1,0:T(8,128)(2,1)}, bf16[8,4,32,256]{3,2,1,0:T(8,128)(2,1)S(1)}, u32[]{:S(2)}, u32[]{:S(2)}) collective-permute-start(bf16[8,4,32,256]{3,2,1,0:T(8,128)(2,1)} %get-tuple-element.52), channel_id=1, source_target_pairs={{0,1},{1,0},{2,3},{3,2},{4,5},{5,4},{6,7},{7,6},{8,9},{9,8},{10,11... | collective-permute-start | bytes 1572872 | tf_op jit(solution)/shard_map/ppermute | solution.py:84
  186.5 4.1 %collective-permute-start.22 = (bf16[8,4,32,256]{3,2,1,0:T(8,128)(2,1)}, bf16[8,4,32,256]{3,2,1,0:T(8,128)(2,1)S(1)}, u32[]{:S(2)}, u32[]{:S(2)}) collective-permute-start(bf16[8,4,32,256]{3,2,1,0:T(8,128)(2,1)} %get-tuple-element.60), channel_id=1, source_target_pairs={{0,1},{1,0},{2,3},{3,2},{4,5},{5,4},{6,7},{7,6},{8,9},{9,8},{10,11... | collective-permute-start | bytes 1572872 | tf_op jit(solution)/shard_map/ppermute | solution.py:84
  186.7 19.4 %collective-permute-start.14 = (bf16[8,4,32,256]{3,2,1,0:T(8,128)(2,1)}, bf16[8,4,32,256]{3,2,1,0:T(8,128)(2,1)S(1)}, u32[]{:S(2)}, u32[]{:S(2)}) collective-permute-start(bf16[8,4,32,256]{3,2,1,0:T(8,128)(2,1)} %get-tuple-element.51), channel_id=1, source_target_pairs={{0,1},{1,0},{2,3},{3,2},{4,5},{5,4},{6,7},{7,6},{8,9},{9,8},{10,11... | collective-permute-start | bytes 1572872 | tf_op jit(solution)/shard_map/ppermute | solution.py:84
  188.9 16.2 %collective-permute-start.19 = (bf16[4,2,4,32,256]{4,3,2,1,0:T(8,128)(2,1)S(1)}, bf16[4,2,4,32,256]{4,3,2,1,0:T(8,128)(2,1)S(1)}, u32[]{:S(2)}, u32[]{:S(2)}) collective-permute-start(bf16[4,2,4,32,256]{4,3,2,1,0:T(8,128)(2,1)S(1)} %get-tuple-element.83), channel_id=1, source_target_pairs={{0,2},{1,3},{2,0},{3,1},{4,6},{5,7},{6,4},{7,5},{8,10},{9,11},{10,... | collective-permute-start | bytes 1572872 | tf_op jit(solution)/shard_map/ppermute | solution.py:84
  191.8 15.5 %collective-permute-start.17 = (bf16[8,4,32,256]{3,2,1,0:T(8,128)(2,1)S(1)}, bf16[8,4,32,256]{3,2,1,0:T(8,128)(2,1)S(1)}, u32[]{:S(2)}, u32[]{:S(2)}) collective-permute-start(bf16[8,4,32,256]{3,2,1,0:T(8,128)(2,1)S(1)} %get-tuple-element.79), channel_id=1, source_target_pairs={{0,4},{4,0},{8,12},{12,8},{16,20},{20,16},{24,28},{28,24},{1,5},{5... | collective-permute-start | bytes 1572872 | tf_op jit(solution)/shard_map/ppermute | solution.py:84
  208.3 50.0 %all-to-all-start.5 = ((bf16[32,96,256]{2,1,0:T(8,128)(2,1)}), bf16[32,96,256]{2,1,0:T(8,128)(2,1)S(1)}, u32[]{:S(2)}, u32[]{:S(2)}) async-start(bf16[32,96,256]{2,1,0:T(8,128)(2,1)} %bitcast.100), calls=%async_computation.5 | async-start | bytes 3145728 | tf_op jit(solution)/shard_map/all_to_all | solution.py:88
  213.4 29.3 %collective-permute-start.20 = (bf16[4,2,4,32,256]{4,3,2,1,0:T(8,128)(2,1)}, bf16[4,2,4,32,256]{4,3,2,1,0:T(8,128)(2,1)S(1)}, u32[]{:S(2)}, u32[]{:S(2)}) collective-permute-start(bf16[4,2,4,32,256]{4,3,2,1,0:T(8,128)(2,1)} %get-tuple-element.58), channel_id=1, source_target_pairs={{0,2},{1,3},{2,0},{3,1},{4,6},{5,7},{6,4},{7,5},{8,10},{9,11},{10,... | collective-permute-start | bytes 1572872 | tf_op jit(solution)/shard_map/ppermute | solution.py:84
  215.2 28.7 %collective-permute-start.21 = (bf16[8,4,32,256]{3,2,1,0:T(8,128)(2,1)}, bf16[8,4,32,256]{3,2,1,0:T(8,128)(2,1)S(1)}, u32[]{:S(2)}, u32[]{:S(2)}) collective-permute-start(bf16[8,4,32,256]{3,2,1,0:T(8,128)(2,1)} %get-tuple-element.59), channel_id=1, source_target_pairs={{0,1},{1,0},{2,3},{3,2},{4,5},{5,4},{6,7},{7,6},{8,9},{9,8},{10,11... | collective-permute-start | bytes 1572872 | tf_op jit(solution)/shard_map/ppermute | solution.py:84
  215.2 28.7 %collective-permute-start.23 = (bf16[8,4,32,256]{3,2,1,0:T(8,128)(2,1)}, bf16[8,4,32,256]{3,2,1,0:T(8,128)(2,1)S(1)}, u32[]{:S(2)}, u32[]{:S(2)}) collective-permute-start(bf16[8,4,32,256]{3,2,1,0:T(8,128)(2,1)} %get-tuple-element.78), channel_id=1, source_target_pairs={{0,4},{4,0},{8,12},{12,8},{16,20},{20,16},{24,28},{28,24},{1,5},{5... | collective-permute-start | bytes 1572872 | tf_op jit(solution)/shard_map/ppermute | solution.py:84
  216.7 38.9 %collective-permute-start.24 = (bf16[8,4,32,256]{3,2,1,0:T(8,128)(2,1)}, bf16[8,4,32,256]{3,2,1,0:T(8,128)(2,1)S(1)}, u32[]{:S(2)}, u32[]{:S(2)}) collective-permute-start(bf16[8,4,32,256]{3,2,1,0:T(8,128)(2,1)} %add_convert_fusion.4), channel_id=1, source_target_pairs={{0,2},{1,3},{2,0},{3,1},{4,6},{5,7},{6,4},{7,5},{8,10},{9,11},{10,... | collective-permute-start | bytes 1572872 | tf_op jit(solution)/shard_map/ppermute | solution.py:84
  258.3 42.8 %all-to-all-start.6 = ((bf16[8,3,4,32,256]{4,3,2,1,0:T(8,128)(2,1)}), bf16[8,3,4,32,256]{4,3,2,1,0:T(8,128)(2,1)}, u32[]{:S(2)}, u32[]{:S(2)}) async-start(bf16[8,3,4,32,256]{4,3,2,1,0:T(8,128)(2,1)} %pad_maximum_fusion.2), calls=%async_computation.6 | async-start | bytes 3145728 | tf_op jit(solution)/shard_map/all_to_all | solution.py:88
  (23 other events, 236.1 us)

commit v10 on v8

--- a/solution.py
+++ b/solution.py
@@ -87,12 +87,11 @@
     return lax.all_to_all(x, axes, split_axis=0, concat_axis=0, tiled=True)
 
 
-def deal_weight(w):
+def weight_sets(w):
     pairs = lax.axis_size("dp") // 2
     sets = w.reshape(pairs, 3, 2, w.shape[1], w.shape[2])
     own = jnp.stack([sets[:, 0], sets[:, 2]], axis=1)
-    mid = sets[:, 1][:, :, None]
-    return jnp.concatenate([own, mid], axis=2).reshape((pairs * 2, 3) + sets.shape[3:])
+    return own.reshape((pairs * 2,) + own.shape[2:]), sets[:, 1].reshape(pairs * 2, *w.shape[1:])
 
 
 def gather_bfly(w, across):
@@ -139,29 +138,28 @@
     return pl.ds(r * (part // 2), part // 2)
 
 
-def weight_of(slot, w, v):
+def weight_of(slot, own, shared):
     def get(m, which, r):
         if slot == 0:
-            return square(w[which // 2][m][:, r, which % 2])
-        ref = w[which // 2][m] if r == 0 else v[which // 2][m]
-        return square(ref[:, 2 if r == 0 else 0, which % 2])
+            return square(own[which // 2][m][:, r, which % 2])
+        return square(shared[r][m][:, which])
 
     return get
 
 
-def wide_weight(slot, w, e_ref, y):
+def wide_weight(slot, own, e_ref, y):
     def get(m, r):
         if slot == 0:
-            return square(w[1][m][half_src(e_ref.shape[1], r), :2, 1])
+            return square(own[1][m][half_src(e_ref.shape[1], r), :, 1])
         return square(e_ref[m, half_src(e_ref.shape[1], r ^ y)])
 
     return get
 
 
-def join_halves(w, v, e_ref, y):
+def join_halves(shared, e_ref, y):
     for m in range(4):
-        e_ref[m, :, y] = w[1][m][:, 2, 1]
-        e_ref[m, :, 1 - y] = v[1][m][:, 0, 1]
+        e_ref[m, :, y] = shared[0][m][:, 3]
+        e_ref[m, :, 1 - y] = shared[1][m][:, 3]
 
 
 def weight_refs(refs):
@@ -174,7 +172,7 @@
     ndp, nb, all_rows, _ = x_ref.shape
     own_rows = 2 * all_rows // 3
     f, y = seat_ref[0], seat_ref[1]
-    join_halves(w, v, e_ref, y)
+    join_halves(v, e_ref, y)
     for slot, (lo, hi) in enumerate(((0, own_rows), (own_rows, all_rows))):
         perm, active, slope, ret = saved[slot]
         weight, wide = weight_of(slot, w, v), wide_weight(slot, w, e_ref, y)
@@ -272,7 +270,7 @@
         perm, active, slope, ret = range(4)
         mid, spread = scratch[slot]
         if slot == 1:
-            join_halves(w, v, e_ref, y)
+            join_halves(v, e_ref, y)
         weight, wide = weight_of(slot, w, v), wide_weight(slot, w, e_ref, y)
         count = ndp * (hi - lo)
         tiles = (nb, BLK // nb, count)
@@ -312,6 +310,22 @@
     send(gin_ref, results[0])
     for copy in sent:
         copy.wait()
+
+
+def grads_kernel(got_ref, a_ref, b_ref, c_ref, e_ref):
+    pairs = got_ref.shape[0] // 2
+    rows = got_ref.shape[3]
+    for which, ref in enumerate((a_ref, b_ref, c_ref, e_ref)):
+        for place in range(6):
+            owner, part = ((0, 0), (0, 1), (0, 2), (1, 2), (1, 0), (1, 1))[place]
+            for i in range(pairs):
+                value = got_ref[2 * i + owner, part, which].astype(jnp.float32)
+                if which == 0:
+                    ref[3 * i + place // 2, :, (place % 2) * BLK : (place % 2 + 1) * BLK] = value
+                elif which == 3:
+                    ref[3 * i + place // 2, (place % 2) * rows : (place % 2 + 1) * rows, :] = value
+                else:
+                    ref[6 * i + place] = value
 
 
 def on_chip(kernel, products, outs, scratch, inputs, results=None):
@@ -347,20 +361,19 @@
 
     everyone = ("dp", "bfly")
     shape = (ndp, nb, -1, BLK)
-    def deal(first, second):
-        return jnp.stack([deal_weight(first), deal_weight(second)], axis=2)
-
-    def halves(w):
-        swapped = xor_permute(w[:, 2:], 1, "dp")
-        return w, xor_permute(w, 2), swapped, xor_permute(swapped, 2)
-
-    ab = halves(exchange(deal(dealt_a, weight_b), "dp"))
-    ce = halves(exchange(after(deal(weight_c, dealt_e), ab[0]), "dp"))
-    x = exchange(after(deal_tokens(tokens), ce[0], ab[1], ab[3]), everyone)
-    g = exchange(after(deal_tokens(grad_out), x, ce[1], ce[3]), everyone).reshape(shape)
+    own, mid = zip(*(weight_sets(w) for w in (dealt_a, weight_b, weight_c, dealt_e)))
+    own_ab = jnp.stack(own[:2], axis=2).reshape(ndp, 4, rows, BLK)
+    first = exchange(jnp.concatenate([own_ab, jnp.stack(mid, axis=1)], axis=1), "dp")
+    ab, mid = first[:, :4].reshape(ndp, 2, 2, rows, BLK), first[:, 4:]
+    ce = exchange(after(jnp.stack(own[2:], axis=2), first), "dp")
+    mid_across, ab_across, ce_across = (xor_permute(part, 2) for part in (mid, ab, ce))
+    swapped, swapped_across = (xor_permute(part, 1, "dp") for part in (mid, mid_across))
+    x = exchange(after(deal_tokens(tokens), ce, mid_across, swapped), everyone)
+    g = after(deal_tokens(grad_out), x, ab_across, ce_across, swapped_across)
+    g = exchange(g, everyone).reshape(shape)
     x = x.reshape(shape)
-    weights = gather_bfly(*ab[:2]) + gather_bfly(*ce[:2])
-    weights += gather_bfly(*ab[2:]) + gather_bfly(*ce[2:])
+    weights = gather_bfly(ab, ab_across) + gather_bfly(ce, ce_across)
+    weights += gather_bfly(mid, mid_across) + gather_bfly(swapped, swapped_across)
 
     own, mid = count * ndp // nb, count * ndp // nb // 2
     saved = []
@@ -397,22 +410,15 @@
     near = add(add(mid_keep[0, 0], xor_permute(sends[2], 1)), near)
     mid = add(near, xor_permute(far, 2))
     dealt = jnp.concatenate([own, mid[:, None]], axis=1)
-    got = exchange(after(dealt, gin), "dp").astype(jnp.float32)
-    got = got.reshape(ndp // 2, 2, 3, 4, rows, BLK)
-
-    def own_rows(which):
-        mid = jnp.stack([got[:, 0, 2, which], got[:, 1, 2, which]], axis=1)
-        return jnp.stack([got[:, 0, :2, which], mid, got[:, 1, :2, which]], axis=1)
-
-    grad_a = own_rows(0).reshape(blocks, 2, rows, BLK).transpose(0, 2, 1, 3)
-    return (
-        undeal_tokens(out, count),
-        undeal_tokens(gin, count),
-        grad_a.reshape(weight_a.shape),
-        own_rows(1).reshape(weight_b.shape),
-        own_rows(2).reshape(weight_c.shape),
-        own_rows(3).reshape(weight_e.shape),
-    )
+    got = exchange(after(dealt, gin), "dp")
+    grads = pl.pallas_call(
+        grads_kernel,
+        out_shape=[
+            jax.ShapeDtypeStruct(w.shape, jnp.float32)
+            for w in (weight_a, weight_b, weight_c, weight_e)
+        ],
+    )(got)
+    return (undeal_tokens(out, count), undeal_tokens(gin, count), *grads)
 
 
 def per_device(tokens, grad_out, weight_a, weight_b, weight_c, weight_e):

time: 302 us -> 300 us (level)
  waiting for transfers between devices: 157 us -> 166 us
  local copies, waits for them, and re-layouts: 31.7 us -> 26.6 us
  other arithmetic: 19.6 us -> 15.5 us
  starting transfers between devices: 55.6 us -> 51.9 us
    all_to_all x7, waiting for transfers between devices: 59.3 us -> 65.7 us  [exchange(): return lax.all_to_all(x, axes, split_axis=0, concat_axis=0, tiled=True)]
    ppermute x25 -> x24, starting transfers between devices: 21.1 us -> 17.4 us  [xor_permute(): lax.ppermute(x, axis, [(i, i ^ mask) for i in range(lax.axis_size(axis))])]
    another operation x5 -> x1, local copies, waits for them, and re-layouts: 3.16 us -> 0.04 us  [token_plan(): own_ab = jnp.stack(own[:2], axis=2).reshape(ndp, 4, rows, BLK)]
    pallas_call x0 -> x1, Pallas kernels: none -> 3.12 us  [token_plan(): pl.pallas_call(grads_kernel, out_shape=[jax.ShapeDtypeStruct(w.shape, jnp...]
    ppermute x25 -> x24, waiting for transfers between devices: 97.9 us -> 100 us  [xor_permute(): lax.ppermute(x, axis, [(i, i ^ mask) for i in range(lax.axis_size(axis))])]
    unnamed x44 -> x40, local copies, waits for them, and re-layouts: 10.9 us -> 12.8 us
  transfers between devices with their start and end apart: 32 -> 31, of which waited for: 17 -> 19; matrix products, arithmetic and copies ran while one was open for 13% -> 11% of each run, Pallas kernels for 12% -> 12%
where the time goes in v10:
time: 300 us; the launch traced here: 299 us
  waiting for transfers between devices  166 us (55%)
  starting transfers between devices  51.9 us (17%)
  Pallas kernels  37.6 us (13%)
  local copies, waits for them, and re-layouts  26.6 us (9%)
  other arithmetic  15.5 us (5%)
    ppermute x24, waiting for transfers between devices, xor_permute(): lax.ppermute(x, axis, [(i, i ^ mask) for i in range(lax.axis_size(axis))])  100 us
    all_to_all x7, waiting for transfers between devices, exchange(): return lax.all_to_all(x, axes, split_axis=0, concat_axis=0, tiled=True)  65.7 us
    pallas_call x2, Pallas kernels, on_chip(): pl.pallas_call(kernel, out_shape=[jax.ShapeDtypeStruct(shape, jnp.bfloat1...  34.5 us
    all_to_all x7, starting transfers between devices, exchange(): return lax.all_to_all(x, axes, split_axis=0, concat_axis=0, tiled=True)  34.5 us
    ppermute x24, starting transfers between devices, xor_permute(): lax.ppermute(x, axis, [(i, i ^ mask) for i in range(lax.axis_size(axis))])  17.4 us
    unnamed x40, local copies, waits for them, and re-layouts  12.8 us
    convert_element_type x5, other arithmetic, add(): return (x.astype(jnp.float32) + y.astype(jnp.float32)).astype(jnp.bfloat16)  7.13 us
  transfers between devices with their start and end apart: 31, of which 19 were waited for; matrix products, arithmetic and copies ran while one was open for 11% of the time, Pallas kernels for 12%

profile of v10, /device:TPU:0, one launch (start us, length us, event | category | flops | bytes accessed | tf_op | source)
XLA Modules:
  0.0 298.8 jit_solution(17905809094715839705)
XLA Ops:
  6.6 7.3 %all-to-all-start = ((bf16[8,8,32,256]{3,2,1,0:T(8,128)(2,1)}), bf16[8,8,32,256]{3,2,1,0:T(8,128)(2,1)S(1)}, u32[]{:S(2)}, u32[]{:S(2)}) async-start(bf16[8,8,32,256]{3,2,1,0:T(8,128)(2,1)} %constant_dynamic-update-slice_fusion), calls=%async_computation | async-start | bytes 2097152 | tf_op jit(solution)/shard_map/all_to_all | solution.py:87
  14.8 24.9 %all-to-all-done = bf16[8,8,32,256]{3,2,1,0:T(8,128)(2,1)S(1)} async-done(((bf16[8,8,32,256]{3,2,1,0:T(8,128)(2,1)}), bf16[8,8,32,256]{3,2,1,0:T(8,128)(2,1)S(1)}, u32[]{:S(2)}, u32[]{:S(2)}) %all-to-all-start) | async-done | bytes 1048608 | tf_op jit(solution)/shard_map/all_to_all | solution.py:87
  39.7 4.1 %all-to-all-start.1 = ((bf16[8,2,2,32,256]{4,3,2,1,0:T(8,128)(2,1)}), bf16[8,2,2,32,256]{4,3,2,1,0:T(8,128)(2,1)}, u32[]{:S(2)}, u32[]{:S(2)}) async-start(bf16[8,2,2,32,256]{4,3,2,1,0:T(8,128)(2,1)} %pad_maximum_fusion.3), calls=%async_computation.1 | async-start | bytes 1048576 | tf_op jit(solution)/shard_map/all_to_all | solution.py:87
  44.9 1.9 collective-permute-start.1
  51.1 12.0 %collective-permute-done.1.refs_12_.refs_14_ = bf16[8,4,32,256]{3,2,1,0:T(8,128)(2,1)} collective-permute-done((bf16[8,4,32,256]{3,2,1,0:T(8,128)(2,1)}, bf16[8,4,32,256]{3,2,1,0:T(8,128)(2,1)}, u32[]{:S(2)}, u32[]{:S(2)}) %collective-permute-start.1) | collective-permute-done | bytes 524320 | tf_op jit(solution)/shard_map/ppermute | solution.py:83
  63.1 4.6 %all-to-all-start.2 = ((bf16[32,96,256]{2,1,0:T(8,128)(2,1)}), bf16[32,96,256]{2,1,0:T(8,128)(2,1)S(1)}, u32[]{:S(2)}, u32[]{:S(2)}) async-start(bf16[32,96,256]{2,1,0:T(8,128)(2,1)} %pad_maximum_fusion), calls=%async_computation.2 | async-start | bytes 3145728 | tf_op jit(solution)/shard_map/all_to_all | solution.py:87
  67.8 1.8 collective-permute-start.3
  71.6 1.7 copy.47
  75.2 1.5 copy.48
  77.8 2.3 pad_maximum_fusion.1
  80.1 17.1 %collective-permute-done.3.refs_2_.refs_4_ = bf16[8,2,2,32,256]{4,3,2,1,0:T(8,128)(2,1)} collective-permute-done((bf16[8,2,2,32,256]{4,3,2,1,0:T(8,128)(2,1)}, bf16[8,2,2,32,256]{4,3,2,1,0:T(8,128)(2,1)}, u32[]{:S(2)}, u32[]{:S(2)}) %collective-permute-start.3) | collective-permute-done | bytes 524320 | tf_op jit(solution)/shard_map/ppermute | solution.py:83
  97.2 12.9 %collective-permute-done.6.refs_6_.refs_8_ = bf16[8,2,2,32,256]{4,3,2,1,0:T(8,128)(2,1)} collective-permute-done((bf16[8,2,2,32,256]{4,3,2,1,0:T(8,128)(2,1)}, bf16[8,2,2,32,256]{4,3,2,1,0:T(8,128)(2,1)}, u32[]{:S(2)}, u32[]{:S(2)}) %collective-permute-start.6) | collective-permute-done | bytes 524320 | tf_op jit(solution)/shard_map/ppermute | solution.py:83
  111.2 4.7 %all-to-all-start.4 = ((bf16[32,96,256]{2,1,0:T(8,128)(2,1)}), bf16[32,96,256]{2,1,0:T(8,128)(2,1)S(1)}, u32[]{:S(2)}, u32[]{:S(2)}) async-start(bf16[32,96,256]{2,1,0:T(8,128)(2,1)} %pad_maximum_fusion.1), calls=%async_computation.4 | async-start | bytes 3145728 | tf_op jit(solution)/shard_map/all_to_all | solution.py:87
  123.5 17.3 %shard_map.109 = (bf16[8,4,96,256]{3,2,1,0:T(8,128)(2,1)}, bf16[2,4,4,64,512]{4,3,2,1,0:T(8,128)(2,1)}, bf16[2,4,256,512]{3,2,1,0:T(8,128)(2,1)}, bf16[2,4,256,5...) custom-call(s32[2]{0:T(128)} %pad_add_fusion.seat_ref, ...), custom_call_target="tpu_custom_call" | custom-call | flops 3221225472 | bytes 24117252 | tf_op jit(solution)/shard_map/pallas_call | solution.py:337
  140.8 12.7 %all-to-all-done.4 = bf16[32,96,256]{2,1,0:T(8,128)(2,1)S(1)} async-done(((bf16[32,96,256]{2,1,0:T(8,128)(2,1)}), bf16[32,96,256]{2,1,0:T(8,128)(2,1)S(1)}, u32[]{:S(2)}, u32[]{:S(2)}) %all-to-all-start.4) | async-done | bytes 1572896 | tf_op jit(solution)/shard_map/all_to_all | solution.py:87
  154.7 4.0 %all-to-all-start.3 = ((bf16[32,96,256]{2,1,0:T(8,128)(2,1)}), bf16[32,96,256]{2,1,0:T(8,128)(2,1)S(1)}, u32[]{:S(2)}, u32[]{:S(2)}) async-start(bf16[32,96,256]{2,1,0:T(8,128)(2,1)} %bitcast.102), calls=%async_computation.3 | async-start | bytes 3145728 | tf_op jit(solution)/shard_map/all_to_all | solution.py:87
  158.7 17.2 %shard_map.110 = (bf16[8,4,96,256]{3,2,1,0:T(8,128)(2,1)}, bf16[2,8,2,4,32,256]{5,4,3,2,1,0:T(8,128)(2,1)}, bf16[8,2,4,32,256]{4,3,2,1,0:T(8,128)(2,1)}, bf16[8,...) custom-call(s32[2]{0:T(128)} %pad_add_fusion.seat_ref, ...), custom_call_target="tpu_custom_call" | custom-call | flops 6442450944 | bytes 34078724 | tf_op jit(solution)/shard_map/pallas_call | solution.py:337
  177.2 3.9 %collective-permute-done.14 = bf16[8,4,32,256]{3,2,1,0:T(8,128)(2,1)S(1)} collective-permute-done((bf16[8,4,32,256]{3,2,1,0:T(8,128)(2,1)}, bf16[8,4,32,256]{3,2,1,0:T(8,128)(2,1)S(1)}, u32[]{:S(2)}, u32[]{:S(2)}) %collective-permute-start.14) | collective-permute-done | bytes 524320 | tf_op jit(solution)/shard_map/ppermute | solution.py:83
  181.8 2.5 fusion.2
  184.4 1.8 collective-permute-start.15
  189.7 11.3 %collective-permute-done.15 = bf16[8,4,32,256]{3,2,1,0:T(8,128)(2,1)S(1)} collective-permute-done((bf16[8,4,32,256]{3,2,1,0:T(8,128)(2,1)S(1)}, bf16[8,4,32,256]{3,2,1,0:T(8,128)(2,1)S(1)}, u32[]{:S(2)}, u32[]{:S(2)}) %collective-permute-start.15) | collective-permute-done | bytes 524320 | tf_op jit(solution)/shard_map/ppermute | solution.py:83
  201.0 2.1 add_convert_fusion.4
  204.9 4.2 %all-to-all-start.5 = ((bf16[32,96,256]{2,1,0:T(8,128)(2,1)}), bf16[32,96,256]{2,1,0:T(8,128)(2,1)S(1)}, u32[]{:S(2)}, u32[]{:S(2)}) async-start(bf16[32,96,256]{2,1,0:T(8,128)(2,1)} %bitcast.101), calls=%async_computation.5 | async-start | bytes 3145728 | tf_op jit(solution)/shard_map/all_to_all | solution.py:87
  209.5 1.7 collective-permute-start.22
  213.2 24.3 %collective-permute-done.22 = bf16[8,4,32,256]{3,2,1,0:T(8,128)(2,1)S(1)} collective-permute-done((bf16[8,4,32,256]{3,2,1,0:T(8,128)(2,1)}, bf16[8,4,32,256]{3,2,1,0:T(8,128)(2,1)S(1)}, u32[]{:S(2)}, u32[]{:S(2)}) %collective-permute-start.22) | collective-permute-done | bytes 524320 | tf_op jit(solution)/shard_map/ppermute | solution.py:83
  239.9 11.5 %collective-permute-done.19 = bf16[4,2,4,32,256]{4,3,2,1,0:T(8,128)(2,1)S(1)} collective-permute-done((bf16[4,2,4,32,256]{4,3,2,1,0:T(8,128)(2,1)}, bf16[4,2,4,32,256]{4,3,2,1,0:T(8,128)(2,1)S(1)}, u32[]{:S(2)}, u32[]{:S(2)}) %collective-permute-start.19) | collective-permute-done | bytes 524320 | tf_op jit(solution)/shard_map/ppermute | solution.py:83
  252.9 5.5 %all-to-all-start.6 = ((bf16[8,3,4,32,256]{4,3,2,1,0:T(8,128)(2,1)}), bf16[8,3,4,32,256]{4,3,2,1,0:T(8,128)(2,1)}, u32[]{:S(2)}, u32[]{:S(2)}) async-start(bf16[8,3,4,32,256]{4,3,2,1,0:T(8,128)(2,1)} %pad_maximum_fusion.2), calls=%async_computation.6 | async-start | bytes 3145728 | tf_op jit(solution)/shard_map/all_to_all | solution.py:87
  259.7 1.6 copy.46
  261.3 2.6 copy.52
  265.8 1.7 copy.53
  267.6 28.1 %all-to-all-done.6.got_ref = bf16[8,3,4,32,256]{4,3,2,1,0:T(8,128)(2,1)} async-done(((bf16[8,3,4,32,256]{4,3,2,1,0:T(8,128)(2,1)}), bf16[8,3,4,32,256]{4,3,2,1,0:T(8,128)(2,1)}, u32[]{:S(2)}, u32[]{:S(2)}) %all-to-all-start.6) | async-done | bytes 1572896 | tf_op jit(solution)/shard_map/all_to_all | solution.py:87
  295.7 3.1 %shard_map.111 = (f32[12,32,512]{2,1,0:T(8,128)}, f32[24,32,256]{2,1,0:T(8,128)}, f32[24,32,256]{2,1,0:T(8,128)}, f32[12,64,256]{2,1,0:T(8,128)}) custom-call(bf16[8,3,4,32,256]{4,3,2,1,0:T(8,128)(2,1)} %all-to-all-done.6.got_ref), custom_call_target="tpu_custom_call" | custom-call | tf_op jit(solution)/shard_map/pallas_call | solution.py:414
  (119 shorter events, 43.9 us)
Async XLA Ops:
  6.6 33.0 %all-to-all-start = ((bf16[8,8,32,256]{3,2,1,0:T(8,128)(2,1)}), bf16[8,8,32,256]{3,2,1,0:T(8,128)(2,1)S(1)}, u32[]{:S(2)}, u32[]{:S(2)}) async-start(bf16[8,8,32,256]{3,2,1,0:T(8,128)(2,1)} %constant_dynamic-update-slice_fusion), calls=%async_computation | async-start | bytes 2097152 | tf_op jit(solution)/shard_map/all_to_all | solution.py:87
  39.7 23.5 %all-to-all-start.1 = ((bf16[8,2,2,32,256]{4,3,2,1,0:T(8,128)(2,1)}), bf16[8,2,2,32,256]{4,3,2,1,0:T(8,128)(2,1)}, u32[]{:S(2)}, u32[]{:S(2)}) async-start(bf16[8,2,2,32,256]{4,3,2,1,0:T(8,128)(2,1)} %pad_maximum_fusion.3), calls=%async_computation.1 | async-start | bytes 1048576 | tf_op jit(solution)/shard_map/all_to_all | solution.py:87
  44.9 18.2 %collective-permute-start.1 = (bf16[8,4,32,256]{3,2,1,0:T(8,128)(2,1)}, bf16[8,4,32,256]{3,2,1,0:T(8,128)(2,1)}, u32[]{:S(2)}, u32[]{:S(2)}) collective-permute-start(bf16[8,4,32,256]{3,2,1,0:T(8,128)(2,1)} %get-tuple-element.85.refs_8_.refs_10_), channel_id=1, source_target_pairs={{0,4},{4,0},{8,12},{12,8},{16,20},{20,16},{24,28},{28,24},{1,5},{5... | collective-permute-start | bytes 1572872 | tf_op jit(solution)/shard_map/ppermute | solution.py:83
  46.8 16.3 %collective-permute-start = (bf16[8,4,32,256]{3,2,1,0:T(8,128)(2,1)}, bf16[8,4,32,256]{3,2,1,0:T(8,128)(2,1)}, u32[]{:S(2)}, u32[]{:S(2)}) collective-permute-start(bf16[8,4,32,256]{3,2,1,0:T(8,128)(2,1)} %get-tuple-element.85.refs_8_.refs_10_), channel_id=1, source_target_pairs={{0,2},{1,3},{2,0},{3,1},{4,6},{5,7},{6,4},{7,5},{8,10},{9,11},{10,... | collective-permute-start | bytes 1572872 | tf_op jit(solution)/shard_map/ppermute | solution.py:83
  63.1 46.9 %all-to-all-start.2 = ((bf16[32,96,256]{2,1,0:T(8,128)(2,1)}), bf16[32,96,256]{2,1,0:T(8,128)(2,1)S(1)}, u32[]{:S(2)}, u32[]{:S(2)}) async-start(bf16[32,96,256]{2,1,0:T(8,128)(2,1)} %pad_maximum_fusion), calls=%async_computation.2 | async-start | bytes 3145728 | tf_op jit(solution)/shard_map/all_to_all | solution.py:87
  67.8 29.4 %collective-permute-start.3 = (bf16[8,2,2,32,256]{4,3,2,1,0:T(8,128)(2,1)}, bf16[8,2,2,32,256]{4,3,2,1,0:T(8,128)(2,1)}, u32[]{:S(2)}, u32[]{:S(2)}) collective-permute-start(bf16[8,2,2,32,256]{4,3,2,1,0:T(8,128)(2,1)} %bitcast.24.refs_0_.refs_2_), channel_id=1, source_target_pairs={{0,2},{1,3},{2,0},{3,1},{4,6},{5,7},{6,4},{7,5},{8,10},{9,11},{10,... | collective-permute-start | bytes 1572872 | tf_op jit(solution)/shard_map/ppermute | solution.py:83
  69.6 27.6 %collective-permute-start.11 = (bf16[8,4,32,256]{3,2,1,0:T(8,128)(2,1)}, bf16[8,4,32,256]{3,2,1,0:T(8,128)(2,1)}, u32[]{:S(2)}, u32[]{:S(2)}) collective-permute-start(bf16[8,4,32,256]{3,2,1,0:T(8,128)(2,1)} %collective-permute-done.refs_10_.refs_12_), channel_id=1, source_target_pairs={{0,4},{4,0},{8,12},{12,8},{16,20},{20,16},{24,28},{28,24},{1,5},{5... | collective-permute-start | bytes 1572872 | tf_op jit(solution)/shard_map/ppermute | solution.py:83
  71.1 39.0 %collective-permute-start.6 = (bf16[8,2,2,32,256]{4,3,2,1,0:T(8,128)(2,1)}, bf16[8,2,2,32,256]{4,3,2,1,0:T(8,128)(2,1)}, u32[]{:S(2)}, u32[]{:S(2)}) collective-permute-start(bf16[8,2,2,32,256]{4,3,2,1,0:T(8,128)(2,1)} %all-to-all-done.1.refs_4_.refs_6_), channel_id=1, source_target_pairs={{0,2},{1,3},{2,0},{3,1},{4,6},{5,7},{6,4},{7,5},{8,10},{9,11},{10,... | collective-permute-start | bytes 1572872 | tf_op jit(solution)/shard_map/ppermute | solution.py:83
  111.2 42.3 %all-to-all-start.4 = ((bf16[32,96,256]{2,1,0:T(8,128)(2,1)}), bf16[32,96,256]{2,1,0:T(8,128)(2,1)S(1)}, u32[]{:S(2)}, u32[]{:S(2)}) async-start(bf16[32,96,256]{2,1,0:T(8,128)(2,1)} %pad_maximum_fusion.1), calls=%async_computation.4 | async-start | bytes 3145728 | tf_op jit(solution)/shard_map/all_to_all | solution.py:87
  116.0 2.2 collective-permute-start.2
  116.1 3.5 %collective-permute-start.8 = (bf16[8,4,32,256]{3,2,1,0:T(8,128)(2,1)}, bf16[8,4,32,256]{3,2,1,0:T(8,128)(2,1)S(1)}, u32[]{:S(2)}, u32[]{:S(2)}) collective-permute-start(bf16[8,4,32,256]{3,2,1,0:T(8,128)(2,1)} %get-tuple-element.85.refs_8_.refs_10_), channel_id=1, source_target_pairs={{0,1},{1,0},{2,3},{3,2},{4,5},{5,4},{6,7},{7,6},{8,9},{9,8},{10,11... | collective-permute-start | bytes 1572872 | tf_op jit(solution)/shard_map/ppermute | solution.py:83
  116.5 4.6 %collective-permute-start.4 = (bf16[8,2,2,32,256]{4,3,2,1,0:T(8,128)(2,1)}, bf16[8,2,2,32,256]{4,3,2,1,0:T(8,128)(2,1)S(1)}, u32[]{:S(2)}, u32[]{:S(2)}) collective-permute-start(bf16[8,2,2,32,256]{4,3,2,1,0:T(8,128)(2,1)} %collective-permute-done.3.refs_2_.refs_4_), channel_id=1, source_target_pairs={{0,1},{1,0},{2,3},{3,2},{4,5},{5,4},{6,7},{7,6},{8,9},{9,8},{10,11... | collective-permute-start | bytes 1572872 | tf_op jit(solution)/shard_map/ppermute | solution.py:83
  116.6 5.3 %collective-permute-start.10 = (bf16[8,4,32,256]{3,2,1,0:T(8,128)(2,1)}, bf16[8,4,32,256]{3,2,1,0:T(8,128)(2,1)}, u32[]{:S(2)}, u32[]{:S(2)}) collective-permute-start(bf16[8,4,32,256]{3,2,1,0:T(8,128)(2,1)} %collective-permute-done.1.refs_12_.refs_14_), channel_id=1, source_target_pairs={{0,1},{1,0},{2,3},{3,2},{4,5},{5,4},{6,7},{7,6},{8,9},{9,8},{10,11... | collective-permute-start | bytes 1572872 | tf_op jit(solution)/shard_map/ppermute | solution.py:83
  117.0 4.9 %collective-permute-start.9 = (bf16[8,4,32,256]{3,2,1,0:T(8,128)(2,1)}, bf16[8,4,32,256]{3,2,1,0:T(8,128)(2,1)}, u32[]{:S(2)}, u32[]{:S(2)}) collective-permute-start(bf16[8,4,32,256]{3,2,1,0:T(8,128)(2,1)} %collective-permute-done.refs_10_.refs_12_), channel_id=1, source_target_pairs={{0,1},{1,0},{2,3},{3,2},{4,5},{5,4},{6,7},{7,6},{8,9},{9,8},{10,11... | collective-permute-start | bytes 1572872 | tf_op jit(solution)/shard_map/ppermute | solution.py:83
  118.1 3.9 %collective-permute-start.5 = (bf16[8,2,2,32,256]{4,3,2,1,0:T(8,128)(2,1)}, bf16[8,2,2,32,256]{4,3,2,1,0:T(8,128)(2,1)}, u32[]{:S(2)}, u32[]{:S(2)}) collective-permute-start(bf16[8,2,2,32,256]{4,3,2,1,0:T(8,128)(2,1)} %all-to-all-done.1.refs_4_.refs_6_), channel_id=1, source_target_pairs={{0,1},{1,0},{2,3},{3,2},{4,5},{5,4},{6,7},{7,6},{8,9},{9,8},{10,11... | collective-permute-start | bytes 1572872 | tf_op jit(solution)/shard_map/ppermute | solution.py:83
  119.6 3.1 %collective-permute-start.12 = (bf16[8,4,32,256]{3,2,1,0:T(8,128)(2,1)}, bf16[8,4,32,256]{3,2,1,0:T(8,128)(2,1)}, u32[]{:S(2)}, u32[]{:S(2)}) collective-permute-start(bf16[8,4,32,256]{3,2,1,0:T(8,128)(2,1)} %collective-permute-done.11.refs_14_.refs_16_), channel_id=1, source_target_pairs={{0,1},{1,0},{2,3},{3,2},{4,5},{5,4},{6,7},{7,6},{8,9},{9,8},{10,11... | collective-permute-start | bytes 1572872 | tf_op jit(solution)/shard_map/ppermute | solution.py:83
  121.1 2.4 collective-permute-start.7
  154.7 50.2 %all-to-all-start.3 = ((bf16[32,96,256]{2,1,0:T(8,128)(2,1)}), bf16[32,96,256]{2,1,0:T(8,128)(2,1)S(1)}, u32[]{:S(2)}, u32[]{:S(2)}) async-start(bf16[32,96,256]{2,1,0:T(8,128)(2,1)} %bitcast.102), calls=%async_computation.3 | async-start | bytes 3145728 | tf_op jit(solution)/shard_map/all_to_all | solution.py:87
  175.9 10.2 %collective-permute-start.16 = (bf16[8,2,4,32,256]{4,3,2,1,0:T(8,128)(2,1)}, bf16[8,2,4,32,256]{4,3,2,1,0:T(8,128)(2,1)S(1)}, u32[]{:S(2)}, u32[]{:S(2)}) collective-permute-start(bf16[8,2,4,32,256]{4,3,2,1,0:T(8,128)(2,1)} %get-tuple-element.51), channel_id=1, source_target_pairs={{0,1},{1,0},{2,3},{3,2},{4,5},{5,4},{6,7},{7,6},{8,9},{9,8},{10,11... | collective-permute-start | bytes 3145736 | tf_op jit(solution)/shard_map/ppermute | solution.py:83
  176.2 9.9 %collective-permute-start.17 = (bf16[8,2,4,32,256]{4,3,2,1,0:T(8,128)(2,1)}, bf16[8,2,4,32,256]{4,3,2,1,0:T(8,128)(2,1)S(1)}, u32[]{:S(2)}, u32[]{:S(2)}) collective-permute-start(bf16[8,2,4,32,256]{4,3,2,1,0:T(8,128)(2,1)} %get-tuple-element.52), channel_id=1, source_target_pairs={{0,1},{1,0},{2,3},{3,2},{4,5},{5,4},{6,7},{7,6},{8,9},{9,8},{10,11... | collective-permute-start | bytes 3145736 | tf_op jit(solution)/shard_map/ppermute | solution.py:83
  176.5 4.6 %collective-permute-start.14 = (bf16[8,4,32,256]{3,2,1,0:T(8,128)(2,1)}, bf16[8,4,32,256]{3,2,1,0:T(8,128)(2,1)S(1)}, u32[]{:S(2)}, u32[]{:S(2)}) collective-permute-start(bf16[8,4,32,256]{3,2,1,0:T(8,128)(2,1)} %get-tuple-element.49), channel_id=1, source_target_pairs={{0,1},{1,0},{2,3},{3,2},{4,5},{5,4},{6,7},{7,6},{8,9},{9,8},{10,11... | collective-permute-start | bytes 1572872 | tf_op jit(solution)/shard_map/ppermute | solution.py:83
  176.7 5.1 %collective-permute-start.21 = (bf16[8,4,32,256]{3,2,1,0:T(8,128)(2,1)}, bf16[8,4,32,256]{3,2,1,0:T(8,128)(2,1)S(1)}, u32[]{:S(2)}, u32[]{:S(2)}) collective-permute-start(bf16[8,4,32,256]{3,2,1,0:T(8,128)(2,1)} %get-tuple-element.56), channel_id=1, source_target_pairs={{0,1},{1,0},{2,3},{3,2},{4,5},{5,4},{6,7},{7,6},{8,9},{9,8},{10,11... | collective-permute-start | bytes 1572872 | tf_op jit(solution)/shard_map/ppermute | solution.py:83
  177.0 12.7 %collective-permute-start.13 = (bf16[8,4,32,256]{3,2,1,0:T(8,128)(2,1)}, bf16[8,4,32,256]{3,2,1,0:T(8,128)(2,1)S(1)}, u32[]{:S(2)}, u32[]{:S(2)}) collective-permute-start(bf16[8,4,32,256]{3,2,1,0:T(8,128)(2,1)} %get-tuple-element.48), channel_id=1, source_target_pairs={{0,1},{1,0},{2,3},{3,2},{4,5},{5,4},{6,7},{7,6},{8,9},{9,8},{10,11... | collective-permute-start | bytes 1572872 | tf_op jit(solution)/shard_map/ppermute | solution.py:83
  184.4 16.6 %collective-permute-start.15 = (bf16[8,4,32,256]{3,2,1,0:T(8,128)(2,1)S(1)}, bf16[8,4,32,256]{3,2,1,0:T(8,128)(2,1)S(1)}, u32[]{:S(2)}, u32[]{:S(2)}) collective-permute-start(bf16[8,4,32,256]{3,2,1,0:T(8,128)(2,1)S(1)} %get-tuple-element.75), channel_id=1, source_target_pairs={{0,4},{4,0},{8,12},{12,8},{16,20},{20,16},{24,28},{28,24},{1,5},{5... | collective-permute-start | bytes 1572872 | tf_op jit(solution)/shard_map/ppermute | solution.py:83
  188.2 15.4 %collective-permute-start.18 = (bf16[4,2,4,32,256]{4,3,2,1,0:T(8,128)(2,1)S(1)}, bf16[4,2,4,32,256]{4,3,2,1,0:T(8,128)(2,1)S(1)}, u32[]{:S(2)}, u32[]{:S(2)}) collective-permute-start(bf16[4,2,4,32,256]{4,3,2,1,0:T(8,128)(2,1)S(1)} %get-tuple-element.79), channel_id=1, source_target_pairs={{0,2},{1,3},{2,0},{3,1},{4,6},{5,7},{6,4},{7,5},{8,10},{9,11},{10,... | collective-permute-start | bytes 1572872 | tf_op jit(solution)/shard_map/ppermute | solution.py:83
  204.9 53.5 %copy-start = (bf16[32,96,256]{2,1,0:T(8,128)(2,1)}, bf16[32,96,256]{2,1,0:T(8,128)(2,1)S(1)}, u32[]{:S(2)}) copy-start(bf16[32,96,256]{2,1,0:T(8,128)(2,1)S(1)} %all-to-all-done.3) | copy-start | bytes 4718596
  204.9 48.0 %all-to-all-start.5 = ((bf16[32,96,256]{2,1,0:T(8,128)(2,1)}), bf16[32,96,256]{2,1,0:T(8,128)(2,1)S(1)}, u32[]{:S(2)}, u32[]{:S(2)}) async-start(bf16[32,96,256]{2,1,0:T(8,128)(2,1)} %bitcast.101), calls=%async_computation.5 | async-start | bytes 3145728 | tf_op jit(solution)/shard_map/all_to_all | solution.py:87
  209.1 4.0 %collective-permute-start.20 = (bf16[8,4,32,256]{3,2,1,0:T(8,128)(2,1)}, bf16[8,4,32,256]{3,2,1,0:T(8,128)(2,1)S(1)}, u32[]{:S(2)}, u32[]{:S(2)}) collective-permute-start(bf16[8,4,32,256]{3,2,1,0:T(8,128)(2,1)} %get-tuple-element.55), channel_id=1, source_target_pairs={{0,1},{1,0},{2,3},{3,2},{4,5},{5,4},{6,7},{7,6},{8,9},{9,8},{10,11... | collective-permute-start | bytes 1572872 | tf_op jit(solution)/shard_map/ppermute | solution.py:83
  209.5 28.0 %collective-permute-start.22 = (bf16[8,4,32,256]{3,2,1,0:T(8,128)(2,1)}, bf16[8,4,32,256]{3,2,1,0:T(8,128)(2,1)S(1)}, u32[]{:S(2)}, u32[]{:S(2)}) collective-permute-start(bf16[8,4,32,256]{3,2,1,0:T(8,128)(2,1)} %get-tuple-element.74), channel_id=1, source_target_pairs={{0,4},{4,0},{8,12},{12,8},{16,20},{20,16},{24,28},{28,24},{1,5},{5... | collective-permute-start | bytes 1572872 | tf_op jit(solution)/shard_map/ppermute | solution.py:83
  211.1 27.3 %collective-permute-start.23 = (bf16[8,4,32,256]{3,2,1,0:T(8,128)(2,1)}, bf16[8,4,32,256]{3,2,1,0:T(8,128)(2,1)S(1)}, u32[]{:S(2)}, u32[]{:S(2)}) collective-permute-start(bf16[8,4,32,256]{3,2,1,0:T(8,128)(2,1)} %add_convert_fusion.4), channel_id=1, source_target_pairs={{0,2},{1,3},{2,0},{3,1},{4,6},{5,7},{6,4},{7,5},{8,10},{9,11},{10,... | collective-permute-start | bytes 1572872 | tf_op jit(solution)/shard_map/ppermute | solution.py:83
  212.6 38.7 %collective-permute-start.19 = (bf16[4,2,4,32,256]{4,3,2,1,0:T(8,128)(2,1)}, bf16[4,2,4,32,256]{4,3,2,1,0:T(8,128)(2,1)S(1)}, u32[]{:S(2)}, u32[]{:S(2)}) collective-permute-start(bf16[4,2,4,32,256]{4,3,2,1,0:T(8,128)(2,1)} %get-tuple-element.54), channel_id=1, source_target_pairs={{0,2},{1,3},{2,0},{3,1},{4,6},{5,7},{6,4},{7,5},{8,10},{9,11},{10,... | collective-permute-start | bytes 1572872 | tf_op jit(solution)/shard_map/ppermute | solution.py:83
  252.9 42.8 %all-to-all-start.6 = ((bf16[8,3,4,32,256]{4,3,2,1,0:T(8,128)(2,1)}), bf16[8,3,4,32,256]{4,3,2,1,0:T(8,128)(2,1)}, u32[]{:S(2)}, u32[]{:S(2)}) async-start(bf16[8,3,4,32,256]{4,3,2,1,0:T(8,128)(2,1)} %pad_maximum_fusion.2), calls=%async_computation.6 | async-start | bytes 3145728 | tf_op jit(solution)/shard_map/all_to_all | solution.py:87
  (17 other events, 167.2 us)

commit v11 on v10

--- a/solution.py
+++ b/solution.py
@@ -87,11 +87,11 @@
     return lax.all_to_all(x, axes, split_axis=0, concat_axis=0, tiled=True)
 
 
-def weight_sets(w):
+def own_sets(w):
     pairs = lax.axis_size("dp") // 2
     sets = w.reshape(pairs, 3, 2, w.shape[1], w.shape[2])
     own = jnp.stack([sets[:, 0], sets[:, 2]], axis=1)
-    return own.reshape((pairs * 2,) + own.shape[2:]), sets[:, 1].reshape(pairs * 2, *w.shape[1:])
+    return own.reshape((pairs * 2,) + own.shape[2:])
 
 
 def gather_bfly(w, across):
@@ -141,7 +141,7 @@
 def weight_of(slot, own, shared):
     def get(m, which, r):
         if slot == 0:
-            return square(own[which // 2][m][:, r, which % 2])
+            return square(own[1][m][:, r, which - 1] if which else own[0][m][:, r])
         return square(shared[r][m][:, which])
 
     return get
@@ -150,7 +150,7 @@
 def wide_weight(slot, own, e_ref, y):
     def get(m, r):
         if slot == 0:
-            return square(own[1][m][half_src(e_ref.shape[1], r), :, 1])
+            return square(own[1][m][half_src(e_ref.shape[1], r), :, 2])
         return square(e_ref[m, half_src(e_ref.shape[1], r ^ y)])
 
     return get
@@ -224,7 +224,7 @@
 
 
 BACKWARD_ORDER = (
-    (1, 6, 21, 7, 8, 9, 2, 18, 19, 20, 3, 4, 5, 0) + tuple(range(14, 18)) + (25,) + tuple(range(10, 14)) + (22, 23, 24)
+    (1, 6, 21, 7, 8, 9, 18, 19, 20, 2, 3, 4, 5, 0) + tuple(range(14, 18)) + (25,) + tuple(range(10, 14)) + (22, 23, 24)
 )
 
 
@@ -294,12 +294,13 @@
         for m in range(nb):
             d = f ^ m
             x = streamed.get(0)[:, d, lo:hi, :].reshape(count, BLK)
+            across = x.T
             total = 0.0
             for r in range(2):
                 back = spread[r, d].reshape(BLK, count)
-                total = total + dot(back, weight(m, 0, r), 0, 1)
-                store(slot, m, 0, r, dot(x, back, 0, 1))
-            gin_ref[:, d, lo:hi, :] = total.astype(jnp.bfloat16).reshape(ndp, hi - lo, BLK)
+                total = total + dot(weight(m, 0, r), back, 1, 0)
+                store(slot, m, 0, r, dot(across, back, 1, 1))
+            gin_ref[:, d, lo:hi, :] = total.astype(jnp.bfloat16).T.reshape(ndp, hi - lo, BLK)
         if slot == 0:
             send(own_keep, results[1])
             send(own_send.at[0], results[2])
@@ -310,6 +311,24 @@
     send(gin_ref, results[0])
     for copy in sent:
         copy.wait()
+
+
+def pack_kernel(a_ref, b_ref, c_ref, e_ref, first_ref):
+    owners, rows = first_ref.shape[0], b_ref.shape[1]
+
+    def piece(which, index, part):
+        if which == 0:
+            return a_ref[index, :, part * BLK : (part + 1) * BLK]
+        if which == 3:
+            return e_ref[index, part * rows : (part + 1) * rows, :]
+        return (b_ref, c_ref)[which - 1][2 * index + part]
+
+    for owner in range(owners):
+        pair, side = owner // 2, owner % 2
+        for part in range(2):
+            first_ref[owner, part] = piece(0, 3 * pair + 2 * side, part)
+        for which in range(4):
+            first_ref[owner, 2 + which] = piece(which, 3 * pair + 1, side)
 
 
 def grads_kernel(got_ref, a_ref, b_ref, c_ref, e_ref):
@@ -355,24 +374,24 @@
     ndp, nb = lax.axis_size("dp"), lax.axis_size("bfly")
     blocks, rows, _ = weight_a.shape
     parts, count = 2 * blocks, tokens.shape[0]
-    dealt_a = weight_a.reshape(blocks, rows, 2, BLK).transpose(0, 2, 1, 3).reshape(parts, rows, BLK)
-    dealt_e = weight_e.reshape(parts, rows, BLK)
     seat = jnp.stack([lax.axis_index("bfly"), lax.axis_index("dp") % 2]).astype(jnp.int32)
 
     everyone = ("dp", "bfly")
     shape = (ndp, nb, -1, BLK)
-    own, mid = zip(*(weight_sets(w) for w in (dealt_a, weight_b, weight_c, dealt_e)))
-    own_ab = jnp.stack(own[:2], axis=2).reshape(ndp, 4, rows, BLK)
-    first = exchange(jnp.concatenate([own_ab, jnp.stack(mid, axis=1)], axis=1), "dp")
-    ab, mid = first[:, :4].reshape(ndp, 2, 2, rows, BLK), first[:, 4:]
-    ce = exchange(after(jnp.stack(own[2:], axis=2), first), "dp")
-    mid_across, ab_across, ce_across = (xor_permute(part, 2) for part in (mid, ab, ce))
+    first = pl.pallas_call(
+        pack_kernel, out_shape=jax.ShapeDtypeStruct((ndp, 6, rows, BLK), jnp.bfloat16)
+    )(weight_a, weight_b, weight_c, weight_e)
+    first = exchange(first, "dp")
+    a, mid = first[:, :2], first[:, 2:]
+    rest = [own_sets(w) for w in (weight_b, weight_c, weight_e.reshape(parts, rows, BLK))]
+    rest = exchange(after(jnp.stack(rest, axis=2), first), "dp")
+    mid_across, a_across, rest_across = (xor_permute(part, 2) for part in (mid, a, rest))
     swapped, swapped_across = (xor_permute(part, 1, "dp") for part in (mid, mid_across))
-    x = exchange(after(deal_tokens(tokens), ce, mid_across, swapped), everyone)
-    g = after(deal_tokens(grad_out), x, ab_across, ce_across, swapped_across)
+    x = exchange(after(deal_tokens(tokens), rest, mid_across, swapped, a_across), everyone)
+    g = after(deal_tokens(grad_out), x, rest_across, swapped_across)
     g = exchange(g, everyone).reshape(shape)
     x = x.reshape(shape)
-    weights = gather_bfly(ab, ab_across) + gather_bfly(ce, ce_across)
+    weights = gather_bfly(a, a_across) + gather_bfly(rest, rest_across)
     weights += gather_bfly(mid, mid_across) + gather_bfly(swapped, swapped_across)
 
     own, mid = count * ndp // nb, count * ndp // nb // 2

time: 300 us -> 289 us (0.963)
  waiting for transfers between devices: 166 us -> 154 us
    ppermute x24, waiting for transfers between devices: 100 us -> 94.4 us  [xor_permute(): lax.ppermute(x, axis, [(i, i ^ mask) for i in range(lax.axis_size(axis))])]
    all_to_all x7, waiting for transfers between devices: 65.7 us -> 60 us  [exchange(): return lax.all_to_all(x, axes, split_axis=0, concat_axis=0, tiled=True)]
    unnamed x40 -> x38, local copies, waits for them, and re-layouts: 12.8 us -> 12.6 us
  transfers between devices with their start and end apart: 31 -> 31, of which waited for: 19 -> 19; matrix products, arithmetic and copies ran while one was open for 11% -> 12% of each run, Pallas kernels for 12% -> 12%
where the time goes in v11:
time: 289 us; the launch traced here: 288 us
  waiting for transfers between devices  154 us (53%)
  starting transfers between devices  51.1 us (18%)
  Pallas kernels  40.1 us (14%)
  local copies, waits for them, and re-layouts  25.7 us (9%)
  other arithmetic  15.5 us (5%)
    ppermute x24, waiting for transfers between devices, xor_permute(): lax.ppermute(x, axis, [(i, i ^ mask) for i in range(lax.axis_size(axis))])  94.4 us
    all_to_all x7, waiting for transfers between devices, exchange(): return lax.all_to_all(x, axes, split_axis=0, concat_axis=0, tiled=True)  60 us
    pallas_call x2, Pallas kernels, on_chip(): pl.pallas_call(kernel, out_shape=[jax.ShapeDtypeStruct(shape, jnp.bfloat1...  34.6 us
    all_to_all x7, starting transfers between devices, exchange(): return lax.all_to_all(x, axes, split_axis=0, concat_axis=0, tiled=True)  33.4 us
    ppermute x24, starting transfers between devices, xor_permute(): lax.ppermute(x, axis, [(i, i ^ mask) for i in range(lax.axis_size(axis))])  17.7 us
    unnamed x38, local copies, waits for them, and re-layouts  12.6 us
    convert_element_type x5, other arithmetic, add(): return (x.astype(jnp.float32) + y.astype(jnp.float32)).astype(jnp.bfloat16)  7.14 us
  transfers between devices with their start and end apart: 31, of which 19 were waited for; matrix products, arithmetic and copies ran while one was open for 12% of the time, Pallas kernels for 12%

profile of v11, /device:TPU:0, one launch (start us, length us, event | category | flops | bytes accessed | tf_op | source)
XLA Modules:
  0.0 287.8 jit_solution(4835873709802366750)
XLA Ops:
  0.6 2.3 shard_map.109
  3.0 7.4 %all-to-all-start = ((bf16[8,6,32,256]{3,2,1,0:T(8,128)(2,1)}), bf16[8,6,32,256]{3,2,1,0:T(8,128)(2,1)S(1)}, u32[]{:S(2)}, u32[]{:S(2)}) async-start(bf16[8,6,32,256]{3,2,1,0:T(8,128)(2,1)} %shard_map.109), calls=%async_computation | async-start | bytes 1572864 | tf_op jit(solution)/shard_map/all_to_all | solution.py:87
  11.6 19.0 %all-to-all-done = bf16[8,6,32,256]{3,2,1,0:T(8,128)(2,1)S(1)} async-done(((bf16[8,6,32,256]{3,2,1,0:T(8,128)(2,1)}), bf16[8,6,32,256]{3,2,1,0:T(8,128)(2,1)S(1)}, u32[]{:S(2)}, u32[]{:S(2)}) %all-to-all-start) | async-done | bytes 786464 | tf_op jit(solution)/shard_map/all_to_all | solution.py:87
  30.6 3.6 %all-to-all-start.1 = ((bf16[8,2,3,32,256]{4,3,2,1,0:T(8,128)(2,1)}), bf16[8,2,3,32,256]{4,3,2,1,0:T(8,128)(2,1)S(1)}, u32[]{:S(2)}, u32[]{:S(2)}) async-start(bf16[8,2,3,32,256]{4,3,2,1,0:T(8,128)(2,1)} %pad_maximum_fusion.3), calls=%async_computation.1 | async-start | bytes 1572864 | tf_op jit(solution)/shard_map/all_to_all | solution.py:87
  35.0 2.0 collective-permute-start.1
  39.8 1.7 copy.30
  44.9 11.0 %collective-permute-done.2.refs_2_.refs_4_ = bf16[8,2,32,256]{3,2,1,0:T(8,128)(2,1)} collective-permute-done((bf16[8,2,32,256]{3,2,1,0:T(8,128)(2,1)}, bf16[8,2,32,256]{3,2,1,0:T(8,128)(2,1)}, u32[]{:S(2)}, u32[]{:S(2)}) %collective-permute-start.2) | collective-permute-done | bytes 262176 | tf_op jit(solution)/shard_map/ppermute | solution.py:83
  57.3 4.6 %all-to-all-start.2 = ((bf16[32,96,256]{2,1,0:T(8,128)(2,1)}), bf16[32,96,256]{2,1,0:T(8,128)(2,1)S(1)}, u32[]{:S(2)}, u32[]{:S(2)}) async-start(bf16[32,96,256]{2,1,0:T(8,128)(2,1)} %pad_maximum_fusion), calls=%async_computation.2 | async-start | bytes 3145728 | tf_op jit(solution)/shard_map/all_to_all | solution.py:87
  61.9 1.8 collective-permute-start.6
  71.3 2.3 pad_maximum_fusion.1
  73.6 16.7 %collective-permute-done.11.refs_14_.refs_16_ = bf16[8,4,32,256]{3,2,1,0:T(8,128)(2,1)} collective-permute-done((bf16[8,4,32,256]{3,2,1,0:T(8,128)(2,1)}, bf16[8,4,32,256]{3,2,1,0:T(8,128)(2,1)}, u32[]{:S(2)}, u32[]{:S(2)}) %collective-permute-start.11) | collective-permute-done | bytes 524320 | tf_op jit(solution)/shard_map/ppermute | solution.py:83
  90.3 8.2 %collective-permute-done.6.refs_6_.refs_8_ = bf16[8,2,3,32,256]{4,3,2,1,0:T(8,128)(2,1)} collective-permute-done((bf16[8,2,3,32,256]{4,3,2,1,0:T(8,128)(2,1)}, bf16[8,2,3,32,256]{4,3,2,1,0:T(8,128)(2,1)}, u32[]{:S(2)}, u32[]{:S(2)}) %collective-permute-start.6) | collective-permute-done | bytes 786464 | tf_op jit(solution)/shard_map/ppermute | solution.py:83
  100.9 3.8 %all-to-all-start.4 = ((bf16[32,96,256]{2,1,0:T(8,128)(2,1)}), bf16[32,96,256]{2,1,0:T(8,128)(2,1)S(1)}, u32[]{:S(2)}, u32[]{:S(2)}) async-start(bf16[32,96,256]{2,1,0:T(8,128)(2,1)} %pad_maximum_fusion.1), calls=%async_computation.4 | async-start | bytes 3145728 | tf_op jit(solution)/shard_map/all_to_all | solution.py:87
  105.9 1.8 collective-permute-done.3.refs_1_.refs_3_
  109.0 1.8 collective-permute-done.10.refs_13_.refs_15_
  113.5 17.3 %shard_map.110 = (bf16[8,4,96,256]{3,2,1,0:T(8,128)(2,1)}, bf16[2,4,4,64,512]{4,3,2,1,0:T(8,128)(2,1)}, bf16[2,4,256,512]{3,2,1,0:T(8,128)(2,1)}, bf16[2,4,256,5...) custom-call(s32[2]{0:T(128)} %pad_add_fusion.seat_ref, ...), custom_call_target="tpu_custom_call" | custom-call | flops 3221225472 | bytes 24117252 | tf_op jit(solution)/shard_map/pallas_call | solution.py:356
  130.8 11.6 %all-to-all-done.4 = bf16[32,96,256]{2,1,0:T(8,128)(2,1)S(1)} async-done(((bf16[32,96,256]{2,1,0:T(8,128)(2,1)}), bf16[32,96,256]{2,1,0:T(8,128)(2,1)S(1)}, u32[]{:S(2)}, u32[]{:S(2)}) %all-to-all-start.4) | async-done | bytes 1572896 | tf_op jit(solution)/shard_map/all_to_all | solution.py:87
  143.5 4.0 %all-to-all-start.3 = ((bf16[32,96,256]{2,1,0:T(8,128)(2,1)}), bf16[32,96,256]{2,1,0:T(8,128)(2,1)S(1)}, u32[]{:S(2)}, u32[]{:S(2)}) async-start(bf16[32,96,256]{2,1,0:T(8,128)(2,1)} %bitcast.86), calls=%async_computation.3 | async-start | bytes 3145728 | tf_op jit(solution)/shard_map/all_to_all | solution.py:87
  147.5 17.4 %shard_map.111 = (bf16[8,4,96,256]{3,2,1,0:T(8,128)(2,1)}, bf16[2,8,2,4,32,256]{5,4,3,2,1,0:T(8,128)(2,1)}, bf16[8,2,4,32,256]{4,3,2,1,0:T(8,128)(2,1)}, bf16[8,...) custom-call(s32[2]{0:T(128)} %pad_add_fusion.seat_ref, ...), custom_call_target="tpu_custom_call" | custom-call | flops 6442450944 | bytes 34078724 | tf_op jit(solution)/shard_map/pallas_call | solution.py:356
  166.2 3.8 %collective-permute-done.14 = bf16[8,4,32,256]{3,2,1,0:T(8,128)(2,1)S(1)} collective-permute-done((bf16[8,4,32,256]{3,2,1,0:T(8,128)(2,1)}, bf16[8,4,32,256]{3,2,1,0:T(8,128)(2,1)S(1)}, u32[]{:S(2)}, u32[]{:S(2)}) %collective-permute-start.14) | collective-permute-done | bytes 524320 | tf_op jit(solution)/shard_map/ppermute | solution.py:83
  170.8 2.5 fusion.2
  173.3 1.8 collective-permute-start.15
  178.7 11.2 %collective-permute-done.15 = bf16[8,4,32,256]{3,2,1,0:T(8,128)(2,1)S(1)} collective-permute-done((bf16[8,4,32,256]{3,2,1,0:T(8,128)(2,1)S(1)}, bf16[8,4,32,256]{3,2,1,0:T(8,128)(2,1)S(1)}, u32[]{:S(2)}, u32[]{:S(2)}) %collective-permute-start.15) | collective-permute-done | bytes 524320 | tf_op jit(solution)/shard_map/ppermute | solution.py:83
  189.9 2.4 add_convert_fusion.4
  193.5 4.6 %all-to-all-start.5 = ((bf16[32,96,256]{2,1,0:T(8,128)(2,1)}), bf16[32,96,256]{2,1,0:T(8,128)(2,1)S(1)}, u32[]{:S(2)}, u32[]{:S(2)}) async-start(bf16[32,96,256]{2,1,0:T(8,128)(2,1)} %bitcast.85), calls=%async_computation.5 | async-start | bytes 3145728 | tf_op jit(solution)/shard_map/all_to_all | solution.py:87
  202.1 24.3 %collective-permute-done.22 = bf16[8,4,32,256]{3,2,1,0:T(8,128)(2,1)S(1)} collective-permute-done((bf16[8,4,32,256]{3,2,1,0:T(8,128)(2,1)}, bf16[8,4,32,256]{3,2,1,0:T(8,128)(2,1)S(1)}, u32[]{:S(2)}, u32[]{:S(2)}) %collective-permute-start.22) | collective-permute-done | bytes 524320 | tf_op jit(solution)/shard_map/ppermute | solution.py:83
  228.8 11.5 %collective-permute-done.19 = bf16[4,2,4,32,256]{4,3,2,1,0:T(8,128)(2,1)S(1)} collective-permute-done((bf16[4,2,4,32,256]{4,3,2,1,0:T(8,128)(2,1)}, bf16[4,2,4,32,256]{4,3,2,1,0:T(8,128)(2,1)S(1)}, u32[]{:S(2)}, u32[]{:S(2)}) %collective-permute-start.19) | collective-permute-done | bytes 524320 | tf_op jit(solution)/shard_map/ppermute | solution.py:83
  241.9 5.5 %all-to-all-start.6 = ((bf16[8,3,4,32,256]{4,3,2,1,0:T(8,128)(2,1)}), bf16[8,3,4,32,256]{4,3,2,1,0:T(8,128)(2,1)}, u32[]{:S(2)}, u32[]{:S(2)}) async-start(bf16[8,3,4,32,256]{4,3,2,1,0:T(8,128)(2,1)} %pad_maximum_fusion.2), calls=%async_computation.6 | async-start | bytes 3145728 | tf_op jit(solution)/shard_map/all_to_all | solution.py:87
  250.2 2.6 copy.40
  254.8 1.7 copy.41
  256.5 28.1 %all-to-all-done.6.got_ref = bf16[8,3,4,32,256]{4,3,2,1,0:T(8,128)(2,1)} async-done(((bf16[8,3,4,32,256]{4,3,2,1,0:T(8,128)(2,1)}), bf16[8,3,4,32,256]{4,3,2,1,0:T(8,128)(2,1)}, u32[]{:S(2)}, u32[]{:S(2)}) %all-to-all-start.6) | async-done | bytes 1572896 | tf_op jit(solution)/shard_map/all_to_all | solution.py:87
  284.7 3.1 %shard_map.112 = (f32[12,32,512]{2,1,0:T(8,128)}, f32[24,32,256]{2,1,0:T(8,128)}, f32[24,32,256]{2,1,0:T(8,128)}, f32[12,64,256]{2,1,0:T(8,128)}) custom-call(bf16[8,3,4,32,256]{4,3,2,1,0:T(8,128)(2,1)} %all-to-all-done.6.got_ref), custom_call_target="tpu_custom_call" | custom-call | tf_op jit(solution)/shard_map/pallas_call | solution.py:433
  (112 shorter events, 45.4 us)
Async XLA Ops:
  3.0 27.6 %all-to-all-start = ((bf16[8,6,32,256]{3,2,1,0:T(8,128)(2,1)}), bf16[8,6,32,256]{3,2,1,0:T(8,128)(2,1)S(1)}, u32[]{:S(2)}, u32[]{:S(2)}) async-start(bf16[8,6,32,256]{3,2,1,0:T(8,128)(2,1)} %shard_map.109), calls=%async_computation | async-start | bytes 1572864 | tf_op jit(solution)/shard_map/all_to_all | solution.py:87
  30.6 25.9 %all-to-all-start.1 = ((bf16[8,2,3,32,256]{4,3,2,1,0:T(8,128)(2,1)}), bf16[8,2,3,32,256]{4,3,2,1,0:T(8,128)(2,1)S(1)}, u32[]{:S(2)}, u32[]{:S(2)}) async-start(bf16[8,2,3,32,256]{4,3,2,1,0:T(8,128)(2,1)} %pad_maximum_fusion.3), calls=%async_computation.1 | async-start | bytes 1572864 | tf_op jit(solution)/shard_map/all_to_all | solution.py:87
  35.0 21.5 %collective-permute-start.1 = (bf16[8,4,32,256]{3,2,1,0:T(8,128)(2,1)}, bf16[8,4,32,256]{3,2,1,0:T(8,128)(2,1)}, u32[]{:S(2)}, u32[]{:S(2)}) collective-permute-start(bf16[8,4,32,256]{3,2,1,0:T(8,128)(2,1)} %slice.127.refs_8_.refs_10_), channel_id=1, source_target_pairs={{0,4},{4,0},{8,12},{12,8},{16,20},{20,16},{24,28},{28,24},{1,5},{5... | collective-permute-start | bytes 1572872 | tf_op jit(solution)/shard_map/ppermute | solution.py:83
  37.0 19.4 %collective-permute-start = (bf16[8,4,32,256]{3,2,1,0:T(8,128)(2,1)}, bf16[8,4,32,256]{3,2,1,0:T(8,128)(2,1)}, u32[]{:S(2)}, u32[]{:S(2)}) collective-permute-start(bf16[8,4,32,256]{3,2,1,0:T(8,128)(2,1)} %slice.127.refs_8_.refs_10_), channel_id=1, source_target_pairs={{0,2},{1,3},{2,0},{3,1},{4,6},{5,7},{6,4},{7,5},{8,10},{9,11},{10,... | collective-permute-start | bytes 1572872 | tf_op jit(solution)/shard_map/ppermute | solution.py:83
  39.2 16.7 %collective-permute-start.2 = (bf16[8,2,32,256]{3,2,1,0:T(8,128)(2,1)}, bf16[8,2,32,256]{3,2,1,0:T(8,128)(2,1)}, u32[]{:S(2)}, u32[]{:S(2)}) collective-permute-start(bf16[8,2,32,256]{3,2,1,0:T(8,128)(2,1)} %slice.128.refs_0_.refs_2_), channel_id=1, source_target_pairs={{0,2},{1,3},{2,0},{3,1},{4,6},{5,7},{6,4},{7,5},{8,10},{9,11},{10,... | collective-permute-start | bytes 786440 | tf_op jit(solution)/shard_map/ppermute | solution.py:83
  57.3 42.5 %all-to-all-start.2 = ((bf16[32,96,256]{2,1,0:T(8,128)(2,1)}), bf16[32,96,256]{2,1,0:T(8,128)(2,1)S(1)}, u32[]{:S(2)}, u32[]{:S(2)}) async-start(bf16[32,96,256]{2,1,0:T(8,128)(2,1)} %pad_maximum_fusion), calls=%async_computation.2 | async-start | bytes 3145728 | tf_op jit(solution)/shard_map/all_to_all | solution.py:87
  61.9 36.7 %collective-permute-start.6 = (bf16[8,2,3,32,256]{4,3,2,1,0:T(8,128)(2,1)}, bf16[8,2,3,32,256]{4,3,2,1,0:T(8,128)(2,1)}, u32[]{:S(2)}, u32[]{:S(2)}) collective-permute-start(bf16[8,2,3,32,256]{4,3,2,1,0:T(8,128)(2,1)} %copy-done.6), channel_id=1, source_target_pairs={{0,2},{1,3},{2,0},{3,1},{4,6},{5,7},{6,4},{7,5},{8,10},{9,11},{10,... | collective-permute-start | bytes 2359304 | tf_op jit(solution)/shard_map/ppermute | solution.py:83
  63.7 26.6 %collective-permute-start.11 = (bf16[8,4,32,256]{3,2,1,0:T(8,128)(2,1)}, bf16[8,4,32,256]{3,2,1,0:T(8,128)(2,1)}, u32[]{:S(2)}, u32[]{:S(2)}) collective-permute-start(bf16[8,4,32,256]{3,2,1,0:T(8,128)(2,1)} %collective-permute-done.refs_10_.refs_12_), channel_id=1, source_target_pairs={{0,4},{4,0},{8,12},{12,8},{16,20},{20,16},{24,28},{28,24},{1,5},{5... | collective-permute-start | bytes 1572872 | tf_op jit(solution)/shard_map/ppermute | solution.py:83
  100.9 41.4 %all-to-all-start.4 = ((bf16[32,96,256]{2,1,0:T(8,128)(2,1)}), bf16[32,96,256]{2,1,0:T(8,128)(2,1)S(1)}, u32[]{:S(2)}, u32[]{:S(2)}) async-start(bf16[32,96,256]{2,1,0:T(8,128)(2,1)} %pad_maximum_fusion.1), calls=%async_computation.4 | async-start | bytes 3145728 | tf_op jit(solution)/shard_map/all_to_all | solution.py:87
  104.8 3.5 %collective-permute-start.8 = (bf16[8,4,32,256]{3,2,1,0:T(8,128)(2,1)}, bf16[8,4,32,256]{3,2,1,0:T(8,128)(2,1)}, u32[]{:S(2)}, u32[]{:S(2)}) collective-permute-start(bf16[8,4,32,256]{3,2,1,0:T(8,128)(2,1)} %slice.127.refs_8_.refs_10_), channel_id=1, source_target_pairs={{0,1},{1,0},{2,3},{3,2},{4,5},{5,4},{6,7},{7,6},{8,9},{9,8},{10,11... | collective-permute-start | bytes 1572872 | tf_op jit(solution)/shard_map/ppermute | solution.py:83
  104.9 2.8 collective-permute-start.3
  105.3 2.5 collective-permute-start.4
  105.4 6.9 %collective-permute-start.5 = (bf16[8,2,3,32,256]{4,3,2,1,0:T(8,128)(2,1)}, bf16[8,2,3,32,256]{4,3,2,1,0:T(8,128)(2,1)S(1)}, u32[]{:S(2)}, u32[]{:S(2)}) collective-permute-start(bf16[8,2,3,32,256]{4,3,2,1,0:T(8,128)(2,1)} %copy-done.6), channel_id=1, source_target_pairs={{0,1},{1,0},{2,3},{3,2},{4,5},{5,4},{6,7},{7,6},{8,9},{9,8},{10,11... | collective-permute-start | bytes 2359304 | tf_op jit(solution)/shard_map/ppermute | solution.py:83
  105.9 6.5 %collective-permute-start.7 = (bf16[8,2,3,32,256]{4,3,2,1,0:T(8,128)(2,1)}, bf16[8,2,3,32,256]{4,3,2,1,0:T(8,128)(2,1)S(1)}, u32[]{:S(2)}, u32[]{:S(2)}) collective-permute-start(bf16[8,2,3,32,256]{4,3,2,1,0:T(8,128)(2,1)} %collective-permute-done.6.refs_6_.refs_8_), channel_id=1, source_target_pairs={{0,1},{1,0},{2,3},{3,2},{4,5},{5,4},{6,7},{7,6},{8,9},{9,8},{10,11... | collective-permute-start | bytes 2359304 | tf_op jit(solution)/shard_map/ppermute | solution.py:83
  107.7 3.1 %collective-permute-start.10 = (bf16[8,4,32,256]{3,2,1,0:T(8,128)(2,1)}, bf16[8,4,32,256]{3,2,1,0:T(8,128)(2,1)}, u32[]{:S(2)}, u32[]{:S(2)}) collective-permute-start(bf16[8,4,32,256]{3,2,1,0:T(8,128)(2,1)} %collective-permute-done.1.refs_12_.refs_14_), channel_id=1, source_target_pairs={{0,1},{1,0},{2,3},{3,2},{4,5},{5,4},{6,7},{7,6},{8,9},{9,8},{10,11... | collective-permute-start | bytes 1572872 | tf_op jit(solution)/shard_map/ppermute | solution.py:83
  107.9 3.7 %collective-permute-start.9 = (bf16[8,4,32,256]{3,2,1,0:T(8,128)(2,1)}, bf16[8,4,32,256]{3,2,1,0:T(8,128)(2,1)}, u32[]{:S(2)}, u32[]{:S(2)}) collective-permute-start(bf16[8,4,32,256]{3,2,1,0:T(8,128)(2,1)} %collective-permute-done.refs_10_.refs_12_), channel_id=1, source_target_pairs={{0,1},{1,0},{2,3},{3,2},{4,5},{5,4},{6,7},{7,6},{8,9},{9,8},{10,11... | collective-permute-start | bytes 1572872 | tf_op jit(solution)/shard_map/ppermute | solution.py:83
  108.2 4.1 %collective-permute-start.12 = (bf16[8,4,32,256]{3,2,1,0:T(8,128)(2,1)}, bf16[8,4,32,256]{3,2,1,0:T(8,128)(2,1)}, u32[]{:S(2)}, u32[]{:S(2)}) collective-permute-start(bf16[8,4,32,256]{3,2,1,0:T(8,128)(2,1)} %collective-permute-done.11.refs_14_.refs_16_), channel_id=1, source_target_pairs={{0,1},{1,0},{2,3},{3,2},{4,5},{5,4},{6,7},{7,6},{8,9},{9,8},{10,11... | collective-permute-start | bytes 1572872 | tf_op jit(solution)/shard_map/ppermute | solution.py:83
  143.5 50.0 %all-to-all-start.3 = ((bf16[32,96,256]{2,1,0:T(8,128)(2,1)}), bf16[32,96,256]{2,1,0:T(8,128)(2,1)S(1)}, u32[]{:S(2)}, u32[]{:S(2)}) async-start(bf16[32,96,256]{2,1,0:T(8,128)(2,1)} %bitcast.86), calls=%async_computation.3 | async-start | bytes 3145728 | tf_op jit(solution)/shard_map/all_to_all | solution.py:87
  164.9 10.3 %collective-permute-start.16 = (bf16[8,2,4,32,256]{4,3,2,1,0:T(8,128)(2,1)}, bf16[8,2,4,32,256]{4,3,2,1,0:T(8,128)(2,1)S(1)}, u32[]{:S(2)}, u32[]{:S(2)}) collective-permute-start(bf16[8,2,4,32,256]{4,3,2,1,0:T(8,128)(2,1)} %get-tuple-element.51), channel_id=1, source_target_pairs={{0,1},{1,0},{2,3},{3,2},{4,5},{5,4},{6,7},{7,6},{8,9},{9,8},{10,11... | collective-permute-start | bytes 3145736 | tf_op jit(solution)/shard_map/ppermute | solution.py:83
  165.2 9.9 %collective-permute-start.17 = (bf16[8,2,4,32,256]{4,3,2,1,0:T(8,128)(2,1)}, bf16[8,2,4,32,256]{4,3,2,1,0:T(8,128)(2,1)S(1)}, u32[]{:S(2)}, u32[]{:S(2)}) collective-permute-start(bf16[8,2,4,32,256]{4,3,2,1,0:T(8,128)(2,1)} %get-tuple-element.52), channel_id=1, source_target_pairs={{0,1},{1,0},{2,3},{3,2},{4,5},{5,4},{6,7},{7,6},{8,9},{9,8},{10,11... | collective-permute-start | bytes 3145736 | tf_op jit(solution)/shard_map/ppermute | solution.py:83
  165.4 4.6 %collective-permute-start.14 = (bf16[8,4,32,256]{3,2,1,0:T(8,128)(2,1)}, bf16[8,4,32,256]{3,2,1,0:T(8,128)(2,1)S(1)}, u32[]{:S(2)}, u32[]{:S(2)}) collective-permute-start(bf16[8,4,32,256]{3,2,1,0:T(8,128)(2,1)} %get-tuple-element.49), channel_id=1, source_target_pairs={{0,1},{1,0},{2,3},{3,2},{4,5},{5,4},{6,7},{7,6},{8,9},{9,8},{10,11... | collective-permute-start | bytes 1572872 | tf_op jit(solution)/shard_map/ppermute | solution.py:83
  165.7 5.1 %collective-permute-start.21 = (bf16[8,4,32,256]{3,2,1,0:T(8,128)(2,1)}, bf16[8,4,32,256]{3,2,1,0:T(8,128)(2,1)S(1)}, u32[]{:S(2)}, u32[]{:S(2)}) collective-permute-start(bf16[8,4,32,256]{3,2,1,0:T(8,128)(2,1)} %get-tuple-element.56), channel_id=1, source_target_pairs={{0,1},{1,0},{2,3},{3,2},{4,5},{5,4},{6,7},{7,6},{8,9},{9,8},{10,11... | collective-permute-start | bytes 1572872 | tf_op jit(solution)/shard_map/ppermute | solution.py:83
  166.0 12.7 %collective-permute-start.13 = (bf16[8,4,32,256]{3,2,1,0:T(8,128)(2,1)}, bf16[8,4,32,256]{3,2,1,0:T(8,128)(2,1)S(1)}, u32[]{:S(2)}, u32[]{:S(2)}) collective-permute-start(bf16[8,4,32,256]{3,2,1,0:T(8,128)(2,1)} %get-tuple-element.48), channel_id=1, source_target_pairs={{0,1},{1,0},{2,3},{3,2},{4,5},{5,4},{6,7},{7,6},{8,9},{9,8},{10,11... | collective-permute-start | bytes 1572872 | tf_op jit(solution)/shard_map/ppermute | solution.py:83
  173.3 16.6 %collective-permute-start.15 = (bf16[8,4,32,256]{3,2,1,0:T(8,128)(2,1)S(1)}, bf16[8,4,32,256]{3,2,1,0:T(8,128)(2,1)S(1)}, u32[]{:S(2)}, u32[]{:S(2)}) collective-permute-start(bf16[8,4,32,256]{3,2,1,0:T(8,128)(2,1)S(1)} %get-tuple-element.75), channel_id=1, source_target_pairs={{0,4},{4,0},{8,12},{12,8},{16,20},{20,16},{24,28},{28,24},{1,5},{5... | collective-permute-start | bytes 1572872 | tf_op jit(solution)/shard_map/ppermute | solution.py:83
  177.2 15.3 %collective-permute-start.18 = (bf16[4,2,4,32,256]{4,3,2,1,0:T(8,128)(2,1)S(1)}, bf16[4,2,4,32,256]{4,3,2,1,0:T(8,128)(2,1)S(1)}, u32[]{:S(2)}, u32[]{:S(2)}) collective-permute-start(bf16[4,2,4,32,256]{4,3,2,1,0:T(8,128)(2,1)S(1)} %get-tuple-element.79), channel_id=1, source_target_pairs={{0,2},{1,3},{2,0},{3,1},{4,6},{5,7},{6,4},{7,5},{8,10},{9,11},{10,... | collective-permute-start | bytes 1572872 | tf_op jit(solution)/shard_map/ppermute | solution.py:83
  193.5 53.8 %copy-start = (bf16[32,96,256]{2,1,0:T(8,128)(2,1)}, bf16[32,96,256]{2,1,0:T(8,128)(2,1)S(1)}, u32[]{:S(2)}) copy-start(bf16[32,96,256]{2,1,0:T(8,128)(2,1)S(1)} %all-to-all-done.3) | copy-start | bytes 4718596
  193.5 48.3 %all-to-all-start.5 = ((bf16[32,96,256]{2,1,0:T(8,128)(2,1)}), bf16[32,96,256]{2,1,0:T(8,128)(2,1)S(1)}, u32[]{:S(2)}, u32[]{:S(2)}) async-start(bf16[32,96,256]{2,1,0:T(8,128)(2,1)} %bitcast.85), calls=%async_computation.5 | async-start | bytes 3145728 | tf_op jit(solution)/shard_map/all_to_all | solution.py:87
  198.1 4.0 %collective-permute-start.20 = (bf16[8,4,32,256]{3,2,1,0:T(8,128)(2,1)}, bf16[8,4,32,256]{3,2,1,0:T(8,128)(2,1)S(1)}, u32[]{:S(2)}, u32[]{:S(2)}) collective-permute-start(bf16[8,4,32,256]{3,2,1,0:T(8,128)(2,1)} %get-tuple-element.55), channel_id=1, source_target_pairs={{0,1},{1,0},{2,3},{3,2},{4,5},{5,4},{6,7},{7,6},{8,9},{9,8},{10,11... | collective-permute-start | bytes 1572872 | tf_op jit(solution)/shard_map/ppermute | solution.py:83
  198.4 28.0 %collective-permute-start.22 = (bf16[8,4,32,256]{3,2,1,0:T(8,128)(2,1)}, bf16[8,4,32,256]{3,2,1,0:T(8,128)(2,1)S(1)}, u32[]{:S(2)}, u32[]{:S(2)}) collective-permute-start(bf16[8,4,32,256]{3,2,1,0:T(8,128)(2,1)} %get-tuple-element.74), channel_id=1, source_target_pairs={{0,4},{4,0},{8,12},{12,8},{16,20},{20,16},{24,28},{28,24},{1,5},{5... | collective-permute-start | bytes 1572872 | tf_op jit(solution)/shard_map/ppermute | solution.py:83
  200.1 27.3 %collective-permute-start.23 = (bf16[8,4,32,256]{3,2,1,0:T(8,128)(2,1)}, bf16[8,4,32,256]{3,2,1,0:T(8,128)(2,1)S(1)}, u32[]{:S(2)}, u32[]{:S(2)}) collective-permute-start(bf16[8,4,32,256]{3,2,1,0:T(8,128)(2,1)} %add_convert_fusion.4), channel_id=1, source_target_pairs={{0,2},{1,3},{2,0},{3,1},{4,6},{5,7},{6,4},{7,5},{8,10},{9,11},{10,... | collective-permute-start | bytes 1572872 | tf_op jit(solution)/shard_map/ppermute | solution.py:83
  201.6 38.7 %collective-permute-start.19 = (bf16[4,2,4,32,256]{4,3,2,1,0:T(8,128)(2,1)}, bf16[4,2,4,32,256]{4,3,2,1,0:T(8,128)(2,1)S(1)}, u32[]{:S(2)}, u32[]{:S(2)}) collective-permute-start(bf16[4,2,4,32,256]{4,3,2,1,0:T(8,128)(2,1)} %get-tuple-element.54), channel_id=1, source_target_pairs={{0,2},{1,3},{2,0},{3,1},{4,6},{5,7},{6,4},{7,5},{8,10},{9,11},{10,... | collective-permute-start | bytes 1572872 | tf_op jit(solution)/shard_map/ppermute | solution.py:83
  241.9 42.8 %all-to-all-start.6 = ((bf16[8,3,4,32,256]{4,3,2,1,0:T(8,128)(2,1)}), bf16[8,3,4,32,256]{4,3,2,1,0:T(8,128)(2,1)}, u32[]{:S(2)}, u32[]{:S(2)}) async-start(bf16[8,3,4,32,256]{4,3,2,1,0:T(8,128)(2,1)} %pad_maximum_fusion.2), calls=%async_computation.6 | async-start | bytes 3145728 | tf_op jit(solution)/shard_map/all_to_all | solution.py:87
  (18 other events, 152.1 us)

commit v12 on v11

--- a/solution.py
+++ b/solution.py
@@ -415,19 +415,24 @@
         [x.shape, own_shape] + [own_shape[1:]] * 2 + [mid_shape] + [mid_shape[2:]] * 4,
     )
     mid_keep = sends.pop(2)
-    far = add(mid_keep[1, 1], xor_permute(sends[5], 1))
-    own_far = add(own_keep[1], xor_permute(sends[1], 1))
-    far = add(add(mid_keep[0, 1], xor_permute(sends[3], 1)), xor_permute(far, 1, "dp"))
-    own_near = add(own_keep[0], xor_permute(sends[0], 1))
-    near = add(mid_keep[1, 0], xor_permute(sends[4], 1))
-    part = ndp // 2
+    own_sends, mid_sends = sends[:2], sends[2:]
+    own_far = add(own_keep[1], xor_permute(own_sends[1], 1))
+    own_near = add(own_keep[0], xor_permute(own_sends[0], 1))
+    there = add(mid_keep[1, 1], after(xor_permute(mid_sends[3], 1), own_far))
+    here = add(mid_keep[0, 1], xor_permute(mid_sends[1], 1))
+    near = add(mid_keep[1, 0], xor_permute(mid_sends[2], 1))
+    part, half = 3 * ndp // 8, ndp // 2
     own_first = add(own_near[:part], xor_permute(own_far[:part], 2))
-    gin = exchange(after(gin.reshape(ndp * nb, -1, BLK), out, far, own_first), everyone)
+    far_first = add(here[:half], xor_permute(there[:half], 1, "dp"))
+    gin = after(gin.reshape(ndp * nb, -1, BLK), out, far_first, own_first)
+    gin = exchange(gin, everyone)
     own_last = add(own_near[part:], xor_permute(after(own_far[part:], own_first), 2))
     own = jnp.concatenate([own_first, own_last], axis=0)
-    near = xor_permute(near, 1, "dp")
-    near = add(add(mid_keep[0, 0], xor_permute(sends[2], 1)), near)
-    mid = add(near, xor_permute(far, 2))
+    far_last = xor_permute(after(there[half:], far_first), 1, "dp")
+    far_last = add(here[half:], far_last)
+    far = jnp.concatenate([xor_permute(far_first, 2), xor_permute(far_last, 2)], axis=0)
+    near = add(add(mid_keep[0, 0], xor_permute(mid_sends[0], 1)), xor_permute(near, 1, "dp"))
+    mid = add(near, far)
     dealt = jnp.concatenate([own, mid[:, None]], axis=1)
     got = exchange(after(dealt, gin), "dp")
     grads = pl.pallas_call(

time: 289 us -> 288 us (level)
    ppermute x24 -> x26, waiting for transfers between devices: 94.4 us -> 93.4 us  [xor_permute(): lax.ppermute(x, axis, [(i, i ^ mask) for i in range(lax.axis_size(axis))])]
    convert_element_type x5 -> x6, other arithmetic: 7.14 us -> 6.3 us  [add(): return (x.astype(jnp.float32) + y.astype(jnp.float32)).astype(jnp.bfloat16)]
    ppermute x24 -> x26, starting transfers between devices: 17.7 us -> 18.6 us  [xor_permute(): lax.ppermute(x, axis, [(i, i ^ mask) for i in range(lax.axis_size(axis))])]
    unnamed x38 -> x40, local copies, waits for them, and re-layouts: 12.6 us -> 12.6 us
  transfers between devices with their start and end apart: 31 -> 33, of which waited for: 19 -> 19; matrix products, arithmetic and copies ran while one was open for 12% -> 12% of each run, Pallas kernels for 12% -> 12%
where the time goes in v12:
time: 288 us; the launch traced here: 287 us
  waiting for transfers between devices  153 us (53%)
  starting transfers between devices  51.4 us (18%)
  Pallas kernels  40 us (14%)
  local copies, waits for them, and re-layouts  26.7 us (9%)
  other arithmetic  14.7 us (5%)
    ppermute x26, waiting for transfers between devices, xor_permute(): lax.ppermute(x, axis, [(i, i ^ mask) for i in range(lax.axis_size(axis))])  93.4 us
    all_to_all x7, waiting for transfers between devices, exchange(): return lax.all_to_all(x, axes, split_axis=0, concat_axis=0, tiled=True)  60 us
    pallas_call x2, Pallas kernels, on_chip(): pl.pallas_call(kernel, out_shape=[jax.ShapeDtypeStruct(shape, jnp.bfloat1...  34.5 us
    all_to_all x7, starting transfers between devices, exchange(): return lax.all_to_all(x, axes, split_axis=0, concat_axis=0, tiled=True)  32.9 us
    ppermute x26, starting transfers between devices, xor_permute(): lax.ppermute(x, axis, [(i, i ^ mask) for i in range(lax.axis_size(axis))])  18.6 us
    unnamed x40, local copies, waits for them, and re-layouts  12.6 us
    convert_element_type x6, other arithmetic, add(): return (x.astype(jnp.float32) + y.astype(jnp.float32)).astype(jnp.bfloat16)  6.3 us
  transfers between devices with their start and end apart: 33, of which 19 were waited for; matrix products, arithmetic and copies ran while one was open for 12% of the time, Pallas kernels for 12%

profile of v12, /device:TPU:0, one launch (start us, length us, event | category | flops | bytes accessed | tf_op | source)
XLA Modules:
  0.0 287.2 jit_solution(9228380109602115589)
XLA Ops:
  0.6 2.3 shard_map.109
  3.0 7.4 %all-to-all-start = ((bf16[8,6,32,256]{3,2,1,0:T(8,128)(2,1)}), bf16[8,6,32,256]{3,2,1,0:T(8,128)(2,1)S(1)}, u32[]{:S(2)}, u32[]{:S(2)}) async-start(bf16[8,6,32,256]{3,2,1,0:T(8,128)(2,1)} %shard_map.109), calls=%async_computation | async-start | bytes 1572864 | tf_op jit(solution)/shard_map/all_to_all | solution.py:87
  11.6 19.0 %all-to-all-done = bf16[8,6,32,256]{3,2,1,0:T(8,128)(2,1)S(1)} async-done(((bf16[8,6,32,256]{3,2,1,0:T(8,128)(2,1)}), bf16[8,6,32,256]{3,2,1,0:T(8,128)(2,1)S(1)}, u32[]{:S(2)}, u32[]{:S(2)}) %all-to-all-start) | async-done | bytes 786464 | tf_op jit(solution)/shard_map/all_to_all | solution.py:87
  30.6 3.6 %all-to-all-start.1 = ((bf16[8,2,3,32,256]{4,3,2,1,0:T(8,128)(2,1)}), bf16[8,2,3,32,256]{4,3,2,1,0:T(8,128)(2,1)S(1)}, u32[]{:S(2)}, u32[]{:S(2)}) async-start(bf16[8,2,3,32,256]{4,3,2,1,0:T(8,128)(2,1)} %pad_maximum_fusion.3), calls=%async_computation.1 | async-start | bytes 1572864 | tf_op jit(solution)/shard_map/all_to_all | solution.py:87
  35.0 2.0 collective-permute-start.1
  44.9 11.0 %collective-permute-done.2.refs_2_.refs_4_ = bf16[8,2,32,256]{3,2,1,0:T(8,128)(2,1)} collective-permute-done((bf16[8,2,32,256]{3,2,1,0:T(8,128)(2,1)}, bf16[8,2,32,256]{3,2,1,0:T(8,128)(2,1)}, u32[]{:S(2)}, u32[]{:S(2)}) %collective-permute-start.2) | collective-permute-done | bytes 262176 | tf_op jit(solution)/shard_map/ppermute | solution.py:83
  57.3 4.6 %all-to-all-start.2 = ((bf16[32,96,256]{2,1,0:T(8,128)(2,1)}), bf16[32,96,256]{2,1,0:T(8,128)(2,1)S(1)}, u32[]{:S(2)}, u32[]{:S(2)}) async-start(bf16[32,96,256]{2,1,0:T(8,128)(2,1)} %pad_maximum_fusion), calls=%async_computation.2 | async-start | bytes 3145728 | tf_op jit(solution)/shard_map/all_to_all | solution.py:87
  61.9 1.8 collective-permute-start.6
  71.3 2.4 pad_maximum_fusion.1
  73.7 16.6 %collective-permute-done.11.refs_14_.refs_16_ = bf16[8,4,32,256]{3,2,1,0:T(8,128)(2,1)} collective-permute-done((bf16[8,4,32,256]{3,2,1,0:T(8,128)(2,1)}, bf16[8,4,32,256]{3,2,1,0:T(8,128)(2,1)}, u32[]{:S(2)}, u32[]{:S(2)}) %collective-permute-start.11) | collective-permute-done | bytes 524320 | tf_op jit(solution)/shard_map/ppermute | solution.py:83
  90.3 8.2 %collective-permute-done.6.refs_6_.refs_8_ = bf16[8,2,3,32,256]{4,3,2,1,0:T(8,128)(2,1)} collective-permute-done((bf16[8,2,3,32,256]{4,3,2,1,0:T(8,128)(2,1)}, bf16[8,2,3,32,256]{4,3,2,1,0:T(8,128)(2,1)}, u32[]{:S(2)}, u32[]{:S(2)}) %collective-permute-start.6) | collective-permute-done | bytes 786464 | tf_op jit(solution)/shard_map/ppermute | solution.py:83
  100.9 3.8 %all-to-all-start.4 = ((bf16[32,96,256]{2,1,0:T(8,128)(2,1)}), bf16[32,96,256]{2,1,0:T(8,128)(2,1)S(1)}, u32[]{:S(2)}, u32[]{:S(2)}) async-start(bf16[32,96,256]{2,1,0:T(8,128)(2,1)} %pad_maximum_fusion.1), calls=%async_computation.4 | async-start | bytes 3145728 | tf_op jit(solution)/shard_map/all_to_all | solution.py:87
  105.9 1.8 collective-permute-done.3.refs_1_.refs_3_
  109.0 1.9 collective-permute-done.10.refs_13_.refs_15_
  113.5 17.3 %shard_map.110 = (bf16[8,4,96,256]{3,2,1,0:T(8,128)(2,1)}, bf16[2,4,4,64,512]{4,3,2,1,0:T(8,128)(2,1)}, bf16[2,4,256,512]{3,2,1,0:T(8,128)(2,1)}, bf16[2,4,256,5...) custom-call(s32[2]{0:T(128)} %pad_add_fusion.seat_ref, ...), custom_call_target="tpu_custom_call" | custom-call | flops 3221225472 | bytes 24117252 | tf_op jit(solution)/shard_map/pallas_call | solution.py:356
  130.8 11.6 %all-to-all-done.4 = bf16[32,96,256]{2,1,0:T(8,128)(2,1)S(1)} async-done(((bf16[32,96,256]{2,1,0:T(8,128)(2,1)}), bf16[32,96,256]{2,1,0:T(8,128)(2,1)S(1)}, u32[]{:S(2)}, u32[]{:S(2)}) %all-to-all-start.4) | async-done | bytes 1572896 | tf_op jit(solution)/shard_map/all_to_all | solution.py:87
  143.5 4.0 %all-to-all-start.3 = ((bf16[32,96,256]{2,1,0:T(8,128)(2,1)}), bf16[32,96,256]{2,1,0:T(8,128)(2,1)S(1)}, u32[]{:S(2)}, u32[]{:S(2)}) async-start(bf16[32,96,256]{2,1,0:T(8,128)(2,1)} %bitcast.86), calls=%async_computation.3 | async-start | bytes 3145728 | tf_op jit(solution)/shard_map/all_to_all | solution.py:87
  147.5 17.3 %shard_map.111 = (bf16[8,4,96,256]{3,2,1,0:T(8,128)(2,1)}, bf16[2,8,2,4,32,256]{5,4,3,2,1,0:T(8,128)(2,1)}, bf16[8,2,4,32,256]{4,3,2,1,0:T(8,128)(2,1)}, bf16[8,...) custom-call(s32[2]{0:T(128)} %pad_add_fusion.seat_ref, ...), custom_call_target="tpu_custom_call" | custom-call | flops 6442450944 | bytes 34078724 | tf_op jit(solution)/shard_map/pallas_call | solution.py:356
  169.2 2.6 fusion
  174.2 1.8 collective-permute-start.16
  177.5 7.2 %collective-permute-done.16 = bf16[4,4,32,256]{3,2,1,0:T(8,128)(2,1)S(1)} collective-permute-done((bf16[4,4,32,256]{3,2,1,0:T(8,128)(2,1)S(1)}, bf16[4,4,32,256]{3,2,1,0:T(8,128)(2,1)S(1)}, u32[]{:S(2)}, u32[]{:S(2)}) %collective-permute-start.16) | collective-permute-done | bytes 262176 | tf_op jit(solution)/shard_map/ppermute | solution.py:83
  185.5 3.5 %collective-permute-done.18 = bf16[3,2,4,32,256]{4,3,2,1,0:T(8,128)(2,1)S(1)} collective-permute-done((bf16[3,2,4,32,256]{4,3,2,1,0:T(8,128)(2,1)S(1)}, bf16[3,2,4,32,256]{4,3,2,1,0:T(8,128)(2,1)S(1)}, u32[]{:S(2)}, u32[]{:S(2)}) %collective-permute-start.18) | collective-permute-done | bytes 393248 | tf_op jit(solution)/shard_map/ppermute | solution.py:83
  189.2 4.1 %all-to-all-start.5 = ((bf16[32,96,256]{2,1,0:T(8,128)(2,1)}), bf16[32,96,256]{2,1,0:T(8,128)(2,1)S(1)}, u32[]{:S(2)}, u32[]{:S(2)}) async-start(bf16[32,96,256]{2,1,0:T(8,128)(2,1)} %bitcast.85), calls=%async_computation.5 | async-start | bytes 3145728 | tf_op jit(solution)/shard_map/all_to_all | solution.py:87
  193.3 1.8 collective-permute-start.24
  196.5 1.8 collective-permute-start.23
  198.6 16.8 %collective-permute-done.24 = bf16[4,4,32,256]{3,2,1,0:T(8,128)(2,1)S(1)} collective-permute-done((bf16[4,4,32,256]{3,2,1,0:T(8,128)(2,1)}, bf16[4,4,32,256]{3,2,1,0:T(8,128)(2,1)S(1)}, u32[]{:S(2)}, u32[]{:S(2)}) %collective-permute-start.24) | collective-permute-done | bytes 262176 | tf_op jit(solution)/shard_map/ppermute | solution.py:83
  217.0 12.8 %collective-permute-done.22 = bf16[8,4,32,256]{3,2,1,0:T(8,128)(2,1)S(1)} collective-permute-done((bf16[8,4,32,256]{3,2,1,0:T(8,128)(2,1)}, bf16[8,4,32,256]{3,2,1,0:T(8,128)(2,1)S(1)}, u32[]{:S(2)}, u32[]{:S(2)}) %collective-permute-start.22) | collective-permute-done | bytes 524320 | tf_op jit(solution)/shard_map/ppermute | solution.py:83
  229.8 8.4 %collective-permute-done.25 = bf16[4,4,32,256]{3,2,1,0:T(8,128)(2,1)S(1)} collective-permute-done((bf16[4,4,32,256]{3,2,1,0:T(8,128)(2,1)S(1)}, bf16[4,4,32,256]{3,2,1,0:T(8,128)(2,1)S(1)}, u32[]{:S(2)}, u32[]{:S(2)}) %collective-permute-start.25) | collective-permute-done | bytes 262176 | tf_op jit(solution)/shard_map/ppermute | solution.py:83
  241.3 5.5 %all-to-all-start.6 = ((bf16[8,3,4,32,256]{4,3,2,1,0:T(8,128)(2,1)}), bf16[8,3,4,32,256]{4,3,2,1,0:T(8,128)(2,1)}, u32[]{:S(2)}, u32[]{:S(2)}) async-start(bf16[8,3,4,32,256]{4,3,2,1,0:T(8,128)(2,1)} %pad_maximum_fusion.2), calls=%async_computation.6 | async-start | bytes 3145728 | tf_op jit(solution)/shard_map/all_to_all | solution.py:87
  249.7 2.6 copy.40
  256.0 28.1 %all-to-all-done.6.got_ref = bf16[8,3,4,32,256]{4,3,2,1,0:T(8,128)(2,1)} async-done(((bf16[8,3,4,32,256]{4,3,2,1,0:T(8,128)(2,1)}), bf16[8,3,4,32,256]{4,3,2,1,0:T(8,128)(2,1)}, u32[]{:S(2)}, u32[]{:S(2)}) %all-to-all-start.6) | async-done | bytes 1572896 | tf_op jit(solution)/shard_map/all_to_all | solution.py:87
  284.1 3.1 %shard_map.112 = (f32[12,32,512]{2,1,0:T(8,128)}, f32[24,32,256]{2,1,0:T(8,128)}, f32[24,32,256]{2,1,0:T(8,128)}, f32[12,64,256]{2,1,0:T(8,128)}) custom-call(bf16[8,3,4,32,256]{4,3,2,1,0:T(8,128)(2,1)} %all-to-all-done.6.got_ref), custom_call_target="tpu_custom_call" | custom-call | tf_op jit(solution)/shard_map/pallas_call | solution.py:438
  (121 shorter events, 49.4 us)
Async XLA Ops:
  3.0 27.6 %all-to-all-start = ((bf16[8,6,32,256]{3,2,1,0:T(8,128)(2,1)}), bf16[8,6,32,256]{3,2,1,0:T(8,128)(2,1)S(1)}, u32[]{:S(2)}, u32[]{:S(2)}) async-start(bf16[8,6,32,256]{3,2,1,0:T(8,128)(2,1)} %shard_map.109), calls=%async_computation | async-start | bytes 1572864 | tf_op jit(solution)/shard_map/all_to_all | solution.py:87
  30.6 25.9 %all-to-all-start.1 = ((bf16[8,2,3,32,256]{4,3,2,1,0:T(8,128)(2,1)}), bf16[8,2,3,32,256]{4,3,2,1,0:T(8,128)(2,1)S(1)}, u32[]{:S(2)}, u32[]{:S(2)}) async-start(bf16[8,2,3,32,256]{4,3,2,1,0:T(8,128)(2,1)} %pad_maximum_fusion.3), calls=%async_computation.1 | async-start | bytes 1572864 | tf_op jit(solution)/shard_map/all_to_all | solution.py:87
  35.0 21.5 %collective-permute-start.1 = (bf16[8,4,32,256]{3,2,1,0:T(8,128)(2,1)}, bf16[8,4,32,256]{3,2,1,0:T(8,128)(2,1)}, u32[]{:S(2)}, u32[]{:S(2)}) collective-permute-start(bf16[8,4,32,256]{3,2,1,0:T(8,128)(2,1)} %slice.143.refs_8_.refs_10_), channel_id=1, source_target_pairs={{0,4},{4,0},{8,12},{12,8},{16,20},{20,16},{24,28},{28,24},{1,5},{5... | collective-permute-start | bytes 1572872 | tf_op jit(solution)/shard_map/ppermute | solution.py:83
  37.0 19.4 %collective-permute-start = (bf16[8,4,32,256]{3,2,1,0:T(8,128)(2,1)}, bf16[8,4,32,256]{3,2,1,0:T(8,128)(2,1)}, u32[]{:S(2)}, u32[]{:S(2)}) collective-permute-start(bf16[8,4,32,256]{3,2,1,0:T(8,128)(2,1)} %slice.143.refs_8_.refs_10_), channel_id=1, source_target_pairs={{0,2},{1,3},{2,0},{3,1},{4,6},{5,7},{6,4},{7,5},{8,10},{9,11},{10,... | collective-permute-start | bytes 1572872 | tf_op jit(solution)/shard_map/ppermute | solution.py:83
  39.2 16.7 %collective-permute-start.2 = (bf16[8,2,32,256]{3,2,1,0:T(8,128)(2,1)}, bf16[8,2,32,256]{3,2,1,0:T(8,128)(2,1)}, u32[]{:S(2)}, u32[]{:S(2)}) collective-permute-start(bf16[8,2,32,256]{3,2,1,0:T(8,128)(2,1)} %slice.144.refs_0_.refs_2_), channel_id=1, source_target_pairs={{0,2},{1,3},{2,0},{3,1},{4,6},{5,7},{6,4},{7,5},{8,10},{9,11},{10,... | collective-permute-start | bytes 786440 | tf_op jit(solution)/shard_map/ppermute | solution.py:83
  57.3 42.5 %all-to-all-start.2 = ((bf16[32,96,256]{2,1,0:T(8,128)(2,1)}), bf16[32,96,256]{2,1,0:T(8,128)(2,1)S(1)}, u32[]{:S(2)}, u32[]{:S(2)}) async-start(bf16[32,96,256]{2,1,0:T(8,128)(2,1)} %pad_maximum_fusion), calls=%async_computation.2 | async-start | bytes 3145728 | tf_op jit(solution)/shard_map/all_to_all | solution.py:87
  61.9 36.7 %collective-permute-start.6 = (bf16[8,2,3,32,256]{4,3,2,1,0:T(8,128)(2,1)}, bf16[8,2,3,32,256]{4,3,2,1,0:T(8,128)(2,1)}, u32[]{:S(2)}, u32[]{:S(2)}) collective-permute-start(bf16[8,2,3,32,256]{4,3,2,1,0:T(8,128)(2,1)} %copy-done.7), channel_id=1, source_target_pairs={{0,2},{1,3},{2,0},{3,1},{4,6},{5,7},{6,4},{7,5},{8,10},{9,11},{10,... | collective-permute-start | bytes 2359304 | tf_op jit(solution)/shard_map/ppermute | solution.py:83
  63.7 26.6 %collective-permute-start.11 = (bf16[8,4,32,256]{3,2,1,0:T(8,128)(2,1)}, bf16[8,4,32,256]{3,2,1,0:T(8,128)(2,1)}, u32[]{:S(2)}, u32[]{:S(2)}) collective-permute-start(bf16[8,4,32,256]{3,2,1,0:T(8,128)(2,1)} %collective-permute-done.refs_10_.refs_12_), channel_id=1, source_target_pairs={{0,4},{4,0},{8,12},{12,8},{16,20},{20,16},{24,28},{28,24},{1,5},{5... | collective-permute-start | bytes 1572872 | tf_op jit(solution)/shard_map/ppermute | solution.py:83
  100.9 41.4 %all-to-all-start.4 = ((bf16[32,96,256]{2,1,0:T(8,128)(2,1)}), bf16[32,96,256]{2,1,0:T(8,128)(2,1)S(1)}, u32[]{:S(2)}, u32[]{:S(2)}) async-start(bf16[32,96,256]{2,1,0:T(8,128)(2,1)} %pad_maximum_fusion.1), calls=%async_computation.4 | async-start | bytes 3145728 | tf_op jit(solution)/shard_map/all_to_all | solution.py:87
  104.8 3.5 %collective-permute-start.8 = (bf16[8,4,32,256]{3,2,1,0:T(8,128)(2,1)}, bf16[8,4,32,256]{3,2,1,0:T(8,128)(2,1)}, u32[]{:S(2)}, u32[]{:S(2)}) collective-permute-start(bf16[8,4,32,256]{3,2,1,0:T(8,128)(2,1)} %slice.143.refs_8_.refs_10_), channel_id=1, source_target_pairs={{0,1},{1,0},{2,3},{3,2},{4,5},{5,4},{6,7},{7,6},{8,9},{9,8},{10,11... | collective-permute-start | bytes 1572872 | tf_op jit(solution)/shard_map/ppermute | solution.py:83
  104.9 2.8 collective-permute-start.3
  105.4 6.9 %collective-permute-start.5 = (bf16[8,2,3,32,256]{4,3,2,1,0:T(8,128)(2,1)}, bf16[8,2,3,32,256]{4,3,2,1,0:T(8,128)(2,1)S(1)}, u32[]{:S(2)}, u32[]{:S(2)}) collective-permute-start(bf16[8,2,3,32,256]{4,3,2,1,0:T(8,128)(2,1)} %copy-done.7), channel_id=1, source_target_pairs={{0,1},{1,0},{2,3},{3,2},{4,5},{5,4},{6,7},{7,6},{8,9},{9,8},{10,11... | collective-permute-start | bytes 2359304 | tf_op jit(solution)/shard_map/ppermute | solution.py:83
  105.9 6.5 %collective-permute-start.7 = (bf16[8,2,3,32,256]{4,3,2,1,0:T(8,128)(2,1)}, bf16[8,2,3,32,256]{4,3,2,1,0:T(8,128)(2,1)S(1)}, u32[]{:S(2)}, u32[]{:S(2)}) collective-permute-start(bf16[8,2,3,32,256]{4,3,2,1,0:T(8,128)(2,1)} %collective-permute-done.6.refs_6_.refs_8_), channel_id=1, source_target_pairs={{0,1},{1,0},{2,3},{3,2},{4,5},{5,4},{6,7},{7,6},{8,9},{9,8},{10,11... | collective-permute-start | bytes 2359304 | tf_op jit(solution)/shard_map/ppermute | solution.py:83
  107.7 3.1 %collective-permute-start.10 = (bf16[8,4,32,256]{3,2,1,0:T(8,128)(2,1)}, bf16[8,4,32,256]{3,2,1,0:T(8,128)(2,1)}, u32[]{:S(2)}, u32[]{:S(2)}) collective-permute-start(bf16[8,4,32,256]{3,2,1,0:T(8,128)(2,1)} %collective-permute-done.1.refs_12_.refs_14_), channel_id=1, source_target_pairs={{0,1},{1,0},{2,3},{3,2},{4,5},{5,4},{6,7},{7,6},{8,9},{9,8},{10,11... | collective-permute-start | bytes 1572872 | tf_op jit(solution)/shard_map/ppermute | solution.py:83
  107.9 3.7 %collective-permute-start.9 = (bf16[8,4,32,256]{3,2,1,0:T(8,128)(2,1)}, bf16[8,4,32,256]{3,2,1,0:T(8,128)(2,1)}, u32[]{:S(2)}, u32[]{:S(2)}) collective-permute-start(bf16[8,4,32,256]{3,2,1,0:T(8,128)(2,1)} %collective-permute-done.refs_10_.refs_12_), channel_id=1, source_target_pairs={{0,1},{1,0},{2,3},{3,2},{4,5},{5,4},{6,7},{7,6},{8,9},{9,8},{10,11... | collective-permute-start | bytes 1572872 | tf_op jit(solution)/shard_map/ppermute | solution.py:83
  108.2 4.1 %collective-permute-start.12 = (bf16[8,4,32,256]{3,2,1,0:T(8,128)(2,1)}, bf16[8,4,32,256]{3,2,1,0:T(8,128)(2,1)}, u32[]{:S(2)}, u32[]{:S(2)}) collective-permute-start(bf16[8,4,32,256]{3,2,1,0:T(8,128)(2,1)} %collective-permute-done.11.refs_14_.refs_16_), channel_id=1, source_target_pairs={{0,1},{1,0},{2,3},{3,2},{4,5},{5,4},{6,7},{7,6},{8,9},{9,8},{10,11... | collective-permute-start | bytes 1572872 | tf_op jit(solution)/shard_map/ppermute | solution.py:83
  143.5 45.7 %all-to-all-start.3 = ((bf16[32,96,256]{2,1,0:T(8,128)(2,1)}), bf16[32,96,256]{2,1,0:T(8,128)(2,1)S(1)}, u32[]{:S(2)}, u32[]{:S(2)}) async-start(bf16[32,96,256]{2,1,0:T(8,128)(2,1)} %bitcast.86), calls=%async_computation.3 | async-start | bytes 3145728 | tf_op jit(solution)/shard_map/all_to_all | solution.py:87
  164.7 2.9 %collective-permute-start.15 = (bf16[8,2,4,32,256]{4,3,2,1,0:T(8,128)(2,1)}, bf16[8,2,4,32,256]{4,3,2,1,0:T(8,128)(2,1)S(1)}, u32[]{:S(2)}, u32[]{:S(2)}) collective-permute-start(bf16[8,2,4,32,256]{4,3,2,1,0:T(8,128)(2,1)} %get-tuple-element.53), channel_id=1, source_target_pairs={{0,1},{1,0},{2,3},{3,2},{4,5},{5,4},{6,7},{7,6},{8,9},{9,8},{10,11... | collective-permute-start | bytes 3145736 | tf_op jit(solution)/shard_map/ppermute | solution.py:83
  165.1 4.1 %collective-permute-start.17 = (bf16[8,2,4,32,256]{4,3,2,1,0:T(8,128)(2,1)}, bf16[8,2,4,32,256]{4,3,2,1,0:T(8,128)(2,1)S(1)}, u32[]{:S(2)}, u32[]{:S(2)}) collective-permute-start(bf16[8,2,4,32,256]{4,3,2,1,0:T(8,128)(2,1)} %get-tuple-element.55), channel_id=1, source_target_pairs={{0,1},{1,0},{2,3},{3,2},{4,5},{5,4},{6,7},{7,6},{8,9},{9,8},{10,11... | collective-permute-start | bytes 3145736 | tf_op jit(solution)/shard_map/ppermute | solution.py:83
  165.3 6.5 %collective-permute-start.14 = (bf16[8,4,32,256]{3,2,1,0:T(8,128)(2,1)}, bf16[8,4,32,256]{3,2,1,0:T(8,128)(2,1)S(1)}, u32[]{:S(2)}, u32[]{:S(2)}) collective-permute-start(bf16[8,4,32,256]{3,2,1,0:T(8,128)(2,1)} %get-tuple-element.51), channel_id=1, source_target_pairs={{0,1},{1,0},{2,3},{3,2},{4,5},{5,4},{6,7},{7,6},{8,9},{9,8},{10,11... | collective-permute-start | bytes 1572872 | tf_op jit(solution)/shard_map/ppermute | solution.py:83
  165.6 6.3 %collective-permute-start.13 = (bf16[8,4,32,256]{3,2,1,0:T(8,128)(2,1)}, bf16[8,4,32,256]{3,2,1,0:T(8,128)(2,1)S(1)}, u32[]{:S(2)}, u32[]{:S(2)}) collective-permute-start(bf16[8,4,32,256]{3,2,1,0:T(8,128)(2,1)} %get-tuple-element.50), channel_id=1, source_target_pairs={{0,1},{1,0},{2,3},{3,2},{4,5},{5,4},{6,7},{7,6},{8,9},{9,8},{10,11... | collective-permute-start | bytes 1572872 | tf_op jit(solution)/shard_map/ppermute | solution.py:83
  165.8 6.0 %collective-permute-start.21 = (bf16[8,4,32,256]{3,2,1,0:T(8,128)(2,1)}, bf16[8,4,32,256]{3,2,1,0:T(8,128)(2,1)S(1)}, u32[]{:S(2)}, u32[]{:S(2)}) collective-permute-start(bf16[8,4,32,256]{3,2,1,0:T(8,128)(2,1)} %get-tuple-element.59), channel_id=1, source_target_pairs={{0,1},{1,0},{2,3},{3,2},{4,5},{5,4},{6,7},{7,6},{8,9},{9,8},{10,11... | collective-permute-start | bytes 1572872 | tf_op jit(solution)/shard_map/ppermute | solution.py:83
  174.2 10.6 %collective-permute-start.16 = (bf16[4,4,32,256]{3,2,1,0:T(8,128)(2,1)S(1)}, bf16[4,4,32,256]{3,2,1,0:T(8,128)(2,1)S(1)}, u32[]{:S(2)}, u32[]{:S(2)}) collective-permute-start(bf16[4,4,32,256]{3,2,1,0:T(8,128)(2,1)S(1)} %get-tuple-element.88), channel_id=1, source_target_pairs={{0,4},{4,0},{8,12},{12,8},{16,20},{20,16},{24,28},{28,24},{1,5},{5... | collective-permute-start | bytes 786440 | tf_op jit(solution)/shard_map/ppermute | solution.py:83
  176.0 13.1 %collective-permute-start.18 = (bf16[3,2,4,32,256]{4,3,2,1,0:T(8,128)(2,1)S(1)}, bf16[3,2,4,32,256]{4,3,2,1,0:T(8,128)(2,1)S(1)}, u32[]{:S(2)}, u32[]{:S(2)}) collective-permute-start(bf16[3,2,4,32,256]{4,3,2,1,0:T(8,128)(2,1)S(1)} %slice.153), channel_id=1, source_target_pairs={{0,2},{1,3},{2,0},{3,1},{4,6},{5,7},{6,4},{7,5},{8,10},{9,11},{10,... | collective-permute-start | bytes 1179656 | tf_op jit(solution)/shard_map/ppermute | solution.py:83
  189.2 52.1 %all-to-all-start.5 = ((bf16[32,96,256]{2,1,0:T(8,128)(2,1)}), bf16[32,96,256]{2,1,0:T(8,128)(2,1)S(1)}, u32[]{:S(2)}, u32[]{:S(2)}) async-start(bf16[32,96,256]{2,1,0:T(8,128)(2,1)} %bitcast.85), calls=%async_computation.5 | async-start | bytes 3145728 | tf_op jit(solution)/shard_map/all_to_all | solution.py:87
  193.3 22.1 %collective-permute-start.24 = (bf16[4,4,32,256]{3,2,1,0:T(8,128)(2,1)}, bf16[4,4,32,256]{3,2,1,0:T(8,128)(2,1)S(1)}, u32[]{:S(2)}, u32[]{:S(2)}) collective-permute-start(bf16[4,4,32,256]{3,2,1,0:T(8,128)(2,1)} %get-tuple-element.60), channel_id=1, source_target_pairs={{0,4},{4,0},{8,12},{12,8},{16,20},{20,16},{24,28},{28,24},{1,5},{5... | collective-permute-start | bytes 786440 | tf_op jit(solution)/shard_map/ppermute | solution.py:83
  195.1 21.9 %collective-permute-start.20 = (bf16[8,4,32,256]{3,2,1,0:T(8,128)(2,1)}, bf16[8,4,32,256]{3,2,1,0:T(8,128)(2,1)S(1)}, u32[]{:S(2)}, u32[]{:S(2)}) collective-permute-start(bf16[8,4,32,256]{3,2,1,0:T(8,128)(2,1)} %get-tuple-element.58), channel_id=1, source_target_pairs={{0,1},{1,0},{2,3},{3,2},{4,5},{5,4},{6,7},{7,6},{8,9},{9,8},{10,11... | collective-permute-start | bytes 1572872 | tf_op jit(solution)/shard_map/ppermute | solution.py:83
  195.1 34.7 %collective-permute-start.22 = (bf16[8,4,32,256]{3,2,1,0:T(8,128)(2,1)}, bf16[8,4,32,256]{3,2,1,0:T(8,128)(2,1)S(1)}, u32[]{:S(2)}, u32[]{:S(2)}) collective-permute-start(bf16[8,4,32,256]{3,2,1,0:T(8,128)(2,1)} %get-tuple-element.78), channel_id=1, source_target_pairs={{0,4},{4,0},{8,12},{12,8},{16,20},{20,16},{24,28},{28,24},{1,5},{5... | collective-permute-start | bytes 1572872 | tf_op jit(solution)/shard_map/ppermute | solution.py:83
  196.5 20.5 %collective-permute-start.23 = (bf16[4,4,32,256]{3,2,1,0:T(8,128)(2,1)}, bf16[4,4,32,256]{3,2,1,0:T(8,128)(2,1)S(1)}, u32[]{:S(2)}, u32[]{:S(2)}) collective-permute-start(bf16[4,4,32,256]{3,2,1,0:T(8,128)(2,1)} %add_convert_fusion.5), channel_id=1, source_target_pairs={{0,2},{1,3},{2,0},{3,1},{4,6},{5,7},{6,4},{7,5},{8,10},{9,11},{10,... | collective-permute-start | bytes 786440 | tf_op jit(solution)/shard_map/ppermute | solution.py:83
  198.3 41.3 %collective-permute-start.19 = (bf16[5,2,4,32,256]{4,3,2,1,0:T(8,128)(2,1)S(1)}, bf16[5,2,4,32,256]{4,3,2,1,0:T(8,128)(2,1)S(1)}, u32[]{:S(2)}, u32[]{:S(2)}) collective-permute-start(bf16[5,2,4,32,256]{4,3,2,1,0:T(8,128)(2,1)S(1)} %slice.159), channel_id=1, source_target_pairs={{0,2},{1,3},{2,0},{3,1},{4,6},{5,7},{6,4},{7,5},{8,10},{9,11},{10,... | collective-permute-start | bytes 1966088 | tf_op jit(solution)/shard_map/ppermute | solution.py:83
  216.4 21.9 %collective-permute-start.25 = (bf16[4,4,32,256]{3,2,1,0:T(8,128)(2,1)S(1)}, bf16[4,4,32,256]{3,2,1,0:T(8,128)(2,1)S(1)}, u32[]{:S(2)}, u32[]{:S(2)}) collective-permute-start(bf16[4,4,32,256]{3,2,1,0:T(8,128)(2,1)S(1)} %add_convert_fusion.4), channel_id=1, source_target_pairs={{0,2},{1,3},{2,0},{3,1},{4,6},{5,7},{6,4},{7,5},{8,10},{9,11},{10,... | collective-permute-start | bytes 786440 | tf_op jit(solution)/shard_map/ppermute | solution.py:83
  241.3 42.8 %all-to-all-start.6 = ((bf16[8,3,4,32,256]{4,3,2,1,0:T(8,128)(2,1)}), bf16[8,3,4,32,256]{4,3,2,1,0:T(8,128)(2,1)}, u32[]{:S(2)}, u32[]{:S(2)}) async-start(bf16[8,3,4,32,256]{4,3,2,1,0:T(8,128)(2,1)} %pad_maximum_fusion.2), calls=%async_computation.6 | async-start | bytes 3145728 | tf_op jit(solution)/shard_map/all_to_all | solution.py:87
  (21 other events, 193.3 us)

commit v13 on v12

--- a/solution.py
+++ b/solution.py
@@ -431,7 +431,7 @@
     far_last = xor_permute(after(there[half:], far_first), 1, "dp")
     far_last = add(here[half:], far_last)
     far = jnp.concatenate([xor_permute(far_first, 2), xor_permute(far_last, 2)], axis=0)
-    near = add(add(mid_keep[0, 0], xor_permute(mid_sends[0], 1)), xor_permute(near, 1, "dp"))
+    near = add(add(mid_keep[0, 0], xor_permute(mid_sends[0], 1)), xor_permute(after(near, far_last), 1, "dp"))
     mid = add(near, far)
     dealt = jnp.concatenate([own, mid[:, None]], axis=1)
     got = exchange(after(dealt, gin), "dp")

time: 288 us -> 288 us (level)
    unnamed x40 -> x44, local copies, waits for them, and re-layouts: 12.6 us -> 12.6 us
  transfers between devices with their start and end apart: 33 -> 33, of which waited for: 19 -> 20; matrix products, arithmetic and copies ran while one was open for 12% -> 12% of each run, Pallas kernels for 12% -> 12%
where the time goes in v13:
time: 288 us; the launch traced here: 287 us
  waiting for transfers between devices  151 us (52%)
  starting transfers between devices  53.1 us (18%)
  Pallas kernels  40 us (14%)
  local copies, waits for them, and re-layouts  26.7 us (9%)
  other arithmetic  14.7 us (5%)
    ppermute x26, waiting for transfers between devices, xor_permute(): lax.ppermute(x, axis, [(i, i ^ mask) for i in range(lax.axis_size(axis))])  91.5 us
    all_to_all x7, waiting for transfers between devices, exchange(): return lax.all_to_all(x, axes, split_axis=0, concat_axis=0, tiled=True)  60 us
    pallas_call x2, Pallas kernels, on_chip(): pl.pallas_call(kernel, out_shape=[jax.ShapeDtypeStruct(shape, jnp.bfloat1...  34.5 us
    all_to_all x7, starting transfers between devices, exchange(): return lax.all_to_all(x, axes, split_axis=0, concat_axis=0, tiled=True)  32.9 us
    ppermute x26, starting transfers between devices, xor_permute(): lax.ppermute(x, axis, [(i, i ^ mask) for i in range(lax.axis_size(axis))])  20.2 us
    unnamed x44, local copies, waits for them, and re-layouts  12.6 us
    convert_element_type x6, other arithmetic, add(): return (x.astype(jnp.float32) + y.astype(jnp.float32)).astype(jnp.bfloat16)  6.3 us
  transfers between devices with their start and end apart: 33, of which 20 were waited for; matrix products, arithmetic and copies ran while one was open for 12% of the time, Pallas kernels for 12%

profile of v13, /device:TPU:0, one launch (start us, length us, event | category | flops | bytes accessed | tf_op | source)
XLA Modules:
  0.0 287.0 jit_solution(14638061759657889176)
XLA Ops:
  0.6 2.3 shard_map.109
  3.0 7.4 %all-to-all-start = ((bf16[8,6,32,256]{3,2,1,0:T(8,128)(2,1)}), bf16[8,6,32,256]{3,2,1,0:T(8,128)(2,1)S(1)}, u32[]{:S(2)}, u32[]{:S(2)}) async-start(bf16[8,6,32,256]{3,2,1,0:T(8,128)(2,1)} %shard_map.109), calls=%async_computation | async-start | bytes 1572864 | tf_op jit(solution)/shard_map/all_to_all | solution.py:87
  11.6 19.0 %all-to-all-done = bf16[8,6,32,256]{3,2,1,0:T(8,128)(2,1)S(1)} async-done(((bf16[8,6,32,256]{3,2,1,0:T(8,128)(2,1)}), bf16[8,6,32,256]{3,2,1,0:T(8,128)(2,1)S(1)}, u32[]{:S(2)}, u32[]{:S(2)}) %all-to-all-start) | async-done | bytes 786464 | tf_op jit(solution)/shard_map/all_to_all | solution.py:87
  30.6 3.6 %all-to-all-start.1 = ((bf16[8,2,3,32,256]{4,3,2,1,0:T(8,128)(2,1)}), bf16[8,2,3,32,256]{4,3,2,1,0:T(8,128)(2,1)S(1)}, u32[]{:S(2)}, u32[]{:S(2)}) async-start(bf16[8,2,3,32,256]{4,3,2,1,0:T(8,128)(2,1)} %pad_maximum_fusion.3), calls=%async_computation.1 | async-start | bytes 1572864 | tf_op jit(solution)/shard_map/all_to_all | solution.py:87
  35.0 2.0 collective-permute-start.1
  44.9 11.0 %collective-permute-done.2.refs_2_.refs_4_ = bf16[8,2,32,256]{3,2,1,0:T(8,128)(2,1)} collective-permute-done((bf16[8,2,32,256]{3,2,1,0:T(8,128)(2,1)}, bf16[8,2,32,256]{3,2,1,0:T(8,128)(2,1)}, u32[]{:S(2)}, u32[]{:S(2)}) %collective-permute-start.2) | collective-permute-done | bytes 262176 | tf_op jit(solution)/shard_map/ppermute | solution.py:83
  57.3 4.6 %all-to-all-start.2 = ((bf16[32,96,256]{2,1,0:T(8,128)(2,1)}), bf16[32,96,256]{2,1,0:T(8,128)(2,1)S(1)}, u32[]{:S(2)}, u32[]{:S(2)}) async-start(bf16[32,96,256]{2,1,0:T(8,128)(2,1)} %pad_maximum_fusion), calls=%async_computation.2 | async-start | bytes 3145728 | tf_op jit(solution)/shard_map/all_to_all | solution.py:87
  61.9 1.8 collective-permute-start.6
  71.3 2.4 pad_maximum_fusion.1
  73.7 16.6 %collective-permute-done.11.refs_14_.refs_16_ = bf16[8,4,32,256]{3,2,1,0:T(8,128)(2,1)} collective-permute-done((bf16[8,4,32,256]{3,2,1,0:T(8,128)(2,1)}, bf16[8,4,32,256]{3,2,1,0:T(8,128)(2,1)}, u32[]{:S(2)}, u32[]{:S(2)}) %collective-permute-start.11) | collective-permute-done | bytes 524320 | tf_op jit(solution)/shard_map/ppermute | solution.py:83
  90.3 8.2 %collective-permute-done.6.refs_6_.refs_8_ = bf16[8,2,3,32,256]{4,3,2,1,0:T(8,128)(2,1)} collective-permute-done((bf16[8,2,3,32,256]{4,3,2,1,0:T(8,128)(2,1)}, bf16[8,2,3,32,256]{4,3,2,1,0:T(8,128)(2,1)}, u32[]{:S(2)}, u32[]{:S(2)}) %collective-permute-start.6) | collective-permute-done | bytes 786464 | tf_op jit(solution)/shard_map/ppermute | solution.py:83
  100.9 3.8 %all-to-all-start.4 = ((bf16[32,96,256]{2,1,0:T(8,128)(2,1)}), bf16[32,96,256]{2,1,0:T(8,128)(2,1)S(1)}, u32[]{:S(2)}, u32[]{:S(2)}) async-start(bf16[32,96,256]{2,1,0:T(8,128)(2,1)} %pad_maximum_fusion.1), calls=%async_computation.4 | async-start | bytes 3145728 | tf_op jit(solution)/shard_map/all_to_all | solution.py:87
  108.9 1.9 collective-permute-done.10.refs_13_.refs_15_
  113.5 17.3 %shard_map.110 = (bf16[8,4,96,256]{3,2,1,0:T(8,128)(2,1)}, bf16[2,4,4,64,512]{4,3,2,1,0:T(8,128)(2,1)}, bf16[2,4,256,512]{3,2,1,0:T(8,128)(2,1)}, bf16[2,4,256,5...) custom-call(s32[2]{0:T(128)} %pad_add_fusion.seat_ref, ...), custom_call_target="tpu_custom_call" | custom-call | flops 3221225472 | bytes 24117252 | tf_op jit(solution)/shard_map/pallas_call | solution.py:356
  130.8 11.6 %all-to-all-done.4 = bf16[32,96,256]{2,1,0:T(8,128)(2,1)S(1)} async-done(((bf16[32,96,256]{2,1,0:T(8,128)(2,1)}), bf16[32,96,256]{2,1,0:T(8,128)(2,1)S(1)}, u32[]{:S(2)}, u32[]{:S(2)}) %all-to-all-start.4) | async-done | bytes 1572896 | tf_op jit(solution)/shard_map/all_to_all | solution.py:87
  143.5 4.0 %all-to-all-start.3 = ((bf16[32,96,256]{2,1,0:T(8,128)(2,1)}), bf16[32,96,256]{2,1,0:T(8,128)(2,1)S(1)}, u32[]{:S(2)}, u32[]{:S(2)}) async-start(bf16[32,96,256]{2,1,0:T(8,128)(2,1)} %bitcast.86), calls=%async_computation.3 | async-start | bytes 3145728 | tf_op jit(solution)/shard_map/all_to_all | solution.py:87
  147.5 17.3 %shard_map.111 = (bf16[8,4,96,256]{3,2,1,0:T(8,128)(2,1)}, bf16[2,8,2,4,32,256]{5,4,3,2,1,0:T(8,128)(2,1)}, bf16[8,2,4,32,256]{4,3,2,1,0:T(8,128)(2,1)}, bf16[8,...) custom-call(s32[2]{0:T(128)} %pad_add_fusion.seat_ref, ...), custom_call_target="tpu_custom_call" | custom-call | flops 6442450944 | bytes 34078724 | tf_op jit(solution)/shard_map/pallas_call | solution.py:356
  169.2 2.6 fusion
  174.2 1.8 collective-permute-start.16
  177.5 7.2 %collective-permute-done.16 = bf16[4,4,32,256]{3,2,1,0:T(8,128)(2,1)S(1)} collective-permute-done((bf16[4,4,32,256]{3,2,1,0:T(8,128)(2,1)S(1)}, bf16[4,4,32,256]{3,2,1,0:T(8,128)(2,1)S(1)}, u32[]{:S(2)}, u32[]{:S(2)}) %collective-permute-start.16) | collective-permute-done | bytes 262176 | tf_op jit(solution)/shard_map/ppermute | solution.py:83
  185.5 3.5 %collective-permute-done.18 = bf16[3,2,4,32,256]{4,3,2,1,0:T(8,128)(2,1)S(1)} collective-permute-done((bf16[3,2,4,32,256]{4,3,2,1,0:T(8,128)(2,1)S(1)}, bf16[3,2,4,32,256]{4,3,2,1,0:T(8,128)(2,1)S(1)}, u32[]{:S(2)}, u32[]{:S(2)}) %collective-permute-start.18) | collective-permute-done | bytes 393248 | tf_op jit(solution)/shard_map/ppermute | solution.py:83
  189.2 4.1 %all-to-all-start.5 = ((bf16[32,96,256]{2,1,0:T(8,128)(2,1)}), bf16[32,96,256]{2,1,0:T(8,128)(2,1)S(1)}, u32[]{:S(2)}, u32[]{:S(2)}) async-start(bf16[32,96,256]{2,1,0:T(8,128)(2,1)} %bitcast.85), calls=%async_computation.5 | async-start | bytes 3145728 | tf_op jit(solution)/shard_map/all_to_all | solution.py:87
  193.3 1.8 collective-permute-start.22
  197.8 16.0 %collective-permute-done.22 = bf16[4,4,32,256]{3,2,1,0:T(8,128)(2,1)S(1)} collective-permute-done((bf16[4,4,32,256]{3,2,1,0:T(8,128)(2,1)}, bf16[4,4,32,256]{3,2,1,0:T(8,128)(2,1)S(1)}, u32[]{:S(2)}, u32[]{:S(2)}) %collective-permute-start.22) | collective-permute-done | bytes 262176 | tf_op jit(solution)/shard_map/ppermute | solution.py:83
  215.3 2.5 collective-permute-start.24
  217.9 8.1 %collective-permute-done.19 = bf16[5,2,4,32,256]{4,3,2,1,0:T(8,128)(2,1)S(1)} collective-permute-done((bf16[5,2,4,32,256]{4,3,2,1,0:T(8,128)(2,1)S(1)}, bf16[5,2,4,32,256]{4,3,2,1,0:T(8,128)(2,1)S(1)}, u32[]{:S(2)}, u32[]{:S(2)}) %collective-permute-start.19) | collective-permute-done | bytes 655392 | tf_op jit(solution)/shard_map/ppermute | solution.py:83
  226.2 6.9 %collective-permute-done.24 = bf16[4,4,32,256]{3,2,1,0:T(8,128)(2,1)S(1)} collective-permute-done((bf16[4,4,32,256]{3,2,1,0:T(8,128)(2,1)S(1)}, bf16[4,4,32,256]{3,2,1,0:T(8,128)(2,1)S(1)}, u32[]{:S(2)}, u32[]{:S(2)}) %collective-permute-start.24) | collective-permute-done | bytes 262176 | tf_op jit(solution)/shard_map/ppermute | solution.py:83
  233.1 5.1 %collective-permute-done.25 = bf16[4,4,32,256]{3,2,1,0:T(8,128)(2,1)S(1)} collective-permute-done((bf16[4,4,32,256]{3,2,1,0:T(8,128)(2,1)S(1)}, bf16[4,4,32,256]{3,2,1,0:T(8,128)(2,1)S(1)}, u32[]{:S(2)}, u32[]{:S(2)}) %collective-permute-start.25) | collective-permute-done | bytes 262176 | tf_op jit(solution)/shard_map/ppermute | solution.py:83
  241.0 5.5 %all-to-all-start.6 = ((bf16[8,3,4,32,256]{4,3,2,1,0:T(8,128)(2,1)}), bf16[8,3,4,32,256]{4,3,2,1,0:T(8,128)(2,1)}, u32[]{:S(2)}, u32[]{:S(2)}) async-start(bf16[8,3,4,32,256]{4,3,2,1,0:T(8,128)(2,1)} %pad_maximum_fusion.2), calls=%async_computation.6 | async-start | bytes 3145728 | tf_op jit(solution)/shard_map/all_to_all | solution.py:87
  249.4 2.6 copy.40
  255.7 28.1 %all-to-all-done.6.got_ref = bf16[8,3,4,32,256]{4,3,2,1,0:T(8,128)(2,1)} async-done(((bf16[8,3,4,32,256]{4,3,2,1,0:T(8,128)(2,1)}), bf16[8,3,4,32,256]{4,3,2,1,0:T(8,128)(2,1)}, u32[]{:S(2)}, u32[]{:S(2)}) %all-to-all-start.6) | async-done | bytes 1572896 | tf_op jit(solution)/shard_map/all_to_all | solution.py:87
  283.8 3.1 %shard_map.112 = (f32[12,32,512]{2,1,0:T(8,128)}, f32[24,32,256]{2,1,0:T(8,128)}, f32[24,32,256]{2,1,0:T(8,128)}, f32[12,64,256]{2,1,0:T(8,128)}) custom-call(bf16[8,3,4,32,256]{4,3,2,1,0:T(8,128)(2,1)} %all-to-all-done.6.got_ref), custom_call_target="tpu_custom_call" | custom-call | tf_op jit(solution)/shard_map/pallas_call | solution.py:438
  (125 shorter events, 52.1 us)
Async XLA Ops:
  3.0 27.6 %all-to-all-start = ((bf16[8,6,32,256]{3,2,1,0:T(8,128)(2,1)}), bf16[8,6,32,256]{3,2,1,0:T(8,128)(2,1)S(1)}, u32[]{:S(2)}, u32[]{:S(2)}) async-start(bf16[8,6,32,256]{3,2,1,0:T(8,128)(2,1)} %shard_map.109), calls=%async_computation | async-start | bytes 1572864 | tf_op jit(solution)/shard_map/all_to_all | solution.py:87
  30.6 25.9 %all-to-all-start.1 = ((bf16[8,2,3,32,256]{4,3,2,1,0:T(8,128)(2,1)}), bf16[8,2,3,32,256]{4,3,2,1,0:T(8,128)(2,1)S(1)}, u32[]{:S(2)}, u32[]{:S(2)}) async-start(bf16[8,2,3,32,256]{4,3,2,1,0:T(8,128)(2,1)} %pad_maximum_fusion.3), calls=%async_computation.1 | async-start | bytes 1572864 | tf_op jit(solution)/shard_map/all_to_all | solution.py:87
  35.0 21.5 %collective-permute-start.1 = (bf16[8,4,32,256]{3,2,1,0:T(8,128)(2,1)}, bf16[8,4,32,256]{3,2,1,0:T(8,128)(2,1)}, u32[]{:S(2)}, u32[]{:S(2)}) collective-permute-start(bf16[8,4,32,256]{3,2,1,0:T(8,128)(2,1)} %slice.143.refs_8_.refs_10_), channel_id=1, source_target_pairs={{0,4},{4,0},{8,12},{12,8},{16,20},{20,16},{24,28},{28,24},{1,5},{5... | collective-permute-start | bytes 1572872 | tf_op jit(solution)/shard_map/ppermute | solution.py:83
  37.0 19.4 %collective-permute-start = (bf16[8,4,32,256]{3,2,1,0:T(8,128)(2,1)}, bf16[8,4,32,256]{3,2,1,0:T(8,128)(2,1)}, u32[]{:S(2)}, u32[]{:S(2)}) collective-permute-start(bf16[8,4,32,256]{3,2,1,0:T(8,128)(2,1)} %slice.143.refs_8_.refs_10_), channel_id=1, source_target_pairs={{0,2},{1,3},{2,0},{3,1},{4,6},{5,7},{6,4},{7,5},{8,10},{9,11},{10,... | collective-permute-start | bytes 1572872 | tf_op jit(solution)/shard_map/ppermute | solution.py:83
  39.2 16.7 %collective-permute-start.2 = (bf16[8,2,32,256]{3,2,1,0:T(8,128)(2,1)}, bf16[8,2,32,256]{3,2,1,0:T(8,128)(2,1)}, u32[]{:S(2)}, u32[]{:S(2)}) collective-permute-start(bf16[8,2,32,256]{3,2,1,0:T(8,128)(2,1)} %slice.144.refs_0_.refs_2_), channel_id=1, source_target_pairs={{0,2},{1,3},{2,0},{3,1},{4,6},{5,7},{6,4},{7,5},{8,10},{9,11},{10,... | collective-permute-start | bytes 786440 | tf_op jit(solution)/shard_map/ppermute | solution.py:83
  57.3 42.5 %all-to-all-start.2 = ((bf16[32,96,256]{2,1,0:T(8,128)(2,1)}), bf16[32,96,256]{2,1,0:T(8,128)(2,1)S(1)}, u32[]{:S(2)}, u32[]{:S(2)}) async-start(bf16[32,96,256]{2,1,0:T(8,128)(2,1)} %pad_maximum_fusion), calls=%async_computation.2 | async-start | bytes 3145728 | tf_op jit(solution)/shard_map/all_to_all | solution.py:87
  61.9 36.7 %collective-permute-start.6 = (bf16[8,2,3,32,256]{4,3,2,1,0:T(8,128)(2,1)}, bf16[8,2,3,32,256]{4,3,2,1,0:T(8,128)(2,1)}, u32[]{:S(2)}, u32[]{:S(2)}) collective-permute-start(bf16[8,2,3,32,256]{4,3,2,1,0:T(8,128)(2,1)} %copy-done.7), channel_id=1, source_target_pairs={{0,2},{1,3},{2,0},{3,1},{4,6},{5,7},{6,4},{7,5},{8,10},{9,11},{10,... | collective-permute-start | bytes 2359304 | tf_op jit(solution)/shard_map/ppermute | solution.py:83
  63.7 26.6 %collective-permute-start.11 = (bf16[8,4,32,256]{3,2,1,0:T(8,128)(2,1)}, bf16[8,4,32,256]{3,2,1,0:T(8,128)(2,1)}, u32[]{:S(2)}, u32[]{:S(2)}) collective-permute-start(bf16[8,4,32,256]{3,2,1,0:T(8,128)(2,1)} %collective-permute-done.refs_10_.refs_12_), channel_id=1, source_target_pairs={{0,4},{4,0},{8,12},{12,8},{16,20},{20,16},{24,28},{28,24},{1,5},{5... | collective-permute-start | bytes 1572872 | tf_op jit(solution)/shard_map/ppermute | solution.py:83
  100.9 41.4 %all-to-all-start.4 = ((bf16[32,96,256]{2,1,0:T(8,128)(2,1)}), bf16[32,96,256]{2,1,0:T(8,128)(2,1)S(1)}, u32[]{:S(2)}, u32[]{:S(2)}) async-start(bf16[32,96,256]{2,1,0:T(8,128)(2,1)} %pad_maximum_fusion.1), calls=%async_computation.4 | async-start | bytes 3145728 | tf_op jit(solution)/shard_map/all_to_all | solution.py:87
  104.8 3.5 %collective-permute-start.8 = (bf16[8,4,32,256]{3,2,1,0:T(8,128)(2,1)}, bf16[8,4,32,256]{3,2,1,0:T(8,128)(2,1)}, u32[]{:S(2)}, u32[]{:S(2)}) collective-permute-start(bf16[8,4,32,256]{3,2,1,0:T(8,128)(2,1)} %slice.143.refs_8_.refs_10_), channel_id=1, source_target_pairs={{0,1},{1,0},{2,3},{3,2},{4,5},{5,4},{6,7},{7,6},{8,9},{9,8},{10,11... | collective-permute-start | bytes 1572872 | tf_op jit(solution)/shard_map/ppermute | solution.py:83
  104.9 2.8 collective-permute-start.3
  105.4 6.9 %collective-permute-start.5 = (bf16[8,2,3,32,256]{4,3,2,1,0:T(8,128)(2,1)}, bf16[8,2,3,32,256]{4,3,2,1,0:T(8,128)(2,1)S(1)}, u32[]{:S(2)}, u32[]{:S(2)}) collective-permute-start(bf16[8,2,3,32,256]{4,3,2,1,0:T(8,128)(2,1)} %copy-done.7), channel_id=1, source_target_pairs={{0,1},{1,0},{2,3},{3,2},{4,5},{5,4},{6,7},{7,6},{8,9},{9,8},{10,11... | collective-permute-start | bytes 2359304 | tf_op jit(solution)/shard_map/ppermute | solution.py:83
  105.9 6.5 %collective-permute-start.7 = (bf16[8,2,3,32,256]{4,3,2,1,0:T(8,128)(2,1)}, bf16[8,2,3,32,256]{4,3,2,1,0:T(8,128)(2,1)S(1)}, u32[]{:S(2)}, u32[]{:S(2)}) collective-permute-start(bf16[8,2,3,32,256]{4,3,2,1,0:T(8,128)(2,1)} %collective-permute-done.6.refs_6_.refs_8_), channel_id=1, source_target_pairs={{0,1},{1,0},{2,3},{3,2},{4,5},{5,4},{6,7},{7,6},{8,9},{9,8},{10,11... | collective-permute-start | bytes 2359304 | tf_op jit(solution)/shard_map/ppermute | solution.py:83
  107.7 3.1 %collective-permute-start.10 = (bf16[8,4,32,256]{3,2,1,0:T(8,128)(2,1)}, bf16[8,4,32,256]{3,2,1,0:T(8,128)(2,1)}, u32[]{:S(2)}, u32[]{:S(2)}) collective-permute-start(bf16[8,4,32,256]{3,2,1,0:T(8,128)(2,1)} %collective-permute-done.1.refs_12_.refs_14_), channel_id=1, source_target_pairs={{0,1},{1,0},{2,3},{3,2},{4,5},{5,4},{6,7},{7,6},{8,9},{9,8},{10,11... | collective-permute-start | bytes 1572872 | tf_op jit(solution)/shard_map/ppermute | solution.py:83
  107.9 3.7 %collective-permute-start.9 = (bf16[8,4,32,256]{3,2,1,0:T(8,128)(2,1)}, bf16[8,4,32,256]{3,2,1,0:T(8,128)(2,1)}, u32[]{:S(2)}, u32[]{:S(2)}) collective-permute-start(bf16[8,4,32,256]{3,2,1,0:T(8,128)(2,1)} %collective-permute-done.refs_10_.refs_12_), channel_id=1, source_target_pairs={{0,1},{1,0},{2,3},{3,2},{4,5},{5,4},{6,7},{7,6},{8,9},{9,8},{10,11... | collective-permute-start | bytes 1572872 | tf_op jit(solution)/shard_map/ppermute | solution.py:83
  108.2 4.1 %collective-permute-start.12 = (bf16[8,4,32,256]{3,2,1,0:T(8,128)(2,1)}, bf16[8,4,32,256]{3,2,1,0:T(8,128)(2,1)}, u32[]{:S(2)}, u32[]{:S(2)}) collective-permute-start(bf16[8,4,32,256]{3,2,1,0:T(8,128)(2,1)} %collective-permute-done.11.refs_14_.refs_16_), channel_id=1, source_target_pairs={{0,1},{1,0},{2,3},{3,2},{4,5},{5,4},{6,7},{7,6},{8,9},{9,8},{10,11... | collective-permute-start | bytes 1572872 | tf_op jit(solution)/shard_map/ppermute | solution.py:83
  143.5 45.7 %all-to-all-start.3 = ((bf16[32,96,256]{2,1,0:T(8,128)(2,1)}), bf16[32,96,256]{2,1,0:T(8,128)(2,1)S(1)}, u32[]{:S(2)}, u32[]{:S(2)}) async-start(bf16[32,96,256]{2,1,0:T(8,128)(2,1)} %bitcast.86), calls=%async_computation.3 | async-start | bytes 3145728 | tf_op jit(solution)/shard_map/all_to_all | solution.py:87
  164.7 2.9 %collective-permute-start.15 = (bf16[8,2,4,32,256]{4,3,2,1,0:T(8,128)(2,1)}, bf16[8,2,4,32,256]{4,3,2,1,0:T(8,128)(2,1)S(1)}, u32[]{:S(2)}, u32[]{:S(2)}) collective-permute-start(bf16[8,2,4,32,256]{4,3,2,1,0:T(8,128)(2,1)} %get-tuple-element.54), channel_id=1, source_target_pairs={{0,1},{1,0},{2,3},{3,2},{4,5},{5,4},{6,7},{7,6},{8,9},{9,8},{10,11... | collective-permute-start | bytes 3145736 | tf_op jit(solution)/shard_map/ppermute | solution.py:83
  165.1 4.1 %collective-permute-start.17 = (bf16[8,2,4,32,256]{4,3,2,1,0:T(8,128)(2,1)}, bf16[8,2,4,32,256]{4,3,2,1,0:T(8,128)(2,1)S(1)}, u32[]{:S(2)}, u32[]{:S(2)}) collective-permute-start(bf16[8,2,4,32,256]{4,3,2,1,0:T(8,128)(2,1)} %get-tuple-element.56), channel_id=1, source_target_pairs={{0,1},{1,0},{2,3},{3,2},{4,5},{5,4},{6,7},{7,6},{8,9},{9,8},{10,11... | collective-permute-start | bytes 3145736 | tf_op jit(solution)/shard_map/ppermute | solution.py:83
  165.3 6.5 %collective-permute-start.14 = (bf16[8,4,32,256]{3,2,1,0:T(8,128)(2,1)}, bf16[8,4,32,256]{3,2,1,0:T(8,128)(2,1)S(1)}, u32[]{:S(2)}, u32[]{:S(2)}) collective-permute-start(bf16[8,4,32,256]{3,2,1,0:T(8,128)(2,1)} %get-tuple-element.52), channel_id=1, source_target_pairs={{0,1},{1,0},{2,3},{3,2},{4,5},{5,4},{6,7},{7,6},{8,9},{9,8},{10,11... | collective-permute-start | bytes 1572872 | tf_op jit(solution)/shard_map/ppermute | solution.py:83
  165.6 6.3 %collective-permute-start.13 = (bf16[8,4,32,256]{3,2,1,0:T(8,128)(2,1)}, bf16[8,4,32,256]{3,2,1,0:T(8,128)(2,1)S(1)}, u32[]{:S(2)}, u32[]{:S(2)}) collective-permute-start(bf16[8,4,32,256]{3,2,1,0:T(8,128)(2,1)} %get-tuple-element.51), channel_id=1, source_target_pairs={{0,1},{1,0},{2,3},{3,2},{4,5},{5,4},{6,7},{7,6},{8,9},{9,8},{10,11... | collective-permute-start | bytes 1572872 | tf_op jit(solution)/shard_map/ppermute | solution.py:83
  165.8 6.0 %collective-permute-start.21 = (bf16[8,4,32,256]{3,2,1,0:T(8,128)(2,1)}, bf16[8,4,32,256]{3,2,1,0:T(8,128)(2,1)S(1)}, u32[]{:S(2)}, u32[]{:S(2)}) collective-permute-start(bf16[8,4,32,256]{3,2,1,0:T(8,128)(2,1)} %get-tuple-element.60), channel_id=1, source_target_pairs={{0,1},{1,0},{2,3},{3,2},{4,5},{5,4},{6,7},{7,6},{8,9},{9,8},{10,11... | collective-permute-start | bytes 1572872 | tf_op jit(solution)/shard_map/ppermute | solution.py:83
  174.2 10.6 %collective-permute-start.16 = (bf16[4,4,32,256]{3,2,1,0:T(8,128)(2,1)S(1)}, bf16[4,4,32,256]{3,2,1,0:T(8,128)(2,1)S(1)}, u32[]{:S(2)}, u32[]{:S(2)}) collective-permute-start(bf16[4,4,32,256]{3,2,1,0:T(8,128)(2,1)S(1)} %get-tuple-element.90), channel_id=1, source_target_pairs={{0,4},{4,0},{8,12},{12,8},{16,20},{20,16},{24,28},{28,24},{1,5},{5... | collective-permute-start | bytes 786440 | tf_op jit(solution)/shard_map/ppermute | solution.py:83
  176.0 13.1 %collective-permute-start.18 = (bf16[3,2,4,32,256]{4,3,2,1,0:T(8,128)(2,1)S(1)}, bf16[3,2,4,32,256]{4,3,2,1,0:T(8,128)(2,1)S(1)}, u32[]{:S(2)}, u32[]{:S(2)}) collective-permute-start(bf16[3,2,4,32,256]{4,3,2,1,0:T(8,128)(2,1)S(1)} %slice.153), channel_id=1, source_target_pairs={{0,2},{1,3},{2,0},{3,1},{4,6},{5,7},{6,4},{7,5},{8,10},{9,11},{10,... | collective-permute-start | bytes 1179656 | tf_op jit(solution)/shard_map/ppermute | solution.py:83
  189.2 51.8 %all-to-all-start.5 = ((bf16[32,96,256]{2,1,0:T(8,128)(2,1)}), bf16[32,96,256]{2,1,0:T(8,128)(2,1)S(1)}, u32[]{:S(2)}, u32[]{:S(2)}) async-start(bf16[32,96,256]{2,1,0:T(8,128)(2,1)} %bitcast.85), calls=%async_computation.5 | async-start | bytes 3145728 | tf_op jit(solution)/shard_map/all_to_all | solution.py:87
  193.3 20.5 %collective-permute-start.22 = (bf16[4,4,32,256]{3,2,1,0:T(8,128)(2,1)}, bf16[4,4,32,256]{3,2,1,0:T(8,128)(2,1)S(1)}, u32[]{:S(2)}, u32[]{:S(2)}) collective-permute-start(bf16[4,4,32,256]{3,2,1,0:T(8,128)(2,1)} %get-tuple-element.61), channel_id=1, source_target_pairs={{0,4},{4,0},{8,12},{12,8},{16,20},{20,16},{24,28},{28,24},{1,5},{5... | collective-permute-start | bytes 786440 | tf_op jit(solution)/shard_map/ppermute | solution.py:83
  196.3 29.7 %collective-permute-start.19 = (bf16[5,2,4,32,256]{4,3,2,1,0:T(8,128)(2,1)S(1)}, bf16[5,2,4,32,256]{4,3,2,1,0:T(8,128)(2,1)S(1)}, u32[]{:S(2)}, u32[]{:S(2)}) collective-permute-start(bf16[5,2,4,32,256]{4,3,2,1,0:T(8,128)(2,1)S(1)} %slice.159), channel_id=1, source_target_pairs={{0,2},{1,3},{2,0},{3,1},{4,6},{5,7},{6,4},{7,5},{8,10},{9,11},{10,... | collective-permute-start | bytes 1966088 | tf_op jit(solution)/shard_map/ppermute | solution.py:83
  197.8 28.4 %collective-permute-start.20 = (bf16[8,4,32,256]{3,2,1,0:T(8,128)(2,1)}, bf16[8,4,32,256]{3,2,1,0:T(8,128)(2,1)S(1)}, u32[]{:S(2)}, u32[]{:S(2)}) collective-permute-start(bf16[8,4,32,256]{3,2,1,0:T(8,128)(2,1)} %get-tuple-element.59), channel_id=1, source_target_pairs={{0,1},{1,0},{2,3},{3,2},{4,5},{5,4},{6,7},{7,6},{8,9},{9,8},{10,11... | collective-permute-start | bytes 1572872 | tf_op jit(solution)/shard_map/ppermute | solution.py:83
  214.8 23.5 %collective-permute-start.23 = (bf16[8,4,32,256]{3,2,1,0:T(8,128)(2,1)S(1)}, bf16[8,4,32,256]{3,2,1,0:T(8,128)(2,1)S(1)}, u32[]{:S(2)}, u32[]{:S(2)}) collective-permute-start(bf16[8,4,32,256]{3,2,1,0:T(8,128)(2,1)S(1)} %copy-done.17), channel_id=1, source_target_pairs={{0,4},{4,0},{8,12},{12,8},{16,20},{20,16},{24,28},{28,24},{1,5},{5... | collective-permute-start | bytes 1572872 | tf_op jit(solution)/shard_map/ppermute | solution.py:83
  215.3 17.8 %collective-permute-start.24 = (bf16[4,4,32,256]{3,2,1,0:T(8,128)(2,1)S(1)}, bf16[4,4,32,256]{3,2,1,0:T(8,128)(2,1)S(1)}, u32[]{:S(2)}, u32[]{:S(2)}) collective-permute-start(bf16[4,4,32,256]{3,2,1,0:T(8,128)(2,1)S(1)} %copy-done.18), channel_id=1, source_target_pairs={{0,2},{1,3},{2,0},{3,1},{4,6},{5,7},{6,4},{7,5},{8,10},{9,11},{10,... | collective-permute-start | bytes 786440 | tf_op jit(solution)/shard_map/ppermute | solution.py:83
  217.8 20.4 %collective-permute-start.25 = (bf16[4,4,32,256]{3,2,1,0:T(8,128)(2,1)S(1)}, bf16[4,4,32,256]{3,2,1,0:T(8,128)(2,1)S(1)}, u32[]{:S(2)}, u32[]{:S(2)}) collective-permute-start(bf16[4,4,32,256]{3,2,1,0:T(8,128)(2,1)S(1)} %add_convert_fusion.4), channel_id=1, source_target_pairs={{0,2},{1,3},{2,0},{3,1},{4,6},{5,7},{6,4},{7,5},{8,10},{9,11},{10,... | collective-permute-start | bytes 786440 | tf_op jit(solution)/shard_map/ppermute | solution.py:83
  241.0 42.8 %all-to-all-start.6 = ((bf16[8,3,4,32,256]{4,3,2,1,0:T(8,128)(2,1)}), bf16[8,3,4,32,256]{4,3,2,1,0:T(8,128)(2,1)}, u32[]{:S(2)}, u32[]{:S(2)}) async-start(bf16[8,3,4,32,256]{4,3,2,1,0:T(8,128)(2,1)} %pad_maximum_fusion.2), calls=%async_computation.6 | async-start | bytes 3145728 | tf_op jit(solution)/shard_map/all_to_all | solution.py:87
  (23 other events, 226.0 us)

commit v14 on v12

--- a/solution.py
+++ b/solution.py
@@ -421,18 +421,15 @@
     there = add(mid_keep[1, 1], after(xor_permute(mid_sends[3], 1), own_far))
     here = add(mid_keep[0, 1], xor_permute(mid_sends[1], 1))
     near = add(mid_keep[1, 0], xor_permute(mid_sends[2], 1))
-    part, half = 3 * ndp // 8, ndp // 2
+    part = 3 * ndp // 8
     own_first = add(own_near[:part], xor_permute(own_far[:part], 2))
-    far_first = add(here[:half], xor_permute(there[:half], 1, "dp"))
-    gin = after(gin.reshape(ndp * nb, -1, BLK), out, far_first, own_first)
+    far = add(here, xor_permute(there, 1, "dp"))
+    gin = after(gin.reshape(ndp * nb, -1, BLK), out, far, own_first)
     gin = exchange(gin, everyone)
     own_last = add(own_near[part:], xor_permute(after(own_far[part:], own_first), 2))
     own = jnp.concatenate([own_first, own_last], axis=0)
-    far_last = xor_permute(after(there[half:], far_first), 1, "dp")
-    far_last = add(here[half:], far_last)
-    far = jnp.concatenate([xor_permute(far_first, 2), xor_permute(far_last, 2)], axis=0)
     near = add(add(mid_keep[0, 0], xor_permute(mid_sends[0], 1)), xor_permute(near, 1, "dp"))
-    mid = add(near, far)
+    mid = add(near, xor_permute(far, 2))
     dealt = jnp.concatenate([own, mid[:, None]], axis=1)
     got = exchange(after(dealt, gin), "dp")
     grads = pl.pallas_call(

time: 288 us -> 291 us (1.010)
  waiting for transfers between devices: 153 us -> 158 us
    ppermute x26 -> x24, waiting for transfers between devices: 93.4 us -> 98.5 us  [xor_permute(): lax.ppermute(x, axis, [(i, i ^ mask) for i in range(lax.axis_size(axis))])]
    ppermute x26 -> x24, starting transfers between devices: 18.6 us -> 17.7 us  [xor_permute(): lax.ppermute(x, axis, [(i, i ^ mask) for i in range(lax.axis_size(axis))])]
    convert_element_type x6 -> x5, other arithmetic: 6.3 us -> 5.56 us  [add(): return (x.astype(jnp.float32) + y.astype(jnp.float32)).astype(jnp.bfloat16)]
    unnamed x40 -> x38, local copies, waits for them, and re-layouts: 12.6 us -> 12.5 us
  transfers between devices with their start and end apart: 33 -> 31, of which waited for: 19 -> 18; matrix products, arithmetic and copies ran while one was open for 12% -> 11% of each run, Pallas kernels for 12% -> 12%
where the time goes in v14:
time: 291 us; the launch traced here: 290 us
  waiting for transfers between devices  158 us (54%)
  starting transfers between devices  50.6 us (17%)
  Pallas kernels  40 us (14%)
  local copies, waits for them, and re-layouts  25.9 us (9%)
  other arithmetic  13.9 us (5%)
    ppermute x24, waiting for transfers between devices, xor_permute(): lax.ppermute(x, axis, [(i, i ^ mask) for i in range(lax.axis_size(axis))])  98.5 us
    all_to_all x7, waiting for transfers between devices, exchange(): return lax.all_to_all(x, axes, split_axis=0, concat_axis=0, tiled=True)  60 us
    pallas_call x2, Pallas kernels, on_chip(): pl.pallas_call(kernel, out_shape=[jax.ShapeDtypeStruct(shape, jnp.bfloat1...  34.5 us
    all_to_all x7, starting transfers between devices, exchange(): return lax.all_to_all(x, axes, split_axis=0, concat_axis=0, tiled=True)  32.9 us
    ppermute x24, starting transfers between devices, xor_permute(): lax.ppermute(x, axis, [(i, i ^ mask) for i in range(lax.axis_size(axis))])  17.7 us
    unnamed x38, local copies, waits for them, and re-layouts  12.5 us
  transfers between devices with their start and end apart: 31, of which 18 were waited for; matrix products, arithmetic and copies ran while one was open for 11% of the time, Pallas kernels for 12%

profile of v14, /device:TPU:0, one launch (start us, length us, event | category | flops | bytes accessed | tf_op | source)
XLA Modules:
  0.0 289.9 jit_solution(15783020049978644469)
XLA Ops:
  0.6 2.3 shard_map.109
  3.0 7.4 %all-to-all-start = ((bf16[8,6,32,256]{3,2,1,0:T(8,128)(2,1)}), bf16[8,6,32,256]{3,2,1,0:T(8,128)(2,1)S(1)}, u32[]{:S(2)}, u32[]{:S(2)}) async-start(bf16[8,6,32,256]{3,2,1,0:T(8,128)(2,1)} %shard_map.109), calls=%async_computation | async-start | bytes 1572864 | tf_op jit(solution)/shard_map/all_to_all | solution.py:87
  11.6 19.0 %all-to-all-done = bf16[8,6,32,256]{3,2,1,0:T(8,128)(2,1)S(1)} async-done(((bf16[8,6,32,256]{3,2,1,0:T(8,128)(2,1)}), bf16[8,6,32,256]{3,2,1,0:T(8,128)(2,1)S(1)}, u32[]{:S(2)}, u32[]{:S(2)}) %all-to-all-start) | async-done | bytes 786464 | tf_op jit(solution)/shard_map/all_to_all | solution.py:87
  30.6 3.6 %all-to-all-start.1 = ((bf16[8,2,3,32,256]{4,3,2,1,0:T(8,128)(2,1)}), bf16[8,2,3,32,256]{4,3,2,1,0:T(8,128)(2,1)S(1)}, u32[]{:S(2)}, u32[]{:S(2)}) async-start(bf16[8,2,3,32,256]{4,3,2,1,0:T(8,128)(2,1)} %pad_maximum_fusion.3), calls=%async_computation.1 | async-start | bytes 1572864 | tf_op jit(solution)/shard_map/all_to_all | solution.py:87
  35.0 2.0 collective-permute-start.1
  39.8 1.7 copy.30
  44.9 11.0 %collective-permute-done.2.refs_2_.refs_4_ = bf16[8,2,32,256]{3,2,1,0:T(8,128)(2,1)} collective-permute-done((bf16[8,2,32,256]{3,2,1,0:T(8,128)(2,1)}, bf16[8,2,32,256]{3,2,1,0:T(8,128)(2,1)}, u32[]{:S(2)}, u32[]{:S(2)}) %collective-permute-start.2) | collective-permute-done | bytes 262176 | tf_op jit(solution)/shard_map/ppermute | solution.py:83
  57.3 4.6 %all-to-all-start.2 = ((bf16[32,96,256]{2,1,0:T(8,128)(2,1)}), bf16[32,96,256]{2,1,0:T(8,128)(2,1)S(1)}, u32[]{:S(2)}, u32[]{:S(2)}) async-start(bf16[32,96,256]{2,1,0:T(8,128)(2,1)} %pad_maximum_fusion), calls=%async_computation.2 | async-start | bytes 3145728 | tf_op jit(solution)/shard_map/all_to_all | solution.py:87
  61.9 1.8 collective-permute-start.6
  71.3 2.3 pad_maximum_fusion.1
  73.7 16.7 %collective-permute-done.11.refs_14_.refs_16_ = bf16[8,4,32,256]{3,2,1,0:T(8,128)(2,1)} collective-permute-done((bf16[8,4,32,256]{3,2,1,0:T(8,128)(2,1)}, bf16[8,4,32,256]{3,2,1,0:T(8,128)(2,1)}, u32[]{:S(2)}, u32[]{:S(2)}) %collective-permute-start.11) | collective-permute-done | bytes 524320 | tf_op jit(solution)/shard_map/ppermute | solution.py:83
  90.3 8.2 %collective-permute-done.6.refs_6_.refs_8_ = bf16[8,2,3,32,256]{4,3,2,1,0:T(8,128)(2,1)} collective-permute-done((bf16[8,2,3,32,256]{4,3,2,1,0:T(8,128)(2,1)}, bf16[8,2,3,32,256]{4,3,2,1,0:T(8,128)(2,1)}, u32[]{:S(2)}, u32[]{:S(2)}) %collective-permute-start.6) | collective-permute-done | bytes 786464 | tf_op jit(solution)/shard_map/ppermute | solution.py:83
  100.9 3.8 %all-to-all-start.4 = ((bf16[32,96,256]{2,1,0:T(8,128)(2,1)}), bf16[32,96,256]{2,1,0:T(8,128)(2,1)S(1)}, u32[]{:S(2)}, u32[]{:S(2)}) async-start(bf16[32,96,256]{2,1,0:T(8,128)(2,1)} %pad_maximum_fusion.1), calls=%async_computation.4 | async-start | bytes 3145728 | tf_op jit(solution)/shard_map/all_to_all | solution.py:87
  105.9 1.8 collective-permute-done.3.refs_1_.refs_3_
  109.0 1.9 collective-permute-done.10.refs_13_.refs_15_
  113.5 17.3 %shard_map.110 = (bf16[8,4,96,256]{3,2,1,0:T(8,128)(2,1)}, bf16[2,4,4,64,512]{4,3,2,1,0:T(8,128)(2,1)}, bf16[2,4,256,512]{3,2,1,0:T(8,128)(2,1)}, bf16[2,4,256,5...) custom-call(s32[2]{0:T(128)} %pad_add_fusion.seat_ref, ...), custom_call_target="tpu_custom_call" | custom-call | flops 3221225472 | bytes 24117252 | tf_op jit(solution)/shard_map/pallas_call | solution.py:356
  130.8 11.6 %all-to-all-done.4 = bf16[32,96,256]{2,1,0:T(8,128)(2,1)S(1)} async-done(((bf16[32,96,256]{2,1,0:T(8,128)(2,1)}), bf16[32,96,256]{2,1,0:T(8,128)(2,1)S(1)}, u32[]{:S(2)}, u32[]{:S(2)}) %all-to-all-start.4) | async-done | bytes 1572896 | tf_op jit(solution)/shard_map/all_to_all | solution.py:87
  143.5 4.0 %all-to-all-start.3 = ((bf16[32,96,256]{2,1,0:T(8,128)(2,1)}), bf16[32,96,256]{2,1,0:T(8,128)(2,1)S(1)}, u32[]{:S(2)}, u32[]{:S(2)}) async-start(bf16[32,96,256]{2,1,0:T(8,128)(2,1)} %bitcast.86), calls=%async_computation.3 | async-start | bytes 3145728 | tf_op jit(solution)/shard_map/all_to_all | solution.py:87
  147.5 17.3 %shard_map.111 = (bf16[8,4,96,256]{3,2,1,0:T(8,128)(2,1)}, bf16[2,8,2,4,32,256]{5,4,3,2,1,0:T(8,128)(2,1)}, bf16[8,2,4,32,256]{4,3,2,1,0:T(8,128)(2,1)}, bf16[8,...) custom-call(s32[2]{0:T(128)} %pad_add_fusion.seat_ref, ...), custom_call_target="tpu_custom_call" | custom-call | flops 6442450944 | bytes 34078724 | tf_op jit(solution)/shard_map/pallas_call | solution.py:356
  169.2 2.6 fusion
  171.9 1.8 collective-permute-start.18
  176.4 8.9 %collective-permute-done.18 = bf16[3,2,4,32,256]{4,3,2,1,0:T(8,128)(2,1)S(1)} collective-permute-done((bf16[3,2,4,32,256]{4,3,2,1,0:T(8,128)(2,1)S(1)}, bf16[3,2,4,32,256]{4,3,2,1,0:T(8,128)(2,1)S(1)}, u32[]{:S(2)}, u32[]{:S(2)}) %collective-permute-start.18) | collective-permute-done | bytes 393248 | tf_op jit(solution)/shard_map/ppermute | solution.py:83
  185.5 5.3 %collective-permute-done.16 = bf16[8,4,32,256]{3,2,1,0:T(8,128)(2,1)S(1)} collective-permute-done((bf16[8,4,32,256]{3,2,1,0:T(8,128)(2,1)S(1)}, bf16[8,4,32,256]{3,2,1,0:T(8,128)(2,1)S(1)}, u32[]{:S(2)}, u32[]{:S(2)}) %collective-permute-start.16) | collective-permute-done | bytes 524320 | tf_op jit(solution)/shard_map/ppermute | solution.py:83
  192.1 4.1 %all-to-all-start.5 = ((bf16[32,96,256]{2,1,0:T(8,128)(2,1)}), bf16[32,96,256]{2,1,0:T(8,128)(2,1)S(1)}, u32[]{:S(2)}, u32[]{:S(2)}) async-start(bf16[32,96,256]{2,1,0:T(8,128)(2,1)} %bitcast.85), calls=%async_computation.5 | async-start | bytes 3145728 | tf_op jit(solution)/shard_map/all_to_all | solution.py:87
  197.5 1.8 collective-permute-start.19
  201.3 27.6 %collective-permute-done.19 = bf16[5,2,4,32,256]{4,3,2,1,0:T(8,128)(2,1)S(1)} collective-permute-done((bf16[5,2,4,32,256]{4,3,2,1,0:T(8,128)(2,1)S(1)}, bf16[5,2,4,32,256]{4,3,2,1,0:T(8,128)(2,1)S(1)}, u32[]{:S(2)}, u32[]{:S(2)}) %collective-permute-start.19) | collective-permute-done | bytes 655392 | tf_op jit(solution)/shard_map/ppermute | solution.py:83
  229.2 12.0 %collective-permute-done.23 = bf16[8,4,32,256]{3,2,1,0:T(8,128)(2,1)S(1)} collective-permute-done((bf16[8,4,32,256]{3,2,1,0:T(8,128)(2,1)}, bf16[8,4,32,256]{3,2,1,0:T(8,128)(2,1)S(1)}, u32[]{:S(2)}, u32[]{:S(2)}) %collective-permute-start.23) | collective-permute-done | bytes 524320 | tf_op jit(solution)/shard_map/ppermute | solution.py:83
  244.0 5.5 %all-to-all-start.6 = ((bf16[8,3,4,32,256]{4,3,2,1,0:T(8,128)(2,1)}), bf16[8,3,4,32,256]{4,3,2,1,0:T(8,128)(2,1)}, u32[]{:S(2)}, u32[]{:S(2)}) async-start(bf16[8,3,4,32,256]{4,3,2,1,0:T(8,128)(2,1)} %pad_maximum_fusion.2), calls=%async_computation.6 | async-start | bytes 3145728 | tf_op jit(solution)/shard_map/all_to_all | solution.py:87
  252.3 2.6 copy.40
  256.9 1.7 copy.41
  258.6 28.1 %all-to-all-done.6.got_ref = bf16[8,3,4,32,256]{4,3,2,1,0:T(8,128)(2,1)} async-done(((bf16[8,3,4,32,256]{4,3,2,1,0:T(8,128)(2,1)}), bf16[8,3,4,32,256]{4,3,2,1,0:T(8,128)(2,1)}, u32[]{:S(2)}, u32[]{:S(2)}) %all-to-all-start.6) | async-done | bytes 1572896 | tf_op jit(solution)/shard_map/all_to_all | solution.py:87
  286.8 3.1 %shard_map.112 = (f32[12,32,512]{2,1,0:T(8,128)}, f32[24,32,256]{2,1,0:T(8,128)}, f32[24,32,256]{2,1,0:T(8,128)}, f32[12,64,256]{2,1,0:T(8,128)}) custom-call(bf16[8,3,4,32,256]{4,3,2,1,0:T(8,128)(2,1)} %all-to-all-done.6.got_ref), custom_call_target="tpu_custom_call" | custom-call | tf_op jit(solution)/shard_map/pallas_call | solution.py:435
  (113 shorter events, 45.3 us)
Async XLA Ops:
  3.0 27.6 %all-to-all-start = ((bf16[8,6,32,256]{3,2,1,0:T(8,128)(2,1)}), bf16[8,6,32,256]{3,2,1,0:T(8,128)(2,1)S(1)}, u32[]{:S(2)}, u32[]{:S(2)}) async-start(bf16[8,6,32,256]{3,2,1,0:T(8,128)(2,1)} %shard_map.109), calls=%async_computation | async-start | bytes 1572864 | tf_op jit(solution)/shard_map/all_to_all | solution.py:87
  30.6 25.9 %all-to-all-start.1 = ((bf16[8,2,3,32,256]{4,3,2,1,0:T(8,128)(2,1)}), bf16[8,2,3,32,256]{4,3,2,1,0:T(8,128)(2,1)S(1)}, u32[]{:S(2)}, u32[]{:S(2)}) async-start(bf16[8,2,3,32,256]{4,3,2,1,0:T(8,128)(2,1)} %pad_maximum_fusion.3), calls=%async_computation.1 | async-start | bytes 1572864 | tf_op jit(solution)/shard_map/all_to_all | solution.py:87
  35.0 21.5 %collective-permute-start.1 = (bf16[8,4,32,256]{3,2,1,0:T(8,128)(2,1)}, bf16[8,4,32,256]{3,2,1,0:T(8,128)(2,1)}, u32[]{:S(2)}, u32[]{:S(2)}) collective-permute-start(bf16[8,4,32,256]{3,2,1,0:T(8,128)(2,1)} %slice.127.refs_8_.refs_10_), channel_id=1, source_target_pairs={{0,4},{4,0},{8,12},{12,8},{16,20},{20,16},{24,28},{28,24},{1,5},{5... | collective-permute-start | bytes 1572872 | tf_op jit(solution)/shard_map/ppermute | solution.py:83
  37.0 19.4 %collective-permute-start = (bf16[8,4,32,256]{3,2,1,0:T(8,128)(2,1)}, bf16[8,4,32,256]{3,2,1,0:T(8,128)(2,1)}, u32[]{:S(2)}, u32[]{:S(2)}) collective-permute-start(bf16[8,4,32,256]{3,2,1,0:T(8,128)(2,1)} %slice.127.refs_8_.refs_10_), channel_id=1, source_target_pairs={{0,2},{1,3},{2,0},{3,1},{4,6},{5,7},{6,4},{7,5},{8,10},{9,11},{10,... | collective-permute-start | bytes 1572872 | tf_op jit(solution)/shard_map/ppermute | solution.py:83
  39.2 16.7 %collective-permute-start.2 = (bf16[8,2,32,256]{3,2,1,0:T(8,128)(2,1)}, bf16[8,2,32,256]{3,2,1,0:T(8,128)(2,1)}, u32[]{:S(2)}, u32[]{:S(2)}) collective-permute-start(bf16[8,2,32,256]{3,2,1,0:T(8,128)(2,1)} %slice.128.refs_0_.refs_2_), channel_id=1, source_target_pairs={{0,2},{1,3},{2,0},{3,1},{4,6},{5,7},{6,4},{7,5},{8,10},{9,11},{10,... | collective-permute-start | bytes 786440 | tf_op jit(solution)/shard_map/ppermute | solution.py:83
  57.3 42.5 %all-to-all-start.2 = ((bf16[32,96,256]{2,1,0:T(8,128)(2,1)}), bf16[32,96,256]{2,1,0:T(8,128)(2,1)S(1)}, u32[]{:S(2)}, u32[]{:S(2)}) async-start(bf16[32,96,256]{2,1,0:T(8,128)(2,1)} %pad_maximum_fusion), calls=%async_computation.2 | async-start | bytes 3145728 | tf_op jit(solution)/shard_map/all_to_all | solution.py:87
  61.9 36.7 %collective-permute-start.6 = (bf16[8,2,3,32,256]{4,3,2,1,0:T(8,128)(2,1)}, bf16[8,2,3,32,256]{4,3,2,1,0:T(8,128)(2,1)}, u32[]{:S(2)}, u32[]{:S(2)}) collective-permute-start(bf16[8,2,3,32,256]{4,3,2,1,0:T(8,128)(2,1)} %copy-done.7), channel_id=1, source_target_pairs={{0,2},{1,3},{2,0},{3,1},{4,6},{5,7},{6,4},{7,5},{8,10},{9,11},{10,... | collective-permute-start | bytes 2359304 | tf_op jit(solution)/shard_map/ppermute | solution.py:83
  63.7 26.6 %collective-permute-start.11 = (bf16[8,4,32,256]{3,2,1,0:T(8,128)(2,1)}, bf16[8,4,32,256]{3,2,1,0:T(8,128)(2,1)}, u32[]{:S(2)}, u32[]{:S(2)}) collective-permute-start(bf16[8,4,32,256]{3,2,1,0:T(8,128)(2,1)} %collective-permute-done.refs_10_.refs_12_), channel_id=1, source_target_pairs={{0,4},{4,0},{8,12},{12,8},{16,20},{20,16},{24,28},{28,24},{1,5},{5... | collective-permute-start | bytes 1572872 | tf_op jit(solution)/shard_map/ppermute | solution.py:83
  100.9 41.4 %all-to-all-start.4 = ((bf16[32,96,256]{2,1,0:T(8,128)(2,1)}), bf16[32,96,256]{2,1,0:T(8,128)(2,1)S(1)}, u32[]{:S(2)}, u32[]{:S(2)}) async-start(bf16[32,96,256]{2,1,0:T(8,128)(2,1)} %pad_maximum_fusion.1), calls=%async_computation.4 | async-start | bytes 3145728 | tf_op jit(solution)/shard_map/all_to_all | solution.py:87
  104.8 3.5 %collective-permute-start.8 = (bf16[8,4,32,256]{3,2,1,0:T(8,128)(2,1)}, bf16[8,4,32,256]{3,2,1,0:T(8,128)(2,1)}, u32[]{:S(2)}, u32[]{:S(2)}) collective-permute-start(bf16[8,4,32,256]{3,2,1,0:T(8,128)(2,1)} %slice.127.refs_8_.refs_10_), channel_id=1, source_target_pairs={{0,1},{1,0},{2,3},{3,2},{4,5},{5,4},{6,7},{7,6},{8,9},{9,8},{10,11... | collective-permute-start | bytes 1572872 | tf_op jit(solution)/shard_map/ppermute | solution.py:83
  104.9 2.8 collective-permute-start.3
  105.3 2.5 collective-permute-start.4
  105.4 6.9 %collective-permute-start.5 = (bf16[8,2,3,32,256]{4,3,2,1,0:T(8,128)(2,1)}, bf16[8,2,3,32,256]{4,3,2,1,0:T(8,128)(2,1)S(1)}, u32[]{:S(2)}, u32[]{:S(2)}) collective-permute-start(bf16[8,2,3,32,256]{4,3,2,1,0:T(8,128)(2,1)} %copy-done.7), channel_id=1, source_target_pairs={{0,1},{1,0},{2,3},{3,2},{4,5},{5,4},{6,7},{7,6},{8,9},{9,8},{10,11... | collective-permute-start | bytes 2359304 | tf_op jit(solution)/shard_map/ppermute | solution.py:83
  105.9 6.5 %collective-permute-start.7 = (bf16[8,2,3,32,256]{4,3,2,1,0:T(8,128)(2,1)}, bf16[8,2,3,32,256]{4,3,2,1,0:T(8,128)(2,1)S(1)}, u32[]{:S(2)}, u32[]{:S(2)}) collective-permute-start(bf16[8,2,3,32,256]{4,3,2,1,0:T(8,128)(2,1)} %collective-permute-done.6.refs_6_.refs_8_), channel_id=1, source_target_pairs={{0,1},{1,0},{2,3},{3,2},{4,5},{5,4},{6,7},{7,6},{8,9},{9,8},{10,11... | collective-permute-start | bytes 2359304 | tf_op jit(solution)/shard_map/ppermute | solution.py:83
  107.7 3.1 %collective-permute-start.10 = (bf16[8,4,32,256]{3,2,1,0:T(8,128)(2,1)}, bf16[8,4,32,256]{3,2,1,0:T(8,128)(2,1)}, u32[]{:S(2)}, u32[]{:S(2)}) collective-permute-start(bf16[8,4,32,256]{3,2,1,0:T(8,128)(2,1)} %collective-permute-done.1.refs_12_.refs_14_), channel_id=1, source_target_pairs={{0,1},{1,0},{2,3},{3,2},{4,5},{5,4},{6,7},{7,6},{8,9},{9,8},{10,11... | collective-permute-start | bytes 1572872 | tf_op jit(solution)/shard_map/ppermute | solution.py:83
  107.9 3.7 %collective-permute-start.9 = (bf16[8,4,32,256]{3,2,1,0:T(8,128)(2,1)}, bf16[8,4,32,256]{3,2,1,0:T(8,128)(2,1)}, u32[]{:S(2)}, u32[]{:S(2)}) collective-permute-start(bf16[8,4,32,256]{3,2,1,0:T(8,128)(2,1)} %collective-permute-done.refs_10_.refs_12_), channel_id=1, source_target_pairs={{0,1},{1,0},{2,3},{3,2},{4,5},{5,4},{6,7},{7,6},{8,9},{9,8},{10,11... | collective-permute-start | bytes 1572872 | tf_op jit(solution)/shard_map/ppermute | solution.py:83
  108.2 4.1 %collective-permute-start.12 = (bf16[8,4,32,256]{3,2,1,0:T(8,128)(2,1)}, bf16[8,4,32,256]{3,2,1,0:T(8,128)(2,1)}, u32[]{:S(2)}, u32[]{:S(2)}) collective-permute-start(bf16[8,4,32,256]{3,2,1,0:T(8,128)(2,1)} %collective-permute-done.11.refs_14_.refs_16_), channel_id=1, source_target_pairs={{0,1},{1,0},{2,3},{3,2},{4,5},{5,4},{6,7},{7,6},{8,9},{9,8},{10,11... | collective-permute-start | bytes 1572872 | tf_op jit(solution)/shard_map/ppermute | solution.py:83
  143.5 48.6 %all-to-all-start.3 = ((bf16[32,96,256]{2,1,0:T(8,128)(2,1)}), bf16[32,96,256]{2,1,0:T(8,128)(2,1)S(1)}, u32[]{:S(2)}, u32[]{:S(2)}) async-start(bf16[32,96,256]{2,1,0:T(8,128)(2,1)} %bitcast.86), calls=%async_computation.3 | async-start | bytes 3145728 | tf_op jit(solution)/shard_map/all_to_all | solution.py:87
  164.7 2.9 %collective-permute-start.15 = (bf16[8,2,4,32,256]{4,3,2,1,0:T(8,128)(2,1)}, bf16[8,2,4,32,256]{4,3,2,1,0:T(8,128)(2,1)S(1)}, u32[]{:S(2)}, u32[]{:S(2)}) collective-permute-start(bf16[8,2,4,32,256]{4,3,2,1,0:T(8,128)(2,1)} %get-tuple-element.52), channel_id=1, source_target_pairs={{0,1},{1,0},{2,3},{3,2},{4,5},{5,4},{6,7},{7,6},{8,9},{9,8},{10,11... | collective-permute-start | bytes 3145736 | tf_op jit(solution)/shard_map/ppermute | solution.py:83
  165.1 4.1 %collective-permute-start.17 = (bf16[8,2,4,32,256]{4,3,2,1,0:T(8,128)(2,1)}, bf16[8,2,4,32,256]{4,3,2,1,0:T(8,128)(2,1)S(1)}, u32[]{:S(2)}, u32[]{:S(2)}) collective-permute-start(bf16[8,2,4,32,256]{4,3,2,1,0:T(8,128)(2,1)} %get-tuple-element.54), channel_id=1, source_target_pairs={{0,1},{1,0},{2,3},{3,2},{4,5},{5,4},{6,7},{7,6},{8,9},{9,8},{10,11... | collective-permute-start | bytes 3145736 | tf_op jit(solution)/shard_map/ppermute | solution.py:83
  165.3 6.6 %collective-permute-start.14 = (bf16[8,4,32,256]{3,2,1,0:T(8,128)(2,1)}, bf16[8,4,32,256]{3,2,1,0:T(8,128)(2,1)S(1)}, u32[]{:S(2)}, u32[]{:S(2)}) collective-permute-start(bf16[8,4,32,256]{3,2,1,0:T(8,128)(2,1)} %get-tuple-element.50), channel_id=1, source_target_pairs={{0,1},{1,0},{2,3},{3,2},{4,5},{5,4},{6,7},{7,6},{8,9},{9,8},{10,11... | collective-permute-start | bytes 1572872 | tf_op jit(solution)/shard_map/ppermute | solution.py:83
  165.6 8.2 %collective-permute-start.21 = (bf16[8,4,32,256]{3,2,1,0:T(8,128)(2,1)}, bf16[8,4,32,256]{3,2,1,0:T(8,128)(2,1)S(1)}, u32[]{:S(2)}, u32[]{:S(2)}) collective-permute-start(bf16[8,4,32,256]{3,2,1,0:T(8,128)(2,1)} %get-tuple-element.58), channel_id=1, source_target_pairs={{0,1},{1,0},{2,3},{3,2},{4,5},{5,4},{6,7},{7,6},{8,9},{9,8},{10,11... | collective-permute-start | bytes 1572872 | tf_op jit(solution)/shard_map/ppermute | solution.py:83
  165.8 19.7 %collective-permute-start.13 = (bf16[8,4,32,256]{3,2,1,0:T(8,128)(2,1)}, bf16[8,4,32,256]{3,2,1,0:T(8,128)(2,1)S(1)}, u32[]{:S(2)}, u32[]{:S(2)}) collective-permute-start(bf16[8,4,32,256]{3,2,1,0:T(8,128)(2,1)} %get-tuple-element.49), channel_id=1, source_target_pairs={{0,1},{1,0},{2,3},{3,2},{4,5},{5,4},{6,7},{7,6},{8,9},{9,8},{10,11... | collective-permute-start | bytes 1572872 | tf_op jit(solution)/shard_map/ppermute | solution.py:83
  171.9 13.4 %collective-permute-start.18 = (bf16[3,2,4,32,256]{4,3,2,1,0:T(8,128)(2,1)S(1)}, bf16[3,2,4,32,256]{4,3,2,1,0:T(8,128)(2,1)S(1)}, u32[]{:S(2)}, u32[]{:S(2)}) collective-permute-start(bf16[3,2,4,32,256]{4,3,2,1,0:T(8,128)(2,1)S(1)} %slice.135), channel_id=1, source_target_pairs={{0,2},{1,3},{2,0},{3,1},{4,6},{5,7},{6,4},{7,5},{8,10},{9,11},{10,... | collective-permute-start | bytes 1179656 | tf_op jit(solution)/shard_map/ppermute | solution.py:83
  175.0 15.8 %collective-permute-start.16 = (bf16[8,4,32,256]{3,2,1,0:T(8,128)(2,1)S(1)}, bf16[8,4,32,256]{3,2,1,0:T(8,128)(2,1)S(1)}, u32[]{:S(2)}, u32[]{:S(2)}) collective-permute-start(bf16[8,4,32,256]{3,2,1,0:T(8,128)(2,1)S(1)} %get-tuple-element.77), channel_id=1, source_target_pairs={{0,4},{4,0},{8,12},{12,8},{16,20},{20,16},{24,28},{28,24},{1,5},{5... | collective-permute-start | bytes 1572872 | tf_op jit(solution)/shard_map/ppermute | solution.py:83
  192.1 57.3 %copy-start = (bf16[32,96,256]{2,1,0:T(8,128)(2,1)}, bf16[32,96,256]{2,1,0:T(8,128)(2,1)S(1)}, u32[]{:S(2)}) copy-start(bf16[32,96,256]{2,1,0:T(8,128)(2,1)S(1)} %all-to-all-done.3) | copy-start | bytes 4718596
  192.1 51.9 %all-to-all-start.5 = ((bf16[32,96,256]{2,1,0:T(8,128)(2,1)}), bf16[32,96,256]{2,1,0:T(8,128)(2,1)S(1)}, u32[]{:S(2)}, u32[]{:S(2)}) async-start(bf16[32,96,256]{2,1,0:T(8,128)(2,1)} %bitcast.85), calls=%async_computation.5 | async-start | bytes 3145728 | tf_op jit(solution)/shard_map/all_to_all | solution.py:87
  197.5 31.4 %collective-permute-start.19 = (bf16[5,2,4,32,256]{4,3,2,1,0:T(8,128)(2,1)S(1)}, bf16[5,2,4,32,256]{4,3,2,1,0:T(8,128)(2,1)S(1)}, u32[]{:S(2)}, u32[]{:S(2)}) collective-permute-start(bf16[5,2,4,32,256]{4,3,2,1,0:T(8,128)(2,1)S(1)} %slice.141), channel_id=1, source_target_pairs={{0,2},{1,3},{2,0},{3,1},{4,6},{5,7},{6,4},{7,5},{8,10},{9,11},{10,... | collective-permute-start | bytes 1966088 | tf_op jit(solution)/shard_map/ppermute | solution.py:83
  199.3 29.9 %collective-permute-start.20 = (bf16[8,4,32,256]{3,2,1,0:T(8,128)(2,1)}, bf16[8,4,32,256]{3,2,1,0:T(8,128)(2,1)S(1)}, u32[]{:S(2)}, u32[]{:S(2)}) collective-permute-start(bf16[8,4,32,256]{3,2,1,0:T(8,128)(2,1)} %get-tuple-element.57), channel_id=1, source_target_pairs={{0,1},{1,0},{2,3},{3,2},{4,5},{5,4},{6,7},{7,6},{8,9},{9,8},{10,11... | collective-permute-start | bytes 1572872 | tf_op jit(solution)/shard_map/ppermute | solution.py:83
  199.3 29.9 %collective-permute-start.22 = (bf16[8,4,32,256]{3,2,1,0:T(8,128)(2,1)}, bf16[8,4,32,256]{3,2,1,0:T(8,128)(2,1)S(1)}, u32[]{:S(2)}, u32[]{:S(2)}) collective-permute-start(bf16[8,4,32,256]{3,2,1,0:T(8,128)(2,1)} %get-tuple-element.76), channel_id=1, source_target_pairs={{0,4},{4,0},{8,12},{12,8},{16,20},{20,16},{24,28},{28,24},{1,5},{5... | collective-permute-start | bytes 1572872 | tf_op jit(solution)/shard_map/ppermute | solution.py:83
  200.8 40.5 %collective-permute-start.23 = (bf16[8,4,32,256]{3,2,1,0:T(8,128)(2,1)}, bf16[8,4,32,256]{3,2,1,0:T(8,128)(2,1)S(1)}, u32[]{:S(2)}, u32[]{:S(2)}) collective-permute-start(bf16[8,4,32,256]{3,2,1,0:T(8,128)(2,1)} %add_convert_fusion.3), channel_id=1, source_target_pairs={{0,2},{1,3},{2,0},{3,1},{4,6},{5,7},{6,4},{7,5},{8,10},{9,11},{10,... | collective-permute-start | bytes 1572872 | tf_op jit(solution)/shard_map/ppermute | solution.py:83
  244.0 42.8 %all-to-all-start.6 = ((bf16[8,3,4,32,256]{4,3,2,1,0:T(8,128)(2,1)}), bf16[8,3,4,32,256]{4,3,2,1,0:T(8,128)(2,1)}, u32[]{:S(2)}, u32[]{:S(2)}) async-start(bf16[8,3,4,32,256]{4,3,2,1,0:T(8,128)(2,1)} %pad_maximum_fusion.2), calls=%async_computation.6 | async-start | bytes 3145728 | tf_op jit(solution)/shard_map/all_to_all | solution.py:87
  (18 other events, 104.2 us)

commit v15 on v12

--- a/solution.py
+++ b/solution.py
@@ -421,7 +421,7 @@
     there = add(mid_keep[1, 1], after(xor_permute(mid_sends[3], 1), own_far))
     here = add(mid_keep[0, 1], xor_permute(mid_sends[1], 1))
     near = add(mid_keep[1, 0], xor_permute(mid_sends[2], 1))
-    part, half = 3 * ndp // 8, ndp // 2
+    part, half = ndp // 4, ndp // 2
     own_first = add(own_near[:part], xor_permute(own_far[:part], 2))
     far_first = add(here[:half], xor_permute(there[:half], 1, "dp"))
     gin = after(gin.reshape(ndp * nb, -1, BLK), out, far_first, own_first)

time: 288 us -> 289 us (level)
    unnamed x40 -> x44, local copies, waits for them, and re-layouts: 12.6 us -> 12.6 us
where the time goes in v15:
time: 289 us; the launch traced here: 288 us
  waiting for transfers between devices  155 us (54%)
  starting transfers between devices  52 us (18%)
  Pallas kernels  40 us (14%)
  local copies, waits for them, and re-layouts  26.7 us (9%)
  other arithmetic  13.7 us (5%)
    ppermute x26, waiting for transfers between devices, xor_permute(): lax.ppermute(x, axis, [(i, i ^ mask) for i in range(lax.axis_size(axis))])  94.6 us
    all_to_all x7, waiting for transfers between devices, exchange(): return lax.all_to_all(x, axes, split_axis=0, concat_axis=0, tiled=True)  60 us
    pallas_call x2, Pallas kernels, on_chip(): pl.pallas_call(kernel, out_shape=[jax.ShapeDtypeStruct(shape, jnp.bfloat1...  34.5 us
    all_to_all x7, starting transfers between devices, exchange(): return lax.all_to_all(x, axes, split_axis=0, concat_axis=0, tiled=True)  33.4 us
    ppermute x26, starting transfers between devices, xor_permute(): lax.ppermute(x, axis, [(i, i ^ mask) for i in range(lax.axis_size(axis))])  18.6 us
    unnamed x44, local copies, waits for them, and re-layouts  12.6 us
  transfers between devices with their start and end apart: 33, of which 19 were waited for; matrix products, arithmetic and copies ran while one was open for 12% of the time, Pallas kernels for 12%

profile of v15, /device:TPU:0, one launch (start us, length us, event | category | flops | bytes accessed | tf_op | source)
XLA Modules:
  0.0 288.0 jit_solution(17873806755073459136)
XLA Ops:
  0.6 2.3 shard_map.109
  3.0 7.4 %all-to-all-start = ((bf16[8,6,32,256]{3,2,1,0:T(8,128)(2,1)}), bf16[8,6,32,256]{3,2,1,0:T(8,128)(2,1)S(1)}, u32[]{:S(2)}, u32[]{:S(2)}) async-start(bf16[8,6,32,256]{3,2,1,0:T(8,128)(2,1)} %shard_map.109), calls=%async_computation | async-start | bytes 1572864 | tf_op jit(solution)/shard_map/all_to_all | solution.py:87
  11.6 19.0 %all-to-all-done = bf16[8,6,32,256]{3,2,1,0:T(8,128)(2,1)S(1)} async-done(((bf16[8,6,32,256]{3,2,1,0:T(8,128)(2,1)}), bf16[8,6,32,256]{3,2,1,0:T(8,128)(2,1)S(1)}, u32[]{:S(2)}, u32[]{:S(2)}) %all-to-all-start) | async-done | bytes 786464 | tf_op jit(solution)/shard_map/all_to_all | solution.py:87
  30.6 3.6 %all-to-all-start.1 = ((bf16[8,2,3,32,256]{4,3,2,1,0:T(8,128)(2,1)}), bf16[8,2,3,32,256]{4,3,2,1,0:T(8,128)(2,1)S(1)}, u32[]{:S(2)}, u32[]{:S(2)}) async-start(bf16[8,2,3,32,256]{4,3,2,1,0:T(8,128)(2,1)} %pad_maximum_fusion.3), calls=%async_computation.1 | async-start | bytes 1572864 | tf_op jit(solution)/shard_map/all_to_all | solution.py:87
  35.0 2.0 collective-permute-start.1
  44.9 11.0 %collective-permute-done.2.refs_2_.refs_4_ = bf16[8,2,32,256]{3,2,1,0:T(8,128)(2,1)} collective-permute-done((bf16[8,2,32,256]{3,2,1,0:T(8,128)(2,1)}, bf16[8,2,32,256]{3,2,1,0:T(8,128)(2,1)}, u32[]{:S(2)}, u32[]{:S(2)}) %collective-permute-start.2) | collective-permute-done | bytes 262176 | tf_op jit(solution)/shard_map/ppermute | solution.py:83
  57.3 4.6 %all-to-all-start.2 = ((bf16[32,96,256]{2,1,0:T(8,128)(2,1)}), bf16[32,96,256]{2,1,0:T(8,128)(2,1)S(1)}, u32[]{:S(2)}, u32[]{:S(2)}) async-start(bf16[32,96,256]{2,1,0:T(8,128)(2,1)} %pad_maximum_fusion), calls=%async_computation.2 | async-start | bytes 3145728 | tf_op jit(solution)/shard_map/all_to_all | solution.py:87
  61.9 1.8 collective-permute-start.6
  71.3 2.4 pad_maximum_fusion.1
  73.7 16.6 %collective-permute-done.11.refs_14_.refs_16_ = bf16[8,4,32,256]{3,2,1,0:T(8,128)(2,1)} collective-permute-done((bf16[8,4,32,256]{3,2,1,0:T(8,128)(2,1)}, bf16[8,4,32,256]{3,2,1,0:T(8,128)(2,1)}, u32[]{:S(2)}, u32[]{:S(2)}) %collective-permute-start.11) | collective-permute-done | bytes 524320 | tf_op jit(solution)/shard_map/ppermute | solution.py:83
  90.3 8.2 %collective-permute-done.6.refs_6_.refs_8_ = bf16[8,2,3,32,256]{4,3,2,1,0:T(8,128)(2,1)} collective-permute-done((bf16[8,2,3,32,256]{4,3,2,1,0:T(8,128)(2,1)}, bf16[8,2,3,32,256]{4,3,2,1,0:T(8,128)(2,1)}, u32[]{:S(2)}, u32[]{:S(2)}) %collective-permute-start.6) | collective-permute-done | bytes 786464 | tf_op jit(solution)/shard_map/ppermute | solution.py:83
  100.9 3.8 %all-to-all-start.4 = ((bf16[32,96,256]{2,1,0:T(8,128)(2,1)}), bf16[32,96,256]{2,1,0:T(8,128)(2,1)S(1)}, u32[]{:S(2)}, u32[]{:S(2)}) async-start(bf16[32,96,256]{2,1,0:T(8,128)(2,1)} %pad_maximum_fusion.1), calls=%async_computation.4 | async-start | bytes 3145728 | tf_op jit(solution)/shard_map/all_to_all | solution.py:87
  105.9 1.8 collective-permute-done.3.refs_1_.refs_3_
  108.9 1.9 collective-permute-done.10.refs_13_.refs_15_
  113.5 17.3 %shard_map.110 = (bf16[8,4,96,256]{3,2,1,0:T(8,128)(2,1)}, bf16[2,4,4,64,512]{4,3,2,1,0:T(8,128)(2,1)}, bf16[2,4,256,512]{3,2,1,0:T(8,128)(2,1)}, bf16[2,4,256,5...) custom-call(s32[2]{0:T(128)} %pad_add_fusion.seat_ref, ...), custom_call_target="tpu_custom_call" | custom-call | flops 3221225472 | bytes 24117252 | tf_op jit(solution)/shard_map/pallas_call | solution.py:356
  130.8 11.6 %all-to-all-done.4 = bf16[32,96,256]{2,1,0:T(8,128)(2,1)S(1)} async-done(((bf16[32,96,256]{2,1,0:T(8,128)(2,1)}), bf16[32,96,256]{2,1,0:T(8,128)(2,1)S(1)}, u32[]{:S(2)}, u32[]{:S(2)}) %all-to-all-start.4) | async-done | bytes 1572896 | tf_op jit(solution)/shard_map/all_to_all | solution.py:87
  143.5 4.0 %all-to-all-start.3 = ((bf16[32,96,256]{2,1,0:T(8,128)(2,1)}), bf16[32,96,256]{2,1,0:T(8,128)(2,1)S(1)}, u32[]{:S(2)}, u32[]{:S(2)}) async-start(bf16[32,96,256]{2,1,0:T(8,128)(2,1)} %bitcast.86), calls=%async_computation.3 | async-start | bytes 3145728 | tf_op jit(solution)/shard_map/all_to_all | solution.py:87
  147.5 17.3 %shard_map.111 = (bf16[8,4,96,256]{3,2,1,0:T(8,128)(2,1)}, bf16[2,8,2,4,32,256]{5,4,3,2,1,0:T(8,128)(2,1)}, bf16[8,2,4,32,256]{4,3,2,1,0:T(8,128)(2,1)}, bf16[8,...) custom-call(s32[2]{0:T(128)} %pad_add_fusion.seat_ref, ...), custom_call_target="tpu_custom_call" | custom-call | flops 6442450944 | bytes 34078724 | tf_op jit(solution)/shard_map/pallas_call | solution.py:356
  169.2 2.6 fusion
  171.9 1.8 collective-permute-start.18
  177.5 4.5 %collective-permute-done.18 = bf16[2,2,4,32,256]{4,3,2,1,0:T(8,128)(2,1)S(1)} collective-permute-done((bf16[2,2,4,32,256]{4,3,2,1,0:T(8,128)(2,1)S(1)}, bf16[2,2,4,32,256]{4,3,2,1,0:T(8,128)(2,1)S(1)}, u32[]{:S(2)}, u32[]{:S(2)}) %collective-permute-start.18) | collective-permute-done | bytes 262176 | tf_op jit(solution)/shard_map/ppermute | solution.py:83
  182.0 3.7 %collective-permute-done.16 = bf16[4,4,32,256]{3,2,1,0:T(8,128)(2,1)S(1)} collective-permute-done((bf16[4,4,32,256]{3,2,1,0:T(8,128)(2,1)S(1)}, bf16[4,4,32,256]{3,2,1,0:T(8,128)(2,1)S(1)}, u32[]{:S(2)}, u32[]{:S(2)}) %collective-permute-start.16) | collective-permute-done | bytes 262176 | tf_op jit(solution)/shard_map/ppermute | solution.py:83
  186.5 4.6 %all-to-all-start.5 = ((bf16[32,96,256]{2,1,0:T(8,128)(2,1)}), bf16[32,96,256]{2,1,0:T(8,128)(2,1)S(1)}, u32[]{:S(2)}, u32[]{:S(2)}) async-start(bf16[32,96,256]{2,1,0:T(8,128)(2,1)} %bitcast.85), calls=%async_computation.5 | async-start | bytes 3145728 | tf_op jit(solution)/shard_map/all_to_all | solution.py:87
  191.1 1.8 collective-permute-start.24
  194.4 1.8 collective-permute-start.19
  196.5 16.7 %collective-permute-done.24 = bf16[4,4,32,256]{3,2,1,0:T(8,128)(2,1)S(1)} collective-permute-done((bf16[4,4,32,256]{3,2,1,0:T(8,128)(2,1)}, bf16[4,4,32,256]{3,2,1,0:T(8,128)(2,1)S(1)}, u32[]{:S(2)}, u32[]{:S(2)}) %collective-permute-start.24) | collective-permute-done | bytes 262176 | tf_op jit(solution)/shard_map/ppermute | solution.py:83
  213.9 19.9 %collective-permute-done.23 = bf16[4,4,32,256]{3,2,1,0:T(8,128)(2,1)S(1)} collective-permute-done((bf16[4,4,32,256]{3,2,1,0:T(8,128)(2,1)S(1)}, bf16[4,4,32,256]{3,2,1,0:T(8,128)(2,1)S(1)}, u32[]{:S(2)}, u32[]{:S(2)}) %collective-permute-start.23) | collective-permute-done | bytes 262176 | tf_op jit(solution)/shard_map/ppermute | solution.py:83
  233.8 5.1 %collective-permute-done.25 = bf16[4,4,32,256]{3,2,1,0:T(8,128)(2,1)S(1)} collective-permute-done((bf16[4,4,32,256]{3,2,1,0:T(8,128)(2,1)S(1)}, bf16[4,4,32,256]{3,2,1,0:T(8,128)(2,1)S(1)}, u32[]{:S(2)}, u32[]{:S(2)}) %collective-permute-start.25) | collective-permute-done | bytes 262176 | tf_op jit(solution)/shard_map/ppermute | solution.py:83
  242.0 5.5 %all-to-all-start.6 = ((bf16[8,3,4,32,256]{4,3,2,1,0:T(8,128)(2,1)}), bf16[8,3,4,32,256]{4,3,2,1,0:T(8,128)(2,1)}, u32[]{:S(2)}, u32[]{:S(2)}) async-start(bf16[8,3,4,32,256]{4,3,2,1,0:T(8,128)(2,1)} %pad_maximum_fusion.2), calls=%async_computation.6 | async-start | bytes 3145728 | tf_op jit(solution)/shard_map/all_to_all | solution.py:87
  250.4 2.6 copy.40
  256.7 28.1 %all-to-all-done.6.got_ref = bf16[8,3,4,32,256]{4,3,2,1,0:T(8,128)(2,1)} async-done(((bf16[8,3,4,32,256]{4,3,2,1,0:T(8,128)(2,1)}), bf16[8,3,4,32,256]{4,3,2,1,0:T(8,128)(2,1)}, u32[]{:S(2)}, u32[]{:S(2)}) %all-to-all-start.6) | async-done | bytes 1572896 | tf_op jit(solution)/shard_map/all_to_all | solution.py:87
  284.8 3.1 %shard_map.112 = (f32[12,32,512]{2,1,0:T(8,128)}, f32[24,32,256]{2,1,0:T(8,128)}, f32[24,32,256]{2,1,0:T(8,128)}, f32[12,64,256]{2,1,0:T(8,128)}) custom-call(bf16[8,3,4,32,256]{4,3,2,1,0:T(8,128)(2,1)} %all-to-all-done.6.got_ref), custom_call_target="tpu_custom_call" | custom-call | tf_op jit(solution)/shard_map/pallas_call | solution.py:438
  (125 shorter events, 48.4 us)
Async XLA Ops:
  3.0 27.6 %all-to-all-start = ((bf16[8,6,32,256]{3,2,1,0:T(8,128)(2,1)}), bf16[8,6,32,256]{3,2,1,0:T(8,128)(2,1)S(1)}, u32[]{:S(2)}, u32[]{:S(2)}) async-start(bf16[8,6,32,256]{3,2,1,0:T(8,128)(2,1)} %shard_map.109), calls=%async_computation | async-start | bytes 1572864 | tf_op jit(solution)/shard_map/all_to_all | solution.py:87
  30.6 25.9 %all-to-all-start.1 = ((bf16[8,2,3,32,256]{4,3,2,1,0:T(8,128)(2,1)}), bf16[8,2,3,32,256]{4,3,2,1,0:T(8,128)(2,1)S(1)}, u32[]{:S(2)}, u32[]{:S(2)}) async-start(bf16[8,2,3,32,256]{4,3,2,1,0:T(8,128)(2,1)} %pad_maximum_fusion.3), calls=%async_computation.1 | async-start | bytes 1572864 | tf_op jit(solution)/shard_map/all_to_all | solution.py:87
  35.0 21.5 %collective-permute-start.1 = (bf16[8,4,32,256]{3,2,1,0:T(8,128)(2,1)}, bf16[8,4,32,256]{3,2,1,0:T(8,128)(2,1)}, u32[]{:S(2)}, u32[]{:S(2)}) collective-permute-start(bf16[8,4,32,256]{3,2,1,0:T(8,128)(2,1)} %slice.143.refs_8_.refs_10_), channel_id=1, source_target_pairs={{0,4},{4,0},{8,12},{12,8},{16,20},{20,16},{24,28},{28,24},{1,5},{5... | collective-permute-start | bytes 1572872 | tf_op jit(solution)/shard_map/ppermute | solution.py:83
  37.0 19.4 %collective-permute-start = (bf16[8,4,32,256]{3,2,1,0:T(8,128)(2,1)}, bf16[8,4,32,256]{3,2,1,0:T(8,128)(2,1)}, u32[]{:S(2)}, u32[]{:S(2)}) collective-permute-start(bf16[8,4,32,256]{3,2,1,0:T(8,128)(2,1)} %slice.143.refs_8_.refs_10_), channel_id=1, source_target_pairs={{0,2},{1,3},{2,0},{3,1},{4,6},{5,7},{6,4},{7,5},{8,10},{9,11},{10,... | collective-permute-start | bytes 1572872 | tf_op jit(solution)/shard_map/ppermute | solution.py:83
  39.2 16.7 %collective-permute-start.2 = (bf16[8,2,32,256]{3,2,1,0:T(8,128)(2,1)}, bf16[8,2,32,256]{3,2,1,0:T(8,128)(2,1)}, u32[]{:S(2)}, u32[]{:S(2)}) collective-permute-start(bf16[8,2,32,256]{3,2,1,0:T(8,128)(2,1)} %slice.144.refs_0_.refs_2_), channel_id=1, source_target_pairs={{0,2},{1,3},{2,0},{3,1},{4,6},{5,7},{6,4},{7,5},{8,10},{9,11},{10,... | collective-permute-start | bytes 786440 | tf_op jit(solution)/shard_map/ppermute | solution.py:83
  57.3 42.5 %all-to-all-start.2 = ((bf16[32,96,256]{2,1,0:T(8,128)(2,1)}), bf16[32,96,256]{2,1,0:T(8,128)(2,1)S(1)}, u32[]{:S(2)}, u32[]{:S(2)}) async-start(bf16[32,96,256]{2,1,0:T(8,128)(2,1)} %pad_maximum_fusion), calls=%async_computation.2 | async-start | bytes 3145728 | tf_op jit(solution)/shard_map/all_to_all | solution.py:87
  61.9 36.7 %collective-permute-start.6 = (bf16[8,2,3,32,256]{4,3,2,1,0:T(8,128)(2,1)}, bf16[8,2,3,32,256]{4,3,2,1,0:T(8,128)(2,1)}, u32[]{:S(2)}, u32[]{:S(2)}) collective-permute-start(bf16[8,2,3,32,256]{4,3,2,1,0:T(8,128)(2,1)} %copy-done.7), channel_id=1, source_target_pairs={{0,2},{1,3},{2,0},{3,1},{4,6},{5,7},{6,4},{7,5},{8,10},{9,11},{10,... | collective-permute-start | bytes 2359304 | tf_op jit(solution)/shard_map/ppermute | solution.py:83
  63.7 26.6 %collective-permute-start.11 = (bf16[8,4,32,256]{3,2,1,0:T(8,128)(2,1)}, bf16[8,4,32,256]{3,2,1,0:T(8,128)(2,1)}, u32[]{:S(2)}, u32[]{:S(2)}) collective-permute-start(bf16[8,4,32,256]{3,2,1,0:T(8,128)(2,1)} %collective-permute-done.refs_10_.refs_12_), channel_id=1, source_target_pairs={{0,4},{4,0},{8,12},{12,8},{16,20},{20,16},{24,28},{28,24},{1,5},{5... | collective-permute-start | bytes 1572872 | tf_op jit(solution)/shard_map/ppermute | solution.py:83
  100.9 41.4 %all-to-all-start.4 = ((bf16[32,96,256]{2,1,0:T(8,128)(2,1)}), bf16[32,96,256]{2,1,0:T(8,128)(2,1)S(1)}, u32[]{:S(2)}, u32[]{:S(2)}) async-start(bf16[32,96,256]{2,1,0:T(8,128)(2,1)} %pad_maximum_fusion.1), calls=%async_computation.4 | async-start | bytes 3145728 | tf_op jit(solution)/shard_map/all_to_all | solution.py:87
  104.8 3.5 %collective-permute-start.8 = (bf16[8,4,32,256]{3,2,1,0:T(8,128)(2,1)}, bf16[8,4,32,256]{3,2,1,0:T(8,128)(2,1)}, u32[]{:S(2)}, u32[]{:S(2)}) collective-permute-start(bf16[8,4,32,256]{3,2,1,0:T(8,128)(2,1)} %slice.143.refs_8_.refs_10_), channel_id=1, source_target_pairs={{0,1},{1,0},{2,3},{3,2},{4,5},{5,4},{6,7},{7,6},{8,9},{9,8},{10,11... | collective-permute-start | bytes 1572872 | tf_op jit(solution)/shard_map/ppermute | solution.py:83
  104.9 2.8 collective-permute-start.3
  105.4 6.9 %collective-permute-start.5 = (bf16[8,2,3,32,256]{4,3,2,1,0:T(8,128)(2,1)}, bf16[8,2,3,32,256]{4,3,2,1,0:T(8,128)(2,1)S(1)}, u32[]{:S(2)}, u32[]{:S(2)}) collective-permute-start(bf16[8,2,3,32,256]{4,3,2,1,0:T(8,128)(2,1)} %copy-done.7), channel_id=1, source_target_pairs={{0,1},{1,0},{2,3},{3,2},{4,5},{5,4},{6,7},{7,6},{8,9},{9,8},{10,11... | collective-permute-start | bytes 2359304 | tf_op jit(solution)/shard_map/ppermute | solution.py:83
  105.9 6.5 %collective-permute-start.7 = (bf16[8,2,3,32,256]{4,3,2,1,0:T(8,128)(2,1)}, bf16[8,2,3,32,256]{4,3,2,1,0:T(8,128)(2,1)S(1)}, u32[]{:S(2)}, u32[]{:S(2)}) collective-permute-start(bf16[8,2,3,32,256]{4,3,2,1,0:T(8,128)(2,1)} %collective-permute-done.6.refs_6_.refs_8_), channel_id=1, source_target_pairs={{0,1},{1,0},{2,3},{3,2},{4,5},{5,4},{6,7},{7,6},{8,9},{9,8},{10,11... | collective-permute-start | bytes 2359304 | tf_op jit(solution)/shard_map/ppermute | solution.py:83
  107.7 3.1 %collective-permute-start.10 = (bf16[8,4,32,256]{3,2,1,0:T(8,128)(2,1)}, bf16[8,4,32,256]{3,2,1,0:T(8,128)(2,1)}, u32[]{:S(2)}, u32[]{:S(2)}) collective-permute-start(bf16[8,4,32,256]{3,2,1,0:T(8,128)(2,1)} %collective-permute-done.1.refs_12_.refs_14_), channel_id=1, source_target_pairs={{0,1},{1,0},{2,3},{3,2},{4,5},{5,4},{6,7},{7,6},{8,9},{9,8},{10,11... | collective-permute-start | bytes 1572872 | tf_op jit(solution)/shard_map/ppermute | solution.py:83
  107.9 3.7 %collective-permute-start.9 = (bf16[8,4,32,256]{3,2,1,0:T(8,128)(2,1)}, bf16[8,4,32,256]{3,2,1,0:T(8,128)(2,1)}, u32[]{:S(2)}, u32[]{:S(2)}) collective-permute-start(bf16[8,4,32,256]{3,2,1,0:T(8,128)(2,1)} %collective-permute-done.refs_10_.refs_12_), channel_id=1, source_target_pairs={{0,1},{1,0},{2,3},{3,2},{4,5},{5,4},{6,7},{7,6},{8,9},{9,8},{10,11... | collective-permute-start | bytes 1572872 | tf_op jit(solution)/shard_map/ppermute | solution.py:83
  108.2 4.1 %collective-permute-start.12 = (bf16[8,4,32,256]{3,2,1,0:T(8,128)(2,1)}, bf16[8,4,32,256]{3,2,1,0:T(8,128)(2,1)}, u32[]{:S(2)}, u32[]{:S(2)}) collective-permute-start(bf16[8,4,32,256]{3,2,1,0:T(8,128)(2,1)} %collective-permute-done.11.refs_14_.refs_16_), channel_id=1, source_target_pairs={{0,1},{1,0},{2,3},{3,2},{4,5},{5,4},{6,7},{7,6},{8,9},{9,8},{10,11... | collective-permute-start | bytes 1572872 | tf_op jit(solution)/shard_map/ppermute | solution.py:83
  143.5 43.0 %all-to-all-start.3 = ((bf16[32,96,256]{2,1,0:T(8,128)(2,1)}), bf16[32,96,256]{2,1,0:T(8,128)(2,1)S(1)}, u32[]{:S(2)}, u32[]{:S(2)}) async-start(bf16[32,96,256]{2,1,0:T(8,128)(2,1)} %bitcast.86), calls=%async_computation.3 | async-start | bytes 3145728 | tf_op jit(solution)/shard_map/all_to_all | solution.py:87
  164.7 2.9 %collective-permute-start.15 = (bf16[8,2,4,32,256]{4,3,2,1,0:T(8,128)(2,1)}, bf16[8,2,4,32,256]{4,3,2,1,0:T(8,128)(2,1)S(1)}, u32[]{:S(2)}, u32[]{:S(2)}) collective-permute-start(bf16[8,2,4,32,256]{4,3,2,1,0:T(8,128)(2,1)} %get-tuple-element.53), channel_id=1, source_target_pairs={{0,1},{1,0},{2,3},{3,2},{4,5},{5,4},{6,7},{7,6},{8,9},{9,8},{10,11... | collective-permute-start | bytes 3145736 | tf_op jit(solution)/shard_map/ppermute | solution.py:83
  165.1 4.1 %collective-permute-start.17 = (bf16[8,2,4,32,256]{4,3,2,1,0:T(8,128)(2,1)}, bf16[8,2,4,32,256]{4,3,2,1,0:T(8,128)(2,1)S(1)}, u32[]{:S(2)}, u32[]{:S(2)}) collective-permute-start(bf16[8,2,4,32,256]{4,3,2,1,0:T(8,128)(2,1)} %get-tuple-element.55), channel_id=1, source_target_pairs={{0,1},{1,0},{2,3},{3,2},{4,5},{5,4},{6,7},{7,6},{8,9},{9,8},{10,11... | collective-permute-start | bytes 3145736 | tf_op jit(solution)/shard_map/ppermute | solution.py:83
  165.3 6.6 %collective-permute-start.14 = (bf16[8,4,32,256]{3,2,1,0:T(8,128)(2,1)}, bf16[8,4,32,256]{3,2,1,0:T(8,128)(2,1)S(1)}, u32[]{:S(2)}, u32[]{:S(2)}) collective-permute-start(bf16[8,4,32,256]{3,2,1,0:T(8,128)(2,1)} %get-tuple-element.51), channel_id=1, source_target_pairs={{0,1},{1,0},{2,3},{3,2},{4,5},{5,4},{6,7},{7,6},{8,9},{9,8},{10,11... | collective-permute-start | bytes 1572872 | tf_op jit(solution)/shard_map/ppermute | solution.py:83
  165.6 8.2 %collective-permute-start.13 = (bf16[8,4,32,256]{3,2,1,0:T(8,128)(2,1)}, bf16[8,4,32,256]{3,2,1,0:T(8,128)(2,1)S(1)}, u32[]{:S(2)}, u32[]{:S(2)}) collective-permute-start(bf16[8,4,32,256]{3,2,1,0:T(8,128)(2,1)} %get-tuple-element.50), channel_id=1, source_target_pairs={{0,1},{1,0},{2,3},{3,2},{4,5},{5,4},{6,7},{7,6},{8,9},{9,8},{10,11... | collective-permute-start | bytes 1572872 | tf_op jit(solution)/shard_map/ppermute | solution.py:83
  165.8 7.9 %collective-permute-start.21 = (bf16[8,4,32,256]{3,2,1,0:T(8,128)(2,1)}, bf16[8,4,32,256]{3,2,1,0:T(8,128)(2,1)S(1)}, u32[]{:S(2)}, u32[]{:S(2)}) collective-permute-start(bf16[8,4,32,256]{3,2,1,0:T(8,128)(2,1)} %get-tuple-element.59), channel_id=1, source_target_pairs={{0,1},{1,0},{2,3},{3,2},{4,5},{5,4},{6,7},{7,6},{8,9},{9,8},{10,11... | collective-permute-start | bytes 1572872 | tf_op jit(solution)/shard_map/ppermute | solution.py:83
  171.9 10.1 %collective-permute-start.18 = (bf16[2,2,4,32,256]{4,3,2,1,0:T(8,128)(2,1)S(1)}, bf16[2,2,4,32,256]{4,3,2,1,0:T(8,128)(2,1)S(1)}, u32[]{:S(2)}, u32[]{:S(2)}) collective-permute-start(bf16[2,2,4,32,256]{4,3,2,1,0:T(8,128)(2,1)S(1)} %slice.153), channel_id=1, source_target_pairs={{0,2},{1,3},{2,0},{3,1},{4,6},{5,7},{6,4},{7,5},{8,10},{9,11},{10,... | collective-permute-start | bytes 786440 | tf_op jit(solution)/shard_map/ppermute | solution.py:83
  176.0 9.7 %collective-permute-start.16 = (bf16[4,4,32,256]{3,2,1,0:T(8,128)(2,1)S(1)}, bf16[4,4,32,256]{3,2,1,0:T(8,128)(2,1)S(1)}, u32[]{:S(2)}, u32[]{:S(2)}) collective-permute-start(bf16[4,4,32,256]{3,2,1,0:T(8,128)(2,1)S(1)} %get-tuple-element.88), channel_id=1, source_target_pairs={{0,4},{4,0},{8,12},{12,8},{16,20},{20,16},{24,28},{28,24},{1,5},{5... | collective-permute-start | bytes 786440 | tf_op jit(solution)/shard_map/ppermute | solution.py:83
  186.5 55.5 %all-to-all-start.5 = ((bf16[32,96,256]{2,1,0:T(8,128)(2,1)}), bf16[32,96,256]{2,1,0:T(8,128)(2,1)S(1)}, u32[]{:S(2)}, u32[]{:S(2)}) async-start(bf16[32,96,256]{2,1,0:T(8,128)(2,1)} %bitcast.85), calls=%async_computation.5 | async-start | bytes 3145728 | tf_op jit(solution)/shard_map/all_to_all | solution.py:87
  191.1 22.1 %collective-permute-start.24 = (bf16[4,4,32,256]{3,2,1,0:T(8,128)(2,1)}, bf16[4,4,32,256]{3,2,1,0:T(8,128)(2,1)S(1)}, u32[]{:S(2)}, u32[]{:S(2)}) collective-permute-start(bf16[4,4,32,256]{3,2,1,0:T(8,128)(2,1)} %get-tuple-element.60), channel_id=1, source_target_pairs={{0,4},{4,0},{8,12},{12,8},{16,20},{20,16},{24,28},{28,24},{1,5},{5... | collective-permute-start | bytes 786440 | tf_op jit(solution)/shard_map/ppermute | solution.py:83
  193.0 20.9 %collective-permute-start.20 = (bf16[8,4,32,256]{3,2,1,0:T(8,128)(2,1)}, bf16[8,4,32,256]{3,2,1,0:T(8,128)(2,1)S(1)}, u32[]{:S(2)}, u32[]{:S(2)}) collective-permute-start(bf16[8,4,32,256]{3,2,1,0:T(8,128)(2,1)} %get-tuple-element.58), channel_id=1, source_target_pairs={{0,1},{1,0},{2,3},{3,2},{4,5},{5,4},{6,7},{7,6},{8,9},{9,8},{10,11... | collective-permute-start | bytes 1572872 | tf_op jit(solution)/shard_map/ppermute | solution.py:83
  193.0 40.8 %collective-permute-start.22 = (bf16[8,4,32,256]{3,2,1,0:T(8,128)(2,1)}, bf16[8,4,32,256]{3,2,1,0:T(8,128)(2,1)S(1)}, u32[]{:S(2)}, u32[]{:S(2)}) collective-permute-start(bf16[8,4,32,256]{3,2,1,0:T(8,128)(2,1)} %get-tuple-element.78), channel_id=1, source_target_pairs={{0,4},{4,0},{8,12},{12,8},{16,20},{20,16},{24,28},{28,24},{1,5},{5... | collective-permute-start | bytes 1572872 | tf_op jit(solution)/shard_map/ppermute | solution.py:83
  194.4 45.9 %collective-permute-start.19 = (bf16[6,2,4,32,256]{4,3,2,1,0:T(8,128)(2,1)S(1)}, bf16[6,2,4,32,256]{4,3,2,1,0:T(8,128)(2,1)S(1)}, u32[]{:S(2)}, u32[]{:S(2)}) collective-permute-start(bf16[6,2,4,32,256]{4,3,2,1,0:T(8,128)(2,1)S(1)} %slice.159), channel_id=1, source_target_pairs={{0,2},{1,3},{2,0},{3,1},{4,6},{5,7},{6,4},{7,5},{8,10},{9,11},{10,... | collective-permute-start | bytes 2359304 | tf_op jit(solution)/shard_map/ppermute | solution.py:83
  196.3 37.5 %collective-permute-start.23 = (bf16[4,4,32,256]{3,2,1,0:T(8,128)(2,1)S(1)}, bf16[4,4,32,256]{3,2,1,0:T(8,128)(2,1)S(1)}, u32[]{:S(2)}, u32[]{:S(2)}) collective-permute-start(bf16[4,4,32,256]{3,2,1,0:T(8,128)(2,1)S(1)} %copy-done.18), channel_id=1, source_target_pairs={{0,2},{1,3},{2,0},{3,1},{4,6},{5,7},{6,4},{7,5},{8,10},{9,11},{10,... | collective-permute-start | bytes 786440 | tf_op jit(solution)/shard_map/ppermute | solution.py:83
  213.3 25.6 %collective-permute-start.25 = (bf16[4,4,32,256]{3,2,1,0:T(8,128)(2,1)S(1)}, bf16[4,4,32,256]{3,2,1,0:T(8,128)(2,1)S(1)}, u32[]{:S(2)}, u32[]{:S(2)}) collective-permute-start(bf16[4,4,32,256]{3,2,1,0:T(8,128)(2,1)S(1)} %add_convert_fusion.3), channel_id=1, source_target_pairs={{0,2},{1,3},{2,0},{3,1},{4,6},{5,7},{6,4},{7,5},{8,10},{9,11},{10,... | collective-permute-start | bytes 786440 | tf_op jit(solution)/shard_map/ppermute | solution.py:83
  242.0 42.8 %all-to-all-start.6 = ((bf16[8,3,4,32,256]{4,3,2,1,0:T(8,128)(2,1)}), bf16[8,3,4,32,256]{4,3,2,1,0:T(8,128)(2,1)}, u32[]{:S(2)}, u32[]{:S(2)}) async-start(bf16[8,3,4,32,256]{4,3,2,1,0:T(8,128)(2,1)} %pad_maximum_fusion.2), calls=%async_computation.6 | async-start | bytes 3145728 | tf_op jit(solution)/shard_map/all_to_all | solution.py:87
  (23 other events, 215.5 us)
